TPU v7x, 32 devices: a whole 2x2x4 slice. The times are simulated.
32 devices in a mesh: grp: 2 (over y), gx: 4 (over z), gy: 2 (over x), gz: 2 (over core).
Axes of the slice: x: 2, y: 2, z: 4, core: 2. Of those that a mesh axis runs over, the one named last changes fastest.
Arguments:
- pressure: float32 [64, 128, 256], P(('grp', 'gx'), 'gy', 'gz'), parts along dimension 0, may hold values from -3 to 3
- previous: float32 [64, 128, 256], P(('grp', 'gx'), 'gy', 'gz'), parts along dimension 0, may hold values from -3 to 3
- material: int32 [64, 128, 256], P(('grp', 'gx'), 'gy', 'gz'), parts along dimension 0, may hold values from 0 to 7
- stiffness: float32 [8], replicated, may hold values from 0.05 to 0.2
- density: float32 [8], replicated, may hold values from 1 to 2
- nonlinear: float32 [8], replicated, may hold values from 0.005 to 0.025
- lift_weight: float32 [4, 20], replicated, may hold values from -3 to 3
- lift_bias: float32 [20], replicated, may hold values from -3 to 3
- mode_weight: float32 [2, 8, 20, 20], replicated, may hold values from -2 to 2
- local_weight: bfloat16 [20, 20], replicated, may hold values from -1.25 to 1.25
Outputs:
- wave_field: float32 [64, 128, 256], P(('grp', 'gx'), 'gy', 'gz'), parts along dimension 0
- features: bfloat16 [64, 128, 20, 256], P(('grp', 'gx', 'gz'), 'gy'), parts along dimension 0
There are 2 independent parts, one for each index of `grp`. A program takes and returns all parts, laid end to end along the dimension named above; an argument that names none is the same for every part. Nothing has to cross between parts.
All inputs are finite; a program needn't handle non-finite values.
Results may differ from a plain program's by a relative error of at most 0.0079.
Values may be sent and summed in bfloat16 or wider, within the bound.
No kernel may reach another device: no remote copies, remote signals or barrier semaphores. Data moves between devices by JAX's collectives and lax.ppermute only.
A program may use at most 64 MiB of HBM per device.

v0:
```python
import math

import jax
import jax.numpy as jnp
from jax import lax
from jax.sharding import PartitionSpec as P

STEPS = 4


stencil_taps = (-205.0 / 72.0, 8.0 / 5.0, -1.0 / 5.0, 8.0 / 315.0, -1.0 / 560.0)


def extended(block, sides, width):
    for axis, dim in sides:
        count = lax.axis_size(axis)
        forward = [(i, i + 1) for i in range(count - 1)]
        backward = [(target, source) for source, target in forward]
        low = lax.ppermute(
            lax.slice_in_dim(block, block.shape[dim] - width, None, axis=dim), axis, forward
        )
        high = lax.ppermute(lax.slice_in_dim(block, 0, width, axis=dim), axis, backward)
        block = jnp.concatenate([low, block, high], axis=dim)
    return block


def shifted(padded, dimension, offset):
    starts = [4, 4, 4]
    starts[dimension] = 4 + offset
    limits = [starts[position] + padded.shape[position] - 8 for position in range(3)]
    return lax.slice(padded, starts, limits)


def laplace(padded, center):
    running = 3.0 * stencil_taps[0] * center
    for offset in range(1, 5):
        for dimension in range(3):
            running = running + stencil_taps[offset] * (
                shifted(padded, dimension, offset) + shifted(padded, dimension, -offset)
            )
    return running


def advance(padded, before, ratio_inner, bend_inner):
    center = shifted(padded, 0, 0)
    change = center - before
    updated = (
        2.0 * center - before + ratio_inner * laplace(padded, center) + bend_inner * change * change
    )
    return (updated, center)


def lookup(material, values):
    result = jnp.zeros(material.shape, jnp.float32)
    for material_id in range(values.shape[0]):
        result = result + jnp.where(material == material_id, values[material_id], 0.0)
    return result


def lift_features(pieces, lift_weight, lift_bias):
    running = lift_bias[None, :, None]
    for feature_id in range(4):
        running = (
            running + pieces[feature_id][:, :, None, :] * lift_weight[feature_id][None, :, None]
        )
    return running.astype(jnp.bfloat16)


def kept_modes(length, mode_count):
    position = jnp.arange(mode_count, dtype=jnp.int32)
    return jnp.where(position < mode_count // 2, position, length - mode_count + position)


def angle_of(source, target, length):
    product = source[:, None] * target[None, :] % length
    return 2.0 * math.pi / length * product.astype(jnp.float32)


def twiddle(source, target, length, direction):
    phases = angle_of(source, target, length)
    cosine = jnp.cos(phases)
    sine = direction * jnp.sin(phases)
    return jnp.stack([jnp.stack([cosine, sine], -1), jnp.stack([-sine, cosine], -1)], 1).astype(
        jnp.bfloat16
    )


def depth_table(length, mode_count):
    phases = angle_of(
        jnp.arange(length, dtype=jnp.int32), jnp.arange(mode_count, dtype=jnp.int32), length
    )
    return jnp.stack([jnp.cos(phases), -jnp.sin(phases)], -1).astype(jnp.bfloat16)


def depth_inverse(length, mode_count):
    phases = angle_of(
        jnp.arange(mode_count, dtype=jnp.int32), jnp.arange(length, dtype=jnp.int32), length
    )
    weight = jnp.where(jnp.arange(mode_count, dtype=jnp.int32) == 0, 1.0, 2.0)[:, None]
    return jnp.stack([weight * jnp.cos(phases), -weight * jnp.sin(phases)], 1).astype(jnp.bfloat16)


def mode_mixer(mode_weight):
    real_part = mode_weight[0]
    imag_part = mode_weight[1]
    return jnp.stack(
        [jnp.stack([real_part, imag_part], -1), jnp.stack([-imag_part, real_part], -1)], 2
    )


def per_device(
    pressure,
    previous,
    material,
    stiffness,
    density,
    nonlinear,
    lift_weight,
    lift_bias,
    mode_weight,
    local_weight,
):
    brick_x, brick_y, brick_z = pressure.shape
    cycle_count = lax.axis_size("gx")
    column_count = lax.axis_size("gy")
    core_count = lax.axis_size("gz")
    total_x = brick_x * cycle_count
    total_y = brick_y * column_count
    total_z = brick_z * core_count
    modes_x = total_x // 4
    modes_y = total_y // 4
    modes_z = total_z // 4
    channels = lift_bias.shape[0]
    slab_rows = brick_x // core_count
    depth_local = modes_z // column_count
    mode_rows = modes_y // (cycle_count * core_count)
    flat_width = channels * depth_local
    ratio_field = lookup(material, stiffness / density)
    bend_field = lookup(material, nonlinear)
    current, before = (pressure, previous)
    for repeat in range(STEPS):
        padded = extended(current, (("gx", 0), ("gy", 1), ("gz", 2)), 4)
        current, before = advance(padded, before, ratio_field, bend_field)
    stiff_field = lookup(material, stiffness)
    dense_field = lookup(material, density)
    brick_lifted = lift_features(
        [current, before, stiff_field, dense_field], lift_weight, lift_bias
    )
    lifted = lax.all_to_all(brick_lifted, "gz", split_axis=0, concat_axis=3, tiled=True)
    forward_depth = (
        depth_table(total_z, modes_z)
        .reshape(total_z, column_count, depth_local, 2)
        .transpose(0, 3, 1, 2)
    )
    depth_modes = jnp.einsum(
        "xycz,zqgk->gqxyck", lifted, forward_depth, preferred_element_type=jnp.float32
    )
    depth_modes = depth_modes.astype(jnp.bfloat16).reshape(
        column_count, 2, slab_rows, brick_y, flat_width
    )
    kept_second = kept_modes(total_y, modes_y)
    kept_first = kept_modes(total_x, modes_x)
    second_table = twiddle(jnp.arange(total_y, dtype=jnp.int32), kept_second, total_y, -1.0)
    result = jnp.einsum(
        "pxyf,ypmq->qxmf",
        lax.all_to_all(depth_modes, "gy", split_axis=0, concat_axis=3, tiled=True)[0],
        second_table,
        preferred_element_type=jnp.float32,
    )
    second_modes = result.astype(jnp.bfloat16)
    position = jnp.arange(total_x, dtype=jnp.int32)
    gathered = lax.all_to_all(second_modes, ("gx", "gz"), split_axis=2, concat_axis=1, tiled=True)
    first_table = twiddle(position, kept_first, total_x, -1.0)
    first_modes = jnp.einsum(
        "pxmf,xpnq->qnmf", gathered, first_table, preferred_element_type=jnp.float32
    )
    mixed = jnp.einsum(
        "pnmck,ncpoq->qnmok",
        first_modes.reshape(2, modes_x, mode_rows, channels, depth_local),
        mode_mixer(mode_weight),
        precision=lax.Precision.HIGHEST,
        preferred_element_type=jnp.float32,
    )
    mixed = mixed.astype(jnp.bfloat16).reshape(2, modes_x, mode_rows, flat_width)
    first_inverse = twiddle(kept_first, jnp.arange(total_x, dtype=jnp.int32), total_x, 1.0)
    back_first = jnp.einsum(
        "pnmf,npxq->qxmf", mixed, first_inverse, preferred_element_type=jnp.float32
    )
    back_first = back_first.astype(jnp.bfloat16)
    returned = lax.all_to_all(back_first, ("gx", "gz"), split_axis=1, concat_axis=2, tiled=True)
    second_inverse = twiddle(kept_second, jnp.arange(total_y, dtype=jnp.int32), total_y, 1.0)
    back_second = jnp.einsum(
        "pxmf,mpyq->qxyf", returned, second_inverse, preferred_element_type=jnp.float32
    )
    back_second = back_second.astype(jnp.bfloat16).reshape(2, slab_rows, total_y, 1, flat_width)
    homeward = lax.all_to_all(back_second, "gy", split_axis=2, concat_axis=3, tiled=True)
    inverse_depth = depth_inverse(total_z, modes_z).reshape(column_count, depth_local, 2, total_z)
    spectral = jnp.einsum(
        "qxygck,gkqz->xycz",
        homeward.reshape(2, slab_rows, brick_y, column_count, channels, depth_local),
        inverse_depth,
        preferred_element_type=jnp.float32,
    )
    spectral = spectral * (1.0 / (total_x * total_y * total_z))
    local_part = jnp.einsum(
        "xycz,co->xyoz", lifted, local_weight, preferred_element_type=jnp.float32
    )
    features = jax.nn.gelu(local_part + spectral, approximate=True).astype(jnp.bfloat16)
    return (current, features)


def solution(mesh):
    placed = (
        P(("grp", "gx"), "gy", "gz"),
        P(("grp", "gx"), "gy", "gz"),
        P(("grp", "gx"), "gy", "gz"),
        P(),
        P(),
        P(),
        P(),
        P(),
        P(),
        P(),
    )
    return jax.shard_map(
        per_device,
        mesh=mesh,
        in_specs=placed,
        out_specs=(P(("grp", "gx"), "gy", "gz"), P(("grp", "gx", "gz"), "gy", None, None)),
        check_vma=False,
    )
```

profile of v0, /device:TPU:0, one launch (start us, length us, event | category | flops | bytes accessed | tf_op | source)
XLA Modules:
  0.0 280.5 jit_solution(4089035976900976864)
XLA Ops:
  3.1 5.6 %collective-permute-start.1 = (f32[4,64,128]{2,0,1:T(4,128)S(1)}, f32[4,64,128]{2,0,1:T(4,128)S(1)}, u32[]{:S(2)}, u32[]{:S(2)}) collective-permute-start(f32[4,64,128]{2,0,1:T(4,128)S(1)} %get-tuple-element.59), channel_id=1, source_target_pairs={{0,4},{4,8},{8,12},{1,5},{5,9},{9,13},{2,6},{6,10},{10,14},{3,7},{... | collective-permute-start | bytes 393224 | tf_op jit(solution)/shard_map/ppermute | solution.py:19
  12.6 7.3 %select_add_fusion.1 = (f32[8,64,128]{2,0,1:T(8,128)}, pred[8,64,128]{2,0,1:T(8,128)(4,1)S(1)}, pred[8,64,128]{2,0,1:T(8,128)(4,1)S(1)}, pred[8,64,128]{2,0,1:T(...) fusion(f32[]{:T(128)} %bitcast.25, f32[]{:T(128)} %bitcast.24, ...), kind=kLoop, calls=%fused_computation.320 | loop fusion | flops 1507328 | bytes 1048608 | tf_op jit(solution)/shard_map/add | solution.py:56
  19.9 6.0 %select_add_fusion = f32[8,64,128]{2,0,1:T(8,128)} fusion(pred[8,64,128]{2,0,1:T(8,128)(4,1)S(1)} %get-tuple-element.22, pred[8,64,128]{2,0,1:T(8,128)(4,1)S(1)} %get-tuple-element.21, pred[8,64,128]{2,0,1:T(8,128)(4,1)S(1)} %get-tuple-element.20, pred[8,64,128]{2,0,1:T(8,128)(4,1)S(1)} %get-tuple-element.19, pred[8,64,128]{2,0,1:T(8,128)(4,1)S(1)} %get-tuple-element.18, ...), kind=kLoop, calls=%fused_computation.319 | loop fusion | flops 983040 | bytes 786464 | tf_op jit(solution)/shard_map/add | solution.py:56
  28.2 3.8 %collective-permute-start.3 = (f32[16,4,128]{2,0,1:T(8,128)S(1)}, f32[16,4,128]{2,0,1:T(8,128)S(1)}, u32[]{:S(2)}, u32[]{:S(2)}) collective-permute-start(f32[16,4,128]{2,0,1:T(8,128)S(1)} %get-tuple-element.48), channel_id=1, source_target_pairs={{0,2},{1,3},{4,6},{5,7},{8,10},{9,11},{12,14},{13,15},{16,18},{17,... | collective-permute-start | bytes 98312 | tf_op jit(solution)/shard_map/ppermute | solution.py:19
  33.7 4.2 %collective-permute-done.2 = f32[16,4,128]{2,0,1:T(8,128)S(1)} collective-permute-done((f32[16,4,128]{2,0,1:T(8,128)S(1)}, f32[16,4,128]{2,0,1:T(8,128)S(1)}, u32[]{:S(2)}, u32[]{:S(2)}) %collective-permute-start.2) | collective-permute-done | bytes 32800 | tf_op jit(solution)/shard_map/ppermute | solution.py:22
  44.8 15.5 %fusion.28 = (f32[8,64,128]{2,0,1:T(8,128)S(1)}, f32[8,64,128]{2,0,1:T(8,128)S(1)}, f32[8,64,128]{2,0,1:T(8,128)S(1)}) fusion(f32[8,64,128]{2,0,1:T(8,128)S(1)} %get-tuple-element.57, f32[4,64,128]{2,0,1:T(4,128)} %copy-done.2, f32[16,72,4]{2,0,1:T(8,128)} %copy.275, f32[16,4,128]{2,0,1:T(8,128)} %copy-done.19, f32[16,4,128]{2,0,1:T(8,128)} %copy-done.18, ...), kind=kLoop, calls=%fused_computation.95 | loop fusion | flops 7798784 | bytes 5345344 | tf_op jit(solution)/shard_map/add | solution.py:48
  61.8 4.6 %collective-permute-start.7 = (f32[4,64,128]{2,0,1:T(4,128)S(1)}, f32[4,64,128]{2,0,1:T(4,128)S(1)}, u32[]{:S(2)}, u32[]{:S(2)}) collective-permute-start(f32[4,64,128]{2,0,1:T(4,128)S(1)} %get-tuple-element.55), channel_id=1, source_target_pairs={{0,4},{4,8},{8,12},{1,5},{5,9},{9,13},{2,6},{6,10},{10,14},{3,7},{... | collective-permute-start | bytes 393224 | tf_op jit(solution)/shard_map/ppermute | solution.py:19
  72.3 4.2 %collective-permute-done.8 = f32[16,4,128]{2,0,1:T(8,128)S(1)} collective-permute-done((f32[16,4,128]{2,0,1:T(8,128)S(1)}, f32[16,4,128]{2,0,1:T(8,128)S(1)}, u32[]{:S(2)}, u32[]{:S(2)}) %collective-permute-start.8) | collective-permute-done | bytes 32800 | tf_op jit(solution)/shard_map/ppermute | solution.py:22
  83.3 3.9 %fusion.29 = f32[8,64,128]{2,0,1:T(8,128)S(1)} fusion(f32[8,64,128]{2,0,1:T(8,128)S(1)} %get-tuple-element.25, f32[8,64,128]{2,0,1:T(8,128)S(1)} %get-tuple-element.24, f32[8,64,128]{2,0,1:T(8,128)S(1)} %get-tuple-element.23, f32[4,64,128]{2,0,1:T(4,128)S(1)} %collective-permute-done.7, f32[4,64,128]{2,0,1:T(4,128)S(1)} %collective-permute-done.6, ...), kind=kLoop, calls=%fused_computation.96 | loop fusion | flops 6094848 | bytes 3772416 | tf_op jit(solution)/shard_map/add | solution.py:48
  88.6 5.0 %collective-permute-start.13 = (f32[4,64,128]{2,0,1:T(4,128)S(1)}, f32[4,64,128]{2,0,1:T(4,128)S(1)}, u32[]{:S(2)}, u32[]{:S(2)}) collective-permute-start(f32[4,64,128]{2,0,1:T(4,128)S(1)} %get-tuple-element.53), channel_id=1, source_target_pairs={{0,4},{4,8},{8,12},{1,5},{5,9},{9,13},{2,6},{6,10},{10,14},{3,7},{... | collective-permute-start | bytes 393224 | tf_op jit(solution)/shard_map/ppermute | solution.py:19
  100.2 3.9 %collective-permute-done.14 = f32[16,4,128]{2,0,1:T(8,128)S(1)} collective-permute-done((f32[16,4,128]{2,0,1:T(8,128)S(1)}, f32[16,4,128]{2,0,1:T(8,128)S(1)}, u32[]{:S(2)}, u32[]{:S(2)}) %collective-permute-start.14) | collective-permute-done | bytes 32800 | tf_op jit(solution)/shard_map/ppermute | solution.py:22
  111.5 3.9 %fusion.30 = f32[8,64,128]{2,0,1:T(8,128)S(1)} fusion(f32[8,64,128]{2,0,1:T(8,128)S(1)} %get-tuple-element.25, f32[8,64,128]{2,0,1:T(8,128)S(1)} %get-tuple-element.24, f32[8,64,128]{2,0,1:T(8,128)S(1)} %fusion.29, f32[4,64,128]{2,0,1:T(4,128)S(1)} %collective-permute-done.13, f32[4,64,128]{2,0,1:T(4,128)S(1)} %collective-permute-done.12, ...), kind=kLoop, calls=%fused_computation.97 | loop fusion | flops 6094848 | bytes 3772416 | tf_op jit(solution)/shard_map/add | solution.py:48
  116.7 5.0 %collective-permute-start.19 = (f32[4,64,128]{2,0,1:T(4,128)S(1)}, f32[4,64,128]{2,0,1:T(4,128)S(1)}, u32[]{:S(2)}, u32[]{:S(2)}) collective-permute-start(f32[4,64,128]{2,0,1:T(4,128)S(1)} %get-tuple-element.51), channel_id=1, source_target_pairs={{0,4},{4,8},{8,12},{1,5},{5,9},{9,13},{2,6},{6,10},{10,14},{3,7},{... | collective-permute-start | bytes 393224 | tf_op jit(solution)/shard_map/ppermute | solution.py:19
  146.8 3.9 %fusion.31 = f32[8,64,128]{2,0,1:T(8,128)S(1)} fusion(f32[8,64,128]{2,0,1:T(8,128)S(1)} %get-tuple-element.25, f32[8,64,128]{2,0,1:T(8,128)S(1)} %get-tuple-element.24, f32[8,64,128]{2,0,1:T(8,128)S(1)} %fusion.30, f32[4,64,128]{2,0,1:T(4,128)S(1)} %collective-permute-done.19, f32[4,64,128]{2,0,1:T(4,128)S(1)} %collective-permute-done.18, ...), kind=kLoop, calls=%fused_computation.98 | loop fusion | flops 6094848 | bytes 3772416 | tf_op jit(solution)/shard_map/add | solution.py:48
  150.8 2.4 add_convert_fusion
  153.2 5.8 %all_to_all.84 = bf16[8,64,20,128]{3,1,2,0:T(8,128)(2,1)S(1)} all-to-all(bf16[8,64,20,128]{3,1,2,0:T(8,128)(2,1)S(1)} %add_convert_fusion), channel_id=1, replica_groups=mesh['grp'=2,'gx'=4,'gy'=2,'gz'=2] {'gz'}, dimensions={0} | all-to-all | bytes 5242880 | tf_op jit(solution)/shard_map/all_to_all | solution.py:149
  159.1 4.2 %copy.296 = bf16[4,64,20,2,128]{4,3,1,2,0:T(2,128)(2,1)} copy(bf16[4,64,20,2,128]{4,1,2,0,3:T(8,128)(2,1)S(1)} %bitcast.218) | data formatting | bytes 5242880 | tf_op jit(solution)/shard_map/all_to_all | solution.py:149
  163.3 5.3 %reshape.773 = bf16[4,64,20,256,1,1]{3,1,2,0,4,5:T(8,128)(2,1)} reshape(bf16[4,64,20,2,128]{4,3,1,2,0:T(2,128)(2,1)} %copy.296) | data formatting | bytes 5242880 | tf_op jit(solution)/shard_map/all_to_all | solution.py:149
  168.6 4.8 %fusion.15 = bf16[2,2,32,4,64,20]{4,2,5,3,1,0:T(8,128)(2,1)} fusion(bf16[4,64,20,256,1,1]{3,1,2,0,4,5:T(8,128)(2,1)} %reshape.773, bf16[256,2,32,1]{0,2,1,3:T(8,128)(2,1)S(1)} %copy-done.25, bf16[256,2,32,1]{0,2,1,3:T(8,128)(2,1)S(1)} %copy-done.24), kind=kOutput, calls=%fused_computation.19 | convolution fusion | flops 336330752 | bytes 3997696 | tf_op jit(solution)/shard_map/xycz,zqgk->gqxyck/dot_general | solution.py:155
  173.4 3.9 %copy.306 = bf16[2,2,4,64,640]{4,3,2,1,0:T(8,128)(2,1)} copy(bf16[2,2,4,64,640]{3,4,2,0,1:T(8,128)(2,1)} %bitcast.221) | data formatting | bytes 2621440 | tf_op jit(solution)/shard_map/reshape | solution.py:158
  177.3 4.6 %all-to-all-start.1 = ((bf16[2,2,4,64,640]{4,3,2,1,0:T(8,128)(2,1)}), bf16[2,2,4,64,640]{4,3,2,1,0:T(8,128)(2,1)}, u32[]{:S(2)}, u32[]{:S(2)}) async-start(bf16[2,2,4,64,640]{4,3,2,1,0:T(8,128)(2,1)} %copy.306), calls=%async_computation.1 | async-start | bytes 2621440 | tf_op jit(solution)/shard_map/all_to_all | solution.py:166
  182.3 17.7 %all-to-all-done.1 = bf16[2,2,4,64,640]{4,3,2,1,0:T(8,128)(2,1)} async-done(((bf16[2,2,4,64,640]{4,3,2,1,0:T(8,128)(2,1)}), bf16[2,2,4,64,640]{4,3,2,1,0:T(8,128)(2,1)}, u32[]{:S(2)}, u32[]{:S(2)}) %all-to-all-start.1) | async-done | bytes 1310752 | tf_op jit(solution)/shard_map/all_to_all | solution.py:166
  202.7 6.1 %all-to-all-start.2 = ((bf16[2,4,32,640]{3,1,0,2:T(4,128)(2,1)}), bf16[2,4,32,640]{3,1,0,2:T(4,128)(2,1)S(1)}, u32[]{:S(2)}, u32[]{:S(2)}) async-start(bf16[2,4,32,640]{3,1,0,2:T(4,128)(2,1)} %copy.308), calls=%async_computation.2 | async-start | bytes 655360 | tf_op jit(solution)/shard_map/all_to_all | solution.py:172
  209.6 10.3 %all-to-all-done.2 = bf16[2,4,32,640]{3,1,0,2:T(4,128)(2,1)S(1)} async-done(((bf16[2,4,32,640]{3,1,0,2:T(4,128)(2,1)}), bf16[2,4,32,640]{3,1,0,2:T(4,128)(2,1)S(1)}, u32[]{:S(2)}, u32[]{:S(2)}) %all-to-all-start.2) | async-done | bytes 327712 | tf_op jit(solution)/shard_map/all_to_all | solution.py:172
  222.2 2.6 fusion.22
  227.2 3.4 %all-to-all-start.3 = ((bf16[2,32,4,640]{3,2,0,1:T(4,128)(2,1)}), bf16[2,32,4,640]{3,2,0,1:T(4,128)(2,1)S(1)}, u32[]{:S(2)}, u32[]{:S(2)}) async-start(bf16[2,32,4,640]{3,2,0,1:T(4,128)(2,1)} %copy.313), calls=%async_computation.3 | async-start | bytes 655360 | tf_op jit(solution)/shard_map/all_to_all | solution.py:190
  230.9 10.9 %all-to-all-done.3 = bf16[2,32,4,640]{3,2,0,1:T(4,128)(2,1)S(1)} async-done(((bf16[2,32,4,640]{3,2,0,1:T(4,128)(2,1)}), bf16[2,32,4,640]{3,2,0,1:T(4,128)(2,1)S(1)}, u32[]{:S(2)}, u32[]{:S(2)}) %all-to-all-start.3) | async-done | bytes 327712 | tf_op jit(solution)/shard_map/all_to_all | solution.py:190
  244.6 4.5 %all-to-all-start.4 = ((bf16[2,4,128,1,640]{4,1,0,3,2:T(4,128)(2,1)}), bf16[2,4,128,1,640]{4,1,0,3,2:T(4,128)(2,1)}, u32[]{:S(2)}, u32[]{:S(2)}) async-start(bf16[2,4,128,1,640]{4,1,0,3,2:T(4,128)(2,1)} %copy.315), calls=%async_computation.4 | async-start | bytes 2621440 | tf_op jit(solution)/shard_map/all_to_all | solution.py:196
  251.4 13.9 %all-to-all-done.4 = bf16[2,4,128,1,640]{4,1,0,3,2:T(4,128)(2,1)} async-done(((bf16[2,4,128,1,640]{4,1,0,3,2:T(4,128)(2,1)}), bf16[2,4,128,1,640]{4,1,0,3,2:T(4,128)(2,1)}, u32[]{:S(2)}, u32[]{:S(2)}) %all-to-all-start.4) | async-done | bytes 1310752 | tf_op jit(solution)/shard_map/all_to_all | solution.py:196
  265.4 2.5 copy.316
  267.9 3.0 %copy.317 = bf16[2,4,64,2,1,640]{2,5,3,1,0,4:T(8,128)(2,1)S(1)} copy(bf16[2,4,64,2,1,640]{5,2,3,1,0,4:T(8,128)(2,1)} %bitcast.223) | data formatting | bytes 2621440 | tf_op jit(solution)/shard_map/all_to_all | solution.py:196
  272.7 5.6 %fusion.7 = bf16[4,64,20,256]{3,2,1,0:T(8,128)(2,1)S(1)} fusion(f32[4,64,20,256]{3,1,2,0:T(8,128)S(1)} %convolution_bitcast_fusion, bf16[4,64,20,256]{3,1,2,0:T(8,128)(2,1)S(1)} %bitcast.224, bf16[20,20]{1,0:T(8,128)(2,1)S(1)} %copy-done), kind=kOutput, calls=%fused_computation.8 | convolution fusion | flops 66846720 | bytes 10486560 | tf_op jit(solution)/shard_map/xycz,co->xyoz/dot_general | solution.py:205
  (186 shorter events, 90.4 us)
Async XLA Ops:
  0.6 271.3 %copy-start = (bf16[20,20]{1,0:T(8,128)(2,1)S(1)}, bf16[20,20]{1,0:T(8,128)(2,1)}, u32[]{:S(2)}) copy-start(bf16[20,20]{1,0:T(8,128)(2,1)} %param.19) | copy-start | bytes 2404
  1.8 26.4 %collective-permute-start = (f32[4,64,128]{2,0,1:T(4,128)S(1)}, f32[4,64,128]{2,0,1:T(4,128)S(1)}, u32[]{:S(2)}, u32[]{:S(2)}) collective-permute-start(f32[4,64,128]{2,0,1:T(4,128)S(1)} %get-tuple-element.58), channel_id=1, source_target_pairs={{4,0},{8,4},{12,8},{5,1},{9,5},{13,9},{6,2},{10,6},{14,10},{7,3},{... | collective-permute-start | bytes 393224 | tf_op jit(solution)/shard_map/ppermute | solution.py:22
  3.1 25.1 %collective-permute-start.1 = (f32[4,64,128]{2,0,1:T(4,128)S(1)}, f32[4,64,128]{2,0,1:T(4,128)S(1)}, u32[]{:S(2)}, u32[]{:S(2)}) collective-permute-start(f32[4,64,128]{2,0,1:T(4,128)S(1)} %get-tuple-element.59), channel_id=1, source_target_pairs={{0,4},{4,8},{8,12},{1,5},{5,9},{9,13},{2,6},{6,10},{10,14},{3,7},{... | collective-permute-start | bytes 393224 | tf_op jit(solution)/shard_map/ppermute | solution.py:19
  28.2 5.4 %collective-permute-start.3 = (f32[16,4,128]{2,0,1:T(8,128)S(1)}, f32[16,4,128]{2,0,1:T(8,128)S(1)}, u32[]{:S(2)}, u32[]{:S(2)}) collective-permute-start(f32[16,4,128]{2,0,1:T(8,128)S(1)} %get-tuple-element.48), channel_id=1, source_target_pairs={{0,2},{1,3},{4,6},{5,7},{8,10},{9,11},{12,14},{13,15},{16,18},{17,... | collective-permute-start | bytes 98312 | tf_op jit(solution)/shard_map/ppermute | solution.py:19
  32.1 5.8 %collective-permute-start.2 = (f32[16,4,128]{2,0,1:T(8,128)S(1)}, f32[16,4,128]{2,0,1:T(8,128)S(1)}, u32[]{:S(2)}, u32[]{:S(2)}) collective-permute-start(f32[16,4,128]{2,0,1:T(8,128)S(1)} %get-tuple-element.49), channel_id=1, source_target_pairs={{2,0},{3,1},{6,4},{7,5},{10,8},{11,9},{14,12},{15,13},{18,16},{19,... | collective-permute-start | bytes 98312 | tf_op jit(solution)/shard_map/ppermute | solution.py:22
  38.9 4.7 %collective-permute-start.5 = (f32[16,72,4]{1,0,2:T(8,128)S(1)}, f32[16,72,4]{1,0,2:T(8,128)S(1)}, u32[]{:S(2)}, u32[]{:S(2)}) collective-permute-start(f32[16,72,4]{1,0,2:T(8,128)S(1)} %copy.274), channel_id=1, source_target_pairs={{0,1},{2,3},{4,5},{6,7},{8,9},{10,11},{12,13},{14,15},{16,17},{18,... | collective-permute-start | bytes 55304 | tf_op jit(solution)/shard_map/ppermute | solution.py:19
  40.2 3.1 %collective-permute-start.4 = (f32[16,72,4]{1,0,2:T(8,128)S(1)}, f32[16,72,4]{1,0,2:T(8,128)S(1)}, u32[]{:S(2)}, u32[]{:S(2)}) collective-permute-start(f32[16,72,4]{1,0,2:T(8,128)S(1)} %copy.272), channel_id=1, source_target_pairs={{1,0},{3,2},{5,4},{7,6},{9,8},{11,10},{13,12},{15,14},{17,16},{19,... | collective-permute-start | bytes 55304 | tf_op jit(solution)/shard_map/ppermute | solution.py:22
  60.4 7.6 %collective-permute-start.6 = (f32[4,64,128]{2,0,1:T(4,128)S(1)}, f32[4,64,128]{2,0,1:T(4,128)S(1)}, u32[]{:S(2)}, u32[]{:S(2)}) collective-permute-start(f32[4,64,128]{2,0,1:T(4,128)S(1)} %get-tuple-element.54), channel_id=1, source_target_pairs={{4,0},{8,4},{12,8},{5,1},{9,5},{13,9},{6,2},{10,6},{14,10},{7,3},{... | collective-permute-start | bytes 393224 | tf_op jit(solution)/shard_map/ppermute | solution.py:22
  61.8 7.3 %collective-permute-start.7 = (f32[4,64,128]{2,0,1:T(4,128)S(1)}, f32[4,64,128]{2,0,1:T(4,128)S(1)}, u32[]{:S(2)}, u32[]{:S(2)}) collective-permute-start(f32[4,64,128]{2,0,1:T(4,128)S(1)} %get-tuple-element.55), channel_id=1, source_target_pairs={{0,4},{4,8},{8,12},{1,5},{5,9},{9,13},{2,6},{6,10},{10,14},{3,7},{... | collective-permute-start | bytes 393224 | tf_op jit(solution)/shard_map/ppermute | solution.py:19
  69.1 3.2 %collective-permute-start.9 = (f32[16,4,128]{2,0,1:T(8,128)S(1)}, f32[16,4,128]{2,0,1:T(8,128)S(1)}, u32[]{:S(2)}, u32[]{:S(2)}) collective-permute-start(f32[16,4,128]{2,0,1:T(8,128)S(1)} %get-tuple-element.44), channel_id=1, source_target_pairs={{0,2},{1,3},{4,6},{5,7},{8,10},{9,11},{12,14},{13,15},{16,18},{17,... | collective-permute-start | bytes 98312 | tf_op jit(solution)/shard_map/ppermute | solution.py:19
  70.8 5.8 %collective-permute-start.8 = (f32[16,4,128]{2,0,1:T(8,128)S(1)}, f32[16,4,128]{2,0,1:T(8,128)S(1)}, u32[]{:S(2)}, u32[]{:S(2)}) collective-permute-start(f32[16,4,128]{2,0,1:T(8,128)S(1)} %get-tuple-element.45), channel_id=1, source_target_pairs={{2,0},{3,1},{6,4},{7,5},{10,8},{11,9},{14,12},{15,13},{18,16},{19,... | collective-permute-start | bytes 98312 | tf_op jit(solution)/shard_map/ppermute | solution.py:22
  77.5 4.7 %collective-permute-start.11 = (f32[16,72,4]{1,0,2:T(8,128)S(1)}, f32[16,72,4]{1,0,2:T(8,128)S(1)}, u32[]{:S(2)}, u32[]{:S(2)}) collective-permute-start(f32[16,72,4]{1,0,2:T(8,128)S(1)} %copy.281), channel_id=1, source_target_pairs={{0,1},{2,3},{4,5},{6,7},{8,9},{10,11},{12,13},{14,15},{16,17},{18,... | collective-permute-start | bytes 55304 | tf_op jit(solution)/shard_map/ppermute | solution.py:19
  78.8 3.1 %collective-permute-start.10 = (f32[16,72,4]{1,0,2:T(8,128)S(1)}, f32[16,72,4]{1,0,2:T(8,128)S(1)}, u32[]{:S(2)}, u32[]{:S(2)}) collective-permute-start(f32[16,72,4]{1,0,2:T(8,128)S(1)} %copy.279), channel_id=1, source_target_pairs={{1,0},{3,2},{5,4},{7,6},{9,8},{11,10},{13,12},{15,14},{17,16},{19,... | collective-permute-start | bytes 55304 | tf_op jit(solution)/shard_map/ppermute | solution.py:22
  87.3 8.2 %collective-permute-start.12 = (f32[4,64,128]{2,0,1:T(4,128)S(1)}, f32[4,64,128]{2,0,1:T(4,128)S(1)}, u32[]{:S(2)}, u32[]{:S(2)}) collective-permute-start(f32[4,64,128]{2,0,1:T(4,128)S(1)} %get-tuple-element.52), channel_id=1, source_target_pairs={{4,0},{8,4},{12,8},{5,1},{9,5},{13,9},{6,2},{10,6},{14,10},{7,3},{... | collective-permute-start | bytes 393224 | tf_op jit(solution)/shard_map/ppermute | solution.py:22
  88.6 8.1 %collective-permute-start.13 = (f32[4,64,128]{2,0,1:T(4,128)S(1)}, f32[4,64,128]{2,0,1:T(4,128)S(1)}, u32[]{:S(2)}, u32[]{:S(2)}) collective-permute-start(f32[4,64,128]{2,0,1:T(4,128)S(1)} %get-tuple-element.53), channel_id=1, source_target_pairs={{0,4},{4,8},{8,12},{1,5},{5,9},{9,13},{2,6},{6,10},{10,14},{3,7},{... | collective-permute-start | bytes 393224 | tf_op jit(solution)/shard_map/ppermute | solution.py:19
  96.7 3.5 %collective-permute-start.15 = (f32[16,4,128]{2,0,1:T(8,128)S(1)}, f32[16,4,128]{2,0,1:T(8,128)S(1)}, u32[]{:S(2)}, u32[]{:S(2)}) collective-permute-start(f32[16,4,128]{2,0,1:T(8,128)S(1)} %get-tuple-element.40), channel_id=1, source_target_pairs={{0,2},{1,3},{4,6},{5,7},{8,10},{9,11},{12,14},{13,15},{16,18},{17,... | collective-permute-start | bytes 98312 | tf_op jit(solution)/shard_map/ppermute | solution.py:19
  98.3 5.8 %collective-permute-start.14 = (f32[16,4,128]{2,0,1:T(8,128)S(1)}, f32[16,4,128]{2,0,1:T(8,128)S(1)}, u32[]{:S(2)}, u32[]{:S(2)}) collective-permute-start(f32[16,4,128]{2,0,1:T(8,128)S(1)} %get-tuple-element.41), channel_id=1, source_target_pairs={{2,0},{3,1},{6,4},{7,5},{10,8},{11,9},{14,12},{15,13},{18,16},{19,... | collective-permute-start | bytes 98312 | tf_op jit(solution)/shard_map/ppermute | solution.py:22
  105.6 4.7 %collective-permute-start.17 = (f32[16,72,4]{1,0,2:T(8,128)}, f32[16,72,4]{1,0,2:T(8,128)S(1)}, u32[]{:S(2)}, u32[]{:S(2)}) collective-permute-start(f32[16,72,4]{1,0,2:T(8,128)} %copy.286), channel_id=1, source_target_pairs={{0,1},{2,3},{4,5},{6,7},{8,9},{10,11},{12,13},{14,15},{16,17},{18,... | collective-permute-start | bytes 55304 | tf_op jit(solution)/shard_map/ppermute | solution.py:19
  106.9 3.1 %collective-permute-start.16 = (f32[16,72,4]{1,0,2:T(8,128)S(1)}, f32[16,72,4]{1,0,2:T(8,128)S(1)}, u32[]{:S(2)}, u32[]{:S(2)}) collective-permute-start(f32[16,72,4]{1,0,2:T(8,128)S(1)} %copy.284), channel_id=1, source_target_pairs={{1,0},{3,2},{5,4},{7,6},{9,8},{11,10},{13,12},{15,14},{17,16},{19,... | collective-permute-start | bytes 55304 | tf_op jit(solution)/shard_map/ppermute | solution.py:22
  115.4 8.2 %collective-permute-start.18 = (f32[4,64,128]{2,0,1:T(4,128)S(1)}, f32[4,64,128]{2,0,1:T(4,128)S(1)}, u32[]{:S(2)}, u32[]{:S(2)}) collective-permute-start(f32[4,64,128]{2,0,1:T(4,128)S(1)} %get-tuple-element.50), channel_id=1, source_target_pairs={{4,0},{8,4},{12,8},{5,1},{9,5},{13,9},{6,2},{10,6},{14,10},{7,3},{... | collective-permute-start | bytes 393224 | tf_op jit(solution)/shard_map/ppermute | solution.py:22
  116.7 8.1 %collective-permute-start.19 = (f32[4,64,128]{2,0,1:T(4,128)S(1)}, f32[4,64,128]{2,0,1:T(4,128)S(1)}, u32[]{:S(2)}, u32[]{:S(2)}) collective-permute-start(f32[4,64,128]{2,0,1:T(4,128)S(1)} %get-tuple-element.51), channel_id=1, source_target_pairs={{0,4},{4,8},{8,12},{1,5},{5,9},{9,13},{2,6},{6,10},{10,14},{3,7},{... | collective-permute-start | bytes 393224 | tf_op jit(solution)/shard_map/ppermute | solution.py:19
  124.8 10.3 %collective-permute-start.21 = (f32[16,4,128]{2,0,1:T(8,128)S(1)}, f32[16,4,128]{2,0,1:T(8,128)S(1)}, u32[]{:S(2)}, u32[]{:S(2)}) collective-permute-start(f32[16,4,128]{2,0,1:T(8,128)S(1)} %get-tuple-element.36), channel_id=1, source_target_pairs={{0,2},{1,3},{4,6},{5,7},{8,10},{9,11},{12,14},{13,15},{16,18},{17,... | collective-permute-start | bytes 98312 | tf_op jit(solution)/shard_map/ppermute | solution.py:19
  126.5 8.7 %collective-permute-start.20 = (f32[16,4,128]{2,0,1:T(8,128)S(1)}, f32[16,4,128]{2,0,1:T(8,128)S(1)}, u32[]{:S(2)}, u32[]{:S(2)}) collective-permute-start(f32[16,4,128]{2,0,1:T(8,128)S(1)} %get-tuple-element.37), channel_id=1, source_target_pairs={{2,0},{3,1},{6,4},{7,5},{10,8},{11,9},{14,12},{15,13},{18,16},{19,... | collective-permute-start | bytes 98312 | tf_op jit(solution)/shard_map/ppermute | solution.py:22
  138.5 6.4 %collective-permute-start.23 = (f32[16,72,4]{1,0,2:T(8,128)}, f32[16,72,4]{1,0,2:T(8,128)}, u32[]{:S(2)}, u32[]{:S(2)}) collective-permute-start(f32[16,72,4]{1,0,2:T(8,128)} %copy.290), channel_id=1, source_target_pairs={{0,1},{2,3},{4,5},{6,7},{8,9},{10,11},{12,13},{14,15},{16,17},{18,... | collective-permute-start | bytes 55304 | tf_op jit(solution)/shard_map/ppermute | solution.py:19
  140.4 3.4 %collective-permute-start.22 = (f32[16,72,4]{1,0,2:T(8,128)}, f32[16,72,4]{1,0,2:T(8,128)}, u32[]{:S(2)}, u32[]{:S(2)}) collective-permute-start(f32[16,72,4]{1,0,2:T(8,128)} %copy.288), channel_id=1, source_target_pairs={{1,0},{3,2},{5,4},{7,6},{9,8},{11,10},{13,12},{15,14},{17,16},{19,... | collective-permute-start | bytes 55304 | tf_op jit(solution)/shard_map/ppermute | solution.py:22
  173.4 35.4 %copy-start.8 = (f32[1,8,20,20]{2,3,1,0:T(8,128)S(1)}, f32[1,8,20,20]{2,3,1,0:T(8,128)}, u32[]{:S(2)}) copy-start(f32[1,8,20,20]{2,3,1,0:T(8,128)} %copy.348) | copy-start | bytes 38404
  177.3 31.5 %copy-start.17 = (f32[1,8,20,20]{2,3,1,0:T(8,128)S(1)}, f32[1,8,20,20]{2,3,1,0:T(8,128)}, u32[]{:S(2)}) copy-start(f32[1,8,20,20]{2,3,1,0:T(8,128)} %copy.347) | copy-start | bytes 38404
  177.3 22.6 %all-to-all-start.1 = ((bf16[2,2,4,64,640]{4,3,2,1,0:T(8,128)(2,1)}), bf16[2,2,4,64,640]{4,3,2,1,0:T(8,128)(2,1)}, u32[]{:S(2)}, u32[]{:S(2)}) async-start(bf16[2,2,4,64,640]{4,3,2,1,0:T(8,128)(2,1)} %copy.306), calls=%async_computation.1 | async-start | bytes 2621440 | tf_op jit(solution)/shard_map/all_to_all | solution.py:166
  201.4 29.3 %copy-start.30 = (s32[32]{0:T(128)S(1)}, s32[32]{0:T(128)}, u32[]{:S(2)}) copy-start(s32[32]{0:T(128)} %compare_select_fusion.1) | copy-start | bytes 388
  202.7 17.2 %all-to-all-start.2 = ((bf16[2,4,32,640]{3,1,0,2:T(4,128)(2,1)}), bf16[2,4,32,640]{3,1,0,2:T(4,128)(2,1)S(1)}, u32[]{:S(2)}, u32[]{:S(2)}) async-start(bf16[2,4,32,640]{3,1,0,2:T(4,128)(2,1)} %copy.308), calls=%async_computation.2 | async-start | bytes 655360 | tf_op jit(solution)/shard_map/all_to_all | solution.py:172
  227.2 14.5 %all-to-all-start.3 = ((bf16[2,32,4,640]{3,2,0,1:T(4,128)(2,1)}), bf16[2,32,4,640]{3,2,0,1:T(4,128)(2,1)S(1)}, u32[]{:S(2)}, u32[]{:S(2)}) async-start(bf16[2,32,4,640]{3,2,0,1:T(4,128)(2,1)} %copy.313), calls=%async_computation.3 | async-start | bytes 655360 | tf_op jit(solution)/shard_map/all_to_all | solution.py:190
  244.6 20.8 %all-to-all-start.4 = ((bf16[2,4,128,1,640]{4,1,0,3,2:T(4,128)(2,1)}), bf16[2,4,128,1,640]{4,1,0,3,2:T(4,128)(2,1)}, u32[]{:S(2)}, u32[]{:S(2)}) async-start(bf16[2,4,128,1,640]{4,1,0,3,2:T(4,128)(2,1)} %copy.315), calls=%async_computation.4 | async-start | bytes 2621440 | tf_op jit(solution)/shard_map/all_to_all | solution.py:196
  (27 other events, 360.8 us)
where the time goes:
time: 283 us; the launch traced here: 281 us
  waiting for transfers between devices  76.8 us (27%)
  starting transfers between devices  69 us (24%)
  local copies, waits for them, and re-layouts  61.5 us (22%)
  other arithmetic  49.8 us (18%)
  matrix products  16 us (6%)
  blocking collectives  5.84 us (2%)
    ppermute x12, starting transfers between devices, extended(): lax.ppermute(lax.slice_in_dim(block, block.shape[dim] - width, None, axis...  34.6 us
    add x4, other arithmetic, advance(): 2.0 * center - before + ratio_inner * laplace(padded, center)  27.2 us
    ppermute x12, waiting for transfers between devices, extended(): lax.ppermute(lax.slice_in_dim(block, 0, width, axis=dim), axis, backward)  20 us
    all_to_all x1, waiting for transfers between devices, per_device(): lax.all_to_all(depth_modes, 'gy', split_axis=0, concat_axis=3, tiled=True)  17.7 us
    ppermute x12, starting transfers between devices, extended(): lax.ppermute(lax.slice_in_dim(block, 0, width, axis=dim), axis, backward)  15.8 us
    all_to_all x1, waiting for transfers between devices, per_device(): lax.all_to_all(back_second, 'gy', split_axis=2, concat_axis=3, tiled=True)  13.9 us
    add x2, other arithmetic, lookup(): result + jnp.where(material == material_id, values[material_id], 0.0)  13.2 us
    all_to_all x3, local copies, waits for them, and re-layouts, per_device(): lax.all_to_all(brick_lifted, 'gz', split_axis=0, concat_axis=3, tiled=True)  11.5 us
  transfers between devices with their start and end apart: 28, of which 18 were waited for; matrix products, arithmetic and copies ran while one was open for 14% of the time, Pallas kernels for 0%

commit v1 on v0

v1 whole, which is shorter than its diff:
```python
import math

import numpy as np
import jax
import jax.numpy as jnp
from jax import lax
from jax.experimental import pallas as pl
from jax.experimental.pallas import tpu as pltpu
from jax.sharding import PartitionSpec as P
import ml_dtypes

STEPS = 4
FIELDS = 4
REACH = 4
EDGE = 8
stencil_taps = (-205.0 / 72.0, 8.0 / 5.0, -1.0 / 5.0, 8.0 / 315.0, -1.0 / 560.0)
F32 = jnp.float32
BF16 = jnp.bfloat16
HIGHEST = lax.Precision.HIGHEST

VMEM = pl.BlockSpec(memory_space=pltpu.VMEM)
SMEM = pl.BlockSpec(memory_space=pltpu.SMEM)


def rounded(table):
    return table.astype(ml_dtypes.bfloat16)


def kept_modes(length, mode_count):
    position = np.arange(mode_count)
    return np.where(position < mode_count // 2, position, length - mode_count + position)


def cos_sin(source, target, length):
    product = (source[:, None] * target[None, :]) % length
    phases = np.float32(2.0 * math.pi / length) * product.astype(np.float32)
    return rounded(np.cos(phases)), rounded(np.sin(phases))


def call(body, outs, in_specs, scratch=(), flops=0, moved=0):
    return pl.pallas_call(
        body,
        out_shape=outs,
        in_specs=in_specs,
        out_specs=jax.tree.map(lambda _: VMEM, outs),
        scratch_shapes=list(scratch),
        compiler_params=pltpu.CompilerParams(vmem_limit_bytes=32 * 1024 * 1024),
        cost_estimate=pl.CostEstimate(flops=flops, bytes_accessed=moved, transcendentals=0),
    )


def high_low(value):
    high = value.astype(BF16)
    return high, (value - high.astype(F32)).astype(BF16)


def turned(value, half, sign):
    lane = lax.broadcasted_iota(jnp.int32, value.shape, value.ndim - 1)
    swapped = pltpu.roll(value, half, value.ndim - 1)
    return jnp.where(lane < half, sign * swapped, -sign * swapped)


def pack_body(where_ref, pressure, previous, material, send):
    core = where_ref[0] % 2
    rows = send.shape[1]
    start = (1 - core) * rows
    send[0] = pressure[pl.ds(start, rows)]
    send[1] = previous[pl.ds(start, rows)]
    send[2] = material[pl.ds(start, rows)].astype(F32)


def looked_up(material, table, entries):
    result = jnp.full(material.shape, table(0), F32)
    for entry in range(1, entries):
        result = jnp.where(material == float(entry), table(entry), result)
    return result


def edges(value_of, outs, row_parity, brick_y):
    for position, out in enumerate(outs):
        upper = row_parity == position
        out[...] = jnp.where(upper, value_of(brick_y - EDGE, brick_y), value_of(0, EDGE))


def assemble_body(where_ref, stiffness, density, nonlinear, pressure, previous, material, got, *outs):
    p_out, q_out, ratio, bend, stiff, dense = outs[:6]
    core = where_ref[0] % 2
    column = where_ref[1]
    rows, brick_y, half = got.shape[1:]
    start = core * rows
    entries = stiffness.shape[0]

    def whole(own, other):
        return jnp.concatenate(
            [jnp.where(core == 0, own, other), jnp.where(core == 0, other, own)], axis=-1
        )

    for row in range(rows):
        p_out[row] = whole(pressure[start + row], got[0, row])
        q_out[row] = whole(previous[start + row], got[1, row])
        cell = whole(material[start + row].astype(F32), got[2, row])
        ratio[row] = looked_up(cell, lambda e: stiffness[e] / density[e], entries)
        bend[row] = looked_up(cell, lambda e: nonlinear[e], entries)
        stiff[row] = looked_up(cell, lambda e: stiffness[e], entries)
        dense[row] = looked_up(cell, lambda e: density[e], entries)
    edges(lambda a, b: p_out[:, a:b, :], outs[6:], column % 2, brick_y)


def step_body(two_sided, last, where_ref, p_ref, q_ref, ratio, bend, mate, far, *rest):
    count = 2 if two_sided else 1
    halos = rest[:count]
    new_ref = rest[count]
    edge_outs = rest[count + 1 : -1]
    padded = rest[-1]
    core = where_ref[0] % 2
    parity = where_ref[1] % 2
    rows, brick_y, depth = p_ref.shape
    lane = lax.broadcasted_iota(jnp.int32, (brick_y, depth), 1)
    zero_edge = jnp.zeros((EDGE, depth), F32)

    def line(index):
        if 0 <= index < rows:
            return p_ref[index]
        if index < 0:
            return jnp.where(core == 0, far[index + rows], mate[index + rows])
        return jnp.where(core == 0, mate[index - rows], far[index - rows])

    for row in range(rows):
        first = halos[0][row]
        second = halos[1][row] if two_sided else zero_edge
        center = p_ref[row]
        padded[0:EDGE, :] = jnp.where(parity == 0, second, first)
        padded[EDGE : EDGE + brick_y, :] = center
        padded[EDGE + brick_y :, :] = jnp.where(parity == 0, first, second)
        total = (3.0 * stencil_taps[0]) * center
        for offset in range(1, REACH + 1):
            low, high = EDGE - offset, EDGE + offset
            pair = padded[low : low + brick_y, :] + padded[high : high + brick_y, :]
            pair = pair + (line(row - offset) + line(row + offset))
            pair = pair + jnp.where(lane >= offset, pltpu.roll(center, offset, 1), 0.0)
            pair = pair + jnp.where(
                lane < depth - offset, pltpu.roll(center, depth - offset, 1), 0.0
            )
            total = total + stencil_taps[offset] * pair
        change = center - q_ref[row]
        new_ref[row] = (center + change) + ratio[row] * total + bend[row] * change * change
    if last:
        half = depth // 2
        edge_outs[0][...] = jnp.where(core == 0, new_ref[:, :, half:], new_ref[:, :, :half])
    else:
        edges(lambda a, b: new_ref[:, a:b, :], edge_outs, parity, brick_y)


def spectrum_body(where_ref, twiddle_x, p_ref, q_ref, stiff, dense, table_z, table_y, keep, send, lines, grid):
    core = where_ref[0] % 2
    column = where_ref[1]
    rows, brick_y, depth = p_ref.shape
    modes_x, modes_y, width = keep.shape[1:]
    half = width // 2
    for field, ref in enumerate((p_ref, q_ref, stiff, dense)):
        for row in range(rows):
            high, low = high_low(ref[row])
            modes = jnp.dot(high, table_z[...], preferred_element_type=F32)
            modes = modes + jnp.dot(low, table_z[...], preferred_element_type=F32)
            back = turned(modes, half, 1.0)
            high, low = high_low(modes)
            back_high, back_low = high_low(back)
            lanes = slice((field * rows + row) * width, (field * rows + row + 1) * width)
            for index, part in enumerate((high, back_high, low, back_low)):
                lines[index * brick_y : (index + 1) * brick_y, lanes] = part
    grid[...] = jnp.dot(table_y[column], lines[...], preferred_element_type=F32)
    first = (where_ref[0] * rows) * modes_x * 2

    def sums(base_field, out, index):
        values, backs = [], []
        for row in range(rows):
            lanes = pl.ds(pl.multiple_of((base_field * rows + row) * width, width), width)
            value = grid[:, lanes]
            values.append(value)
            backs.append(turned(value, half, 1.0))

        @pl.loop(0, modes_x)
        def _(mode):
            total = jnp.zeros((modes_y, width), F32)
            for row in range(rows):
                at = first + (row * modes_x + mode) * 2
                total = total + twiddle_x[at] * values[row] + twiddle_x[at + 1] * backs[row]
            out[index, mode] = total

    for index in range(2):
        sums(core * 2 + index, keep, index)
        sums((1 - core) * 2 + index, send, index)


def prepare_body(where_ref, mode_ref, lift_ref, bias_ref, local_ref, spread_ref, place_ref, owner_ref, turn_ref, left, offset):
    block = where_ref[0]
    modes = spread_ref.shape[0]
    total = left.shape[1]
    half = place_ref.shape[1]
    spread = owner_ref[...]
    channels = lift_ref.shape[1]

    def dot(a, b, dims=((1,), (0,))):
        return lax.dot_general(a, b, (dims, ((), ())), precision=HIGHEST, preferred_element_type=F32)

    lifted = dot(dot(spread_ref[:, :channels], lift_ref[...], ((1,), (1,))), place_ref[...])
    same = spread_ref[:, channels : channels + half]
    lifted = lifted * same
    real = dot(dot(spread, mode_ref[0], ((1,), (1,))), lifted)
    imag = dot(dot(spread, mode_ref[1], ((1,), (1,))), lifted)
    cosine = turn_ref[block, 0]
    sine = turn_ref[block, 1]
    first = cosine * real - sine * imag
    second = -(cosine * imag + sine * real)
    left[...] = jnp.zeros_like(left)
    coupled = jnp.concatenate([first, second], axis=1).astype(BF16)
    width = 2 * half
    left[:, 0:width] = coupled
    left[:, width : 2 * width] = coupled
    constant = dot(spread, mode_ref[0, 0:channels, :], ((1,), (1,)))
    offset[...] = jnp.sum(constant * bias_ref[...], axis=1, keepdims=True)


def kernel_sizes(rows, channels, modes_x):
    padded_channels = -(-channels // 8) * 8
    height = rows * padded_channels
    coupled = FIELDS * modes_x * 2
    depth = -(-(2 * coupled + height) // 256) * 256
    return padded_channels, height, coupled, depth


def output_body(
    where_ref, mine, other, p_ref, q_ref, stiff, dense, lift_ref, left, offset, table_y, table_z,
    wave_ref, wave_other, features, wave_out, modes, right,
):
    step = pl.program_id(0)
    core = where_ref[0] % 2
    column = where_ref[1]
    modes_x, modes_y, width = mine.shape[1:]
    half = width // 2
    rows, group, depth = p_ref.shape
    brick_y = modes.shape[0]
    channels = features.shape[2]
    padded_channels = lift_ref.shape[0]
    height = rows * padded_channels
    coupled = FIELDS * modes_x

    @pl.when(step == 0)
    def _():
        chunk = 4
        left_y = table_y[column]
        for field in range(FIELDS):
            index = field % 2
            for start in range(0, modes_x, chunk):
                parts = [[], [], [], []]
                for mode in range(start, start + chunk):
                    own, far = mine[index, mode], other[index, mode]
                    value = jnp.where(core == field // 2, own, far)
                    high, low = high_low(value)
                    back_high, back_low = high_low(turned(value, half, -1.0))
                    for position, part in enumerate((high, back_high, low, back_low)):
                        parts[position].append(part)
                stacked = jnp.concatenate([jnp.concatenate(part, axis=1) for part in parts], axis=0)
                result = jnp.dot(left_y, stacked, preferred_element_type=F32)
                for mode in range(start, start + chunk):
                    lanes = slice((mode - start) * width, (mode - start + 1) * width)
                    modes[:, mode * FIELDS + field, :] = result[:, lanes]
        right[...] = jnp.zeros_like(right)
        z_half = depth // 2
        for row in range(rows):
            own = jnp.where(core == 0, wave_ref[row, :, :z_half], wave_ref[row, :, z_half:])
            wave_out[core * rows + row] = own
            wave_out[(1 - core) * rows + row] = wave_other[row]

    base = pl.multiple_of(step * group, group)
    high, low = high_low(modes[pl.ds(base, group)].reshape(group * coupled, width))
    waves = jnp.dot(high, table_z[...], preferred_element_type=F32)
    waves = waves + jnp.dot(low, table_z[...], preferred_element_type=F32)
    high, low = high_low(waves)
    weights = [lift_ref[:, index : index + 1] for index in range(FIELDS + 1)]
    for y in range(group):
        lines = slice(y * coupled, (y + 1) * coupled)
        position = 0
        for part in (high, low):
            for lanes in (slice(0, depth), slice(depth, 2 * depth)):
                right[y, position : position + coupled, :] = part[lines, lanes]
                position += coupled
        lifted = []
        for row in range(rows):
            total = jnp.broadcast_to(weights[FIELDS], (padded_channels, depth))
            for index, ref in enumerate((p_ref, q_ref, stiff, dense)):
                total = total + ref[row, y : y + 1, :] * weights[index]
            lifted.append(total)
        right[y, position : position + height, :] = jnp.concatenate(lifted, axis=0).astype(BF16)
        total = jnp.dot(left[...], right[y], preferred_element_type=F32) + offset[...]
        inner = math.sqrt(2.0 / math.pi) * (total + 0.044715 * (total * total * total))
        total = (0.5 * total) * (1.0 + jnp.tanh(inner))
        total = total.astype(BF16)
        for row in range(rows):
            at = row * padded_channels
            features[row, y] = total[at : at + channels]


def xor_pairs(count, distance):
    return [(index, index ^ distance) for index in range(count)]


def odd_pairs(count):
    pairs = [(index, index + 1) for index in range(1, count - 1, 2)]
    return pairs + [(target, source) for source, target in pairs]


def per_device(
    pressure,
    previous,
    material,
    stiffness,
    density,
    nonlinear,
    lift_weight,
    lift_bias,
    mode_weight,
    local_weight,
):
    brick_x, brick_y, brick_z = pressure.shape
    cycle_count = lax.axis_size("gx")
    column_count = lax.axis_size("gy")
    core_count = lax.axis_size("gz")
    total_x = brick_x * cycle_count
    total_y = brick_y * column_count
    total_z = brick_z * core_count
    modes_x = total_x // 4
    modes_y = total_y // 4
    modes_z = total_z // 4
    width = 2 * modes_z
    channels = lift_bias.shape[0]
    rows = brick_x // core_count
    assert core_count == 2 and rows >= REACH
    blocks = cycle_count * core_count
    padded_channels, height, coupled, right_depth = kernel_sizes(rows, channels, modes_x)
    two_sided = column_count > 2

    kept_first = kept_modes(total_x, modes_x)
    kept_second = kept_modes(total_y, modes_y)
    kept_third = np.arange(modes_z)
    cz, sz = cos_sin(np.arange(total_z), kept_third, total_z)
    forward_z = np.concatenate([cz, -sz], 1)
    weight = np.where(kept_third == 0, 1.0, 2.0) / (total_x * total_y * total_z)
    wc, ws = [rounded((t.astype(np.float32) * weight).T.astype(np.float32)) for t in (cz, sz)]
    inverse_z = np.concatenate(
        [np.concatenate([wc, ws], 1), np.concatenate([-ws.astype(np.float32), wc.astype(np.float32)], 1)], 0
    )
    inverse_z = rounded(inverse_z)
    cy, sy = cos_sin(kept_second, np.arange(total_y), total_y)
    cy3, sy3 = [t.reshape(modes_y, column_count, brick_y).transpose(1, 0, 2) for t in (cy, sy)]
    forward_y = np.concatenate([cy3, sy3, cy3, sy3], 2)
    cy3, sy3 = [t.transpose(0, 2, 1) for t in (cy3, sy3)]
    inverse_y = np.concatenate([cy3, sy3, cy3, sy3], 2)
    cx, sx = [t.astype(np.float32) for t in cos_sin(np.arange(total_x), kept_first, total_x)]
    twiddle_x = np.stack([cx, sx], -1).reshape(-1)
    owner = np.zeros((height, channels), np.float32)
    turn = np.zeros((blocks, 2, height, modes_x * FIELDS), np.float32)
    for row in range(rows):
        owner[row * padded_channels : row * padded_channels + channels] = np.eye(channels)
    for source, table in enumerate((cx, sx)):
        turn[:, source] = np.repeat(
            np.repeat(table.reshape(blocks, rows, modes_x), padded_channels, 1), FIELDS, 2
        )
    spread = np.tile(np.eye(channels, dtype=np.float32), (modes_x, 1))
    same = np.repeat(
        np.repeat(np.eye(modes_x, dtype=np.float32), channels, 0), FIELDS, 1
    )
    spread = np.concatenate([spread, same], 1)
    place = np.tile(np.eye(FIELDS, dtype=np.float32), (1, modes_x))

    core = lax.axis_index("gz")
    where = jnp.array([1, 0], jnp.int32) * (lax.axis_index("gx") * core_count + core) + jnp.array(
        [0, 1], jnp.int32
    ) * lax.axis_index("gy")

    def shape(*dims, dtype=F32):
        return jax.ShapeDtypeStruct(dims, dtype)

    cells = rows * brick_y * total_z
    field = shape(rows, brick_y, total_z)
    edge = [shape(rows, EDGE, total_z)] * (2 if two_sided else 1)
    half = shape(rows, brick_y, brick_z)

    send = call(pack_body, shape(3, rows, brick_y, brick_z), [SMEM] + [VMEM] * 3, moved=cells * 24)(
        where, pressure, previous, material
    )
    swap_core = xor_pairs(core_count, 1)
    got = lax.ppermute(send, "gz", swap_core)
    current, before, ratio, bend, stiff, dense, *edge_values = call(
        assemble_body, [field] * 6 + edge, [SMEM] * 4 + [VMEM] * 4, moved=cells * 36
    )(where, stiffness, density, nonlinear, pressure, previous, material, got)

    left, offset = call(
        prepare_body, [shape(height, right_depth, dtype=BF16), shape(height, 1)], [SMEM] + [VMEM] * 8
    )(
        where, mode_weight.reshape(2, modes_x * channels, channels), lift_weight,
        lift_bias.reshape(1, channels), local_weight, spread, place, owner, turn,
    )
    wide = jnp.zeros((rows, padded_channels, rows, padded_channels), BF16)
    small = jnp.pad(local_weight.T, ((0, padded_channels - channels),) * 2)
    wide = (np.eye(rows, dtype=ml_dtypes.bfloat16)[:, None, :, None] * small[None, :, None, :]).reshape(height, height)
    left = left.at[:, 2 * coupled : 2 * coupled + height].set(wide)
    lift_table = jnp.pad(
        jnp.concatenate([lift_weight, lift_bias[None]], 0).T, ((0, padded_channels - channels), (0, 0))
    )

    for repeat in range(STEPS):
        last = repeat == STEPS - 1
        far = lax.ppermute(current, ("gx", "gz"), odd_pairs(blocks))
        mate = lax.ppermute(current, "gz", swap_core)
        halos = [lax.ppermute(edge_values[0], "gy", xor_pairs(column_count, 1))]
        if two_sided:
            halos.append(lax.ppermute(edge_values[1], "gy", odd_pairs(column_count)))
        outs = [field] + ([half] if last else edge)
        body = lambda *refs, last=last: step_body(two_sided, last, *refs)
        new, *edge_values = call(
            body, outs, [SMEM] + [VMEM] * (6 + len(halos)),
            [pltpu.VMEM((brick_y + 2 * EDGE, total_z), F32)], flops=cells * 60, moved=cells * 28,
        )(where, current, before, ratio, bend, mate, far, *halos)
        current, before = new, current

    wave_other = lax.ppermute(edge_values[0], "gz", swap_core)
    part = shape(2, modes_x, modes_y, width)
    keep, send = call(
        spectrum_body, [part, part], [SMEM] * 2 + [VMEM] * 6,
        [pltpu.VMEM((4 * brick_y, FIELDS * rows * width), BF16), pltpu.VMEM((modes_y, FIELDS * rows * width), F32)],
        flops=cells * 2048, moved=cells * 32,
    )(where, twiddle_x, current, before, stiff, dense, forward_z, forward_y)
    total = keep + lax.ppermute(send, "gz", swap_core)
    for axis, count in (("gy", column_count), ("gx", cycle_count)):
        distance = 1
        while distance < count:
            total = total + lax.ppermute(total, axis, xor_pairs(count, distance))
            distance *= 2
    other = lax.ppermute(total, "gz", swap_core)

    group = 8
    whole = lambda array: pl.BlockSpec(array.shape, lambda i: (0,) * len(array.shape))
    slab = pl.BlockSpec((rows, group, total_z), lambda i: (0, i, 0))
    features, wave = pl.pallas_call(
        output_body,
        grid=(brick_y // group,),
        out_shape=[shape(rows, brick_y, channels, total_z, dtype=BF16), shape(*pressure.shape)],
        in_specs=[SMEM, whole(part), whole(part), slab, slab, slab, slab, whole(lift_table), whole(left),
                  whole(offset), whole(inverse_y), whole(inverse_z), whole(field), whole(half)],
        out_specs=[pl.BlockSpec((rows, group, channels, total_z), lambda i: (0, i, 0, 0)), whole(pressure)],
        scratch_shapes=[
            pltpu.VMEM((brick_y, FIELDS * modes_x, width), F32),
            pltpu.VMEM((group, right_depth, total_z), BF16),
        ],
        compiler_params=pltpu.CompilerParams(vmem_limit_bytes=56 * 1024 * 1024),
        cost_estimate=pl.CostEstimate(flops=cells * 2000, bytes_accessed=cells * 60, transcendentals=cells * 20),
    )(where, total, other, current, before, stiff, dense, lift_table, left, offset, inverse_y, inverse_z, current, wave_other)
    return (wave, features)


def solution(mesh):
    placed = (
        P(("grp", "gx"), "gy", "gz"),
        P(("grp", "gx"), "gy", "gz"),
        P(("grp", "gx"), "gy", "gz"),
        P(),
        P(),
        P(),
        P(),
        P(),
        P(),
        P(),
    )
    return jax.shard_map(
        per_device,
        mesh=mesh,
        in_specs=placed,
        out_specs=(P(("grp", "gx"), "gy", "gz"), P(("grp", "gx", "gz"), "gy", None, None)),
        check_vma=False,
    )
```

time: 283 us -> 102 us (0.36)
  local copies, waits for them, and re-layouts: 61.5 us -> 10.8 us
  other arithmetic: 49.8 us -> 2.24 us
  waiting for transfers between devices: 76.8 us -> 35.6 us
  starting transfers between devices: 69 us -> 29.6 us
  Pallas kernels: 0 us -> 21.8 us
  matrix products: 16 us -> 0 us
  blocking collectives: 5.84 us -> 0 us
    all_to_all x4 -> x0, waiting for transfers between devices: 52.8 us -> none  [the longest x1 17.7 us: per_device(): lax.all_to_all(depth_modes, 'gy', split_axis=0, concat_axis=3, tiled=True)]
    add x6 -> x5, other arithmetic: 40.4 us -> 0.83 us  [the longest x1 0.66 us: per_device(): jnp.array([1, 0], jnp.int32) * (lax.axis_index('gx') * core_count + core)]
    pallas_call x0 -> x9, Pallas kernels: none -> 21.8 us  [the longest x1 9.91 us: per_device(): pl.pallas_call(output_body, grid=(brick_y // group,), out_shape=[shape(ro...]
    ppermute x24 -> x19, starting transfers between devices: 50.4 us -> 29.6 us  [the longest x4 13.6 us: per_device(): mate = lax.ppermute(current, 'gz', swap_core)]
    all_to_all x10 -> x0, local copies, waits for them, and re-layouts: 18.9 us -> none  [the longest x3 11.5 us: per_device(): lax.all_to_all(brick_lifted, 'gz', split_axis=0, concat_axis=3, tiled=True)]
    all_to_all x4 -> x0, starting transfers between devices: 18.7 us -> none  [the longest x1 6.09 us: per_device(): lax.all_to_all(second_modes, ('gx', 'gz'), split_axis=2, concat_axis=1, t...]
    dot_general x8 -> x0, matrix products: 16 us -> none  [the longest x1 5.64 us: per_device(): jnp.einsum('xycz,co->xyoz', lifted, local_weight, preferred_element_type=...]
    slice x21 -> x0, local copies, waits for them, and re-layouts: 12.4 us -> none  [the longest x4 5.57 us: lookup(): values[material_id]]
  transfers between devices with their start and end apart: 28 -> 19, of which waited for: 18 -> 10; matrix products, arithmetic and copies ran while one was open for 14% -> 3% of each run, Pallas kernels for 0% -> 2%
where the time goes in v1:
time: 102 us; the launch traced here: 101 us
  waiting for transfers between devices  35.6 us (35%)
  starting transfers between devices  29.6 us (29%)
  Pallas kernels  21.8 us (21%)
  local copies, waits for them, and re-layouts  10.8 us (11%)
  other arithmetic  2.24 us (2%)
  between operations  1.02 us (1%)
    ppermute x3, waiting for transfers between devices, per_device(): total = total + lax.ppermute(total, axis, xor_pairs(count, distance))  23 us
    ppermute x4, starting transfers between devices, per_device(): mate = lax.ppermute(current, 'gz', swap_core)  13.6 us
    pallas_call x1, Pallas kernels, per_device(): pl.pallas_call(output_body, grid=(brick_y // group,), out_shape=[shape(ro...  9.91 us
    unnamed x58, local copies, waits for them, and re-layouts  9.75 us
    ppermute x4, waiting for transfers between devices, per_device(): halos = [lax.ppermute(edge_values[0], 'gy', xor_pairs(column_count, 1))]  9.69 us
    ppermute x4, starting transfers between devices, per_device(): halos = [lax.ppermute(edge_values[0], 'gy', xor_pairs(column_count, 1))]  6.03 us
    pallas_call x4, Pallas kernels, per_device(): call(body, outs, [SMEM] + [VMEM] * (6 + len(halos)), [pltpu.VMEM((brick_y...  6 us
    ppermute x3, starting transfers between devices, per_device(): total = total + lax.ppermute(total, axis, xor_pairs(count, distance))  5.91 us
  transfers between devices with their start and end apart: 19, of which 10 were waited for; matrix products, arithmetic and copies ran while one was open for 3% of the time, Pallas kernels for 2%

profile of v1, /device:TPU:0, one launch (start us, length us, event | category | flops | bytes accessed | tf_op | source)
XLA Modules:
  0.0 101.1 jit_solution(14037543448889270116)
XLA Ops:
  1.3 0.9 copy-done
  2.3 0.9 copy-done.1
  3.2 0.9 copy-done.2
  5.3 1.3 %collective-permute-done.got = f32[3,4,64,128]{3,2,1,0:T(8,128)S(1)} collective-permute-done((f32[3,4,64,128]{3,2,1,0:T(8,128)S(1)}, f32[3,4,64,128]{3,2,1,0:T(8,128)S(1)}, u32[]{:S(2)}, u32[]{:S(2)}) %collective-permute-start) | collective-permute-done | bytes 393248 | tf_op jit(solution)/shard_map/ppermute | solution.py:393
  8.6 1.0 shard_map.222
  10.3 4.4 %collective-permute-start.1 = (f32[4,64,256]{2,1,0:T(8,128)S(1)}, f32[4,64,256]{2,1,0:T(8,128)S(1)}, u32[]{:S(2)}, u32[]{:S(2)}) collective-permute-start(f32[4,64,256]{2,1,0:T(8,128)S(1)} %get-tuple-element.35.refs_1_.refs_2_), channel_id=1, source_target_pairs={{0,1},{1,0},{2,3},{3,2},{4,5},{5,4},{6,7},{7,6},{8,9},{9,8},{10,11... | collective-permute-start | bytes 786440 | tf_op jit(solution)/shard_map/ppermute | solution.py:415
  14.6 1.5 %collective-permute-start.3 = (f32[4,8,256]{2,1,0:T(8,128)S(1)}, f32[4,8,256]{2,1,0:T(8,128)S(1)}, u32[]{:S(2)}, u32[]{:S(2)}) collective-permute-start(f32[4,8,256]{2,1,0:T(8,128)S(1)} %get-tuple-element.39), channel_id=1, source_target_pairs={{0,2},{2,0},{1,3},{3,1},{4,6},{6,4},{5,7},{7,5},{8,10},{10,8},{9,1... | collective-permute-start | bytes 98312 | tf_op jit(solution)/shard_map/ppermute | solution.py:416
  16.1 2.4 %collective-permute-done.3.refs_7_ = f32[4,8,256]{2,1,0:T(8,128)S(1)} collective-permute-done((f32[4,8,256]{2,1,0:T(8,128)S(1)}, f32[4,8,256]{2,1,0:T(8,128)S(1)}, u32[]{:S(2)}, u32[]{:S(2)}) %collective-permute-start.3) | collective-permute-done | bytes 32800 | tf_op jit(solution)/shard_map/ppermute | solution.py:416
  18.6 1.5 %shard_map.223 = (f32[4,64,256]{2,1,0:T(8,128)S(1)}, f32[4,8,256]{2,1,0:T(8,128)S(1)}) custom-call(s32[2]{0:T(128)S(1)} %multiply_add_fusion.where_ref.refs_0_, f32[4,64,256]{2,1,0:T(8,128)S(1)} %get-tuple-element.35.refs_1_.refs_2_, f32[4,64,256]{2,1,0:T(8,128)S(1)} %get-tuple-element.36.refs_2_, f32[4,64,256]{2,1,0:T(8,128)S(1)} %get-tuple-element.37.refs_3_, ...), custom_call_target="tpu_custom_call" | custom-call | flops 3932160 | bytes 1835008 | tf_op jit(solution)/shard_map/pallas_call | solution.py:421
  20.8 3.1 %collective-permute-start.4 = (f32[4,64,256]{2,1,0:T(8,128)S(1)}, f32[4,64,256]{2,1,0:T(8,128)S(1)}, u32[]{:S(2)}, u32[]{:S(2)}) collective-permute-start(f32[4,64,256]{2,1,0:T(8,128)S(1)} %get-tuple-element.40.refs_1_.refs_2_), channel_id=1, source_target_pairs={{0,1},{1,0},{2,3},{3,2},{4,5},{5,4},{6,7},{7,6},{8,9},{9,8},{10,11... | collective-permute-start | bytes 786440 | tf_op jit(solution)/shard_map/ppermute | solution.py:415
  23.9 1.5 %collective-permute-start.6 = (f32[4,8,256]{2,1,0:T(8,128)S(1)}, f32[4,8,256]{2,1,0:T(8,128)S(1)}, u32[]{:S(2)}, u32[]{:S(2)}) collective-permute-start(f32[4,8,256]{2,1,0:T(8,128)S(1)} %get-tuple-element.41), channel_id=1, source_target_pairs={{0,2},{2,0},{1,3},{3,1},{4,6},{6,4},{5,7},{7,5},{8,10},{10,8},{9,1... | collective-permute-start | bytes 98312 | tf_op jit(solution)/shard_map/ppermute | solution.py:416
  25.3 2.4 %collective-permute-done.6.refs_7_ = f32[4,8,256]{2,1,0:T(8,128)S(1)} collective-permute-done((f32[4,8,256]{2,1,0:T(8,128)S(1)}, f32[4,8,256]{2,1,0:T(8,128)S(1)}, u32[]{:S(2)}, u32[]{:S(2)}) %collective-permute-start.6) | collective-permute-done | bytes 32800 | tf_op jit(solution)/shard_map/ppermute | solution.py:416
  27.8 1.5 %shard_map.224 = (f32[4,64,256]{2,1,0:T(8,128)S(1)}, f32[4,8,256]{2,1,0:T(8,128)S(1)}) custom-call(s32[2]{0:T(128)S(1)} %multiply_add_fusion.where_ref.refs_0_, f32[4,64,256]{2,1,0:T(8,128)S(1)} %get-tuple-element.40.refs_1_.refs_2_, f32[4,64,256]{2,1,0:T(8,128)S(1)} %get-tuple-element.35.refs_1_.refs_2_, f32[4,64,256]{2,1,0:T(8,128)S(1)} %get-tuple-element.37.refs_3_, ...), custom_call_target="tpu_custom_call" | custom-call | flops 3932160 | bytes 1835008 | tf_op jit(solution)/shard_map/pallas_call | solution.py:421
  30.0 3.1 %collective-permute-start.7 = (f32[4,64,256]{2,1,0:T(8,128)S(1)}, f32[4,64,256]{2,1,0:T(8,128)S(1)}, u32[]{:S(2)}, u32[]{:S(2)}) collective-permute-start(f32[4,64,256]{2,1,0:T(8,128)S(1)} %get-tuple-element.42.refs_1_.refs_2_), channel_id=1, source_target_pairs={{0,1},{1,0},{2,3},{3,2},{4,5},{5,4},{6,7},{7,6},{8,9},{9,8},{10,11... | collective-permute-start | bytes 786440 | tf_op jit(solution)/shard_map/ppermute | solution.py:415
  33.1 1.5 %collective-permute-start.9 = (f32[4,8,256]{2,1,0:T(8,128)S(1)}, f32[4,8,256]{2,1,0:T(8,128)S(1)}, u32[]{:S(2)}, u32[]{:S(2)}) collective-permute-start(f32[4,8,256]{2,1,0:T(8,128)S(1)} %get-tuple-element.43), channel_id=1, source_target_pairs={{0,2},{2,0},{1,3},{3,1},{4,6},{6,4},{5,7},{7,5},{8,10},{10,8},{9,1... | collective-permute-start | bytes 98312 | tf_op jit(solution)/shard_map/ppermute | solution.py:416
  34.6 2.4 %collective-permute-done.9.refs_7_ = f32[4,8,256]{2,1,0:T(8,128)S(1)} collective-permute-done((f32[4,8,256]{2,1,0:T(8,128)S(1)}, f32[4,8,256]{2,1,0:T(8,128)S(1)}, u32[]{:S(2)}, u32[]{:S(2)}) %collective-permute-start.9) | collective-permute-done | bytes 32800 | tf_op jit(solution)/shard_map/ppermute | solution.py:416
  37.0 1.5 %shard_map.225 = (f32[4,64,256]{2,1,0:T(8,128)S(1)}, f32[4,8,256]{2,1,0:T(8,128)S(1)}) custom-call(s32[2]{0:T(128)S(1)} %multiply_add_fusion.where_ref.refs_0_, f32[4,64,256]{2,1,0:T(8,128)S(1)} %get-tuple-element.42.refs_1_.refs_2_, f32[4,64,256]{2,1,0:T(8,128)S(1)} %get-tuple-element.40.refs_1_.refs_2_, f32[4,64,256]{2,1,0:T(8,128)S(1)} %get-tuple-element.37.refs_3_, ...), custom_call_target="tpu_custom_call" | custom-call | flops 3932160 | bytes 1835008 | tf_op jit(solution)/shard_map/pallas_call | solution.py:421
  39.4 3.1 %collective-permute-start.10 = (f32[4,64,256]{2,1,0:T(8,128)S(1)}, f32[4,64,256]{2,1,0:T(8,128)S(1)}, u32[]{:S(2)}, u32[]{:S(2)}) collective-permute-start(f32[4,64,256]{2,1,0:T(8,128)S(1)} %get-tuple-element.44.refs_1_.q_ref), channel_id=1, source_target_pairs={{0,1},{1,0},{2,3},{3,2},{4,5},{5,4},{6,7},{7,6},{8,9},{9,8},{10,11... | collective-permute-start | bytes 786440 | tf_op jit(solution)/shard_map/ppermute | solution.py:415
  42.5 1.6 %collective-permute-start.12 = (f32[4,8,256]{2,1,0:T(8,128)S(1)}, f32[4,8,256]{2,1,0:T(8,128)S(1)}, u32[]{:S(2)}, u32[]{:S(2)}) collective-permute-start(f32[4,8,256]{2,1,0:T(8,128)S(1)} %get-tuple-element.45), channel_id=1, source_target_pairs={{0,2},{2,0},{1,3},{3,1},{4,6},{6,4},{5,7},{7,5},{8,10},{10,8},{9,1... | collective-permute-start | bytes 98312 | tf_op jit(solution)/shard_map/ppermute | solution.py:416
  44.0 2.4 %collective-permute-done.12.refs_7_ = f32[4,8,256]{2,1,0:T(8,128)S(1)} collective-permute-done((f32[4,8,256]{2,1,0:T(8,128)S(1)}, f32[4,8,256]{2,1,0:T(8,128)S(1)}, u32[]{:S(2)}, u32[]{:S(2)}) %collective-permute-start.12) | collective-permute-done | bytes 32800 | tf_op jit(solution)/shard_map/ppermute | solution.py:416
  46.4 1.5 %shard_map.226 = (f32[4,64,256]{2,1,0:T(8,128)S(1)}, f32[4,64,128]{2,1,0:T(8,128)S(1)}) custom-call(s32[2]{0:T(128)S(1)} %multiply_add_fusion.where_ref.refs_0_, f32[4,64,256]{2,1,0:T(8,128)S(1)} %get-tuple-element.44.refs_1_.q_ref, f32[4,64,256]{2,1,0:T(8,128)S(1)} %get-tuple-element.42.refs_1_.refs_2_, f32[4,64,256]{2,1,0:T(8,128)S(1)} %get-tuple-element.37.refs_3_, ...), custom_call_target="tpu_custom_call" | custom-call | flops 3932160 | bytes 1835008 | tf_op jit(solution)/shard_map/pallas_call | solution.py:421
  48.0 2.1 %shard_map.227 = (f32[2,8,32,128]{3,2,1,0:T(8,128)S(1)}, f32[2,8,32,128]{3,2,1,0:T(8,128)S(1)}) custom-call(s32[2]{0:T(128)S(1)} %multiply_add_fusion.where_ref.refs_0_, f32[512]{0:T(512)S(1)} %copy-done.18, f32[4,64,256]{2,1,0:T(8,128)S(1)} %get-tuple-element.46.p_ref.wave_ref, f32[4,64,256]{2,1,0:T(8,128)S(1)} %get-tuple-element.44.refs_1_.q_ref, ...), custom_call_target="tpu_custom_call" | custom-call | flops 134217728 | bytes 2097152 | tf_op jit(solution)/shard_map/pallas_call | solution.py:429
  50.3 1.4 %collective-permute-done.13 = f32[2,8,32,128]{3,2,1,0:T(8,128)S(1)} collective-permute-done((f32[2,8,32,128]{3,2,1,0:T(8,128)S(1)}, f32[2,8,32,128]{3,2,1,0:T(8,128)S(1)}, u32[]{:S(2)}, u32[]{:S(2)}) %collective-permute-start.13) | collective-permute-done | bytes 262176 | tf_op jit(solution)/shard_map/ppermute | solution.py:434
  51.8 1.6 %collective-permute-start.14 = (f32[2,8,32,128]{3,2,1,0:T(8,128)S(1)}, f32[2,8,32,128]{3,2,1,0:T(8,128)S(1)}, u32[]{:S(2)}, u32[]{:S(2)}) collective-permute-start(f32[2,8,32,128]{3,2,1,0:T(8,128)S(1)} %add.26), channel_id=1, source_target_pairs={{0,2},{2,0},{1,3},{3,1},{4,6},{6,4},{5,7},{7,5},{8,10},{10,8},{9,1... | collective-permute-start | bytes 786440 | tf_op jit(solution)/shard_map/ppermute | solution.py:438
  53.4 6.9 %collective-permute-done.14 = f32[2,8,32,128]{3,2,1,0:T(8,128)S(1)} collective-permute-done((f32[2,8,32,128]{3,2,1,0:T(8,128)S(1)}, f32[2,8,32,128]{3,2,1,0:T(8,128)S(1)}, u32[]{:S(2)}, u32[]{:S(2)}) %collective-permute-start.14) | collective-permute-done | bytes 262176 | tf_op jit(solution)/shard_map/ppermute | solution.py:438
  60.3 1.7 %collective-permute-start.15 = (f32[2,8,32,128]{3,2,1,0:T(8,128)S(1)}, f32[2,8,32,128]{3,2,1,0:T(8,128)S(1)}, u32[]{:S(2)}, u32[]{:S(2)}) collective-permute-start(f32[2,8,32,128]{3,2,1,0:T(8,128)S(1)} %add.27), channel_id=1, source_target_pairs={{0,4},{4,0},{8,12},{12,8},{1,5},{5,1},{9,13},{13,9},{2,6},{6,2},{1... | collective-permute-start | bytes 786440 | tf_op jit(solution)/shard_map/ppermute | solution.py:438
  61.9 5.9 %collective-permute-done.15 = f32[2,8,32,128]{3,2,1,0:T(8,128)S(1)} collective-permute-done((f32[2,8,32,128]{3,2,1,0:T(8,128)S(1)}, f32[2,8,32,128]{3,2,1,0:T(8,128)S(1)}, u32[]{:S(2)}, u32[]{:S(2)}) %collective-permute-start.15) | collective-permute-done | bytes 262176 | tf_op jit(solution)/shard_map/ppermute | solution.py:438
  67.9 2.7 %collective-permute-start.16 = (f32[2,8,32,128]{3,2,1,0:T(8,128)S(1)}, f32[2,8,32,128]{3,2,1,0:T(8,128)S(1)}, u32[]{:S(2)}, u32[]{:S(2)}) collective-permute-start(f32[2,8,32,128]{3,2,1,0:T(8,128)S(1)} %add.28), channel_id=1, source_target_pairs={{0,8},{4,12},{8,0},{12,4},{1,9},{5,13},{9,1},{13,5},{2,10},{6,14},... | collective-permute-start | bytes 786440 | tf_op jit(solution)/shard_map/ppermute | solution.py:438
  70.8 10.3 %collective-permute-done.16 = f32[2,8,32,128]{3,2,1,0:T(8,128)S(1)} collective-permute-done((f32[2,8,32,128]{3,2,1,0:T(8,128)S(1)}, f32[2,8,32,128]{3,2,1,0:T(8,128)S(1)}, u32[]{:S(2)}, u32[]{:S(2)}) %collective-permute-start.16) | collective-permute-done | bytes 262176 | tf_op jit(solution)/shard_map/ppermute | solution.py:438
  82.2 2.1 %shard_map.228 = (bf16[96,256]{1,0:T(8,128)(2,1)S(1)}, f32[96,1]{1,0:T(8,128)S(1)}) custom-call(s32[2]{0:T(128)S(1)} %multiply_add_fusion.where_ref.refs_0_, f32[2,160,20]{2,1,0:T(8,128)S(1)} %reshape.40.mode_ref, f32[4,20]{1,0:T(4,128)S(1)} %copy-done.15, f32[1,20]{1,0:T(1,128)S(1)} %bitcast.5, bf16[20,20]{1,0:T(8,128)(2,1)S(1)} %copy-done.13, ...), custom_call_target="tpu_custom_call" | custom-call | tf_op jit(solution)/shard_map/pallas_call | solution.py:398
  87.2 9.9 %shard_map.229 = (bf16[4,64,20,256]{3,2,1,0:T(8,128)(2,1)}, f32[8,64,128]{2,1,0:T(8,128)}) custom-call(s32[2]{0:T(128)} %copy-done.11, f32[2,8,32,128]{3,2,1,0:T(8,128)} %copy-done.23, f32[2,8,32,128]{3,2,1,0:T(8,128)} %copy-done.26, f32[4,64,256]{2,1,0:T(8,128)} %copy-done.7, f32[4,64,256]{2,1,0:T(8,128)} %copy-done.3, f32[4,64,256]{2,1,0:T(8,128)} %copy-done.5, ...), custom_call_target="tpu_custom_call" | custom-call | flops 131072000 | bytes 3932160 | tf_op jit(solution)/shard_map/pallas_call | solution.py:445
  97.1 4.0 %copy.39 = bf16[4,64,20,256]{3,1,2,0:T(8,128)(2,1)} copy(bf16[4,64,20,256]{3,2,1,0:T(8,128)(2,1)} %get-tuple-element.61) | data formatting | bytes 5242880
  (89 shorter events, 11.0 us)
Async XLA Ops:
  4.2 78.0 %copy-start.11 = (s32[2]{0:T(128)}, s32[2]{0:T(128)S(1)}, u32[]{:S(2)}) copy-start(s32[2]{0:T(128)S(1)} %multiply_add_fusion.where_ref.refs_0_) | copy-start | bytes 28
  4.7 1.9 %collective-permute-start = (f32[3,4,64,128]{3,2,1,0:T(8,128)S(1)}, f32[3,4,64,128]{3,2,1,0:T(8,128)S(1)}, u32[]{:S(2)}, u32[]{:S(2)}) collective-permute-start(f32[3,4,64,128]{3,2,1,0:T(8,128)S(1)} %shard_map.221), channel_id=1, source_target_pairs={{0,1},{1,0},{2,3},{3,2},{4,5},{5,4},{6,7},{7,6},{8,9},{9,8},{10,11... | collective-permute-start | bytes 1179656 | tf_op jit(solution)/shard_map/ppermute | solution.py:393
  9.6 38.4 %copy-start.5 = (f32[4,64,256]{2,1,0:T(8,128)}, f32[4,64,256]{2,1,0:T(8,128)S(1)}, u32[]{:S(2)}) copy-start(f32[4,64,256]{2,1,0:T(8,128)S(1)} %get-tuple-element.47.stiff) | copy-start | bytes 786436
  9.6 38.4 %copy-start.6 = (f32[4,64,256]{2,1,0:T(8,128)}, f32[4,64,256]{2,1,0:T(8,128)S(1)}, u32[]{:S(2)}) copy-start(f32[4,64,256]{2,1,0:T(8,128)S(1)} %get-tuple-element.48.dense) | copy-start | bytes 786436
  9.6 9.0 %collective-permute-start.2 = (f32[4,64,256]{2,1,0:T(8,128)S(1)}, f32[4,64,256]{2,1,0:T(8,128)S(1)}, u32[]{:S(2)}, u32[]{:S(2)}) collective-permute-start(f32[4,64,256]{2,1,0:T(8,128)S(1)} %get-tuple-element.35.refs_1_.refs_2_), channel_id=1, source_target_pairs={{1,4},{5,8},{9,12},{4,1},{8,5},{12,9},{3,6},{7,10},{11,14},{6,3},{... | collective-permute-start | bytes 786440 | tf_op jit(solution)/shard_map/ppermute | solution.py:414
  10.3 8.3 %collective-permute-start.1 = (f32[4,64,256]{2,1,0:T(8,128)S(1)}, f32[4,64,256]{2,1,0:T(8,128)S(1)}, u32[]{:S(2)}, u32[]{:S(2)}) collective-permute-start(f32[4,64,256]{2,1,0:T(8,128)S(1)} %get-tuple-element.35.refs_1_.refs_2_), channel_id=1, source_target_pairs={{0,1},{1,0},{2,3},{3,2},{4,5},{5,4},{6,7},{7,6},{8,9},{9,8},{10,11... | collective-permute-start | bytes 786440 | tf_op jit(solution)/shard_map/ppermute | solution.py:415
  14.6 3.9 %collective-permute-start.3 = (f32[4,8,256]{2,1,0:T(8,128)S(1)}, f32[4,8,256]{2,1,0:T(8,128)S(1)}, u32[]{:S(2)}, u32[]{:S(2)}) collective-permute-start(f32[4,8,256]{2,1,0:T(8,128)S(1)} %get-tuple-element.39), channel_id=1, source_target_pairs={{0,2},{2,0},{1,3},{3,1},{4,6},{6,4},{5,7},{7,5},{8,10},{10,8},{9,1... | collective-permute-start | bytes 98312 | tf_op jit(solution)/shard_map/ppermute | solution.py:416
  20.1 7.7 %collective-permute-start.5 = (f32[4,64,256]{2,1,0:T(8,128)S(1)}, f32[4,64,256]{2,1,0:T(8,128)S(1)}, u32[]{:S(2)}, u32[]{:S(2)}) collective-permute-start(f32[4,64,256]{2,1,0:T(8,128)S(1)} %get-tuple-element.40.refs_1_.refs_2_), channel_id=1, source_target_pairs={{1,4},{5,8},{9,12},{4,1},{8,5},{12,9},{3,6},{7,10},{11,14},{6,3},{... | collective-permute-start | bytes 786440 | tf_op jit(solution)/shard_map/ppermute | solution.py:414
  20.8 7.0 %collective-permute-start.4 = (f32[4,64,256]{2,1,0:T(8,128)S(1)}, f32[4,64,256]{2,1,0:T(8,128)S(1)}, u32[]{:S(2)}, u32[]{:S(2)}) collective-permute-start(f32[4,64,256]{2,1,0:T(8,128)S(1)} %get-tuple-element.40.refs_1_.refs_2_), channel_id=1, source_target_pairs={{0,1},{1,0},{2,3},{3,2},{4,5},{5,4},{6,7},{7,6},{8,9},{9,8},{10,11... | collective-permute-start | bytes 786440 | tf_op jit(solution)/shard_map/ppermute | solution.py:415
  23.9 3.9 %collective-permute-start.6 = (f32[4,8,256]{2,1,0:T(8,128)S(1)}, f32[4,8,256]{2,1,0:T(8,128)S(1)}, u32[]{:S(2)}, u32[]{:S(2)}) collective-permute-start(f32[4,8,256]{2,1,0:T(8,128)S(1)} %get-tuple-element.41), channel_id=1, source_target_pairs={{0,2},{2,0},{1,3},{3,1},{4,6},{6,4},{5,7},{7,5},{8,10},{10,8},{9,1... | collective-permute-start | bytes 98312 | tf_op jit(solution)/shard_map/ppermute | solution.py:416
  29.3 7.7 %collective-permute-start.8 = (f32[4,64,256]{2,1,0:T(8,128)S(1)}, f32[4,64,256]{2,1,0:T(8,128)S(1)}, u32[]{:S(2)}, u32[]{:S(2)}) collective-permute-start(f32[4,64,256]{2,1,0:T(8,128)S(1)} %get-tuple-element.42.refs_1_.refs_2_), channel_id=1, source_target_pairs={{1,4},{5,8},{9,12},{4,1},{8,5},{12,9},{3,6},{7,10},{11,14},{6,3},{... | collective-permute-start | bytes 786440 | tf_op jit(solution)/shard_map/ppermute | solution.py:414
  30.0 7.0 %collective-permute-start.7 = (f32[4,64,256]{2,1,0:T(8,128)S(1)}, f32[4,64,256]{2,1,0:T(8,128)S(1)}, u32[]{:S(2)}, u32[]{:S(2)}) collective-permute-start(f32[4,64,256]{2,1,0:T(8,128)S(1)} %get-tuple-element.42.refs_1_.refs_2_), channel_id=1, source_target_pairs={{0,1},{1,0},{2,3},{3,2},{4,5},{5,4},{6,7},{7,6},{8,9},{9,8},{10,11... | collective-permute-start | bytes 786440 | tf_op jit(solution)/shard_map/ppermute | solution.py:415
  33.1 37.5 %copy-start.13 = (bf16[20,20]{1,0:T(8,128)(2,1)S(1)}, bf16[20,20]{1,0:T(8,128)(2,1)}, u32[]{:S(2)}) copy-start(bf16[20,20]{1,0:T(8,128)(2,1)} %local_ref.1) | copy-start | bytes 2404
  33.1 37.6 %copy-start.25 = (bf16[4,4]{1,0:T(4,128)(2,1)S(1)}, bf16[4,4]{1,0:T(4,128)(2,1)}, u32[]{:S(2)}) copy-start(bf16[4,4]{1,0:T(4,128)(2,1)} %constant.88) | copy-start | bytes 100
  33.1 3.9 %collective-permute-start.9 = (f32[4,8,256]{2,1,0:T(8,128)S(1)}, f32[4,8,256]{2,1,0:T(8,128)S(1)}, u32[]{:S(2)}, u32[]{:S(2)}) collective-permute-start(f32[4,8,256]{2,1,0:T(8,128)S(1)} %get-tuple-element.43), channel_id=1, source_target_pairs={{0,2},{2,0},{1,3},{3,1},{4,6},{6,4},{5,7},{7,5},{8,10},{10,8},{9,1... | collective-permute-start | bytes 98312 | tf_op jit(solution)/shard_map/ppermute | solution.py:416
  38.5 43.0 %copy-start.3 = (f32[4,64,256]{2,1,0:T(8,128)}, f32[4,64,256]{2,1,0:T(8,128)S(1)}, u32[]{:S(2)}) copy-start(f32[4,64,256]{2,1,0:T(8,128)S(1)} %get-tuple-element.44.refs_1_.q_ref) | copy-start | bytes 786436
  38.5 42.7 %copy-start.15 = (f32[4,20]{1,0:T(4,128)S(1)}, f32[4,20]{1,0:T(4,128)}, u32[]{:S(2)}) copy-start(f32[4,20]{1,0:T(4,128)} %lift_ref.1) | copy-start | bytes 964
  38.5 42.7 %copy-start.16 = (f32[20]{0:T(128)S(1)}, f32[20]{0:T(128)}, u32[]{:S(2)}) copy-start(f32[20]{0:T(128)} %param.31) | copy-start | bytes 244
  38.5 42.9 %copy-start.24 = (f32[2,8,20,20]{3,1,2,0:T(8,128)S(1)}, f32[2,8,20,20]{3,1,2,0:T(8,128)}, u32[]{:S(2)}) copy-start(f32[2,8,20,20]{3,1,2,0:T(8,128)} %param.32) | copy-start | bytes 76804
  38.5 7.9 %collective-permute-start.11 = (f32[4,64,256]{2,1,0:T(8,128)S(1)}, f32[4,64,256]{2,1,0:T(8,128)S(1)}, u32[]{:S(2)}, u32[]{:S(2)}) collective-permute-start(f32[4,64,256]{2,1,0:T(8,128)S(1)} %get-tuple-element.44.refs_1_.q_ref), channel_id=1, source_target_pairs={{1,4},{5,8},{9,12},{4,1},{8,5},{12,9},{3,6},{7,10},{11,14},{6,3},{... | collective-permute-start | bytes 786440 | tf_op jit(solution)/shard_map/ppermute | solution.py:414
  39.4 7.1 %collective-permute-start.10 = (f32[4,64,256]{2,1,0:T(8,128)S(1)}, f32[4,64,256]{2,1,0:T(8,128)S(1)}, u32[]{:S(2)}, u32[]{:S(2)}) collective-permute-start(f32[4,64,256]{2,1,0:T(8,128)S(1)} %get-tuple-element.44.refs_1_.q_ref), channel_id=1, source_target_pairs={{0,1},{1,0},{2,3},{3,2},{4,5},{5,4},{6,7},{7,6},{8,9},{9,8},{10,11... | collective-permute-start | bytes 786440 | tf_op jit(solution)/shard_map/ppermute | solution.py:415
  42.4 39.7 %copy-start.4 = (f32[8,2,96,32]{3,2,1,0:T(8,128)S(1)}, f32[8,2,96,32]{3,2,1,0:T(8,128)}, u32[]{:S(2)}) copy-start(f32[8,2,96,32]{3,2,1,0:T(8,128)} %constant.77.clone.turn_ref) | copy-start | bytes 589828
  42.4 39.7 %copy-start.8 = (f32[160,52]{1,0:T(8,128)S(1)}, f32[160,52]{1,0:T(8,128)}, u32[]{:S(2)}) copy-start(f32[160,52]{1,0:T(8,128)} %constant.74.clone.spread_ref) | copy-start | bytes 99844
  42.4 39.7 %copy-start.10 = (f32[96,20]{1,0:T(8,128)S(1)}, f32[96,20]{1,0:T(8,128)}, u32[]{:S(2)}) copy-start(f32[96,20]{1,0:T(8,128)} %constant.76.clone.owner_ref) | copy-start | bytes 23044
  42.4 39.7 %copy-start.17 = (f32[4,32]{1,0:T(4,128)S(1)}, f32[4,32]{1,0:T(4,128)}, u32[]{:S(2)}) copy-start(f32[4,32]{1,0:T(4,128)} %constant.75.clone.place_ref) | copy-start | bytes 1540
  42.5 4.0 %collective-permute-start.12 = (f32[4,8,256]{2,1,0:T(8,128)S(1)}, f32[4,8,256]{2,1,0:T(8,128)S(1)}, u32[]{:S(2)}, u32[]{:S(2)}) collective-permute-start(f32[4,8,256]{2,1,0:T(8,128)S(1)} %get-tuple-element.45), channel_id=1, source_target_pairs={{0,2},{2,0},{1,3},{3,1},{4,6},{6,4},{5,7},{7,5},{8,10},{10,8},{9,1... | collective-permute-start | bytes 98312 | tf_op jit(solution)/shard_map/ppermute | solution.py:416
  50.1 1.6 %collective-permute-start.13 = (f32[2,8,32,128]{3,2,1,0:T(8,128)S(1)}, f32[2,8,32,128]{3,2,1,0:T(8,128)S(1)}, u32[]{:S(2)}, u32[]{:S(2)}) collective-permute-start(f32[2,8,32,128]{3,2,1,0:T(8,128)S(1)} %get-tuple-element.50), channel_id=1, source_target_pairs={{0,1},{1,0},{2,3},{3,2},{4,5},{5,4},{6,7},{7,6},{8,9},{9,8},{10,11... | collective-permute-start | bytes 786440 | tf_op jit(solution)/shard_map/ppermute | solution.py:434
  51.8 8.4 %collective-permute-start.14 = (f32[2,8,32,128]{3,2,1,0:T(8,128)S(1)}, f32[2,8,32,128]{3,2,1,0:T(8,128)S(1)}, u32[]{:S(2)}, u32[]{:S(2)}) collective-permute-start(f32[2,8,32,128]{3,2,1,0:T(8,128)S(1)} %add.26), channel_id=1, source_target_pairs={{0,2},{2,0},{1,3},{3,1},{4,6},{6,4},{5,7},{7,5},{8,10},{10,8},{9,1... | collective-permute-start | bytes 786440 | tf_op jit(solution)/shard_map/ppermute | solution.py:438
  60.3 7.6 %collective-permute-start.15 = (f32[2,8,32,128]{3,2,1,0:T(8,128)S(1)}, f32[2,8,32,128]{3,2,1,0:T(8,128)S(1)}, u32[]{:S(2)}, u32[]{:S(2)}) collective-permute-start(f32[2,8,32,128]{3,2,1,0:T(8,128)S(1)} %add.27), channel_id=1, source_target_pairs={{0,4},{4,0},{8,12},{12,8},{1,5},{5,1},{9,13},{13,9},{2,6},{6,2},{1... | collective-permute-start | bytes 786440 | tf_op jit(solution)/shard_map/ppermute | solution.py:438
  67.9 13.2 %collective-permute-start.16 = (f32[2,8,32,128]{3,2,1,0:T(8,128)S(1)}, f32[2,8,32,128]{3,2,1,0:T(8,128)S(1)}, u32[]{:S(2)}, u32[]{:S(2)}) collective-permute-start(f32[2,8,32,128]{3,2,1,0:T(8,128)S(1)} %add.28), channel_id=1, source_target_pairs={{0,8},{4,12},{8,0},{12,4},{1,9},{5,13},{9,1},{13,5},{2,10},{6,14},... | collective-permute-start | bytes 786440 | tf_op jit(solution)/shard_map/ppermute | solution.py:438
  81.1 5.3 %collective-permute-start.17 = (f32[2,8,32,128]{3,2,1,0:T(8,128)S(1)}, f32[2,8,32,128]{3,2,1,0:T(8,128)S(1)}, u32[]{:S(2)}, u32[]{:S(2)}) collective-permute-start(f32[2,8,32,128]{3,2,1,0:T(8,128)S(1)} %add.29.mine), channel_id=1, source_target_pairs={{0,1},{1,0},{2,3},{3,2},{4,5},{5,4},{6,7},{7,6},{8,9},{9,8},{10,11... | collective-permute-start | bytes 786440 | tf_op jit(solution)/shard_map/ppermute | solution.py:440
  85.0 1.5 %collective-permute-start.18 = (f32[4,64,128]{2,1,0:T(8,128)S(1)}, f32[4,64,128]{2,1,0:T(8,128)S(1)}, u32[]{:S(2)}, u32[]{:S(2)}) collective-permute-start(f32[4,64,128]{2,1,0:T(8,128)S(1)} %get-tuple-element.53), channel_id=1, source_target_pairs={{0,1},{1,0},{2,3},{3,2},{4,5},{5,4},{6,7},{7,6},{8,9},{9,8},{10,11... | collective-permute-start | bytes 393224 | tf_op jit(solution)/shard_map/ppermute | solution.py:427
  (15 other events, 138.9 us)

commit v2 on v1

--- a/solution.py
+++ b/solution.py
@@ -44,7 +44,7 @@
         in_specs=in_specs,
         out_specs=jax.tree.map(lambda _: VMEM, outs),
         scratch_shapes=list(scratch),
-        compiler_params=pltpu.CompilerParams(vmem_limit_bytes=32 * 1024 * 1024),
+        compiler_params=pltpu.CompilerParams(vmem_limit_bytes=16 * 1024 * 1024),
         cost_estimate=pl.CostEstimate(flops=flops, bytes_accessed=moved, transcendentals=0),
     )
 
@@ -60,19 +60,10 @@
     return jnp.where(lane < half, sign * swapped, -sign * swapped)
 
 
-def pack_body(where_ref, pressure, previous, material, send):
-    core = where_ref[0] % 2
-    rows = send.shape[1]
-    start = (1 - core) * rows
-    send[0] = pressure[pl.ds(start, rows)]
-    send[1] = previous[pl.ds(start, rows)]
-    send[2] = material[pl.ds(start, rows)].astype(F32)
-
-
 def looked_up(material, table, entries):
     result = jnp.full(material.shape, table(0), F32)
     for entry in range(1, entries):
-        result = jnp.where(material == float(entry), table(entry), result)
+        result = jnp.where(material == entry, table(entry), result)
     return result
 
 
@@ -82,11 +73,11 @@
         out[...] = jnp.where(upper, value_of(brick_y - EDGE, brick_y), value_of(0, EDGE))
 
 
-def assemble_body(where_ref, stiffness, density, nonlinear, pressure, previous, material, got, *outs):
+def assemble_body(where_ref, stiffness, density, nonlinear, pressure, previous, material, got_p, got_q, got_m, *outs):
     p_out, q_out, ratio, bend, stiff, dense = outs[:6]
     core = where_ref[0] % 2
     column = where_ref[1]
-    rows, brick_y, half = got.shape[1:]
+    rows, brick_y = p_out.shape[:2]
     start = core * rows
     entries = stiffness.shape[0]
 
@@ -96,9 +87,9 @@
         )
 
     for row in range(rows):
-        p_out[row] = whole(pressure[start + row], got[0, row])
-        q_out[row] = whole(previous[start + row], got[1, row])
-        cell = whole(material[start + row].astype(F32), got[2, row])
+        p_out[row] = whole(pressure[start + row], got_p[start + row])
+        q_out[row] = whole(previous[start + row], got_q[start + row])
+        cell = whole(material[start + row], got_m[start + row])
         ratio[row] = looked_up(cell, lambda e: stiffness[e] / density[e], entries)
         bend[row] = looked_up(cell, lambda e: nonlinear[e], entries)
         stiff[row] = looked_up(cell, lambda e: stiffness[e], entries)
@@ -192,57 +183,70 @@
         sums((1 - core) * 2 + index, send, index)
 
 
-def prepare_body(where_ref, mode_ref, lift_ref, bias_ref, local_ref, spread_ref, place_ref, owner_ref, turn_ref, left, offset):
+def prepare_body(
+    where_ref, mode_ref, lift_ref, bias_ref, local_ref, spread_ref, place_ref, owner_ref, turn_ref,
+    wide_ref, mixing, pointwise, lift_table, offset,
+):
     block = where_ref[0]
-    modes = spread_ref.shape[0]
-    total = left.shape[1]
     half = place_ref.shape[1]
+    channels = lift_ref.shape[1]
     spread = owner_ref[...]
-    channels = lift_ref.shape[1]
 
     def dot(a, b, dims=((1,), (0,))):
         return lax.dot_general(a, b, (dims, ((), ())), precision=HIGHEST, preferred_element_type=F32)
 
-    lifted = dot(dot(spread_ref[:, :channels], lift_ref[...], ((1,), (1,))), place_ref[...])
-    same = spread_ref[:, channels : channels + half]
-    lifted = lifted * same
-    real = dot(dot(spread, mode_ref[0], ((1,), (1,))), lifted)
-    imag = dot(dot(spread, mode_ref[1], ((1,), (1,))), lifted)
+    across = ((1,), (1,))
+    lifted = dot(dot(spread_ref[:, :channels], lift_ref[...], across), place_ref[...])
+    lifted = lifted * spread_ref[:, channels : channels + half]
+    real = dot(dot(spread, mode_ref[0], across), lifted)
+    imag = dot(dot(spread, mode_ref[1], across), lifted)
     cosine = turn_ref[block, 0]
     sine = turn_ref[block, 1]
-    first = cosine * real - sine * imag
-    second = -(cosine * imag + sine * real)
-    left[...] = jnp.zeros_like(left)
-    coupled = jnp.concatenate([first, second], axis=1).astype(BF16)
-    width = 2 * half
-    left[:, 0:width] = coupled
-    left[:, width : 2 * width] = coupled
-    constant = dot(spread, mode_ref[0, 0:channels, :], ((1,), (1,)))
+    coupled = jnp.concatenate([cosine * real - sine * imag, -(cosine * imag + sine * real)], axis=1)
+    coupled = coupled.astype(BF16)
+    mixing[...] = jnp.concatenate([coupled, coupled], axis=1)
+    constant = dot(spread, mode_ref[0, 0:channels, :], across)
     offset[...] = jnp.sum(constant * bias_ref[...], axis=1, keepdims=True)
-
-
-def kernel_sizes(rows, channels, modes_x):
-    padded_channels = -(-channels // 8) * 8
+    height = spread.shape[0]
+    widest = wide_ref[0:channels, :]
+    repeated = dot(dot(spread, local_ref[...].astype(F32), across), widest)
+    pointwise[...] = (repeated * wide_ref[channels : channels + height, :]).astype(BF16)
+    padded = wide_ref[channels + height :, 0:channels]
+    lift_table[:, 0:FIELDS] = dot(padded, lift_ref[...], across)
+    lift_table[:, FIELDS : FIELDS + 1] = dot(padded, bias_ref[...], across)
+
+
+def pointwise_body(p_ref, q_ref, stiff, dense, lift_ref, left, offset, out, right):
+    rows, group, depth = p_ref.shape
+    padded_channels = lift_ref.shape[0]
     height = rows * padded_channels
-    coupled = FIELDS * modes_x * 2
-    depth = -(-(2 * coupled + height) // 256) * 256
-    return padded_channels, height, coupled, depth
+
+    @pl.when(pl.program_id(0) == 0)
+    def _():
+        right[...] = jnp.zeros_like(right)
+
+    weights = [lift_ref[:, index : index + 1] for index in range(FIELDS + 1)]
+    for y in range(group):
+        lifted = []
+        for row in range(rows):
+            total = jnp.broadcast_to(weights[FIELDS], (padded_channels, depth))
+            for index, ref in enumerate((p_ref, q_ref, stiff, dense)):
+                total = total + ref[row, y : y + 1, :] * weights[index]
+            lifted.append(total)
+        right[y, 0:height, :] = jnp.concatenate(lifted, axis=0).astype(BF16)
+        out[:, y, :] = jnp.dot(left[...], right[y], preferred_element_type=F32) + offset[...]
 
 
 def output_body(
-    where_ref, mine, other, p_ref, q_ref, stiff, dense, lift_ref, left, offset, table_y, table_z,
-    wave_ref, wave_other, features, wave_out, modes, right,
+    where_ref, mine, other, local, left, table_y, table_z, wave_ref, wave_other,
+    features, wave_out, modes, right, sums,
 ):
     step = pl.program_id(0)
     core = where_ref[0] % 2
     column = where_ref[1]
     modes_x, modes_y, width = mine.shape[1:]
     half = width // 2
-    rows, group, depth = p_ref.shape
-    brick_y = modes.shape[0]
-    channels = features.shape[2]
-    padded_channels = lift_ref.shape[0]
-    height = rows * padded_channels
+    rows, channels, group, depth = features.shape
     coupled = FIELDS * modes_x
 
     @pl.when(step == 0)
@@ -265,7 +269,6 @@
                 for mode in range(start, start + chunk):
                     lanes = slice((mode - start) * width, (mode - start + 1) * width)
                     modes[:, mode * FIELDS + field, :] = result[:, lanes]
-        right[...] = jnp.zeros_like(right)
         z_half = depth // 2
         for row in range(rows):
             own = jnp.where(core == 0, wave_ref[row, :, :z_half], wave_ref[row, :, z_half:])
@@ -277,7 +280,6 @@
     waves = jnp.dot(high, table_z[...], preferred_element_type=F32)
     waves = waves + jnp.dot(low, table_z[...], preferred_element_type=F32)
     high, low = high_low(waves)
-    weights = [lift_ref[:, index : index + 1] for index in range(FIELDS + 1)]
     for y in range(group):
         lines = slice(y * coupled, (y + 1) * coupled)
         position = 0
@@ -285,20 +287,14 @@
             for lanes in (slice(0, depth), slice(depth, 2 * depth)):
                 right[y, position : position + coupled, :] = part[lines, lanes]
                 position += coupled
-        lifted = []
-        for row in range(rows):
-            total = jnp.broadcast_to(weights[FIELDS], (padded_channels, depth))
-            for index, ref in enumerate((p_ref, q_ref, stiff, dense)):
-                total = total + ref[row, y : y + 1, :] * weights[index]
-            lifted.append(total)
-        right[y, position : position + height, :] = jnp.concatenate(lifted, axis=0).astype(BF16)
-        total = jnp.dot(left[...], right[y], preferred_element_type=F32) + offset[...]
-        inner = math.sqrt(2.0 / math.pi) * (total + 0.044715 * (total * total * total))
-        total = (0.5 * total) * (1.0 + jnp.tanh(inner))
-        total = total.astype(BF16)
-        for row in range(rows):
-            at = row * padded_channels
-            features[row, y] = total[at : at + channels]
+        sums[:, y, :] = jnp.dot(left[...], right[y], preferred_element_type=F32)
+    for row in range(rows):
+        for channel in range(channels):
+            at = row * channels + channel
+            total = sums[at] + local[at]
+            inner = math.sqrt(2.0 / math.pi) * (total + 0.044715 * (total * total * total))
+            total = (0.5 * total) * (1.0 + jnp.tanh(inner))
+            features[row, channel] = total.astype(BF16)
 
 
 def xor_pairs(count, distance):
@@ -337,7 +333,10 @@
     rows = brick_x // core_count
     assert core_count == 2 and rows >= REACH
     blocks = cycle_count * core_count
-    padded_channels, height, coupled, right_depth = kernel_sizes(rows, channels, modes_x)
+    padded_channels = -(-channels // 8) * 8
+    height = rows * channels
+    coupled = FIELDS * modes_x
+    right_depth = -(-rows * padded_channels // 128) * 128
     two_sided = column_count > 2
 
     kept_first = kept_modes(total_x, modes_x)
@@ -358,14 +357,19 @@
     inverse_y = np.concatenate([cy3, sy3, cy3, sy3], 2)
     cx, sx = [t.astype(np.float32) for t in cos_sin(np.arange(total_x), kept_first, total_x)]
     twiddle_x = np.stack([cx, sx], -1).reshape(-1)
-    owner = np.zeros((height, channels), np.float32)
-    turn = np.zeros((blocks, 2, height, modes_x * FIELDS), np.float32)
-    for row in range(rows):
-        owner[row * padded_channels : row * padded_channels + channels] = np.eye(channels)
+    owner = np.tile(np.eye(channels, dtype=np.float32), (rows, 1))
+    turn = np.zeros((blocks, 2, height, coupled), np.float32)
     for source, table in enumerate((cx, sx)):
         turn[:, source] = np.repeat(
-            np.repeat(table.reshape(blocks, rows, modes_x), padded_channels, 1), FIELDS, 2
+            np.repeat(table.reshape(blocks, rows, modes_x), channels, 1), FIELDS, 2
         )
+    padded_eye = np.eye(channels, padded_channels, dtype=np.float32)
+    wide = np.zeros((channels + height + padded_channels, right_depth), np.float32)
+    wide[:channels, : rows * padded_channels] = np.tile(padded_eye, (1, rows))
+    wide[channels : channels + height, : rows * padded_channels] = np.kron(
+        np.eye(rows), np.ones((channels, padded_channels))
+    )
+    wide[channels + height :, :channels] = padded_eye.T
     spread = np.tile(np.eye(channels, dtype=np.float32), (modes_x, 1))
     same = np.repeat(
         np.repeat(np.eye(modes_x, dtype=np.float32), channels, 0), FIELDS, 1
@@ -386,27 +390,20 @@
     edge = [shape(rows, EDGE, total_z)] * (2 if two_sided else 1)
     half = shape(rows, brick_y, brick_z)
 
-    send = call(pack_body, shape(3, rows, brick_y, brick_z), [SMEM] + [VMEM] * 3, moved=cells * 24)(
-        where, pressure, previous, material
-    )
     swap_core = xor_pairs(core_count, 1)
-    got = lax.ppermute(send, "gz", swap_core)
+    got = [lax.ppermute(array, "gz", swap_core) for array in (pressure, previous, material)]
     current, before, ratio, bend, stiff, dense, *edge_values = call(
-        assemble_body, [field] * 6 + edge, [SMEM] * 4 + [VMEM] * 4, moved=cells * 36
-    )(where, stiffness, density, nonlinear, pressure, previous, material, got)
-
-    left, offset = call(
-        prepare_body, [shape(height, right_depth, dtype=BF16), shape(height, 1)], [SMEM] + [VMEM] * 8
+        assemble_body, [field] * 6 + edge, [SMEM] * 4 + [VMEM] * 6, moved=cells * 36
+    )(where, stiffness, density, nonlinear, pressure, previous, material, *got)
+
+    mixing, pointwise, lift_table, offset = call(
+        prepare_body,
+        [shape(height, 4 * coupled, dtype=BF16), shape(height, right_depth, dtype=BF16),
+         shape(padded_channels, FIELDS + 1), shape(height, 1)],
+        [SMEM] + [VMEM] * 9, flops=2_000_000_000, moved=4_000_000,
     )(
         where, mode_weight.reshape(2, modes_x * channels, channels), lift_weight,
-        lift_bias.reshape(1, channels), local_weight, spread, place, owner, turn,
-    )
-    wide = jnp.zeros((rows, padded_channels, rows, padded_channels), BF16)
-    small = jnp.pad(local_weight.T, ((0, padded_channels - channels),) * 2)
-    wide = (np.eye(rows, dtype=ml_dtypes.bfloat16)[:, None, :, None] * small[None, :, None, :]).reshape(height, height)
-    left = left.at[:, 2 * coupled : 2 * coupled + height].set(wide)
-    lift_table = jnp.pad(
-        jnp.concatenate([lift_weight, lift_bias[None]], 0).T, ((0, padded_channels - channels), (0, 0))
+        lift_bias.reshape(1, channels), local_weight, spread, place, owner, turn, wide,
     )
 
     for repeat in range(STEPS):
@@ -432,30 +429,50 @@
         flops=cells * 2048, moved=cells * 32,
     )(where, twiddle_x, current, before, stiff, dense, forward_z, forward_y)
     total = keep + lax.ppermute(send, "gz", swap_core)
-    for axis, count in (("gy", column_count), ("gx", cycle_count)):
-        distance = 1
-        while distance < count:
-            total = total + lax.ppermute(total, axis, xor_pairs(count, distance))
-            distance *= 2
-    other = lax.ppermute(total, "gz", swap_core)
-
     group = 8
     whole = lambda array: pl.BlockSpec(array.shape, lambda i: (0,) * len(array.shape))
     slab = pl.BlockSpec((rows, group, total_z), lambda i: (0, i, 0))
+    strip = pl.BlockSpec((height, group, total_z), lambda i: (0, i, 0))
+    stages = [(axis, count, 2**bit) for axis, count in (("gy", column_count), ("gx", cycle_count))
+              for bit in range((count - 1).bit_length())]
+    for index, (axis, count, distance) in enumerate(stages):
+        arrived = lax.ppermute(total, axis, xor_pairs(count, distance))
+        if index == 0:
+            arrived, mixing, pointwise, lift_table, offset = lax.optimization_barrier(
+                (arrived, mixing, pointwise, lift_table, offset)
+            )
+        if index == len(stages) - 1:
+            local = pl.pallas_call(
+                pointwise_body,
+                grid=(brick_y // group,),
+                out_shape=shape(height, brick_y, total_z),
+                in_specs=[slab] * 4 + [whole(lift_table), whole(pointwise), whole(offset)],
+                out_specs=strip,
+                scratch_shapes=[pltpu.VMEM((group, right_depth, total_z), BF16)],
+                compiler_params=pltpu.CompilerParams(vmem_limit_bytes=24 * 1024 * 1024),
+                cost_estimate=pl.CostEstimate(flops=cells * 40000, bytes_accessed=cells * 100, transcendentals=0),
+            )(current, before, stiff, dense, lift_table, pointwise, offset)
+            arrived, local = lax.optimization_barrier((arrived, local))
+        total = total + arrived
+    other = lax.ppermute(total, "gz", swap_core)
+
+    scoped = 12 * 2**20 + 4 * (6 * 2 * modes_x * modes_y * width + brick_y * coupled * width + 6 * group * coupled * total_z)
     features, wave = pl.pallas_call(
         output_body,
         grid=(brick_y // group,),
-        out_shape=[shape(rows, brick_y, channels, total_z, dtype=BF16), shape(*pressure.shape)],
-        in_specs=[SMEM, whole(part), whole(part), slab, slab, slab, slab, whole(lift_table), whole(left),
-                  whole(offset), whole(inverse_y), whole(inverse_z), whole(field), whole(half)],
-        out_specs=[pl.BlockSpec((rows, group, channels, total_z), lambda i: (0, i, 0, 0)), whole(pressure)],
+        out_shape=[shape(rows, channels, brick_y, total_z, dtype=BF16), shape(*pressure.shape)],
+        in_specs=[SMEM, whole(part), whole(part), strip, whole(mixing), whole(inverse_y), whole(inverse_z),
+                  whole(field), whole(half)],
+        out_specs=[pl.BlockSpec((rows, channels, group, total_z), lambda i: (0, 0, i, 0)), whole(pressure)],
         scratch_shapes=[
-            pltpu.VMEM((brick_y, FIELDS * modes_x, width), F32),
-            pltpu.VMEM((group, right_depth, total_z), BF16),
+            pltpu.VMEM((brick_y, coupled, width), F32),
+            pltpu.VMEM((group, 4 * coupled, total_z), BF16),
+            pltpu.VMEM((height, group, total_z), F32),
         ],
-        compiler_params=pltpu.CompilerParams(vmem_limit_bytes=56 * 1024 * 1024),
+        compiler_params=pltpu.CompilerParams(vmem_limit_bytes=scoped),
         cost_estimate=pl.CostEstimate(flops=cells * 2000, bytes_accessed=cells * 60, transcendentals=cells * 20),
-    )(where, total, other, current, before, stiff, dense, lift_table, left, offset, inverse_y, inverse_z, current, wave_other)
+    )(where, total, other, local, mixing, inverse_y, inverse_z, current, wave_other)
+    features = features.transpose(0, 2, 1, 3)
     return (wave, features)
 
 

time: 102 us -> 91.7 us (0.90)
  waiting for transfers between devices: 35.6 us -> 29 us
  local copies, waits for them, and re-layouts: 10.8 us -> 4.94 us
  Pallas kernels: 21.8 us -> 25.5 us
  other arithmetic: 2.24 us -> 0.83 us
    ppermute x4 -> x6, waiting for transfers between devices: 24.4 us -> 16.7 us  [the longest x3 15.7 us: per_device(): arrived = lax.ppermute(total, axis, xor_pairs(count, distance))]
    unnamed x58 -> x40, local copies, waits for them, and re-layouts: 9.75 us -> 4.89 us
    pallas_call x3, Pallas kernels: 3.73 us -> 8.27 us  [the longest x1 5.07 us: per_device(): pl.pallas_call(pointwise_body, grid=(brick_y // group,), out_shape=shape(...]
    another operation x2 -> x0, other arithmetic: 1.29 us -> none
    ppermute x1, waiting for transfers between devices: 0.12 us -> 1.21 us  [per_device(): wave_other = lax.ppermute(edge_values[0], 'gz', swap_core)]
    ppermute x4 -> x6, starting transfers between devices: 6.43 us -> 7.09 us  [the longest x3 6.06 us: per_device(): arrived = lax.ppermute(total, axis, xor_pairs(count, distance))]
  transfers between devices with their start and end apart: 19 -> 21, of which waited for: 10 -> 12; matrix products, arithmetic and copies ran while one was open for 3% -> 1% of each run, Pallas kernels for 2% -> 8%
where the time goes in v2:
time: 91.7 us; the launch traced here: 91.3 us
  starting transfers between devices  30.1 us (33%)
  waiting for transfers between devices  29 us (32%)
  Pallas kernels  25.5 us (28%)
  local copies, waits for them, and re-layouts  4.94 us (5%)
  between operations  0.93 us (1%)
    ppermute x3, waiting for transfers between devices, per_device(): arrived = lax.ppermute(total, axis, xor_pairs(count, distance))  15.7 us
    ppermute x4, starting transfers between devices, per_device(): mate = lax.ppermute(current, 'gz', swap_core)  13.6 us
    ppermute x4, waiting for transfers between devices, per_device(): halos = [lax.ppermute(edge_values[0], 'gy', xor_pairs(column_count, 1))]  9.69 us
    pallas_call x1, Pallas kernels, per_device(): pl.pallas_call(output_body, grid=(brick_y // group,), out_shape=[shape(ro...  9.12 us
    ppermute x3, starting transfers between devices, per_device(): arrived = lax.ppermute(total, axis, xor_pairs(count, distance))  6.06 us
    ppermute x4, starting transfers between devices, per_device(): halos = [lax.ppermute(edge_values[0], 'gy', xor_pairs(column_count, 1))]  5.96 us
    pallas_call x4, Pallas kernels, per_device(): call(body, outs, [SMEM] + [VMEM] * (6 + len(halos)), [pltpu.VMEM((brick_y...  5.96 us
    pallas_call x1, Pallas kernels, per_device(): pl.pallas_call(pointwise_body, grid=(brick_y // group,), out_shape=shape(...  5.07 us
  transfers between devices with their start and end apart: 21, of which 12 were waited for; matrix products, arithmetic and copies ran while one was open for 1% of the time, Pallas kernels for 8%

profile of v2, /device:TPU:0, one launch (start us, length us, event | category | flops | bytes accessed | tf_op | source)
XLA Modules:
  0.0 91.3 jit_solution(13361864392518482238)
XLA Ops:
  3.3 0.9 %copy-done = f32[8,64,128]{2,1,0:T(8,128)S(1)} copy-done((f32[8,64,128]{2,1,0:T(8,128)S(1)}, f32[8,64,128]{2,1,0:T(8,128)}, u32[]{:S(2)}) %copy-start) | copy-done | bytes 262168
  4.2 0.9 %copy-done.1 = f32[8,64,128]{2,1,0:T(8,128)S(1)} copy-done((f32[8,64,128]{2,1,0:T(8,128)S(1)}, f32[8,64,128]{2,1,0:T(8,128)}, u32[]{:S(2)}) %copy-start.1) | copy-done | bytes 262168
  5.2 0.9 %copy-done.2 = s32[8,64,128]{2,1,0:T(8,128)S(1)} copy-done((s32[8,64,128]{2,1,0:T(8,128)S(1)}, s32[8,64,128]{2,1,0:T(8,128)}, u32[]{:S(2)}) %copy-start.2) | copy-done | bytes 262168
  8.2 1.0 %shard_map.221 = (f32[4,64,256]{2,1,0:T(8,128)S(1)}, f32[4,64,256]{2,1,0:T(8,128)S(1)}, f32[4,64,256]{2,1,0:T(8,128)S(1)}, f32[4,64,256]{2,1,0:T(8,128)S(1)}, f3...) custom-call(s32[2]{0:T(128)S(1)} %multiply_add_fusion.where_ref.refs_0_, ...), custom_call_target="tpu_custom_call" | custom-call | bytes 2359296 | tf_op jit(solution)/shard_map/pallas_call | solution.py:395
  9.9 4.4 %collective-permute-start.3 = (f32[4,64,256]{2,1,0:T(8,128)S(1)}, f32[4,64,256]{2,1,0:T(8,128)S(1)}, u32[]{:S(2)}, u32[]{:S(2)}) collective-permute-start(f32[4,64,256]{2,1,0:T(8,128)S(1)} %get-tuple-element.32.refs_1_.refs_2_), channel_id=1, source_target_pairs={{0,1},{1,0},{2,3},{3,2},{4,5},{5,4},{6,7},{7,6},{8,9},{9,8},{10,11... | collective-permute-start | bytes 786440 | tf_op jit(solution)/shard_map/ppermute | solution.py:412
  14.2 1.5 %collective-permute-start.5 = (f32[4,8,256]{2,1,0:T(8,128)S(1)}, f32[4,8,256]{2,1,0:T(8,128)S(1)}, u32[]{:S(2)}, u32[]{:S(2)}) collective-permute-start(f32[4,8,256]{2,1,0:T(8,128)S(1)} %get-tuple-element.36), channel_id=1, source_target_pairs={{0,2},{2,0},{1,3},{3,1},{4,6},{6,4},{5,7},{7,5},{8,10},{10,8},{9,1... | collective-permute-start | bytes 98312 | tf_op jit(solution)/shard_map/ppermute | solution.py:413
  15.7 2.4 %collective-permute-done.5.refs_7_ = f32[4,8,256]{2,1,0:T(8,128)S(1)} collective-permute-done((f32[4,8,256]{2,1,0:T(8,128)S(1)}, f32[4,8,256]{2,1,0:T(8,128)S(1)}, u32[]{:S(2)}, u32[]{:S(2)}) %collective-permute-start.5) | collective-permute-done | bytes 32800 | tf_op jit(solution)/shard_map/ppermute | solution.py:413
  18.1 1.5 %shard_map.222 = (f32[4,64,256]{2,1,0:T(8,128)S(1)}, f32[4,8,256]{2,1,0:T(8,128)S(1)}) custom-call(s32[2]{0:T(128)S(1)} %multiply_add_fusion.where_ref.refs_0_, f32[4,64,256]{2,1,0:T(8,128)S(1)} %get-tuple-element.32.refs_1_.refs_2_, f32[4,64,256]{2,1,0:T(8,128)S(1)} %get-tuple-element.33.refs_2_, f32[4,64,256]{2,1,0:T(8,128)S(1)} %get-tuple-element.34.refs_3_, ...), custom_call_target="tpu_custom_call" | custom-call | flops 3932160 | bytes 1835008 | tf_op jit(solution)/shard_map/pallas_call | solution.py:418
  20.3 3.1 %collective-permute-start.6 = (f32[4,64,256]{2,1,0:T(8,128)S(1)}, f32[4,64,256]{2,1,0:T(8,128)S(1)}, u32[]{:S(2)}, u32[]{:S(2)}) collective-permute-start(f32[4,64,256]{2,1,0:T(8,128)S(1)} %get-tuple-element.37.refs_1_.refs_2_), channel_id=1, source_target_pairs={{0,1},{1,0},{2,3},{3,2},{4,5},{5,4},{6,7},{7,6},{8,9},{9,8},{10,11... | collective-permute-start | bytes 786440 | tf_op jit(solution)/shard_map/ppermute | solution.py:412
  23.4 1.5 %collective-permute-start.8 = (f32[4,8,256]{2,1,0:T(8,128)S(1)}, f32[4,8,256]{2,1,0:T(8,128)S(1)}, u32[]{:S(2)}, u32[]{:S(2)}) collective-permute-start(f32[4,8,256]{2,1,0:T(8,128)S(1)} %get-tuple-element.38), channel_id=1, source_target_pairs={{0,2},{2,0},{1,3},{3,1},{4,6},{6,4},{5,7},{7,5},{8,10},{10,8},{9,1... | collective-permute-start | bytes 98312 | tf_op jit(solution)/shard_map/ppermute | solution.py:413
  24.9 2.4 %collective-permute-done.8.refs_7_ = f32[4,8,256]{2,1,0:T(8,128)S(1)} collective-permute-done((f32[4,8,256]{2,1,0:T(8,128)S(1)}, f32[4,8,256]{2,1,0:T(8,128)S(1)}, u32[]{:S(2)}, u32[]{:S(2)}) %collective-permute-start.8) | collective-permute-done | bytes 32800 | tf_op jit(solution)/shard_map/ppermute | solution.py:413
  27.3 1.5 %shard_map.223 = (f32[4,64,256]{2,1,0:T(8,128)S(1)}, f32[4,8,256]{2,1,0:T(8,128)S(1)}) custom-call(s32[2]{0:T(128)S(1)} %multiply_add_fusion.where_ref.refs_0_, f32[4,64,256]{2,1,0:T(8,128)S(1)} %get-tuple-element.37.refs_1_.refs_2_, f32[4,64,256]{2,1,0:T(8,128)S(1)} %get-tuple-element.32.refs_1_.refs_2_, f32[4,64,256]{2,1,0:T(8,128)S(1)} %get-tuple-element.34.refs_3_, ...), custom_call_target="tpu_custom_call" | custom-call | flops 3932160 | bytes 1835008 | tf_op jit(solution)/shard_map/pallas_call | solution.py:418
  29.5 3.1 %collective-permute-start.9 = (f32[4,64,256]{2,1,0:T(8,128)S(1)}, f32[4,64,256]{2,1,0:T(8,128)S(1)}, u32[]{:S(2)}, u32[]{:S(2)}) collective-permute-start(f32[4,64,256]{2,1,0:T(8,128)S(1)} %get-tuple-element.39.refs_1_.refs_2_), channel_id=1, source_target_pairs={{0,1},{1,0},{2,3},{3,2},{4,5},{5,4},{6,7},{7,6},{8,9},{9,8},{10,11... | collective-permute-start | bytes 786440 | tf_op jit(solution)/shard_map/ppermute | solution.py:412
  32.6 1.5 %collective-permute-start.11 = (f32[4,8,256]{2,1,0:T(8,128)S(1)}, f32[4,8,256]{2,1,0:T(8,128)S(1)}, u32[]{:S(2)}, u32[]{:S(2)}) collective-permute-start(f32[4,8,256]{2,1,0:T(8,128)S(1)} %get-tuple-element.40), channel_id=1, source_target_pairs={{0,2},{2,0},{1,3},{3,1},{4,6},{6,4},{5,7},{7,5},{8,10},{10,8},{9,1... | collective-permute-start | bytes 98312 | tf_op jit(solution)/shard_map/ppermute | solution.py:413
  34.1 2.4 %collective-permute-done.11.refs_7_ = f32[4,8,256]{2,1,0:T(8,128)S(1)} collective-permute-done((f32[4,8,256]{2,1,0:T(8,128)S(1)}, f32[4,8,256]{2,1,0:T(8,128)S(1)}, u32[]{:S(2)}, u32[]{:S(2)}) %collective-permute-start.11) | collective-permute-done | bytes 32800 | tf_op jit(solution)/shard_map/ppermute | solution.py:413
  36.5 1.5 %shard_map.224 = (f32[4,64,256]{2,1,0:T(8,128)S(1)}, f32[4,8,256]{2,1,0:T(8,128)S(1)}) custom-call(s32[2]{0:T(128)S(1)} %multiply_add_fusion.where_ref.refs_0_, f32[4,64,256]{2,1,0:T(8,128)S(1)} %get-tuple-element.39.refs_1_.refs_2_, f32[4,64,256]{2,1,0:T(8,128)S(1)} %get-tuple-element.37.refs_1_.refs_2_, f32[4,64,256]{2,1,0:T(8,128)S(1)} %get-tuple-element.34.refs_3_, ...), custom_call_target="tpu_custom_call" | custom-call | flops 3932160 | bytes 1835008 | tf_op jit(solution)/shard_map/pallas_call | solution.py:418
  38.7 3.1 %collective-permute-start.12 = (f32[4,64,256]{2,1,0:T(8,128)S(1)}, f32[4,64,256]{2,1,0:T(8,128)S(1)}, u32[]{:S(2)}, u32[]{:S(2)}) collective-permute-start(f32[4,64,256]{2,1,0:T(8,128)S(1)} %get-tuple-element.41.refs_1_.q_ref), channel_id=1, source_target_pairs={{0,1},{1,0},{2,3},{3,2},{4,5},{5,4},{6,7},{7,6},{8,9},{9,8},{10,11... | collective-permute-start | bytes 786440 | tf_op jit(solution)/shard_map/ppermute | solution.py:412
  41.8 1.5 %collective-permute-start.14 = (f32[4,8,256]{2,1,0:T(8,128)S(1)}, f32[4,8,256]{2,1,0:T(8,128)S(1)}, u32[]{:S(2)}, u32[]{:S(2)}) collective-permute-start(f32[4,8,256]{2,1,0:T(8,128)S(1)} %get-tuple-element.42), channel_id=1, source_target_pairs={{0,2},{2,0},{1,3},{3,1},{4,6},{6,4},{5,7},{7,5},{8,10},{10,8},{9,1... | collective-permute-start | bytes 98312 | tf_op jit(solution)/shard_map/ppermute | solution.py:413
  43.3 2.4 %collective-permute-done.14.refs_7_ = f32[4,8,256]{2,1,0:T(8,128)S(1)} collective-permute-done((f32[4,8,256]{2,1,0:T(8,128)S(1)}, f32[4,8,256]{2,1,0:T(8,128)S(1)}, u32[]{:S(2)}, u32[]{:S(2)}) %collective-permute-start.14) | collective-permute-done | bytes 32800 | tf_op jit(solution)/shard_map/ppermute | solution.py:413
  45.7 1.5 %shard_map.225 = (f32[4,64,256]{2,1,0:T(8,128)S(1)}, f32[4,64,128]{2,1,0:T(8,128)S(1)}) custom-call(s32[2]{0:T(128)S(1)} %multiply_add_fusion.where_ref.refs_0_, f32[4,64,256]{2,1,0:T(8,128)S(1)} %get-tuple-element.41.refs_1_.q_ref, f32[4,64,256]{2,1,0:T(8,128)S(1)} %get-tuple-element.39.refs_1_.refs_2_, f32[4,64,256]{2,1,0:T(8,128)S(1)} %get-tuple-element.34.refs_3_, ...), custom_call_target="tpu_custom_call" | custom-call | flops 3932160 | bytes 1835008 | tf_op jit(solution)/shard_map/pallas_call | solution.py:418
  47.3 2.1 %shard_map.226 = (f32[2,8,32,128]{3,2,1,0:T(8,128)S(1)}, f32[2,8,32,128]{3,2,1,0:T(8,128)S(1)}) custom-call(s32[2]{0:T(128)S(1)} %multiply_add_fusion.where_ref.refs_0_, f32[512]{0:T(512)S(1)} %copy-done.7, f32[4,64,256]{2,1,0:T(8,128)S(1)} %get-tuple-element.43.p_ref.wave_ref, f32[4,64,256]{2,1,0:T(8,128)S(1)} %get-tuple-element.41.refs_1_.q_ref, ...), custom_call_target="tpu_custom_call" | custom-call | flops 134217728 | bytes 2097152 | tf_op jit(solution)/shard_map/pallas_call | solution.py:426
  49.6 1.4 %collective-permute-done.15 = f32[2,8,32,128]{3,2,1,0:T(8,128)S(1)} collective-permute-done((f32[2,8,32,128]{3,2,1,0:T(8,128)S(1)}, f32[2,8,32,128]{3,2,1,0:T(8,128)S(1)}, u32[]{:S(2)}, u32[]{:S(2)}) %collective-permute-start.15) | collective-permute-done | bytes 262176 | tf_op jit(solution)/shard_map/ppermute | solution.py:431
  51.0 1.6 %collective-permute-start.16 = (f32[2,8,32,128]{3,2,1,0:T(8,128)S(1)}, f32[2,8,32,128]{3,2,1,0:T(8,128)S(1)}, u32[]{:S(2)}, u32[]{:S(2)}) collective-permute-start(f32[2,8,32,128]{3,2,1,0:T(8,128)S(1)} %add.20), channel_id=1, source_target_pairs={{0,2},{2,0},{1,3},{3,1},{4,6},{6,4},{5,7},{7,5},{8,10},{10,8},{9,1... | collective-permute-start | bytes 786440 | tf_op jit(solution)/shard_map/ppermute | solution.py:439
  52.7 2.2 %shard_map.227 = (bf16[80,128]{1,0:T(8,128)(2,1)S(1)}, bf16[80,128]{1,0:T(8,128)(2,1)S(1)}, f32[24,5]{1,0:T(8,128)S(1)}, f32[80,1]{1,0:T(8,128)S(1)}) custom-call(s32[2]{0:T(128)S(1)} %multiply_add_fusion.where_ref.refs_0_, f32[2,160,20]{2,1,0:T(8,128)S(1)} %reshape.12.mode_ref, f32[4,20]{1,0:T(4,128)S(1)} %copy-done.12, f32[1,20]{1,0:T(1,128)S(1)} %bitcast.2, ...), custom_call_target="tpu_custom_call" | custom-call | flops 2000000000 | bytes 4000000 | tf_op jit(solution)/shard_map/pallas_call | solution.py:399
  54.9 4.5 %collective-permute-done.16 = f32[2,8,32,128]{3,2,1,0:T(8,128)S(1)} collective-permute-done((f32[2,8,32,128]{3,2,1,0:T(8,128)S(1)}, f32[2,8,32,128]{3,2,1,0:T(8,128)S(1)}, u32[]{:S(2)}, u32[]{:S(2)}) %collective-permute-start.16) | collective-permute-done | bytes 262176 | tf_op jit(solution)/shard_map/ppermute | solution.py:439
  59.5 1.7 %collective-permute-start.17 = (f32[2,8,32,128]{3,2,1,0:T(8,128)S(1)}, f32[2,8,32,128]{3,2,1,0:T(8,128)S(1)}, u32[]{:S(2)}, u32[]{:S(2)}) collective-permute-start(f32[2,8,32,128]{3,2,1,0:T(8,128)S(1)} %add.21), channel_id=1, source_target_pairs={{0,4},{4,0},{8,12},{12,8},{1,5},{5,1},{9,13},{13,9},{2,6},{6,2},{1... | collective-permute-start | bytes 786440 | tf_op jit(solution)/shard_map/ppermute | solution.py:439
  61.2 5.8 %collective-permute-done.17 = f32[2,8,32,128]{3,2,1,0:T(8,128)S(1)} collective-permute-done((f32[2,8,32,128]{3,2,1,0:T(8,128)S(1)}, f32[2,8,32,128]{3,2,1,0:T(8,128)S(1)}, u32[]{:S(2)}, u32[]{:S(2)}) %collective-permute-start.17) | collective-permute-done | bytes 262176 | tf_op jit(solution)/shard_map/ppermute | solution.py:439
  67.1 2.8 %collective-permute-start.18 = (f32[2,8,32,128]{3,2,1,0:T(8,128)S(1)}, f32[2,8,32,128]{3,2,1,0:T(8,128)S(1)}, u32[]{:S(2)}, u32[]{:S(2)}) collective-permute-start(f32[2,8,32,128]{3,2,1,0:T(8,128)S(1)} %add.22), channel_id=1, source_target_pairs={{0,8},{4,12},{8,0},{12,4},{1,9},{5,13},{9,1},{13,5},{2,10},{6,14},... | collective-permute-start | bytes 786440 | tf_op jit(solution)/shard_map/ppermute | solution.py:439
  69.9 5.1 %shard_map.228.local = f32[80,64,256]{2,1,0:T(8,128)S(1)} custom-call(f32[4,64,256]{2,1,0:T(8,128)S(1)} %get-tuple-element.43.p_ref.wave_ref, f32[4,64,256]{2,1,0:T(8,128)S(1)} %get-tuple-element.41.refs_1_.q_ref, f32[4,64,256]{2,1,0:T(8,128)S(1)} %get-tuple-element.44.stiff, f32[4,64,256]{2,1,0:T(8,128)S(1)} %get-tuple-element.45.dense, ...), custom_call_target="tpu_custom_call" | custom-call | flops 2621440000 | bytes 6553600 | tf_op jit(solution)/shard_map/pallas_call | solution.py:445
  75.0 5.4 %collective-permute-done.18 = f32[2,8,32,128]{3,2,1,0:T(8,128)S(1)} collective-permute-done((f32[2,8,32,128]{3,2,1,0:T(8,128)S(1)}, f32[2,8,32,128]{3,2,1,0:T(8,128)S(1)}, u32[]{:S(2)}, u32[]{:S(2)}) %collective-permute-start.18) | collective-permute-done | bytes 262176 | tf_op jit(solution)/shard_map/ppermute | solution.py:439
  81.0 1.2 %collective-permute-done.20.wave_other = f32[4,64,128]{2,1,0:T(8,128)S(1)} collective-permute-done((f32[4,64,128]{2,1,0:T(8,128)S(1)}, f32[4,64,128]{2,1,0:T(8,128)S(1)}, u32[]{:S(2)}, u32[]{:S(2)}) %collective-permute-start.20) | collective-permute-done | bytes 131104 | tf_op jit(solution)/shard_map/ppermute | solution.py:424
  82.2 9.1 %shard_map.229 = (bf16[4,20,64,256]{3,2,1,0:T(8,128)(2,1)}, f32[8,64,128]{2,1,0:T(8,128)}) custom-call(s32[2]{0:T(128)S(1)} %multiply_add_fusion.where_ref.refs_0_, f32[2,8,32,128]{3,2,1,0:T(8,128)S(1)} %add.23.mine, f32[2,8,32,128]{3,2,1,0:T(8,128)S(1)} %collective-permute-done.19.other, f32[80,64,256]{2,1,0:T(8,128)S(1)} %shard_map.228.local, ...), custom_call_target="tpu_custom_call" | custom-call | flops 131072000 | bytes 3932160 | tf_op jit(solution)/shard_map/pallas_call | solution.py:460
  (66 shorter events, 8.4 us)
Async XLA Ops:
  0.6 46.6 %copy-start.6 = (bf16[2,32,256]{2,1,0:T(8,128)(2,1)S(1)}, bf16[2,32,256]{2,1,0:T(8,128)(2,1)}, u32[]{:S(2)}) copy-start(bf16[2,32,256]{2,1,0:T(8,128)(2,1)} %constant.45.clone.table_y) | copy-start | bytes 98308
  0.6 46.6 %copy-start.7 = (f32[512]{0:T(512)S(1)}, f32[512]{0:T(512)}, u32[]{:S(2)}) copy-start(f32[512]{0:T(512)} %constant.43.clone.twiddle_x) | copy-start | bytes 6148
  0.7 1.9 %collective-permute-start = (f32[8,64,128]{2,1,0:T(8,128)}, f32[8,64,128]{2,1,0:T(8,128)S(1)}, u32[]{:S(2)}, u32[]{:S(2)}) collective-permute-start(f32[8,64,128]{2,1,0:T(8,128)} %pressure.1), channel_id=1, source_target_pairs={{0,1},{1,0},{2,3},{3,2},{4,5},{5,4},{6,7},{7,6},{8,9},{9,8},{10,11... | collective-permute-start | bytes 786440 | tf_op jit(solution)/shard_map/ppermute | solution.py:394
  1.2 1.7 %collective-permute-start.1 = (f32[8,64,128]{2,1,0:T(8,128)}, f32[8,64,128]{2,1,0:T(8,128)S(1)}, u32[]{:S(2)}, u32[]{:S(2)}) collective-permute-start(f32[8,64,128]{2,1,0:T(8,128)} %previous.1), channel_id=1, source_target_pairs={{0,1},{1,0},{2,3},{3,2},{4,5},{5,4},{6,7},{7,6},{8,9},{9,8},{10,11... | collective-permute-start | bytes 786440 | tf_op jit(solution)/shard_map/ppermute | solution.py:394
  1.3 2.0 %collective-permute-start.2 = (s32[8,64,128]{2,1,0:T(8,128)}, s32[8,64,128]{2,1,0:T(8,128)S(1)}, u32[]{:S(2)}, u32[]{:S(2)}) collective-permute-start(s32[8,64,128]{2,1,0:T(8,128)} %material.1), channel_id=1, source_target_pairs={{0,1},{1,0},{2,3},{3,2},{4,5},{5,4},{6,7},{7,6},{8,9},{9,8},{10,11... | collective-permute-start | bytes 786440 | tf_op jit(solution)/shard_map/ppermute | solution.py:394
  1.7 51.0 %copy-start.13 = (f32[20]{0:T(128)S(1)}, f32[20]{0:T(128)}, u32[]{:S(2)}) copy-start(f32[20]{0:T(128)} %param.29) | copy-start | bytes 244
  1.7 51.0 %copy-start.12 = (f32[4,20]{1,0:T(4,128)S(1)}, f32[4,20]{1,0:T(4,128)}, u32[]{:S(2)}) copy-start(f32[4,20]{1,0:T(4,128)} %lift_ref.1) | copy-start | bytes 964
  8.1 44.5 %copy-start.19 = (f32[2,8,20,20]{3,1,2,0:T(8,128)S(1)}, f32[2,8,20,20]{3,1,2,0:T(8,128)}, u32[]{:S(2)}) copy-start(f32[2,8,20,20]{3,1,2,0:T(8,128)} %param.30) | copy-start | bytes 76804
  8.1 44.6 %copy-start.11 = (bf16[20,20]{1,0:T(8,128)(2,1)S(1)}, bf16[20,20]{1,0:T(8,128)(2,1)}, u32[]{:S(2)}) copy-start(bf16[20,20]{1,0:T(8,128)(2,1)} %local_ref.1) | copy-start | bytes 2404
  8.1 44.6 %copy-start.14 = (f32[8,2,80,32]{3,2,1,0:T(8,128)S(1)}, f32[8,2,80,32]{3,2,1,0:T(8,128)}, u32[]{:S(2)}) copy-start(f32[8,2,80,32]{3,2,1,0:T(8,128)} %constant.41.clone.turn_ref) | copy-start | bytes 491524
  8.1 44.6 %copy-start.15 = (f32[160,52]{1,0:T(8,128)S(1)}, f32[160,52]{1,0:T(8,128)}, u32[]{:S(2)}) copy-start(f32[160,52]{1,0:T(8,128)} %constant.38.clone.spread_ref) | copy-start | bytes 99844
  8.1 44.6 %copy-start.16 = (f32[124,128]{1,0:T(8,128)S(1)}, f32[124,128]{1,0:T(8,128)}, u32[]{:S(2)}) copy-start(f32[124,128]{1,0:T(8,128)} %constant.42.clone.wide_ref) | copy-start | bytes 190468
  8.2 44.6 %copy-start.17 = (f32[80,20]{1,0:T(8,128)S(1)}, f32[80,20]{1,0:T(8,128)}, u32[]{:S(2)}) copy-start(f32[80,20]{1,0:T(8,128)} %constant.40.clone.owner_ref) | copy-start | bytes 19204
  8.2 44.6 %copy-start.18 = (f32[4,32]{1,0:T(4,128)S(1)}, f32[4,32]{1,0:T(4,128)}, u32[]{:S(2)}) copy-start(f32[4,32]{1,0:T(4,128)} %constant.39.clone.place_ref) | copy-start | bytes 1540
  9.2 9.0 %collective-permute-start.4 = (f32[4,64,256]{2,1,0:T(8,128)S(1)}, f32[4,64,256]{2,1,0:T(8,128)S(1)}, u32[]{:S(2)}, u32[]{:S(2)}) collective-permute-start(f32[4,64,256]{2,1,0:T(8,128)S(1)} %get-tuple-element.32.refs_1_.refs_2_), channel_id=1, source_target_pairs={{1,4},{5,8},{9,12},{4,1},{8,5},{12,9},{3,6},{7,10},{11,14},{6,3},{... | collective-permute-start | bytes 786440 | tf_op jit(solution)/shard_map/ppermute | solution.py:411
  9.9 8.3 %collective-permute-start.3 = (f32[4,64,256]{2,1,0:T(8,128)S(1)}, f32[4,64,256]{2,1,0:T(8,128)S(1)}, u32[]{:S(2)}, u32[]{:S(2)}) collective-permute-start(f32[4,64,256]{2,1,0:T(8,128)S(1)} %get-tuple-element.32.refs_1_.refs_2_), channel_id=1, source_target_pairs={{0,1},{1,0},{2,3},{3,2},{4,5},{5,4},{6,7},{7,6},{8,9},{9,8},{10,11... | collective-permute-start | bytes 786440 | tf_op jit(solution)/shard_map/ppermute | solution.py:412
  14.2 3.9 %collective-permute-start.5 = (f32[4,8,256]{2,1,0:T(8,128)S(1)}, f32[4,8,256]{2,1,0:T(8,128)S(1)}, u32[]{:S(2)}, u32[]{:S(2)}) collective-permute-start(f32[4,8,256]{2,1,0:T(8,128)S(1)} %get-tuple-element.36), channel_id=1, source_target_pairs={{0,2},{2,0},{1,3},{3,1},{4,6},{6,4},{5,7},{7,5},{8,10},{10,8},{9,1... | collective-permute-start | bytes 98312 | tf_op jit(solution)/shard_map/ppermute | solution.py:413
  19.6 7.7 %collective-permute-start.7 = (f32[4,64,256]{2,1,0:T(8,128)S(1)}, f32[4,64,256]{2,1,0:T(8,128)S(1)}, u32[]{:S(2)}, u32[]{:S(2)}) collective-permute-start(f32[4,64,256]{2,1,0:T(8,128)S(1)} %get-tuple-element.37.refs_1_.refs_2_), channel_id=1, source_target_pairs={{1,4},{5,8},{9,12},{4,1},{8,5},{12,9},{3,6},{7,10},{11,14},{6,3},{... | collective-permute-start | bytes 786440 | tf_op jit(solution)/shard_map/ppermute | solution.py:411
  20.3 7.0 %collective-permute-start.6 = (f32[4,64,256]{2,1,0:T(8,128)S(1)}, f32[4,64,256]{2,1,0:T(8,128)S(1)}, u32[]{:S(2)}, u32[]{:S(2)}) collective-permute-start(f32[4,64,256]{2,1,0:T(8,128)S(1)} %get-tuple-element.37.refs_1_.refs_2_), channel_id=1, source_target_pairs={{0,1},{1,0},{2,3},{3,2},{4,5},{5,4},{6,7},{7,6},{8,9},{9,8},{10,11... | collective-permute-start | bytes 786440 | tf_op jit(solution)/shard_map/ppermute | solution.py:412
  23.4 3.9 %collective-permute-start.8 = (f32[4,8,256]{2,1,0:T(8,128)S(1)}, f32[4,8,256]{2,1,0:T(8,128)S(1)}, u32[]{:S(2)}, u32[]{:S(2)}) collective-permute-start(f32[4,8,256]{2,1,0:T(8,128)S(1)} %get-tuple-element.38), channel_id=1, source_target_pairs={{0,2},{2,0},{1,3},{3,1},{4,6},{6,4},{5,7},{7,5},{8,10},{10,8},{9,1... | collective-permute-start | bytes 98312 | tf_op jit(solution)/shard_map/ppermute | solution.py:413
  28.8 7.7 %collective-permute-start.10 = (f32[4,64,256]{2,1,0:T(8,128)S(1)}, f32[4,64,256]{2,1,0:T(8,128)S(1)}, u32[]{:S(2)}, u32[]{:S(2)}) collective-permute-start(f32[4,64,256]{2,1,0:T(8,128)S(1)} %get-tuple-element.39.refs_1_.refs_2_), channel_id=1, source_target_pairs={{1,4},{5,8},{9,12},{4,1},{8,5},{12,9},{3,6},{7,10},{11,14},{6,3},{... | collective-permute-start | bytes 786440 | tf_op jit(solution)/shard_map/ppermute | solution.py:411
  29.5 7.0 %collective-permute-start.9 = (f32[4,64,256]{2,1,0:T(8,128)S(1)}, f32[4,64,256]{2,1,0:T(8,128)S(1)}, u32[]{:S(2)}, u32[]{:S(2)}) collective-permute-start(f32[4,64,256]{2,1,0:T(8,128)S(1)} %get-tuple-element.39.refs_1_.refs_2_), channel_id=1, source_target_pairs={{0,1},{1,0},{2,3},{3,2},{4,5},{5,4},{6,7},{7,6},{8,9},{9,8},{10,11... | collective-permute-start | bytes 786440 | tf_op jit(solution)/shard_map/ppermute | solution.py:412
  32.6 3.9 %collective-permute-start.11 = (f32[4,8,256]{2,1,0:T(8,128)S(1)}, f32[4,8,256]{2,1,0:T(8,128)S(1)}, u32[]{:S(2)}, u32[]{:S(2)}) collective-permute-start(f32[4,8,256]{2,1,0:T(8,128)S(1)} %get-tuple-element.40), channel_id=1, source_target_pairs={{0,2},{2,0},{1,3},{3,1},{4,6},{6,4},{5,7},{7,5},{8,10},{10,8},{9,1... | collective-permute-start | bytes 98312 | tf_op jit(solution)/shard_map/ppermute | solution.py:413
  38.0 7.7 %collective-permute-start.13 = (f32[4,64,256]{2,1,0:T(8,128)S(1)}, f32[4,64,256]{2,1,0:T(8,128)S(1)}, u32[]{:S(2)}, u32[]{:S(2)}) collective-permute-start(f32[4,64,256]{2,1,0:T(8,128)S(1)} %get-tuple-element.41.refs_1_.q_ref), channel_id=1, source_target_pairs={{1,4},{5,8},{9,12},{4,1},{8,5},{12,9},{3,6},{7,10},{11,14},{6,3},{... | collective-permute-start | bytes 786440 | tf_op jit(solution)/shard_map/ppermute | solution.py:411
  38.7 7.0 %collective-permute-start.12 = (f32[4,64,256]{2,1,0:T(8,128)S(1)}, f32[4,64,256]{2,1,0:T(8,128)S(1)}, u32[]{:S(2)}, u32[]{:S(2)}) collective-permute-start(f32[4,64,256]{2,1,0:T(8,128)S(1)} %get-tuple-element.41.refs_1_.q_ref), channel_id=1, source_target_pairs={{0,1},{1,0},{2,3},{3,2},{4,5},{5,4},{6,7},{7,6},{8,9},{9,8},{10,11... | collective-permute-start | bytes 786440 | tf_op jit(solution)/shard_map/ppermute | solution.py:412
  41.8 3.9 %collective-permute-start.14 = (f32[4,8,256]{2,1,0:T(8,128)S(1)}, f32[4,8,256]{2,1,0:T(8,128)S(1)}, u32[]{:S(2)}, u32[]{:S(2)}) collective-permute-start(f32[4,8,256]{2,1,0:T(8,128)S(1)} %get-tuple-element.42), channel_id=1, source_target_pairs={{0,2},{2,0},{1,3},{3,1},{4,6},{6,4},{5,7},{7,5},{8,10},{10,8},{9,1... | collective-permute-start | bytes 98312 | tf_op jit(solution)/shard_map/ppermute | solution.py:413
  49.4 1.6 %collective-permute-start.15 = (f32[2,8,32,128]{3,2,1,0:T(8,128)S(1)}, f32[2,8,32,128]{3,2,1,0:T(8,128)S(1)}, u32[]{:S(2)}, u32[]{:S(2)}) collective-permute-start(f32[2,8,32,128]{3,2,1,0:T(8,128)S(1)} %get-tuple-element.47), channel_id=1, source_target_pairs={{0,1},{1,0},{2,3},{3,2},{4,5},{5,4},{6,7},{7,6},{8,9},{9,8},{10,11... | collective-permute-start | bytes 786440 | tf_op jit(solution)/shard_map/ppermute | solution.py:431
  51.0 8.4 %collective-permute-start.16 = (f32[2,8,32,128]{3,2,1,0:T(8,128)S(1)}, f32[2,8,32,128]{3,2,1,0:T(8,128)S(1)}, u32[]{:S(2)}, u32[]{:S(2)}) collective-permute-start(f32[2,8,32,128]{3,2,1,0:T(8,128)S(1)} %add.20), channel_id=1, source_target_pairs={{0,2},{2,0},{1,3},{3,1},{4,6},{6,4},{5,7},{7,5},{8,10},{10,8},{9,1... | collective-permute-start | bytes 786440 | tf_op jit(solution)/shard_map/ppermute | solution.py:439
  59.5 7.6 %collective-permute-start.17 = (f32[2,8,32,128]{3,2,1,0:T(8,128)S(1)}, f32[2,8,32,128]{3,2,1,0:T(8,128)S(1)}, u32[]{:S(2)}, u32[]{:S(2)}) collective-permute-start(f32[2,8,32,128]{3,2,1,0:T(8,128)S(1)} %add.21), channel_id=1, source_target_pairs={{0,4},{4,0},{8,12},{12,8},{1,5},{5,1},{9,13},{13,9},{2,6},{6,2},{1... | collective-permute-start | bytes 786440 | tf_op jit(solution)/shard_map/ppermute | solution.py:439
  67.1 13.2 %collective-permute-start.18 = (f32[2,8,32,128]{3,2,1,0:T(8,128)S(1)}, f32[2,8,32,128]{3,2,1,0:T(8,128)S(1)}, u32[]{:S(2)}, u32[]{:S(2)}) collective-permute-start(f32[2,8,32,128]{3,2,1,0:T(8,128)S(1)} %add.22), channel_id=1, source_target_pairs={{0,8},{4,12},{8,0},{12,4},{1,9},{5,13},{9,1},{13,5},{2,10},{6,14},... | collective-permute-start | bytes 786440 | tf_op jit(solution)/shard_map/ppermute | solution.py:439
  80.4 1.8 %collective-permute-start.19 = (f32[2,8,32,128]{3,2,1,0:T(8,128)S(1)}, f32[2,8,32,128]{3,2,1,0:T(8,128)S(1)}, u32[]{:S(2)}, u32[]{:S(2)}) collective-permute-start(f32[2,8,32,128]{3,2,1,0:T(8,128)S(1)} %add.23.mine), channel_id=1, source_target_pairs={{0,1},{1,0},{2,3},{3,2},{4,5},{5,4},{6,7},{7,6},{8,9},{9,8},{10,11... | collective-permute-start | bytes 786440 | tf_op jit(solution)/shard_map/ppermute | solution.py:457
  80.5 1.7 %collective-permute-start.20 = (f32[4,64,128]{2,1,0:T(8,128)S(1)}, f32[4,64,128]{2,1,0:T(8,128)S(1)}, u32[]{:S(2)}, u32[]{:S(2)}) collective-permute-start(f32[4,64,128]{2,1,0:T(8,128)S(1)} %get-tuple-element.59), channel_id=1, source_target_pairs={{0,1},{1,0},{2,3},{3,2},{4,5},{5,4},{6,7},{7,6},{8,9},{9,8},{10,11... | collective-permute-start | bytes 393224 | tf_op jit(solution)/shard_map/ppermute | solution.py:424
  (9 other events, 74.1 us)

commit v3 on v2

--- a/solution.py
+++ b/solution.py
@@ -20,6 +20,7 @@
 
 VMEM = pl.BlockSpec(memory_space=pltpu.VMEM)
 SMEM = pl.BlockSpec(memory_space=pltpu.SMEM)
+HBM = pl.BlockSpec(memory_space=pltpu.HBM)
 
 
 def rounded(table):
@@ -67,44 +68,68 @@
     return result
 
 
+def middle(table):
+    total = table[0]
+    for entry in range(1, table.shape[0]):
+        total = total + table[entry]
+    return total * (1.0 / table.shape[0])
+
+
 def edges(value_of, outs, row_parity, brick_y):
     for position, out in enumerate(outs):
         upper = row_parity == position
         out[...] = jnp.where(upper, value_of(brick_y - EDGE, brick_y), value_of(0, EDGE))
 
 
-def assemble_body(where_ref, stiffness, density, nonlinear, pressure, previous, material, got_p, got_q, got_m, *outs):
-    p_out, q_out, ratio, bend, stiff, dense = outs[:6]
-    core = where_ref[0] % 2
-    column = where_ref[1]
+def assemble_body(count, *refs):
+    tables_in, own_in, got = refs[:3], refs[3:6], refs[6:9]
+    p_out, q_out, ratio, bend, stiff, dense, sent = refs[9:16]
+    edge_outs = refs[16 : 16 + count]
+    tables, own, semaphores = refs[16 + count : 19 + count], refs[19 + count : 22 + count], refs[22 + count]
+    core, column = lax.axis_index("gz"), lax.axis_index("gy")
     rows, brick_y = p_out.shape[:2]
     start = core * rows
+    copies = [
+        pltpu.make_async_copy(source, target, semaphores.at[index])
+        for index, (source, target) in enumerate(zip(tables_in, tables))
+    ] + [
+        pltpu.make_async_copy(source.at[pl.ds(start, rows)], target, semaphores.at[3 + index])
+        for index, (source, target) in enumerate(zip(own_in, own))
+    ]
+    for copy in copies:
+        copy.start()
+    for copy in copies:
+        copy.wait()
+    stiffness, density, nonlinear = tables
     entries = stiffness.shape[0]
 
-    def whole(own, other):
+    def whole(mine, other):
         return jnp.concatenate(
-            [jnp.where(core == 0, own, other), jnp.where(core == 0, other, own)], axis=-1
+            [jnp.where(core == 0, mine, other), jnp.where(core == 0, other, mine)], axis=-1
         )
 
+    stiff_middle, dense_middle = middle(stiffness), middle(density)
     for row in range(rows):
-        p_out[row] = whole(pressure[start + row], got_p[start + row])
-        q_out[row] = whole(previous[start + row], got_q[start + row])
-        cell = whole(material[start + row], got_m[start + row])
+        value = whole(own[0][row], got[0][start + row])
+        p_out[row] = value
+        sent[row] = value.astype(BF16)
+        q_out[row] = whole(own[1][row], got[1][start + row])
+        cell = whole(own[2][row], got[2][start + row])
         ratio[row] = looked_up(cell, lambda e: stiffness[e] / density[e], entries)
         bend[row] = looked_up(cell, lambda e: nonlinear[e], entries)
-        stiff[row] = looked_up(cell, lambda e: stiffness[e], entries)
-        dense[row] = looked_up(cell, lambda e: density[e], entries)
-    edges(lambda a, b: p_out[:, a:b, :], outs[6:], column % 2, brick_y)
-
-
-def step_body(two_sided, last, where_ref, p_ref, q_ref, ratio, bend, mate, far, *rest):
+        stiff[row] = looked_up(cell, lambda e: stiffness[e] - stiff_middle, entries)
+        dense[row] = looked_up(cell, lambda e: density[e] - dense_middle, entries)
+    edges(lambda a, b: p_out[:, a:b, :], edge_outs, column % 2, brick_y)
+
+
+def step_body(two_sided, last, p_ref, q_ref, ratio, bend, mate, far, *rest):
     count = 2 if two_sided else 1
     halos = rest[:count]
-    new_ref = rest[count]
-    edge_outs = rest[count + 1 : -1]
+    new_ref, sent = rest[count : count + 2]
+    edge_outs = rest[count + 2 : -1]
     padded = rest[-1]
-    core = where_ref[0] % 2
-    parity = where_ref[1] % 2
+    core = lax.axis_index("gz")
+    parity = lax.axis_index("gy") % 2
     rows, brick_y, depth = p_ref.shape
     lane = lax.broadcasted_iota(jnp.int32, (brick_y, depth), 1)
     zero_edge = jnp.zeros((EDGE, depth), F32)
@@ -113,8 +138,8 @@
         if 0 <= index < rows:
             return p_ref[index]
         if index < 0:
-            return jnp.where(core == 0, far[index + rows], mate[index + rows])
-        return jnp.where(core == 0, mate[index - rows], far[index - rows])
+            return jnp.where(core == 0, far[index + rows], mate[index + rows]).astype(F32)
+        return jnp.where(core == 0, mate[index - rows], far[index - rows]).astype(F32)
 
     for row in range(rows):
         first = halos[0][row]
@@ -134,21 +159,26 @@
             )
             total = total + stencil_taps[offset] * pair
         change = center - q_ref[row]
-        new_ref[row] = (center + change) + ratio[row] * total + bend[row] * change * change
+        value = (center + change) + ratio[row] * total + bend[row] * change * change
+        new_ref[row] = value
+        if not last:
+            sent[row] = value.astype(BF16)
     if last:
         half = depth // 2
-        edge_outs[0][...] = jnp.where(core == 0, new_ref[:, :, half:], new_ref[:, :, :half])
+        sent[...] = jnp.where(core == 0, new_ref[:, :, half:], new_ref[:, :, :half])
     else:
         edges(lambda a, b: new_ref[:, a:b, :], edge_outs, parity, brick_y)
 
 
-def spectrum_body(where_ref, twiddle_x, p_ref, q_ref, stiff, dense, table_z, table_y, keep, send, lines, grid):
-    core = where_ref[0] % 2
-    column = where_ref[1]
-    rows, brick_y, depth = p_ref.shape
+def spectrum_body(twiddle_x, *refs):
+    count = (len(refs) - 6) or 1
+    sources = refs[:count]
+    table_z, table_y, keep, send, lines, grid = refs[count:]
+    core, column = lax.axis_index("gz"), lax.axis_index("gy")
+    rows, brick_y, depth = sources[0].shape
     modes_x, modes_y, width = keep.shape[1:]
     half = width // 2
-    for field, ref in enumerate((p_ref, q_ref, stiff, dense)):
+    for field, ref in enumerate(sources):
         for row in range(rows):
             high, low = high_low(ref[row])
             modes = jnp.dot(high, table_z[...], preferred_element_type=F32)
@@ -160,34 +190,34 @@
             for index, part in enumerate((high, back_high, low, back_low)):
                 lines[index * brick_y : (index + 1) * brick_y, lanes] = part
     grid[...] = jnp.dot(table_y[column], lines[...], preferred_element_type=F32)
-    first = (where_ref[0] * rows) * modes_x * 2
-
-    def sums(base_field, out, index):
+    block = lax.axis_index("gx") * 2 + core
+    first = block * (rows * modes_x * 4)
+
+    for field in range(count):
         values, backs = [], []
         for row in range(rows):
-            lanes = pl.ds(pl.multiple_of((base_field * rows + row) * width, width), width)
-            value = grid[:, lanes]
-            values.append(value)
-            backs.append(turned(value, half, 1.0))
+            lanes = slice((field * rows + row) * width, (field * rows + row + 1) * width)
+            values.append(grid[:, lanes])
+            backs.append(turned(values[-1], half, 1.0))
+
+        def summed(mode):
+            total = jnp.zeros((modes_y, width), F32)
+            for row in range(rows):
+                at = first + (row * modes_x * 2 + mode) * 2
+                total = total + twiddle_x[at] * values[row] + twiddle_x[at + 1] * backs[row]
+            return total
 
         @pl.loop(0, modes_x)
         def _(mode):
-            total = jnp.zeros((modes_y, width), F32)
-            for row in range(rows):
-                at = first + (row * modes_x + mode) * 2
-                total = total + twiddle_x[at] * values[row] + twiddle_x[at + 1] * backs[row]
-            out[index, mode] = total
-
-    for index in range(2):
-        sums(core * 2 + index, keep, index)
-        sums((1 - core) * 2 + index, send, index)
+            keep[field, mode] = summed(core * modes_x + mode)
+            send[field, mode] = summed((1 - core) * modes_x + mode).astype(BF16)
 
 
 def prepare_body(
-    where_ref, mode_ref, lift_ref, bias_ref, local_ref, spread_ref, place_ref, owner_ref, turn_ref,
+    stiffness, density, mode_ref, lift_ref, bias_ref, local_ref, spread_ref, place_ref, owner_ref, turn_ref,
     wide_ref, mixing, pointwise, lift_table, offset,
 ):
-    block = where_ref[0]
+    block = lax.axis_index("gx") * 2 + lax.axis_index("gz")
     half = place_ref.shape[1]
     channels = lift_ref.shape[1]
     spread = owner_ref[...]
@@ -203,10 +233,10 @@
     cosine = turn_ref[block, 0]
     sine = turn_ref[block, 1]
     coupled = jnp.concatenate([cosine * real - sine * imag, -(cosine * imag + sine * real)], axis=1)
-    coupled = coupled.astype(BF16)
-    mixing[...] = jnp.concatenate([coupled, coupled], axis=1)
+    mixing[...] = coupled.astype(BF16)
     constant = dot(spread, mode_ref[0, 0:channels, :], across)
-    offset[...] = jnp.sum(constant * bias_ref[...], axis=1, keepdims=True)
+    bias = bias_ref[...] + middle(stiffness) * lift_ref[2:3, :] + middle(density) * lift_ref[3:4, :]
+    offset[...] = jnp.sum(constant * bias, axis=1, keepdims=True)
     height = spread.shape[0]
     widest = wide_ref[0:channels, :]
     repeated = dot(dot(spread, local_ref[...].astype(F32), across), widest)
@@ -214,9 +244,10 @@
     padded = wide_ref[channels + height :, 0:channels]
     lift_table[:, 0:FIELDS] = dot(padded, lift_ref[...], across)
     lift_table[:, FIELDS : FIELDS + 1] = dot(padded, bias_ref[...], across)
-
-
-def pointwise_body(p_ref, q_ref, stiff, dense, lift_ref, left, offset, out, right):
+    lift_table[:, FIELDS + 1 :] = jnp.zeros_like(lift_table[:, FIELDS + 1 :])
+
+
+def pointwise_body(stiffness, density, p_ref, q_ref, stiff, dense, lift_ref, left, offset, out, right):
     rows, group, depth = p_ref.shape
     padded_channels = lift_ref.shape[0]
     height = rows * padded_channels
@@ -226,25 +257,28 @@
         right[...] = jnp.zeros_like(right)
 
     weights = [lift_ref[:, index : index + 1] for index in range(FIELDS + 1)]
+    stiff_middle, dense_middle = middle(stiffness), middle(density)
     for y in range(group):
         lifted = []
         for row in range(rows):
             total = jnp.broadcast_to(weights[FIELDS], (padded_channels, depth))
-            for index, ref in enumerate((p_ref, q_ref, stiff, dense)):
-                total = total + ref[row, y : y + 1, :] * weights[index]
+            line = slice(y, y + 1)
+            values = (p_ref[row, line], q_ref[row, line], stiff[row, line] + stiff_middle, dense[row, line] + dense_middle)
+            for value, weight in zip(values, weights):
+                total = total + value * weight
             lifted.append(total)
         right[y, 0:height, :] = jnp.concatenate(lifted, axis=0).astype(BF16)
         out[:, y, :] = jnp.dot(left[...], right[y], preferred_element_type=F32) + offset[...]
 
 
 def output_body(
-    where_ref, mine, other, local, left, table_y, table_z, wave_ref, wave_other,
+    mine, other, mine_early, other_early, local, left, table_y, table_z, wave_ref, wave_other,
     features, wave_out, modes, right, sums,
 ):
     step = pl.program_id(0)
-    core = where_ref[0] % 2
-    column = where_ref[1]
-    modes_x, modes_y, width = mine.shape[1:]
+    core, column = lax.axis_index("gz"), lax.axis_index("gy")
+    half_x, modes_y, width = mine.shape[1:]
+    modes_x = 2 * half_x
     half = width // 2
     rows, channels, group, depth = features.shape
     coupled = FIELDS * modes_x
@@ -254,16 +288,14 @@
         chunk = 4
         left_y = table_y[column]
         for field in range(FIELDS):
-            index = field % 2
+            own, far = ((mine, other), (mine_early, other_early))[field // 2]
             for start in range(0, modes_x, chunk):
-                parts = [[], [], [], []]
+                parts = [[], []]
                 for mode in range(start, start + chunk):
-                    own, far = mine[index, mode], other[index, mode]
-                    value = jnp.where(core == field // 2, own, far)
-                    high, low = high_low(value)
-                    back_high, back_low = high_low(turned(value, half, -1.0))
-                    for position, part in enumerate((high, back_high, low, back_low)):
-                        parts[position].append(part)
+                    at = (field % 2, mode % half_x)
+                    value = jnp.where(core == mode // half_x, own[at], far[at].astype(F32))
+                    parts[0].append(value.astype(BF16))
+                    parts[1].append(turned(value, half, -1.0).astype(BF16))
                 stacked = jnp.concatenate([jnp.concatenate(part, axis=1) for part in parts], axis=0)
                 result = jnp.dot(left_y, stacked, preferred_element_type=F32)
                 for mode in range(start, start + chunk):
@@ -276,17 +308,12 @@
             wave_out[(1 - core) * rows + row] = wave_other[row]
 
     base = pl.multiple_of(step * group, group)
-    high, low = high_low(modes[pl.ds(base, group)].reshape(group * coupled, width))
-    waves = jnp.dot(high, table_z[...], preferred_element_type=F32)
-    waves = waves + jnp.dot(low, table_z[...], preferred_element_type=F32)
-    high, low = high_low(waves)
+    lines = modes[pl.ds(base, group)].reshape(group * coupled, width).astype(BF16)
+    waves = jnp.dot(lines, table_z[...], preferred_element_type=F32).astype(BF16)
     for y in range(group):
         lines = slice(y * coupled, (y + 1) * coupled)
-        position = 0
-        for part in (high, low):
-            for lanes in (slice(0, depth), slice(depth, 2 * depth)):
-                right[y, position : position + coupled, :] = part[lines, lanes]
-                position += coupled
+        right[y, 0:coupled, :] = waves[lines, :depth]
+        right[y, coupled:, :] = waves[lines, depth:]
         sums[:, y, :] = jnp.dot(left[...], right[y], preferred_element_type=F32)
     for row in range(rows):
         for channel in range(channels):
@@ -354,7 +381,7 @@
     cy3, sy3 = [t.reshape(modes_y, column_count, brick_y).transpose(1, 0, 2) for t in (cy, sy)]
     forward_y = np.concatenate([cy3, sy3, cy3, sy3], 2)
     cy3, sy3 = [t.transpose(0, 2, 1) for t in (cy3, sy3)]
-    inverse_y = np.concatenate([cy3, sy3, cy3, sy3], 2)
+    inverse_y = np.concatenate([cy3, sy3], 2)
     cx, sx = [t.astype(np.float32) for t in cos_sin(np.arange(total_x), kept_first, total_x)]
     twiddle_x = np.stack([cx, sx], -1).reshape(-1)
     owner = np.tile(np.eye(channels, dtype=np.float32), (rows, 1))
@@ -377,11 +404,6 @@
     spread = np.concatenate([spread, same], 1)
     place = np.tile(np.eye(FIELDS, dtype=np.float32), (1, modes_x))
 
-    core = lax.axis_index("gz")
-    where = jnp.array([1, 0], jnp.int32) * (lax.axis_index("gx") * core_count + core) + jnp.array(
-        [0, 1], jnp.int32
-    ) * lax.axis_index("gy")
-
     def shape(*dims, dtype=F32):
         return jax.ShapeDtypeStruct(dims, dtype)
 
@@ -392,51 +414,74 @@
 
     swap_core = xor_pairs(core_count, 1)
     got = [lax.ppermute(array, "gz", swap_core) for array in (pressure, previous, material)]
-    current, before, ratio, bend, stiff, dense, *edge_values = call(
-        assemble_body, [field] * 6 + edge, [SMEM] * 4 + [VMEM] * 6, moved=cells * 36
-    )(where, stiffness, density, nonlinear, pressure, previous, material, *got)
+    sending = shape(rows, brick_y, total_z, dtype=BF16)
+    current, before, ratio, bend, stiff, dense, sent, *edge_values = call(
+        lambda *refs: assemble_body(len(edge), *refs), [field] * 6 + [sending] + edge, [HBM] * 6 + [VMEM] * 3,
+        [pltpu.SMEM(stiffness.shape, F32)] * 3 + [pltpu.VMEM((rows, brick_y, brick_z), F32)] * 2
+        + [pltpu.VMEM((rows, brick_y, brick_z), jnp.int32), pltpu.SemaphoreType.DMA((6,))], moved=cells * 36
+    )(stiffness, density, nonlinear, pressure, previous, material, *got)
 
     mixing, pointwise, lift_table, offset = call(
         prepare_body,
-        [shape(height, 4 * coupled, dtype=BF16), shape(height, right_depth, dtype=BF16),
-         shape(padded_channels, FIELDS + 1), shape(height, 1)],
-        [SMEM] + [VMEM] * 9, flops=2_000_000_000, moved=4_000_000,
+        [shape(height, 2 * coupled, dtype=BF16), shape(height, right_depth, dtype=BF16),
+         shape(padded_channels, 8), shape(height, 1)],
+        [SMEM] * 2 + [VMEM] * 9, flops=2_000_000_000, moved=4_000_000,
     )(
-        where, mode_weight.reshape(2, modes_x * channels, channels), lift_weight,
+        stiffness, density, mode_weight.reshape(2, modes_x * channels, channels), lift_weight,
         lift_bias.reshape(1, channels), local_weight, spread, place, owner, turn, wide,
     )
+
+    part = [shape(2, modes_x // 2, modes_y, width, dtype=dtype) for dtype in (F32, BF16)]
+    spectrum = call(
+        spectrum_body, part, [SMEM] + [VMEM] * 4,
+        [pltpu.VMEM((4 * brick_y, 2 * rows * width), BF16), pltpu.VMEM((modes_y, 2 * rows * width), F32)],
+        flops=cells * 1024, moved=cells * 16,
+    )
+    stages = [(axis, count, 2**bit) for axis, count in (("gy", column_count), ("gx", cycle_count))
+              for bit in range((count - 1).bit_length())]
+    swap = lambda value: lax.ppermute(value, "gz", swap_core)
+
+    early, early_sent = spectrum(twiddle_x, stiff, dense, forward_z, forward_y)
+    moves = [lambda value: swap(early_sent)] + [
+        lambda value, stage=stage: lax.ppermute(value.astype(BF16), stage[0], xor_pairs(*stage[1:])) for stage in stages
+    ]
+    pending = None
 
     for repeat in range(STEPS):
         last = repeat == STEPS - 1
-        far = lax.ppermute(current, ("gx", "gz"), odd_pairs(blocks))
-        mate = lax.ppermute(current, "gz", swap_core)
+        far = lax.ppermute(sent, ("gx", "gz"), odd_pairs(blocks))
+        mate = swap(sent)
         halos = [lax.ppermute(edge_values[0], "gy", xor_pairs(column_count, 1))]
         if two_sided:
             halos.append(lax.ppermute(edge_values[1], "gy", odd_pairs(column_count)))
-        outs = [field] + ([half] if last else edge)
+        if pending is not None:
+            early = early + pending.astype(F32)
+            pending = None
+        if moves:
+            halos[0], early, early_sent = lax.optimization_barrier((halos[0], early, early_sent))
+            pending = moves.pop(0)(early)
+        outs = [field] + ([half] if last else [sending] + edge)
         body = lambda *refs, last=last: step_body(two_sided, last, *refs)
-        new, *edge_values = call(
-            body, outs, [SMEM] + [VMEM] * (6 + len(halos)),
+        new, sent, *edge_values = call(
+            body, outs, [VMEM] * (6 + len(halos)),
             [pltpu.VMEM((brick_y + 2 * EDGE, total_z), F32)], flops=cells * 60, moved=cells * 28,
-        )(where, current, before, ratio, bend, mate, far, *halos)
+        )(current, before, ratio, bend, mate, far, *halos)
         current, before = new, current
 
-    wave_other = lax.ppermute(edge_values[0], "gz", swap_core)
-    part = shape(2, modes_x, modes_y, width)
-    keep, send = call(
-        spectrum_body, [part, part], [SMEM] * 2 + [VMEM] * 6,
-        [pltpu.VMEM((4 * brick_y, FIELDS * rows * width), BF16), pltpu.VMEM((modes_y, FIELDS * rows * width), F32)],
-        flops=cells * 2048, moved=cells * 32,
-    )(where, twiddle_x, current, before, stiff, dense, forward_z, forward_y)
-    total = keep + lax.ppermute(send, "gz", swap_core)
+    wave_other = swap(sent)
+    total, sent = spectrum(twiddle_x, current, before, forward_z, forward_y)
+    total = total + swap(sent).astype(F32)
+    while moves:
+        early = early + pending.astype(F32)
+        pending = moves.pop(0)(early)
+    early = early + pending.astype(F32)
+    early_other = swap(early.astype(BF16))
     group = 8
     whole = lambda array: pl.BlockSpec(array.shape, lambda i: (0,) * len(array.shape))
     slab = pl.BlockSpec((rows, group, total_z), lambda i: (0, i, 0))
     strip = pl.BlockSpec((height, group, total_z), lambda i: (0, i, 0))
-    stages = [(axis, count, 2**bit) for axis, count in (("gy", column_count), ("gx", cycle_count))
-              for bit in range((count - 1).bit_length())]
     for index, (axis, count, distance) in enumerate(stages):
-        arrived = lax.ppermute(total, axis, xor_pairs(count, distance))
+        arrived = lax.ppermute(total.astype(BF16), axis, xor_pairs(count, distance))
         if index == 0:
             arrived, mixing, pointwise, lift_table, offset = lax.optimization_barrier(
                 (arrived, mixing, pointwise, lift_table, offset)
@@ -446,32 +491,32 @@
                 pointwise_body,
                 grid=(brick_y // group,),
                 out_shape=shape(height, brick_y, total_z),
-                in_specs=[slab] * 4 + [whole(lift_table), whole(pointwise), whole(offset)],
+                in_specs=[SMEM] * 2 + [slab] * 4 + [whole(lift_table), whole(pointwise), whole(offset)],
                 out_specs=strip,
                 scratch_shapes=[pltpu.VMEM((group, right_depth, total_z), BF16)],
                 compiler_params=pltpu.CompilerParams(vmem_limit_bytes=24 * 1024 * 1024),
                 cost_estimate=pl.CostEstimate(flops=cells * 40000, bytes_accessed=cells * 100, transcendentals=0),
-            )(current, before, stiff, dense, lift_table, pointwise, offset)
+            )(stiffness, density, current, before, stiff, dense, lift_table, pointwise, offset)
             arrived, local = lax.optimization_barrier((arrived, local))
-        total = total + arrived
-    other = lax.ppermute(total, "gz", swap_core)
+        total = total + arrived.astype(F32)
+    other = swap(total.astype(BF16))
 
     scoped = 12 * 2**20 + 4 * (6 * 2 * modes_x * modes_y * width + brick_y * coupled * width + 6 * group * coupled * total_z)
     features, wave = pl.pallas_call(
         output_body,
         grid=(brick_y // group,),
         out_shape=[shape(rows, channels, brick_y, total_z, dtype=BF16), shape(*pressure.shape)],
-        in_specs=[SMEM, whole(part), whole(part), strip, whole(mixing), whole(inverse_y), whole(inverse_z),
+        in_specs=[whole(part[0]), whole(part[1])] * 2 + [strip, whole(mixing), whole(inverse_y), whole(inverse_z),
                   whole(field), whole(half)],
         out_specs=[pl.BlockSpec((rows, channels, group, total_z), lambda i: (0, 0, i, 0)), whole(pressure)],
         scratch_shapes=[
             pltpu.VMEM((brick_y, coupled, width), F32),
-            pltpu.VMEM((group, 4 * coupled, total_z), BF16),
+            pltpu.VMEM((group, 2 * coupled, total_z), BF16),
             pltpu.VMEM((height, group, total_z), F32),
         ],
         compiler_params=pltpu.CompilerParams(vmem_limit_bytes=scoped),
         cost_estimate=pl.CostEstimate(flops=cells * 2000, bytes_accessed=cells * 60, transcendentals=cells * 20),
-    )(where, total, other, local, mixing, inverse_y, inverse_z, current, wave_other)
+    )(total, other, early, early_other, local, mixing, inverse_y, inverse_z, current, wave_other)
     features = features.transpose(0, 2, 1, 3)
     return (wave, features)
 

time: 91.7 us -> 77.6 us (0.85)
  waiting for transfers between devices: 29 us -> 16.3 us
  local copies, waits for them, and re-layouts: 4.94 us -> 7.21 us
  Pallas kernels: 25.5 us -> 23.8 us
  starting transfers between devices: 30.1 us -> 28.5 us
    ppermute x14 -> x19, waiting for transfers between devices: 18.4 us -> 6.52 us  [the longest x3 4.06 us: per_device(): lax.ppermute(value.astype(BF16), stage[0], xor_pairs(*stage[1:]))]
    unnamed x40 -> x44, local copies, waits for them, and re-layouts: 4.89 us -> 7.16 us
    ppermute x4, waiting for transfers between devices: 9.69 us -> 8.16 us  [per_device(): halos = [lax.ppermute(edge_values[0], 'gy', xor_pairs(column_count, 1))]]
    pallas_call x7 -> x8, Pallas kernels: 11.3 us -> 9.85 us  [the longest x4 3.77 us: per_device(): call(body, outs, [VMEM] * (6 + len(halos)), [pltpu.VMEM((brick_y + 2 * ED...]
    pallas_call x1, Pallas kernels: 9.12 us -> 7.92 us  [per_device(): pl.pallas_call(output_body, grid=(brick_y // group,), out_shape=[shape(ro...]
    pallas_call x1, Pallas kernels: 5.07 us -> 6.04 us  [per_device(): pl.pallas_call(pointwise_body, grid=(brick_y // group,), out_shape=shape(...]
    ppermute x4, starting transfers between devices: 5.96 us -> 5.01 us  [per_device(): halos = [lax.ppermute(edge_values[0], 'gy', xor_pairs(column_count, 1))]]
    ppermute x14 -> x19, starting transfers between devices: 23.1 us -> 22.5 us  [the longest x9 14.1 us: per_device(): swap = lambda value: lax.ppermute(value, 'gz', swap_core)]
  transfers between devices with their start and end apart: 21 -> 26, of which waited for: 12 -> 9; matrix products, arithmetic and copies ran while one was open for 1% -> 0% of each run, Pallas kernels for 8% -> 16%
where the time goes in v3:
time: 77.6 us; the launch traced here: 77.1 us
  starting transfers between devices  28.5 us (37%)
  Pallas kernels  23.8 us (31%)
  waiting for transfers between devices  16.3 us (21%)
  local copies, waits for them, and re-layouts  7.21 us (9%)
  between operations  1.04 us (1%)
    ppermute x9, starting transfers between devices, per_device(): swap = lambda value: lax.ppermute(value, 'gz', swap_core)  14.1 us
    ppermute x4, waiting for transfers between devices, per_device(): halos = [lax.ppermute(edge_values[0], 'gy', xor_pairs(column_count, 1))]  8.16 us
    pallas_call x1, Pallas kernels, per_device(): pl.pallas_call(output_body, grid=(brick_y // group,), out_shape=[shape(ro...  7.92 us
    unnamed x44, local copies, waits for them, and re-layouts  7.16 us
    pallas_call x1, Pallas kernels, per_device(): pl.pallas_call(pointwise_body, grid=(brick_y // group,), out_shape=shape(...  6.04 us
    ppermute x4, starting transfers between devices, per_device(): halos = [lax.ppermute(edge_values[0], 'gy', xor_pairs(column_count, 1))]  5.01 us
    ppermute x3, waiting for transfers between devices, per_device(): lax.ppermute(value.astype(BF16), stage[0], xor_pairs(*stage[1:]))  4.06 us
    pallas_call x4, Pallas kernels, per_device(): call(body, outs, [VMEM] * (6 + len(halos)), [pltpu.VMEM((brick_y + 2 * ED...  3.77 us
  transfers between devices with their start and end apart: 26, of which 9 were waited for; matrix products, arithmetic and copies ran while one was open for 0% of the time, Pallas kernels for 16%

profile of v3, /device:TPU:0, one launch (start us, length us, event | category | flops | bytes accessed | tf_op | source)
XLA Modules:
  0.0 77.1 jit_solution(7771677840472640804)
XLA Ops:
  1.7 0.9 %collective-permute-done.refs_6_ = f32[8,64,128]{2,1,0:T(8,128)S(1)} collective-permute-done((f32[8,64,128]{2,1,0:T(8,128)}, f32[8,64,128]{2,1,0:T(8,128)S(1)}, u32[]{:S(2)}, u32[]{:S(2)}) %collective-permute-start) | collective-permute-done | bytes 262176 | tf_op jit(solution)/shard_map/ppermute | solution.py:416
  3.3 0.9 %copy-done = f32[8,64,128]{2,1,0:T(8,128)S(1)} copy-done((f32[8,64,128]{2,1,0:T(8,128)S(1)}, f32[8,64,128]{2,1,0:T(8,128)}, u32[]{:S(2)}) %copy-start) | copy-done | bytes 262168
  4.2 0.9 %copy-done.1 = f32[8,64,128]{2,1,0:T(8,128)S(1)} copy-done((f32[8,64,128]{2,1,0:T(8,128)S(1)}, f32[8,64,128]{2,1,0:T(8,128)}, u32[]{:S(2)}) %copy-start.1) | copy-done | bytes 262168
  5.2 0.9 %copy-done.2 = s32[8,64,128]{2,1,0:T(8,128)S(1)} copy-done((s32[8,64,128]{2,1,0:T(8,128)S(1)}, s32[8,64,128]{2,1,0:T(8,128)}, u32[]{:S(2)}) %copy-start.2) | copy-done | bytes 262168
  8.2 1.1 %shard_map.203 = (f32[4,64,256]{2,1,0:T(8,128)S(1)}, f32[4,64,256]{2,1,0:T(8,128)S(1)}, f32[4,64,256]{2,1,0:T(8,128)S(1)}, f32[4,64,256]{2,1,0:T(8,128)S(1)}, f3...) custom-call(f32[8]{0:T(128)S(1)} %copy-done.9, ...), custom_call_target="tpu_custom_call" | custom-call | bytes 2359296 | tf_op jit(solution)/shard_map/pallas_call | solution.py:418
  9.9 4.4 %collective-permute-start.3 = (bf16[4,64,256]{2,1,0:T(8,128)(2,1)S(1)}, bf16[4,64,256]{2,1,0:T(8,128)(2,1)S(1)}, u32[]{:S(2)}, u32[]{:S(2)}) collective-permute-start(bf16[4,64,256]{2,1,0:T(8,128)(2,1)S(1)} %get-tuple-element.51), channel_id=1, source_target_pairs={{0,1},{1,0},{2,3},{3,2},{4,5},{5,4},{6,7},{7,6},{8,9},{9,8},{10,11... | collective-permute-start | bytes 393224 | tf_op jit(solution)/shard_map/ppermute | solution.py:442
  14.3 1.5 %collective-permute-start.5 = (f32[4,8,256]{2,1,0:T(8,128)S(1)}, f32[4,8,256]{2,1,0:T(8,128)S(1)}, u32[]{:S(2)}, u32[]{:S(2)}) collective-permute-start(f32[4,8,256]{2,1,0:T(8,128)S(1)} %get-tuple-element.52), channel_id=1, source_target_pairs={{0,2},{2,0},{1,3},{3,1},{4,6},{6,4},{5,7},{7,5},{8,10},{10,8},{9,1... | collective-permute-start | bytes 98312 | tf_op jit(solution)/shard_map/ppermute | solution.py:454
  15.8 0.8 %copy-done.3 = bf16[256,128]{1,0:T(8,128)(2,1)S(1)} copy-done((bf16[256,128]{1,0:T(8,128)(2,1)S(1)}, bf16[256,128]{1,0:T(8,128)(2,1)}, u32[]{:S(2)}) %copy-start.3) | copy-done | bytes 65560
  16.6 0.8 copy-done.5
  18.1 1.4 %shard_map.204 = (f32[2,4,32,128]{3,2,1,0:T(8,128)S(1)}, bf16[2,4,32,128]{3,2,1,0:T(8,128)(2,1)S(1)}) custom-call(f32[512]{0:T(512)S(1)} %copy-done.7, f32[4,64,256]{2,1,0:T(8,128)S(1)} %get-tuple-element.53.refs_0_.stiff, f32[4,64,256]{2,1,0:T(8,128)S(1)} %get-tuple-element.54.refs_1_.dense, bf16[256,128]{1,0:T(8,128)(2,1)S(1)} %copy-done.3, ...), custom_call_target="tpu_custom_call" | custom-call | flops 67108864 | bytes 1048576 | tf_op jit(solution)/shard_map/pallas_call | solution.py:444
  19.6 1.0 %shard_map.205 = (f32[4,64,256]{2,1,0:T(8,128)S(1)}, bf16[4,64,256]{2,1,0:T(8,128)(2,1)S(1)}, f32[4,8,256]{2,1,0:T(8,128)S(1)}) custom-call(f32[4,64,256]{2,1,0:T(8,128)S(1)} %get-tuple-element.47.refs_0_.refs_1_, f32[4,64,256]{2,1,0:T(8,128)S(1)} %get-tuple-element.48.refs_1_, f32[4,64,256]{2,1,0:T(8,128)S(1)} %get-tuple-element.49.refs_2_, ...), custom_call_target="tpu_custom_call" | custom-call | flops 3932160 | bytes 1835008 | tf_op jit(solution)/shard_map/pallas_call | solution.py:465
  21.3 3.0 %collective-permute-start.6 = (bf16[4,64,256]{2,1,0:T(8,128)(2,1)S(1)}, bf16[4,64,256]{2,1,0:T(8,128)(2,1)S(1)}, u32[]{:S(2)}, u32[]{:S(2)}) collective-permute-start(bf16[4,64,256]{2,1,0:T(8,128)(2,1)S(1)} %get-tuple-element.59), channel_id=1, source_target_pairs={{0,1},{1,0},{2,3},{3,2},{4,5},{5,4},{6,7},{7,6},{8,9},{9,8},{10,11... | collective-permute-start | bytes 393224 | tf_op jit(solution)/shard_map/ppermute | solution.py:442
  24.8 3.4 %collective-permute-done.8.refs_6_ = f32[4,8,256]{2,1,0:T(8,128)S(1)} collective-permute-done((f32[4,8,256]{2,1,0:T(8,128)S(1)}, f32[4,8,256]{2,1,0:T(8,128)S(1)}, u32[]{:S(2)}, u32[]{:S(2)}) %collective-permute-start.8) | collective-permute-done | bytes 32800 | tf_op jit(solution)/shard_map/ppermute | solution.py:454
  28.8 0.9 %shard_map.206 = (f32[4,64,256]{2,1,0:T(8,128)S(1)}, bf16[4,64,256]{2,1,0:T(8,128)(2,1)S(1)}, f32[4,8,256]{2,1,0:T(8,128)S(1)}) custom-call(f32[4,64,256]{2,1,0:T(8,128)S(1)} %get-tuple-element.58.refs_0_.refs_1_, f32[4,64,256]{2,1,0:T(8,128)S(1)} %get-tuple-element.47.refs_0_.refs_1_, f32[4,64,256]{2,1,0:T(8,128)S(1)} %get-tuple-element.49.refs_2_, ...), custom_call_target="tpu_custom_call" | custom-call | flops 3932160 | bytes 1835008 | tf_op jit(solution)/shard_map/pallas_call | solution.py:465
  30.4 3.0 %collective-permute-start.10 = (bf16[4,64,256]{2,1,0:T(8,128)(2,1)S(1)}, bf16[4,64,256]{2,1,0:T(8,128)(2,1)S(1)}, u32[]{:S(2)}, u32[]{:S(2)}) collective-permute-start(bf16[4,64,256]{2,1,0:T(8,128)(2,1)S(1)} %get-tuple-element.65), channel_id=1, source_target_pairs={{0,1},{1,0},{2,3},{3,2},{4,5},{5,4},{6,7},{7,6},{8,9},{9,8},{10,11... | collective-permute-start | bytes 393224 | tf_op jit(solution)/shard_map/ppermute | solution.py:442
  33.4 1.5 %collective-permute-start.12 = (f32[4,8,256]{2,1,0:T(8,128)S(1)}, f32[4,8,256]{2,1,0:T(8,128)S(1)}, u32[]{:S(2)}, u32[]{:S(2)}) collective-permute-start(f32[4,8,256]{2,1,0:T(8,128)S(1)} %get-tuple-element.66), channel_id=1, source_target_pairs={{0,2},{2,0},{1,3},{3,1},{4,6},{6,4},{5,7},{7,5},{8,10},{10,8},{9,1... | collective-permute-start | bytes 98312 | tf_op jit(solution)/shard_map/ppermute | solution.py:454
  34.9 2.4 %collective-permute-done.12.refs_6_ = f32[4,8,256]{2,1,0:T(8,128)S(1)} collective-permute-done((f32[4,8,256]{2,1,0:T(8,128)S(1)}, f32[4,8,256]{2,1,0:T(8,128)S(1)}, u32[]{:S(2)}, u32[]{:S(2)}) %collective-permute-start.12) | collective-permute-done | bytes 32800 | tf_op jit(solution)/shard_map/ppermute | solution.py:454
  37.9 0.9 %shard_map.207 = (f32[4,64,256]{2,1,0:T(8,128)S(1)}, bf16[4,64,256]{2,1,0:T(8,128)(2,1)S(1)}, f32[4,8,256]{2,1,0:T(8,128)S(1)}) custom-call(f32[4,64,256]{2,1,0:T(8,128)S(1)} %get-tuple-element.64.refs_0_.refs_1_, f32[4,64,256]{2,1,0:T(8,128)S(1)} %get-tuple-element.58.refs_0_.refs_1_, f32[4,64,256]{2,1,0:T(8,128)S(1)} %get-tuple-element.49.refs_2_, ...), custom_call_target="tpu_custom_call" | custom-call | flops 3932160 | bytes 1835008 | tf_op jit(solution)/shard_map/pallas_call | solution.py:465
  39.5 2.9 %collective-permute-start.14 = (bf16[4,64,256]{2,1,0:T(8,128)(2,1)S(1)}, bf16[4,64,256]{2,1,0:T(8,128)(2,1)S(1)}, u32[]{:S(2)}, u32[]{:S(2)}) collective-permute-start(bf16[4,64,256]{2,1,0:T(8,128)(2,1)S(1)} %get-tuple-element.70), channel_id=1, source_target_pairs={{0,1},{1,0},{2,3},{3,2},{4,5},{5,4},{6,7},{7,6},{8,9},{9,8},{10,11... | collective-permute-start | bytes 393224 | tf_op jit(solution)/shard_map/ppermute | solution.py:442
  42.5 1.5 %collective-permute-start.16 = (f32[4,8,256]{2,1,0:T(8,128)S(1)}, f32[4,8,256]{2,1,0:T(8,128)S(1)}, u32[]{:S(2)}, u32[]{:S(2)}) collective-permute-start(f32[4,8,256]{2,1,0:T(8,128)S(1)} %get-tuple-element.71), channel_id=1, source_target_pairs={{0,2},{2,0},{1,3},{3,1},{4,6},{6,4},{5,7},{7,5},{8,10},{10,8},{9,1... | collective-permute-start | bytes 98312 | tf_op jit(solution)/shard_map/ppermute | solution.py:454
  44.0 2.4 %collective-permute-done.16.refs_6_ = f32[4,8,256]{2,1,0:T(8,128)S(1)} collective-permute-done((f32[4,8,256]{2,1,0:T(8,128)S(1)}, f32[4,8,256]{2,1,0:T(8,128)S(1)}, u32[]{:S(2)}, u32[]{:S(2)}) %collective-permute-start.16) | collective-permute-done | bytes 32800 | tf_op jit(solution)/shard_map/ppermute | solution.py:454
  46.4 0.9 %shard_map.208 = (f32[4,64,256]{2,1,0:T(8,128)S(1)}, f32[4,64,128]{2,1,0:T(8,128)S(1)}) custom-call(f32[4,64,256]{2,1,0:T(8,128)S(1)} %get-tuple-element.69.refs_0_.refs_1_.q_ref, f32[4,64,256]{2,1,0:T(8,128)S(1)} %get-tuple-element.64.refs_0_.refs_1_, f32[4,64,256]{2,1,0:T(8,128)S(1)} %get-tuple-element.49.refs_2_, ...), custom_call_target="tpu_custom_call" | custom-call | flops 3932160 | bytes 1835008 | tf_op jit(solution)/shard_map/pallas_call | solution.py:465
  47.4 1.4 %shard_map.209 = (f32[2,4,32,128]{3,2,1,0:T(8,128)S(1)}, bf16[2,4,32,128]{3,2,1,0:T(8,128)(2,1)S(1)}) custom-call(f32[512]{0:T(512)S(1)} %copy-done.7, f32[4,64,256]{2,1,0:T(8,128)S(1)} %get-tuple-element.74.refs_0_.p_ref.wave_ref, f32[4,64,256]{2,1,0:T(8,128)S(1)} %get-tuple-element.69.refs_0_.refs_1_.q_ref, bf16[256,128]{1,0:T(8,128)(2,1)S(1)} %copy-done.3, ...), custom_call_target="tpu_custom_call" | custom-call | flops 67108864 | bytes 1048576 | tf_op jit(solution)/shard_map/pallas_call | solution.py:472
  48.9 1.2 %collective-permute-done.18 = bf16[2,4,32,128]{3,2,1,0:T(8,128)(2,1)S(1)} collective-permute-done((bf16[2,4,32,128]{3,2,1,0:T(8,128)(2,1)S(1)}, bf16[2,4,32,128]{3,2,1,0:T(8,128)(2,1)S(1)}, u32[]{:S(2)}, u32[]{:S(2)}) %collective-permute-start.18) | collective-permute-done | bytes 65568 | tf_op jit(solution)/shard_map/ppermute | solution.py:442
  50.1 1.6 %collective-permute-start.19 = (bf16[2,4,32,128]{3,2,1,0:T(8,128)(2,1)S(1)}, bf16[2,4,32,128]{3,2,1,0:T(8,128)(2,1)S(1)}, u32[]{:S(2)}, u32[]{:S(2)}) collective-permute-start(bf16[2,4,32,128]{3,2,1,0:T(8,128)(2,1)S(1)} %fusion), channel_id=1, source_target_pairs={{0,2},{2,0},{1,3},{3,1},{4,6},{6,4},{5,7},{7,5},{8,10},{10,8},{9,1... | collective-permute-start | bytes 196616 | tf_op jit(solution)/shard_map/ppermute | solution.py:484
  51.8 2.2 %shard_map.210 = (bf16[80,64]{1,0:T(8,128)(2,1)S(1)}, bf16[80,128]{1,0:T(8,128)(2,1)S(1)}, f32[24,8]{1,0:T(8,128)S(1)}, f32[80,1]{1,0:T(8,128)S(1)}) custom-call(f32[8]{0:T(128)S(1)} %copy-done.10, f32[8]{0:T(128)S(1)} %copy-done.12, f32[2,160,20]{2,1,0:T(8,128)S(1)} %reshape.12.mode_ref, f32[4,20]{1,0:T(4,128)S(1)} %copy-done.14, f32[1,20]{1,0:T(1,128)S(1)} %bitcast.2, ...), custom_call_target="tpu_custom_call" | custom-call | flops 2000000000 | bytes 4000000 | tf_op jit(solution)/shard_map/pallas_call | solution.py:424
  54.0 1.6 %collective-permute-start.23 = (bf16[2,4,32,128]{3,2,1,0:T(8,128)(2,1)S(1)}, bf16[2,4,32,128]{3,2,1,0:T(8,128)(2,1)S(1)}, u32[]{:S(2)}, u32[]{:S(2)}) collective-permute-start(bf16[2,4,32,128]{3,2,1,0:T(8,128)(2,1)S(1)} %convert_element_type.61), channel_id=1, source_target_pairs={{0,8},{4,12},{8,0},{12,4},{1,9},{5,13},{9,1},{13,5},{2,10},{6,14},... | collective-permute-start | bytes 196616 | tf_op jit(solution)/shard_map/ppermute | solution.py:446
  55.9 4.1 %collective-permute-done.23 = bf16[2,4,32,128]{3,2,1,0:T(8,128)(2,1)S(1)} collective-permute-done((bf16[2,4,32,128]{3,2,1,0:T(8,128)(2,1)S(1)}, bf16[2,4,32,128]{3,2,1,0:T(8,128)(2,1)S(1)}, u32[]{:S(2)}, u32[]{:S(2)}) %collective-permute-start.23) | collective-permute-done | bytes 65568 | tf_op jit(solution)/shard_map/ppermute | solution.py:446
  60.7 1.1 %collective-permute-start.21 = (bf16[2,4,32,128]{3,2,1,0:T(8,128)(2,1)S(1)}, bf16[2,4,32,128]{3,2,1,0:T(8,128)(2,1)S(1)}, u32[]{:S(2)}, u32[]{:S(2)}) collective-permute-start(bf16[2,4,32,128]{3,2,1,0:T(8,128)(2,1)S(1)} %fusion.1), channel_id=1, source_target_pairs={{0,8},{4,12},{8,0},{12,4},{1,9},{5,13},{9,1},{13,5},{2,10},{6,14},... | collective-permute-start | bytes 196616 | tf_op jit(solution)/shard_map/ppermute | solution.py:484
  61.8 6.0 %shard_map.211.local = f32[80,64,256]{2,1,0:T(8,128)S(1)} custom-call(f32[8]{0:T(128)S(1)} %copy-done.10, f32[8]{0:T(128)S(1)} %copy-done.12, f32[4,64,256]{2,1,0:T(8,128)S(1)} %get-tuple-element.74.refs_0_.p_ref.wave_ref, f32[4,64,256]{2,1,0:T(8,128)S(1)} %get-tuple-element.69.refs_0_.refs_1_.q_ref, f32[4,64,256]{2,1,0:T(8,128)S(1)} %get-tuple-element.53.refs_0_.stiff, ...), custom_call_target="tpu_custom_call" | custom-call | flops 2621440000 | bytes 6553600 | tf_op jit(solution)/shard_map/pallas_call | solution.py:490
  68.0 1.2 %collective-permute-done.22.other = bf16[2,4,32,128]{3,2,1,0:T(8,128)(2,1)S(1)} collective-permute-done((bf16[2,4,32,128]{3,2,1,0:T(8,128)(2,1)S(1)}, bf16[2,4,32,128]{3,2,1,0:T(8,128)(2,1)S(1)}, u32[]{:S(2)}, u32[]{:S(2)}) %collective-permute-start.22) | collective-permute-done | bytes 65568 | tf_op jit(solution)/shard_map/ppermute | solution.py:442
  69.2 7.9 %shard_map.212 = (bf16[4,20,64,256]{3,2,1,0:T(8,128)(2,1)}, f32[8,64,128]{2,1,0:T(8,128)}) custom-call(f32[2,4,32,128]{3,2,1,0:T(8,128)S(1)} %get-tuple-element.95.mine, bf16[2,4,32,128]{3,2,1,0:T(8,128)(2,1)S(1)} %collective-permute-done.22.other, f32[2,4,32,128]{3,2,1,0:T(8,128)S(1)} %get-tuple-element.93.mine_early, ...), custom_call_target="tpu_custom_call" | custom-call | flops 131072000 | bytes 3932160 | tf_op jit(solution)/shard_map/pallas_call | solution.py:505
  (87 shorter events, 10.4 us)
Async XLA Ops:
  0.6 51.1 %copy-start.20 = (f32[4,32]{1,0:T(4,128)S(1)}, f32[4,32]{1,0:T(4,128)}, u32[]{:S(2)}) copy-start(f32[4,32]{1,0:T(4,128)} %constant.21.clone.place_ref) | copy-start | bytes 1540
  0.6 1.9 %collective-permute-start = (f32[8,64,128]{2,1,0:T(8,128)}, f32[8,64,128]{2,1,0:T(8,128)S(1)}, u32[]{:S(2)}, u32[]{:S(2)}) collective-permute-start(f32[8,64,128]{2,1,0:T(8,128)} %refs_3_.3), channel_id=1, source_target_pairs={{0,1},{1,0},{2,3},{3,2},{4,5},{5,4},{6,7},{7,6},{8,9},{9,8},{10,11... | collective-permute-start | bytes 786440 | tf_op jit(solution)/shard_map/ppermute | solution.py:416
  1.2 1.7 %collective-permute-start.1 = (f32[8,64,128]{2,1,0:T(8,128)}, f32[8,64,128]{2,1,0:T(8,128)S(1)}, u32[]{:S(2)}, u32[]{:S(2)}) collective-permute-start(f32[8,64,128]{2,1,0:T(8,128)} %refs_4_.1), channel_id=1, source_target_pairs={{0,1},{1,0},{2,3},{3,2},{4,5},{5,4},{6,7},{7,6},{8,9},{9,8},{10,11... | collective-permute-start | bytes 786440 | tf_op jit(solution)/shard_map/ppermute | solution.py:416
  1.2 2.0 %collective-permute-start.2 = (s32[8,64,128]{2,1,0:T(8,128)}, s32[8,64,128]{2,1,0:T(8,128)S(1)}, u32[]{:S(2)}, u32[]{:S(2)}) collective-permute-start(s32[8,64,128]{2,1,0:T(8,128)} %refs_5_.1), channel_id=1, source_target_pairs={{0,1},{1,0},{2,3},{3,2},{4,5},{5,4},{6,7},{7,6},{8,9},{9,8},{10,11... | collective-permute-start | bytes 786440 | tf_op jit(solution)/shard_map/ppermute | solution.py:416
  8.1 43.6 %copy-start.12 = (f32[8]{0:T(128)S(1)}, f32[8]{0:T(128)}, u32[]{:S(2)}) copy-start(f32[8]{0:T(128)} %density.3) | copy-start | bytes 100
  8.1 43.6 %copy-start.13 = (bf16[20,20]{1,0:T(8,128)(2,1)S(1)}, bf16[20,20]{1,0:T(8,128)(2,1)}, u32[]{:S(2)}) copy-start(bf16[20,20]{1,0:T(8,128)(2,1)} %local_ref.1) | copy-start | bytes 2404
  8.1 43.6 %copy-start.14 = (f32[4,20]{1,0:T(4,128)S(1)}, f32[4,20]{1,0:T(4,128)}, u32[]{:S(2)}) copy-start(f32[4,20]{1,0:T(4,128)} %lift_ref.1) | copy-start | bytes 964
  8.1 43.6 %copy-start.15 = (f32[20]{0:T(128)S(1)}, f32[20]{0:T(128)}, u32[]{:S(2)}) copy-start(f32[20]{0:T(128)} %param.27) | copy-start | bytes 244
  8.1 43.6 %copy-start.16 = (f32[8,2,80,32]{3,2,1,0:T(8,128)S(1)}, f32[8,2,80,32]{3,2,1,0:T(8,128)}, u32[]{:S(2)}) copy-start(f32[8,2,80,32]{3,2,1,0:T(8,128)} %constant.23.clone.turn_ref) | copy-start | bytes 491524
  9.3 10.3 %collective-permute-start.4 = (bf16[4,64,256]{2,1,0:T(8,128)(2,1)S(1)}, bf16[4,64,256]{2,1,0:T(8,128)(2,1)S(1)}, u32[]{:S(2)}, u32[]{:S(2)}) collective-permute-start(bf16[4,64,256]{2,1,0:T(8,128)(2,1)S(1)} %get-tuple-element.51), channel_id=1, source_target_pairs={{1,4},{5,8},{9,12},{4,1},{8,5},{12,9},{3,6},{7,10},{11,14},{6,3},{... | collective-permute-start | bytes 393224 | tf_op jit(solution)/shard_map/ppermute | solution.py:452
  9.9 9.7 %collective-permute-start.3 = (bf16[4,64,256]{2,1,0:T(8,128)(2,1)S(1)}, bf16[4,64,256]{2,1,0:T(8,128)(2,1)S(1)}, u32[]{:S(2)}, u32[]{:S(2)}) collective-permute-start(bf16[4,64,256]{2,1,0:T(8,128)(2,1)S(1)} %get-tuple-element.51), channel_id=1, source_target_pairs={{0,1},{1,0},{2,3},{3,2},{4,5},{5,4},{6,7},{7,6},{8,9},{9,8},{10,11... | collective-permute-start | bytes 393224 | tf_op jit(solution)/shard_map/ppermute | solution.py:442
  14.3 5.2 %collective-permute-start.5 = (f32[4,8,256]{2,1,0:T(8,128)S(1)}, f32[4,8,256]{2,1,0:T(8,128)S(1)}, u32[]{:S(2)}, u32[]{:S(2)}) collective-permute-start(f32[4,8,256]{2,1,0:T(8,128)S(1)} %get-tuple-element.52), channel_id=1, source_target_pairs={{0,2},{2,0},{1,3},{3,1},{4,6},{6,4},{5,7},{7,5},{8,10},{10,8},{9,1... | collective-permute-start | bytes 98312 | tf_op jit(solution)/shard_map/ppermute | solution.py:454
  19.5 5.3 %collective-permute-start.9 = (bf16[2,4,32,128]{3,2,1,0:T(8,128)(2,1)S(1)}, bf16[2,4,32,128]{3,2,1,0:T(8,128)(2,1)S(1)}, u32[]{:S(2)}, u32[]{:S(2)}) collective-permute-start(bf16[2,4,32,128]{3,2,1,0:T(8,128)(2,1)S(1)} %get-tuple-element.62), channel_id=1, source_target_pairs={{0,1},{1,0},{2,3},{3,2},{4,5},{5,4},{6,7},{7,6},{8,9},{9,8},{10,11... | collective-permute-start | bytes 196616 | tf_op jit(solution)/shard_map/ppermute | solution.py:442
  20.6 8.2 %collective-permute-start.7 = (bf16[4,64,256]{2,1,0:T(8,128)(2,1)S(1)}, bf16[4,64,256]{2,1,0:T(8,128)(2,1)S(1)}, u32[]{:S(2)}, u32[]{:S(2)}) collective-permute-start(bf16[4,64,256]{2,1,0:T(8,128)(2,1)S(1)} %get-tuple-element.59), channel_id=1, source_target_pairs={{1,4},{5,8},{9,12},{4,1},{8,5},{12,9},{3,6},{7,10},{11,14},{6,3},{... | collective-permute-start | bytes 393224 | tf_op jit(solution)/shard_map/ppermute | solution.py:452
  21.3 7.5 %collective-permute-start.6 = (bf16[4,64,256]{2,1,0:T(8,128)(2,1)S(1)}, bf16[4,64,256]{2,1,0:T(8,128)(2,1)S(1)}, u32[]{:S(2)}, u32[]{:S(2)}) collective-permute-start(bf16[4,64,256]{2,1,0:T(8,128)(2,1)S(1)} %get-tuple-element.59), channel_id=1, source_target_pairs={{0,1},{1,0},{2,3},{3,2},{4,5},{5,4},{6,7},{7,6},{8,9},{9,8},{10,11... | collective-permute-start | bytes 393224 | tf_op jit(solution)/shard_map/ppermute | solution.py:442
  24.3 3.9 %collective-permute-start.8 = (f32[4,8,256]{2,1,0:T(8,128)S(1)}, f32[4,8,256]{2,1,0:T(8,128)S(1)}, u32[]{:S(2)}, u32[]{:S(2)}) collective-permute-start(f32[4,8,256]{2,1,0:T(8,128)S(1)} %get-tuple-element.60), channel_id=1, source_target_pairs={{0,2},{2,0},{1,3},{3,1},{4,6},{6,4},{5,7},{7,5},{8,10},{10,8},{9,1... | collective-permute-start | bytes 98312 | tf_op jit(solution)/shard_map/ppermute | solution.py:454
  28.2 6.7 %collective-permute-start.13 = (bf16[2,4,32,128]{3,2,1,0:T(8,128)(2,1)S(1)}, bf16[2,4,32,128]{3,2,1,0:T(8,128)(2,1)S(1)}, u32[]{:S(2)}, u32[]{:S(2)}) collective-permute-start(bf16[2,4,32,128]{3,2,1,0:T(8,128)(2,1)S(1)} %convert_element_type.49), channel_id=1, source_target_pairs={{0,2},{2,0},{1,3},{3,1},{4,6},{6,4},{5,7},{7,5},{8,10},{10,8},{9,1... | collective-permute-start | bytes 196616 | tf_op jit(solution)/shard_map/ppermute | solution.py:446
  29.7 8.2 %collective-permute-start.11 = (bf16[4,64,256]{2,1,0:T(8,128)(2,1)S(1)}, bf16[4,64,256]{2,1,0:T(8,128)(2,1)S(1)}, u32[]{:S(2)}, u32[]{:S(2)}) collective-permute-start(bf16[4,64,256]{2,1,0:T(8,128)(2,1)S(1)} %get-tuple-element.65), channel_id=1, source_target_pairs={{1,4},{5,8},{9,12},{4,1},{8,5},{12,9},{3,6},{7,10},{11,14},{6,3},{... | collective-permute-start | bytes 393224 | tf_op jit(solution)/shard_map/ppermute | solution.py:452
  30.4 7.5 %collective-permute-start.10 = (bf16[4,64,256]{2,1,0:T(8,128)(2,1)S(1)}, bf16[4,64,256]{2,1,0:T(8,128)(2,1)S(1)}, u32[]{:S(2)}, u32[]{:S(2)}) collective-permute-start(bf16[4,64,256]{2,1,0:T(8,128)(2,1)S(1)} %get-tuple-element.65), channel_id=1, source_target_pairs={{0,1},{1,0},{2,3},{3,2},{4,5},{5,4},{6,7},{7,6},{8,9},{9,8},{10,11... | collective-permute-start | bytes 393224 | tf_op jit(solution)/shard_map/ppermute | solution.py:442
  33.4 3.9 %collective-permute-start.12 = (f32[4,8,256]{2,1,0:T(8,128)S(1)}, f32[4,8,256]{2,1,0:T(8,128)S(1)}, u32[]{:S(2)}, u32[]{:S(2)}) collective-permute-start(f32[4,8,256]{2,1,0:T(8,128)S(1)} %get-tuple-element.66), channel_id=1, source_target_pairs={{0,2},{2,0},{1,3},{3,1},{4,6},{6,4},{5,7},{7,5},{8,10},{10,8},{9,1... | collective-permute-start | bytes 98312 | tf_op jit(solution)/shard_map/ppermute | solution.py:454
  37.3 6.6 %collective-permute-start.17 = (bf16[2,4,32,128]{3,2,1,0:T(8,128)(2,1)S(1)}, bf16[2,4,32,128]{3,2,1,0:T(8,128)(2,1)S(1)}, u32[]{:S(2)}, u32[]{:S(2)}) collective-permute-start(bf16[2,4,32,128]{3,2,1,0:T(8,128)(2,1)S(1)} %convert_element_type.51), channel_id=1, source_target_pairs={{0,4},{4,0},{8,12},{12,8},{1,5},{5,1},{9,13},{13,9},{2,6},{6,2},{1... | collective-permute-start | bytes 196616 | tf_op jit(solution)/shard_map/ppermute | solution.py:446
  38.9 7.5 %collective-permute-start.15 = (bf16[4,64,256]{2,1,0:T(8,128)(2,1)S(1)}, bf16[4,64,256]{2,1,0:T(8,128)(2,1)S(1)}, u32[]{:S(2)}, u32[]{:S(2)}) collective-permute-start(bf16[4,64,256]{2,1,0:T(8,128)(2,1)S(1)} %get-tuple-element.70), channel_id=1, source_target_pairs={{1,4},{5,8},{9,12},{4,1},{8,5},{12,9},{3,6},{7,10},{11,14},{6,3},{... | collective-permute-start | bytes 393224 | tf_op jit(solution)/shard_map/ppermute | solution.py:452
  39.5 6.9 %collective-permute-start.14 = (bf16[4,64,256]{2,1,0:T(8,128)(2,1)S(1)}, bf16[4,64,256]{2,1,0:T(8,128)(2,1)S(1)}, u32[]{:S(2)}, u32[]{:S(2)}) collective-permute-start(bf16[4,64,256]{2,1,0:T(8,128)(2,1)S(1)} %get-tuple-element.70), channel_id=1, source_target_pairs={{0,1},{1,0},{2,3},{3,2},{4,5},{5,4},{6,7},{7,6},{8,9},{9,8},{10,11... | collective-permute-start | bytes 393224 | tf_op jit(solution)/shard_map/ppermute | solution.py:442
  42.5 3.9 %collective-permute-start.16 = (f32[4,8,256]{2,1,0:T(8,128)S(1)}, f32[4,8,256]{2,1,0:T(8,128)S(1)}, u32[]{:S(2)}, u32[]{:S(2)}) collective-permute-start(f32[4,8,256]{2,1,0:T(8,128)S(1)} %get-tuple-element.71), channel_id=1, source_target_pairs={{0,2},{2,0},{1,3},{3,1},{4,6},{6,4},{5,7},{7,5},{8,10},{10,8},{9,1... | collective-permute-start | bytes 98312 | tf_op jit(solution)/shard_map/ppermute | solution.py:454
  48.8 1.3 %collective-permute-start.18 = (bf16[2,4,32,128]{3,2,1,0:T(8,128)(2,1)S(1)}, bf16[2,4,32,128]{3,2,1,0:T(8,128)(2,1)S(1)}, u32[]{:S(2)}, u32[]{:S(2)}) collective-permute-start(bf16[2,4,32,128]{3,2,1,0:T(8,128)(2,1)S(1)} %get-tuple-element.76), channel_id=1, source_target_pairs={{0,1},{1,0},{2,3},{3,2},{4,5},{5,4},{6,7},{7,6},{8,9},{9,8},{10,11... | collective-permute-start | bytes 196616 | tf_op jit(solution)/shard_map/ppermute | solution.py:442
  50.1 5.4 %collective-permute-start.19 = (bf16[2,4,32,128]{3,2,1,0:T(8,128)(2,1)S(1)}, bf16[2,4,32,128]{3,2,1,0:T(8,128)(2,1)S(1)}, u32[]{:S(2)}, u32[]{:S(2)}) collective-permute-start(bf16[2,4,32,128]{3,2,1,0:T(8,128)(2,1)S(1)} %fusion), channel_id=1, source_target_pairs={{0,2},{2,0},{1,3},{3,1},{4,6},{6,4},{5,7},{7,5},{8,10},{10,8},{9,1... | collective-permute-start | bytes 196616 | tf_op jit(solution)/shard_map/ppermute | solution.py:484
  54.0 6.0 %collective-permute-start.23 = (bf16[2,4,32,128]{3,2,1,0:T(8,128)(2,1)S(1)}, bf16[2,4,32,128]{3,2,1,0:T(8,128)(2,1)S(1)}, u32[]{:S(2)}, u32[]{:S(2)}) collective-permute-start(bf16[2,4,32,128]{3,2,1,0:T(8,128)(2,1)S(1)} %convert_element_type.61), channel_id=1, source_target_pairs={{0,8},{4,12},{8,0},{12,4},{1,9},{5,13},{9,1},{13,5},{2,10},{6,14},... | collective-permute-start | bytes 196616 | tf_op jit(solution)/shard_map/ppermute | solution.py:446
  55.6 5.0 %collective-permute-start.20 = (bf16[2,4,32,128]{3,2,1,0:T(8,128)(2,1)S(1)}, bf16[2,4,32,128]{3,2,1,0:T(8,128)(2,1)S(1)}, u32[]{:S(2)}, u32[]{:S(2)}) collective-permute-start(bf16[2,4,32,128]{3,2,1,0:T(8,128)(2,1)S(1)} %fusion.2), channel_id=1, source_target_pairs={{0,4},{4,0},{8,12},{12,8},{1,5},{5,1},{9,13},{13,9},{2,6},{6,2},{1... | collective-permute-start | bytes 196616 | tf_op jit(solution)/shard_map/ppermute | solution.py:484
  60.0 7.9 %collective-permute-start.24 = (bf16[2,4,32,128]{3,2,1,0:T(8,128)(2,1)S(1)}, bf16[2,4,32,128]{3,2,1,0:T(8,128)(2,1)S(1)}, u32[]{:S(2)}, u32[]{:S(2)}) collective-permute-start(bf16[2,4,32,128]{3,2,1,0:T(8,128)(2,1)S(1)} %get-tuple-element.92), channel_id=1, source_target_pairs={{0,1},{1,0},{2,3},{3,2},{4,5},{5,4},{6,7},{7,6},{8,9},{9,8},{10,11... | collective-permute-start | bytes 196616 | tf_op jit(solution)/shard_map/ppermute | solution.py:442
  60.1 7.9 %collective-permute-start.25 = (f32[4,64,128]{2,1,0:T(8,128)S(1)}, f32[4,64,128]{2,1,0:T(8,128)S(1)}, u32[]{:S(2)}, u32[]{:S(2)}) collective-permute-start(f32[4,64,128]{2,1,0:T(8,128)S(1)} %get-tuple-element.89), channel_id=1, source_target_pairs={{0,1},{1,0},{2,3},{3,2},{4,5},{5,4},{6,7},{7,6},{8,9},{9,8},{10,11... | collective-permute-start | bytes 393224 | tf_op jit(solution)/shard_map/ppermute | solution.py:442
  60.7 7.1 %collective-permute-start.21 = (bf16[2,4,32,128]{3,2,1,0:T(8,128)(2,1)S(1)}, bf16[2,4,32,128]{3,2,1,0:T(8,128)(2,1)S(1)}, u32[]{:S(2)}, u32[]{:S(2)}) collective-permute-start(bf16[2,4,32,128]{3,2,1,0:T(8,128)(2,1)S(1)} %fusion.1), channel_id=1, source_target_pairs={{0,8},{4,12},{8,0},{12,4},{1,9},{5,13},{9,1},{13,5},{2,10},{6,14},... | collective-permute-start | bytes 196616 | tf_op jit(solution)/shard_map/ppermute | solution.py:484
  67.9 1.3 %collective-permute-start.22 = (bf16[2,4,32,128]{3,2,1,0:T(8,128)(2,1)S(1)}, bf16[2,4,32,128]{3,2,1,0:T(8,128)(2,1)S(1)}, u32[]{:S(2)}, u32[]{:S(2)}) collective-permute-start(bf16[2,4,32,128]{3,2,1,0:T(8,128)(2,1)S(1)} %get-tuple-element.94), channel_id=1, source_target_pairs={{0,1},{1,0},{2,3},{3,2},{4,5},{5,4},{6,7},{7,6},{8,9},{9,8},{10,11... | collective-permute-start | bytes 196616 | tf_op jit(solution)/shard_map/ppermute | solution.py:442
  (16 other events, 239.3 us)

commit v4 on v3

--- a/solution.py
+++ b/solution.py
@@ -81,20 +81,22 @@
         out[...] = jnp.where(upper, value_of(brick_y - EDGE, brick_y), value_of(0, EDGE))
 
 
+def slot():
+    return (lax.axis_index("gz") + lax.axis_index("gx")) % 2
+
+
 def assemble_body(count, *refs):
     tables_in, own_in, got = refs[:3], refs[3:6], refs[6:9]
-    p_out, q_out, ratio, bend, stiff, dense, sent = refs[9:16]
-    edge_outs = refs[16 : 16 + count]
-    tables, own, semaphores = refs[16 + count : 19 + count], refs[19 + count : 22 + count], refs[22 + count]
+    p_out, q_out, ratio, bend, sent, cells = refs[9:15]
+    edge_outs = refs[15 : 15 + count]
+    tables, own, semaphores = refs[15 + count : 18 + count], refs[18 + count : 21 + count], refs[21 + count]
     core, column = lax.axis_index("gz"), lax.axis_index("gy")
     rows, brick_y = p_out.shape[:2]
-    start = core * rows
+    start = slot() * rows
+    sources = [source.at[pl.ds(start, rows)] for source in own_in[:2]] + [own_in[2]]
     copies = [
         pltpu.make_async_copy(source, target, semaphores.at[index])
-        for index, (source, target) in enumerate(zip(tables_in, tables))
-    ] + [
-        pltpu.make_async_copy(source.at[pl.ds(start, rows)], target, semaphores.at[3 + index])
-        for index, (source, target) in enumerate(zip(own_in, own))
+        for index, (source, target) in enumerate(zip(list(tables_in) + sources, list(tables) + list(own)))
     ]
     for copy in copies:
         copy.start()
@@ -108,27 +110,27 @@
             [jnp.where(core == 0, mine, other), jnp.where(core == 0, other, mine)], axis=-1
         )
 
-    stiff_middle, dense_middle = middle(stiffness), middle(density)
+    for row in range(cells.shape[0]):
+        cells[row] = whole(own[2][row], got[2][row])
     for row in range(rows):
         value = whole(own[0][row], got[0][start + row])
         p_out[row] = value
         sent[row] = value.astype(BF16)
         q_out[row] = whole(own[1][row], got[1][start + row])
-        cell = whole(own[2][row], got[2][start + row])
+        cell = cells[start + row]
         ratio[row] = looked_up(cell, lambda e: stiffness[e] / density[e], entries)
         bend[row] = looked_up(cell, lambda e: nonlinear[e], entries)
-        stiff[row] = looked_up(cell, lambda e: stiffness[e] - stiff_middle, entries)
-        dense[row] = looked_up(cell, lambda e: density[e] - dense_middle, entries)
     edges(lambda a, b: p_out[:, a:b, :], edge_outs, column % 2, brick_y)
 
 
 def step_body(two_sided, last, p_ref, q_ref, ratio, bend, mate, far, *rest):
     count = 2 if two_sided else 1
     halos = rest[:count]
-    new_ref, sent = rest[count : count + 2]
+    new_ref = rest[count]
+    sent = None if last else rest[count + 1]
     edge_outs = rest[count + 2 : -1]
     padded = rest[-1]
-    core = lax.axis_index("gz")
+    place = slot()
     parity = lax.axis_index("gy") % 2
     rows, brick_y, depth = p_ref.shape
     lane = lax.broadcasted_iota(jnp.int32, (brick_y, depth), 1)
@@ -138,8 +140,8 @@
         if 0 <= index < rows:
             return p_ref[index]
         if index < 0:
-            return jnp.where(core == 0, far[index + rows], mate[index + rows]).astype(F32)
-        return jnp.where(core == 0, mate[index - rows], far[index - rows]).astype(F32)
+            return jnp.where(place == 0, far[index + rows].astype(F32), mate[index + rows])
+        return jnp.where(place == 0, mate[index - rows], far[index - rows].astype(F32))
 
     for row in range(rows):
         first = halos[0][row]
@@ -163,54 +165,100 @@
         new_ref[row] = value
         if not last:
             sent[row] = value.astype(BF16)
-    if last:
-        half = depth // 2
-        sent[...] = jnp.where(core == 0, new_ref[:, :, half:], new_ref[:, :, :half])
-    else:
+    if not last:
         edges(lambda a, b: new_ref[:, a:b, :], edge_outs, parity, brick_y)
 
 
-def spectrum_body(twiddle_x, *refs):
-    count = (len(refs) - 6) or 1
-    sources = refs[:count]
-    table_z, table_y, keep, send, lines, grid = refs[count:]
-    core, column = lax.axis_index("gz"), lax.axis_index("gy")
-    rows, brick_y, depth = sources[0].shape
-    modes_x, modes_y, width = keep.shape[1:]
+def transformed(sources, first, twiddle_x, table_z, table_y, lines, grid):
+    column = lax.axis_index("gy")
+    brick_y = lines.shape[0] // 4
+    modes_y = grid.shape[0]
+    width = table_z.shape[1]
     half = width // 2
-    for field, ref in enumerate(sources):
-        for row in range(rows):
-            high, low = high_low(ref[row])
+    for field, rows in enumerate(sources):
+        for row, load in enumerate(rows):
+            high, low = high_low(load())
             modes = jnp.dot(high, table_z[...], preferred_element_type=F32)
             modes = modes + jnp.dot(low, table_z[...], preferred_element_type=F32)
             back = turned(modes, half, 1.0)
             high, low = high_low(modes)
             back_high, back_low = high_low(back)
-            lanes = slice((field * rows + row) * width, (field * rows + row + 1) * width)
+            lanes = slice((field * len(rows) + row) * width, (field * len(rows) + row + 1) * width)
             for index, part in enumerate((high, back_high, low, back_low)):
                 lines[index * brick_y : (index + 1) * brick_y, lanes] = part
     grid[...] = jnp.dot(table_y[column], lines[...], preferred_element_type=F32)
-    block = lax.axis_index("gx") * 2 + core
-    first = block * (rows * modes_x * 4)
-
-    for field in range(count):
-        values, backs = [], []
-        for row in range(rows):
-            lanes = slice((field * rows + row) * width, (field * rows + row + 1) * width)
-            values.append(grid[:, lanes])
-            backs.append(turned(values[-1], half, 1.0))
+
+    def at_mode(field, modes_x):
+        count = len(sources[field])
+        values = [
+            grid[:, (field * count + row) * width : (field * count + row + 1) * width] for row in range(count)
+        ]
+        backs = [turned(value, half, 1.0) for value in values]
 
         def summed(mode):
             total = jnp.zeros((modes_y, width), F32)
-            for row in range(rows):
-                at = first + (row * modes_x * 2 + mode) * 2
+            for row in range(count):
+                at = ((first + row) * modes_x + mode) * 2
                 total = total + twiddle_x[at] * values[row] + twiddle_x[at + 1] * backs[row]
             return total
 
-        @pl.loop(0, modes_x)
+        return summed
+
+    return at_mode
+
+
+def materials_body(twiddle_x, stiffness, density, cells, table_z, table_y, keep, lines, grid):
+    half_x = keep.shape[1]
+    entries = stiffness.shape[0]
+    rows = cells.shape[0]
+    sources = []
+    for table in (stiffness, density):
+        center = middle(table)
+        sources.append([
+            lambda row=row, table=table, center=center: looked_up(cells[row], lambda e: table[e] - center, entries)
+            for row in range(rows)
+        ])
+    at_mode = transformed(sources, lax.axis_index("gx") * rows, twiddle_x, table_z, table_y, lines, grid)
+    core = lax.axis_index("gz")
+    for field in range(2):
+        summed = at_mode(field, 2 * half_x)
+
+        @pl.loop(0, half_x)
         def _(mode):
-            keep[field, mode] = summed(core * modes_x + mode)
-            send[field, mode] = summed((1 - core) * modes_x + mode).astype(BF16)
+            keep[field, mode] = summed(core * half_x + mode)
+
+
+def prior_body(twiddle_x, own, mate, table_z, table_y, keep, lines, grid):
+    half_x = keep.shape[0]
+    rows = own.shape[0]
+    place = slot()
+    sources = [
+        (lambda row=row: jnp.where(place == 0, own[row], mate[row])) for row in range(rows)
+    ] + [(lambda row=row: jnp.where(place == 0, mate[row], own[row])) for row in range(rows)]
+    at_mode = transformed([sources], lax.axis_index("gx") * (2 * rows), twiddle_x, table_z, table_y, lines, grid)
+    core = lax.axis_index("gz")
+    summed = at_mode(0, 2 * half_x)
+
+    @pl.loop(0, half_x)
+    def _(mode):
+        keep[mode] = summed(core * half_x + mode)
+
+
+def wave_body(twiddle_x, own, prior, table_z, table_y, keep, send, lines, grid):
+    half_x = keep.shape[1]
+    rows = own.shape[0]
+    first = (lax.axis_index("gx") * 2 + slot()) * rows
+    sources = [(lambda row=row: own[row]) for row in range(rows)]
+    at_mode = transformed([sources], first, twiddle_x, table_z, table_y, lines, grid)
+    core = lax.axis_index("gz")
+    summed = at_mode(0, 2 * half_x)
+    keep[1] = prior[...]
+    send[1] = jnp.zeros_like(send[1])
+
+    @pl.loop(0, half_x)
+    def _(mode):
+        keep[0, mode] = summed(core * half_x + mode)
+        send[0, mode] = summed((1 - core) * half_x + mode).astype(BF16)
 
 
 def prepare_body(
@@ -247,32 +295,41 @@
     lift_table[:, FIELDS + 1 :] = jnp.zeros_like(lift_table[:, FIELDS + 1 :])
 
 
-def pointwise_body(stiffness, density, p_ref, q_ref, stiff, dense, lift_ref, left, offset, out, right):
+def pointwise_body(stiffness, density, p_ref, q_ref, p_mate, q_mate, cells, lift_ref, left, offset, out, right):
     rows, group, depth = p_ref.shape
     padded_channels = lift_ref.shape[0]
     height = rows * padded_channels
+    entries = stiffness.shape[0]
+    core = lax.axis_index("gz")
+    own = slot() == core
 
     @pl.when(pl.program_id(0) == 0)
     def _():
         right[...] = jnp.zeros_like(right)
 
     weights = [lift_ref[:, index : index + 1] for index in range(FIELDS + 1)]
-    stiff_middle, dense_middle = middle(stiffness), middle(density)
+    values = []
+    for row in range(rows):
+        cell = cells[core * rows + row]
+        values.append((
+            jnp.where(own, p_ref[row], p_mate[row]),
+            jnp.where(own, q_ref[row], q_mate[row]),
+            looked_up(cell, lambda e: stiffness[e], entries),
+            looked_up(cell, lambda e: density[e], entries),
+        ))
     for y in range(group):
         lifted = []
         for row in range(rows):
             total = jnp.broadcast_to(weights[FIELDS], (padded_channels, depth))
-            line = slice(y, y + 1)
-            values = (p_ref[row, line], q_ref[row, line], stiff[row, line] + stiff_middle, dense[row, line] + dense_middle)
-            for value, weight in zip(values, weights):
-                total = total + value * weight
+            for value, weight in zip(values[row], weights):
+                total = total + value[y : y + 1, :] * weight
             lifted.append(total)
         right[y, 0:height, :] = jnp.concatenate(lifted, axis=0).astype(BF16)
         out[:, y, :] = jnp.dot(left[...], right[y], preferred_element_type=F32) + offset[...]
 
 
 def output_body(
-    mine, other, mine_early, other_early, local, left, table_y, table_z, wave_ref, wave_other,
+    mine, other, mine_early, other_early, local_low, local_high, left, table_y, table_z, wave_ref, wave_other,
     features, wave_out, modes, right, sums,
 ):
     step = pl.program_id(0)
@@ -302,10 +359,10 @@
                     lanes = slice((mode - start) * width, (mode - start + 1) * width)
                     modes[:, mode * FIELDS + field, :] = result[:, lanes]
         z_half = depth // 2
+        place = slot()
         for row in range(rows):
-            own = jnp.where(core == 0, wave_ref[row, :, :z_half], wave_ref[row, :, z_half:])
-            wave_out[core * rows + row] = own
-            wave_out[(1 - core) * rows + row] = wave_other[row]
+            for ref, start in ((wave_ref, place * rows), (wave_other, (1 - place) * rows)):
+                wave_out[start + row] = jnp.where(core == 0, ref[row, :, :z_half], ref[row, :, z_half:])
 
     base = pl.multiple_of(step * group, group)
     lines = modes[pl.ds(base, group)].reshape(group * coupled, width).astype(BF16)
@@ -318,7 +375,7 @@
     for row in range(rows):
         for channel in range(channels):
             at = row * channels + channel
-            total = sums[at] + local[at]
+            total = sums[at] + jnp.where(step < pl.num_programs(0) // 2, local_low[at], local_high[at])
             inner = math.sqrt(2.0 / math.pi) * (total + 0.044715 * (total * total * total))
             total = (0.5 * total) * (1.0 + jnp.tanh(inner))
             features[row, channel] = total.astype(BF16)
@@ -330,6 +387,11 @@
 
 def odd_pairs(count):
     pairs = [(index, index + 1) for index in range(1, count - 1, 2)]
+    return pairs + [(target, source) for source, target in pairs]
+
+
+def like_core_pairs(count):
+    pairs = [(2 * chip + 1 - chip % 2, 2 * chip + 3 - chip % 2) for chip in range(count - 1)]
     return pairs + [(target, source) for source, target in pairs]
 
 
@@ -407,19 +469,20 @@
     def shape(*dims, dtype=F32):
         return jax.ShapeDtypeStruct(dims, dtype)
 
-    cells = rows * brick_y * total_z
+    cells_count = rows * brick_y * total_z
     field = shape(rows, brick_y, total_z)
     edge = [shape(rows, EDGE, total_z)] * (2 if two_sided else 1)
-    half = shape(rows, brick_y, brick_z)
 
     swap_core = xor_pairs(core_count, 1)
     got = [lax.ppermute(array, "gz", swap_core) for array in (pressure, previous, material)]
     sending = shape(rows, brick_y, total_z, dtype=BF16)
-    current, before, ratio, bend, stiff, dense, sent, *edge_values = call(
-        lambda *refs: assemble_body(len(edge), *refs), [field] * 6 + [sending] + edge, [HBM] * 6 + [VMEM] * 3,
+    here = lambda *arrays: [pltpu.with_memory_space_constraint(array, pltpu.HBM) for array in arrays]
+    current, before, ratio, bend, sent, cells, *edge_values = call(
+        lambda *refs: assemble_body(len(edge), *refs),
+        [field] * 4 + [sending, shape(brick_x, brick_y, total_z, dtype=jnp.int32)] + edge, [HBM] * 6 + [VMEM] * 3,
         [pltpu.SMEM(stiffness.shape, F32)] * 3 + [pltpu.VMEM((rows, brick_y, brick_z), F32)] * 2
-        + [pltpu.VMEM((rows, brick_y, brick_z), jnp.int32), pltpu.SemaphoreType.DMA((6,))], moved=cells * 36
-    )(stiffness, density, nonlinear, pressure, previous, material, *got)
+        + [pltpu.VMEM((brick_x, brick_y, brick_z), jnp.int32), pltpu.SemaphoreType.DMA((6,))], moved=cells_count * 36
+    )(*here(stiffness, density, nonlinear, pressure, previous, material), *got)
 
     mixing, pointwise, lift_table, offset = call(
         prepare_body,
@@ -432,82 +495,109 @@
     )
 
     part = [shape(2, modes_x // 2, modes_y, width, dtype=dtype) for dtype in (F32, BF16)]
-    spectrum = call(
-        spectrum_body, part, [SMEM] + [VMEM] * 4,
-        [pltpu.VMEM((4 * brick_y, 2 * rows * width), BF16), pltpu.VMEM((modes_y, 2 * rows * width), F32)],
-        flops=cells * 1024, moved=cells * 16,
-    )
+
+    def spectrum(body, outs, inputs, lines, extra=0):
+        return call(
+            body, outs, [SMEM] * (1 + extra) + [VMEM] * (inputs + 2),
+            [pltpu.VMEM((4 * brick_y, lines * width), BF16), pltpu.VMEM((modes_y, lines * width), F32)],
+            flops=cells_count * 256 * lines, moved=cells_count * 2 * lines,
+        )
+
     stages = [(axis, count, 2**bit) for axis, count in (("gy", column_count), ("gx", cycle_count))
               for bit in range((count - 1).bit_length())]
     swap = lambda value: lax.ppermute(value, "gz", swap_core)
 
-    early, early_sent = spectrum(twiddle_x, stiff, dense, forward_z, forward_y)
-    moves = [lambda value: swap(early_sent)] + [
-        lambda value, stage=stage: lax.ppermute(value.astype(BF16), stage[0], xor_pairs(*stage[1:])) for stage in stages
-    ]
-    pending = None
+    def exchange(value, axis, count, distance):
+        return lax.ppermute(value.astype(BF16), axis, xor_pairs(count, distance))
+
+    early = spectrum(materials_body, part[0], 1, 2 * brick_x, 2)(
+        twiddle_x, stiffness, density, cells, forward_z, forward_y
+    )
+    moves = list(stages)
+    pending = early_other = None
+
+    def settle(value):
+        return value if pending is None else value + pending.astype(F32)
 
     for repeat in range(STEPS):
         last = repeat == STEPS - 1
-        far = lax.ppermute(sent, ("gx", "gz"), odd_pairs(blocks))
-        mate = swap(sent)
+        far = lax.ppermute(sent, ("gx", "gz"), like_core_pairs(cycle_count))
+        mate = swap(current)
         halos = [lax.ppermute(edge_values[0], "gy", xor_pairs(column_count, 1))]
         if two_sided:
             halos.append(lax.ppermute(edge_values[1], "gy", odd_pairs(column_count)))
-        if pending is not None:
-            early = early + pending.astype(F32)
-            pending = None
+        early, pending = settle(early), None
+        halos[0], early = lax.optimization_barrier((halos[0], early))
         if moves:
-            halos[0], early, early_sent = lax.optimization_barrier((halos[0], early, early_sent))
-            pending = moves.pop(0)(early)
-        outs = [field] + ([half] if last else [sending] + edge)
+            pending = exchange(early, *moves.pop(0))
+        elif early_other is None:
+            early_other = swap(early.astype(BF16))
+        if last:
+            prior = spectrum(prior_body, shape(modes_x // 2, modes_y, width), 2, brick_x)(
+                twiddle_x, current, mate, forward_z, forward_y
+            )
+            far, prior = lax.optimization_barrier((far, prior))
+            prior_mate = mate
+        outs = [field] + ([] if last else [sending] + edge)
         body = lambda *refs, last=last: step_body(two_sided, last, *refs)
-        new, sent, *edge_values = call(
+        new, *others = call(
             body, outs, [VMEM] * (6 + len(halos)),
-            [pltpu.VMEM((brick_y + 2 * EDGE, total_z), F32)], flops=cells * 60, moved=cells * 28,
+            [pltpu.VMEM((brick_y + 2 * EDGE, total_z), F32)], flops=cells_count * 60, moved=cells_count * 28,
         )(current, before, ratio, bend, mate, far, *halos)
+        if not last:
+            sent, *edge_values = others
         current, before = new, current
 
-    wave_other = swap(sent)
-    total, sent = spectrum(twiddle_x, current, before, forward_z, forward_y)
+    total, sent = spectrum(wave_body, part, 2, rows)(twiddle_x, current, prior, forward_z, forward_y)
     total = total + swap(sent).astype(F32)
-    while moves:
-        early = early + pending.astype(F32)
-        pending = moves.pop(0)(early)
-    early = early + pending.astype(F32)
-    early_other = swap(early.astype(BF16))
+    wave_other = swap(current)
+    while moves or pending is not None:
+        early, pending = settle(early), None
+        if moves:
+            pending = exchange(early, *moves.pop(0))
+    if early_other is None:
+        early_other = swap(early.astype(BF16))
     group = 8
+    steps = brick_y // group
     whole = lambda array: pl.BlockSpec(array.shape, lambda i: (0,) * len(array.shape))
-    slab = pl.BlockSpec((rows, group, total_z), lambda i: (0, i, 0))
-    strip = pl.BlockSpec((height, group, total_z), lambda i: (0, i, 0))
-    for index, (axis, count, distance) in enumerate(stages):
-        arrived = lax.ppermute(total.astype(BF16), axis, xor_pairs(count, distance))
+
+    def pointwise_part(start):
+        slab = lambda count: pl.BlockSpec((count, group, total_z), lambda i: (0, i + start, 0))
+        return pl.pallas_call(
+            pointwise_body,
+            grid=(steps // 2,),
+            out_shape=shape(height, brick_y // 2, total_z),
+            in_specs=[SMEM] * 2 + [slab(rows)] * 4 + [slab(brick_x), whole(lift_table), whole(pointwise), whole(offset)],
+            out_specs=pl.BlockSpec((height, group, total_z), lambda i: (0, i, 0)),
+            scratch_shapes=[pltpu.VMEM((group, right_depth, total_z), BF16)],
+            compiler_params=pltpu.CompilerParams(vmem_limit_bytes=16 * 1024 * 1024),
+            cost_estimate=pl.CostEstimate(flops=cells_count * 20000, bytes_accessed=cells_count * 50, transcendentals=0),
+        )(stiffness, density, current, before, wave_other, prior_mate, cells, lift_table, pointwise, offset)
+
+    for index, stage in enumerate(stages):
+        arrived = exchange(total, *stage)
         if index == 0:
             arrived, mixing, pointwise, lift_table, offset = lax.optimization_barrier(
                 (arrived, mixing, pointwise, lift_table, offset)
             )
+        if index == len(stages) - 2:
+            local_low = pointwise_part(0)
+            arrived, local_low = lax.optimization_barrier((arrived, local_low))
         if index == len(stages) - 1:
-            local = pl.pallas_call(
-                pointwise_body,
-                grid=(brick_y // group,),
-                out_shape=shape(height, brick_y, total_z),
-                in_specs=[SMEM] * 2 + [slab] * 4 + [whole(lift_table), whole(pointwise), whole(offset)],
-                out_specs=strip,
-                scratch_shapes=[pltpu.VMEM((group, right_depth, total_z), BF16)],
-                compiler_params=pltpu.CompilerParams(vmem_limit_bytes=24 * 1024 * 1024),
-                cost_estimate=pl.CostEstimate(flops=cells * 40000, bytes_accessed=cells * 100, transcendentals=0),
-            )(stiffness, density, current, before, stiff, dense, lift_table, pointwise, offset)
-            arrived, local = lax.optimization_barrier((arrived, local))
+            local_high = pointwise_part(steps // 2)
+            arrived, local_high = lax.optimization_barrier((arrived, local_high))
         total = total + arrived.astype(F32)
     other = swap(total.astype(BF16))
-
     scoped = 12 * 2**20 + 4 * (6 * 2 * modes_x * modes_y * width + brick_y * coupled * width + 6 * group * coupled * total_z)
     features, wave = pl.pallas_call(
         output_body,
-        grid=(brick_y // group,),
+        grid=(steps,),
         out_shape=[shape(rows, channels, brick_y, total_z, dtype=BF16), shape(*pressure.shape)],
-        in_specs=[whole(part[0]), whole(part[1])] * 2 + [strip, whole(mixing), whole(inverse_y), whole(inverse_z),
-                  whole(field), whole(half)],
+        in_specs=[whole(part[0]), whole(part[1])] * 2
+        + [pl.BlockSpec((height, group, total_z), lambda i: (0, jnp.minimum(i, steps // 2 - 1), 0)),
+           pl.BlockSpec((height, group, total_z), lambda i: (0, jnp.maximum(i - steps // 2, 0), 0)),
+           whole(mixing), whole(inverse_y), whole(inverse_z),
+                  whole(field), whole(field)],
         out_specs=[pl.BlockSpec((rows, channels, group, total_z), lambda i: (0, 0, i, 0)), whole(pressure)],
         scratch_shapes=[
             pltpu.VMEM((brick_y, coupled, width), F32),
@@ -515,8 +605,8 @@
             pltpu.VMEM((height, group, total_z), F32),
         ],
         compiler_params=pltpu.CompilerParams(vmem_limit_bytes=scoped),
-        cost_estimate=pl.CostEstimate(flops=cells * 2000, bytes_accessed=cells * 60, transcendentals=cells * 20),
-    )(total, other, early, early_other, local, mixing, inverse_y, inverse_z, current, wave_other)
+        cost_estimate=pl.CostEstimate(flops=cells_count * 2000, bytes_accessed=cells_count * 60, transcendentals=cells_count * 20),
+    )(total, other, early, early_other, local_low, local_high, mixing, inverse_y, inverse_z, current, wave_other)
     features = features.transpose(0, 2, 1, 3)
     return (wave, features)
 

time: 77.6 us -> 75.7 us (0.976)
  waiting for transfers between devices: 16.3 us -> 9.66 us
  starting transfers between devices: 28.5 us -> 33.9 us
  local copies, waits for them, and re-layouts: 7.21 us -> 3.74 us
  Pallas kernels: 23.8 us -> 26.8 us
    ppermute x4, waiting for transfers between devices: 8.16 us -> 0.63 us  [per_device(): halos = [lax.ppermute(edge_values[0], 'gy', xor_pairs(column_count, 1))]]
    ppermute x10, starting transfers between devices: 8.38 us -> 14 us  [the longest x6 11.2 us: exchange(): return lax.ppermute(value.astype(BF16), axis, xor_pairs(count, distance))]
    unnamed x44 -> x42, local copies, waits for them, and re-layouts: 7.16 us -> 3.69 us
    pallas_call x5 -> x7, Pallas kernels: 17.9 us -> 20.9 us  [the longest x1 8.25 us: per_device(): pl.pallas_call(output_body, grid=(steps,), out_shape=[shape(rows, channel...]
    ppermute x9 -> x8, starting transfers between devices: 14.1 us -> 11.1 us  [per_device(): swap = lambda value: lax.ppermute(value, 'gz', swap_core)]
    ppermute x4, starting transfers between devices: 5.01 us -> 7.73 us  [per_device(): halos = [lax.ppermute(edge_values[0], 'gy', xor_pairs(column_count, 1))]]
    ppermute x10, waiting for transfers between devices: 4.12 us -> 5.43 us  [the longest x6 5.42 us: exchange(): return lax.ppermute(value.astype(BF16), axis, xor_pairs(count, distance))]
    ppermute x9 -> x8, waiting for transfers between devices: 2.4 us -> 1.99 us  [per_device(): swap = lambda value: lax.ppermute(value, 'gz', swap_core)]
  transfers between devices with their start and end apart: 26 -> 25, of which waited for: 9 -> 9; matrix products, arithmetic and copies ran while one was open for 0% -> 0% of each run, Pallas kernels for 16% -> 20%
where the time goes in v4:
time: 75.7 us; the launch traced here: 75.4 us
  starting transfers between devices  33.9 us (45%)
  Pallas kernels  26.8 us (35%)
  waiting for transfers between devices  9.66 us (13%)
  local copies, waits for them, and re-layouts  3.74 us (5%)
  between operations  1.11 us (1%)
    ppermute x6, starting transfers between devices, exchange(): return lax.ppermute(value.astype(BF16), axis, xor_pairs(count, distance))  11.2 us
    ppermute x8, starting transfers between devices, per_device(): swap = lambda value: lax.ppermute(value, 'gz', swap_core)  11.1 us
    pallas_call x1, Pallas kernels, per_device(): pl.pallas_call(output_body, grid=(steps,), out_shape=[shape(rows, channel...  8.25 us
    ppermute x4, starting transfers between devices, per_device(): halos = [lax.ppermute(edge_values[0], 'gy', xor_pairs(column_count, 1))]  7.73 us
    pallas_call x2, Pallas kernels, pointwise_part(): pl.pallas_call(pointwise_body, grid=(steps // 2,), out_shape=shape(height...  6.61 us
    ppermute x6, waiting for transfers between devices, exchange(): return lax.ppermute(value.astype(BF16), axis, xor_pairs(count, distance))  5.42 us
    pallas_call x4, Pallas kernels, per_device(): call(body, outs, [VMEM] * (6 + len(halos)), [pltpu.VMEM((brick_y + 2 * ED...  3.7 us
    unnamed x42, local copies, waits for them, and re-layouts  3.69 us
  transfers between devices with their start and end apart: 25, of which 9 were waited for; matrix products, arithmetic and copies ran while one was open for 0% of the time, Pallas kernels for 20%

profile of v4, /device:TPU:0, one launch (start us, length us, event | category | flops | bytes accessed | tf_op | source)
XLA Modules:
  0.0 75.4 jit_solution(16706872474355762870)
XLA Ops:
  1.7 0.9 %collective-permute-done.refs_6_ = f32[8,64,128]{2,1,0:T(8,128)S(1)} collective-permute-done((f32[8,64,128]{2,1,0:T(8,128)}, f32[8,64,128]{2,1,0:T(8,128)S(1)}, u32[]{:S(2)}, u32[]{:S(2)}) %collective-permute-start) | collective-permute-done | bytes 262176 | tf_op jit(solution)/shard_map/ppermute | solution.py:477
  3.3 1.5 %shard_map.203 = (f32[4,64,256]{2,1,0:T(8,128)S(1)}, f32[4,64,256]{2,1,0:T(8,128)S(1)}, f32[4,64,256]{2,1,0:T(8,128)S(1)}, f32[4,64,256]{2,1,0:T(8,128)S(1)}, bf...) custom-call(f32[8]{0:T(128)} %stiffness.7, f32[8]{0:T(128)} %density.7, ...), custom_call_target="tpu_custom_call" | custom-call | bytes 2359296 | tf_op jit(solution)/shard_map/pallas_call | solution.py:480
  5.9 2.7 %collective-permute-start.5 = (f32[4,8,256]{2,1,0:T(8,128)S(1)}, f32[4,8,256]{2,1,0:T(8,128)S(1)}, u32[]{:S(2)}, u32[]{:S(2)}) collective-permute-start(f32[4,8,256]{2,1,0:T(8,128)S(1)} %get-tuple-element.50), channel_id=1, source_target_pairs={{0,2},{2,0},{1,3},{3,1},{4,6},{6,4},{5,7},{7,5},{8,10},{10,8},{9,1... | collective-permute-start | bytes 98312 | tf_op jit(solution)/shard_map/ppermute | solution.py:526
  8.5 0.8 %copy-done = bf16[256,128]{1,0:T(8,128)(2,1)S(1)} copy-done((bf16[256,128]{1,0:T(8,128)(2,1)S(1)}, bf16[256,128]{1,0:T(8,128)(2,1)}, u32[]{:S(2)}) %copy-start) | copy-done | bytes 65560
  9.4 0.8 %copy-done.3 = bf16[2,32,256]{2,1,0:T(8,128)(2,1)S(1)} copy-done((bf16[2,32,256]{2,1,0:T(8,128)(2,1)S(1)}, bf16[2,32,256]{2,1,0:T(8,128)(2,1)}, u32[]{:S(2)}) %copy-start.3) | copy-done | bytes 32792
  10.1 0.7 copy-done.6
  12.1 2.0 %shard_map.204 = f32[2,4,32,128]{3,2,1,0:T(8,128)S(1)} custom-call(f32[512]{0:T(512)S(1)} %copy-done.6, f32[8]{0:T(128)S(1)} %copy-done.8, f32[8]{0:T(128)S(1)} %copy-done.10, s32[8,64,256]{2,1,0:T(8,128)S(1)} %get-tuple-element.51.cells, bf16[256,128]{1,0:T(8,128)(2,1)S(1)} %copy-done, bf16[2,32,256]{2,1,0:T(8,128)(2,1)S(1)} %copy-done.3), custom_call_target="tpu_custom_call" | custom-call | flops 268435456 | bytes 2097152 | tf_op jit(solution)/shard_map/pallas_call | solution.py:513
  14.3 0.9 %shard_map.205 = (f32[4,64,256]{2,1,0:T(8,128)S(1)}, bf16[4,64,256]{2,1,0:T(8,128)(2,1)S(1)}, f32[4,8,256]{2,1,0:T(8,128)S(1)}) custom-call(f32[4,64,256]{2,1,0:T(8,128)S(1)} %get-tuple-element.45.refs_0_.refs_1_, f32[4,64,256]{2,1,0:T(8,128)S(1)} %get-tuple-element.46.refs_1_, f32[4,64,256]{2,1,0:T(8,128)S(1)} %get-tuple-element.47.refs_2_, ...), custom_call_target="tpu_custom_call" | custom-call | flops 3932160 | bytes 1835008 | tf_op jit(solution)/shard_map/pallas_call | solution.py:543
  15.3 2.1 %collective-permute-start.8 = (f32[4,8,256]{2,1,0:T(8,128)S(1)}, f32[4,8,256]{2,1,0:T(8,128)S(1)}, u32[]{:S(2)}, u32[]{:S(2)}) collective-permute-start(f32[4,8,256]{2,1,0:T(8,128)S(1)} %get-tuple-element.55), channel_id=1, source_target_pairs={{0,2},{2,0},{1,3},{3,1},{4,6},{6,4},{5,7},{7,5},{8,10},{10,8},{9,1... | collective-permute-start | bytes 98312 | tf_op jit(solution)/shard_map/ppermute | solution.py:526
  18.0 3.5 %collective-permute-start.6 = (f32[4,64,256]{2,1,0:T(8,128)S(1)}, f32[4,64,256]{2,1,0:T(8,128)S(1)}, u32[]{:S(2)}, u32[]{:S(2)}) collective-permute-start(f32[4,64,256]{2,1,0:T(8,128)S(1)} %get-tuple-element.53.refs_0_.refs_1_), channel_id=1, source_target_pairs={{0,1},{1,0},{2,3},{3,2},{4,5},{5,4},{6,7},{7,6},{8,9},{9,8},{10,11... | collective-permute-start | bytes 786440 | tf_op jit(solution)/shard_map/ppermute | solution.py:508
  21.6 2.7 %collective-permute-start.13 = (bf16[2,4,32,128]{3,2,1,0:T(8,128)(2,1)S(1)}, bf16[2,4,32,128]{3,2,1,0:T(8,128)(2,1)S(1)}, u32[]{:S(2)}, u32[]{:S(2)}) collective-permute-start(bf16[2,4,32,128]{3,2,1,0:T(8,128)(2,1)S(1)} %convert_element_type.47), channel_id=1, source_target_pairs={{0,4},{4,0},{8,12},{12,8},{1,5},{5,1},{9,13},{13,9},{2,6},{6,2},{1... | collective-permute-start | bytes 196616 | tf_op jit(solution)/shard_map/ppermute | solution.py:511
  24.3 0.9 %shard_map.206 = (f32[4,64,256]{2,1,0:T(8,128)S(1)}, bf16[4,64,256]{2,1,0:T(8,128)(2,1)S(1)}, f32[4,8,256]{2,1,0:T(8,128)S(1)}) custom-call(f32[4,64,256]{2,1,0:T(8,128)S(1)} %get-tuple-element.53.refs_0_.refs_1_, f32[4,64,256]{2,1,0:T(8,128)S(1)} %get-tuple-element.45.refs_0_.refs_1_, f32[4,64,256]{2,1,0:T(8,128)S(1)} %get-tuple-element.47.refs_2_, ...), custom_call_target="tpu_custom_call" | custom-call | flops 3932160 | bytes 1835008 | tf_op jit(solution)/shard_map/pallas_call | solution.py:543
  25.2 1.5 %collective-permute-start.12 = (f32[4,8,256]{2,1,0:T(8,128)S(1)}, f32[4,8,256]{2,1,0:T(8,128)S(1)}, u32[]{:S(2)}, u32[]{:S(2)}) collective-permute-start(f32[4,8,256]{2,1,0:T(8,128)S(1)} %get-tuple-element.60), channel_id=1, source_target_pairs={{0,2},{2,0},{1,3},{3,1},{4,6},{6,4},{5,7},{7,5},{8,10},{10,8},{9,1... | collective-permute-start | bytes 98312 | tf_op jit(solution)/shard_map/ppermute | solution.py:526
  27.4 1.4 %collective-permute-start.10 = (f32[4,64,256]{2,1,0:T(8,128)S(1)}, f32[4,64,256]{2,1,0:T(8,128)S(1)}, u32[]{:S(2)}, u32[]{:S(2)}) collective-permute-start(f32[4,64,256]{2,1,0:T(8,128)S(1)} %get-tuple-element.58.refs_0_.refs_1_), channel_id=1, source_target_pairs={{0,1},{1,0},{2,3},{3,2},{4,5},{5,4},{6,7},{7,6},{8,9},{9,8},{10,11... | collective-permute-start | bytes 786440 | tf_op jit(solution)/shard_map/ppermute | solution.py:508
  29.5 4.3 %collective-permute-start.17 = (bf16[2,4,32,128]{3,2,1,0:T(8,128)(2,1)S(1)}, bf16[2,4,32,128]{3,2,1,0:T(8,128)(2,1)S(1)}, u32[]{:S(2)}, u32[]{:S(2)}) collective-permute-start(bf16[2,4,32,128]{3,2,1,0:T(8,128)(2,1)S(1)} %convert_element_type.49), channel_id=1, source_target_pairs={{0,8},{4,12},{8,0},{12,4},{1,9},{5,13},{9,1},{13,5},{2,10},{6,14},... | collective-permute-start | bytes 196616 | tf_op jit(solution)/shard_map/ppermute | solution.py:511
  33.8 0.9 %shard_map.207 = (f32[4,64,256]{2,1,0:T(8,128)S(1)}, bf16[4,64,256]{2,1,0:T(8,128)(2,1)S(1)}, f32[4,8,256]{2,1,0:T(8,128)S(1)}) custom-call(f32[4,64,256]{2,1,0:T(8,128)S(1)} %get-tuple-element.58.refs_0_.refs_1_, f32[4,64,256]{2,1,0:T(8,128)S(1)} %get-tuple-element.53.refs_0_.refs_1_, f32[4,64,256]{2,1,0:T(8,128)S(1)} %get-tuple-element.47.refs_2_, ...), custom_call_target="tpu_custom_call" | custom-call | flops 3932160 | bytes 1835008 | tf_op jit(solution)/shard_map/pallas_call | solution.py:543
  35.0 1.5 %collective-permute-start.16 = (f32[4,8,256]{2,1,0:T(8,128)S(1)}, f32[4,8,256]{2,1,0:T(8,128)S(1)}, u32[]{:S(2)}, u32[]{:S(2)}) collective-permute-start(f32[4,8,256]{2,1,0:T(8,128)S(1)} %get-tuple-element.66), channel_id=1, source_target_pairs={{0,2},{2,0},{1,3},{3,1},{4,6},{6,4},{5,7},{7,5},{8,10},{10,8},{9,1... | collective-permute-start | bytes 98312 | tf_op jit(solution)/shard_map/ppermute | solution.py:526
  36.5 0.8 %collective-permute-start.15 = (bf16[4,64,256]{2,1,0:T(8,128)(2,1)S(1)}, bf16[4,64,256]{2,1,0:T(8,128)(2,1)S(1)}, u32[]{:S(2)}, u32[]{:S(2)}) collective-permute-start(bf16[4,64,256]{2,1,0:T(8,128)(2,1)S(1)} %get-tuple-element.64), channel_id=1, source_target_pairs={{1,5},{4,8},{9,13},{5,1},{8,4},{13,9},{3,7},{6,10},{11,15},{7,3},{... | collective-permute-start | bytes 393224 | tf_op jit(solution)/shard_map/ppermute | solution.py:524
  37.4 1.9 %collective-permute-done.17 = bf16[2,4,32,128]{3,2,1,0:T(8,128)(2,1)S(1)} collective-permute-done((bf16[2,4,32,128]{3,2,1,0:T(8,128)(2,1)S(1)}, bf16[2,4,32,128]{3,2,1,0:T(8,128)(2,1)S(1)}, u32[]{:S(2)}, u32[]{:S(2)}) %collective-permute-start.17) | collective-permute-done | bytes 65568 | tf_op jit(solution)/shard_map/ppermute | solution.py:511
  39.3 1.3 %shard_map.208.prior = f32[4,32,128]{2,1,0:T(8,128)S(1)} custom-call(f32[512]{0:T(512)S(1)} %copy-done.7, f32[4,64,256]{2,1,0:T(8,128)S(1)} %get-tuple-element.63.own.refs_0_.q_ref, f32[4,64,256]{2,1,0:T(8,128)S(1)} %collective-permute-done.14.mate.refs_4_.q_mate, bf16[256,128]{1,0:T(8,128)(2,1)S(1)} %copy-done.1, bf16[2,32,256]{2,1,0:T(8,128)(2,1)S(1)} %copy-done.4), custom_call_target="tpu_custom_call" | custom-call | flops 134217728 | bytes 1048576 | tf_op jit(solution)/shard_map/pallas_call | solution.py:536
  40.6 0.9 %shard_map.209.own.p_ref.wave_ref = f32[4,64,256]{2,1,0:T(8,128)S(1)} custom-call(f32[4,64,256]{2,1,0:T(8,128)S(1)} %get-tuple-element.63.own.refs_0_.q_ref, f32[4,64,256]{2,1,0:T(8,128)S(1)} %get-tuple-element.58.refs_0_.refs_1_, f32[4,64,256]{2,1,0:T(8,128)S(1)} %get-tuple-element.47.refs_2_, f32[4,64,256]{2,1,0:T(8,128)S(1)} %get-tuple-element.48.refs_3_, ...), custom_call_target="tpu_custom_call" | custom-call | flops 3932160 | bytes 1835008 | tf_op jit(solution)/shard_map/pallas_call | solution.py:543
  41.6 1.2 %shard_map.210 = (f32[2,4,32,128]{3,2,1,0:T(8,128)S(1)}, bf16[2,4,32,128]{3,2,1,0:T(8,128)(2,1)S(1)}) custom-call(f32[512]{0:T(512)S(1)} %copy-done.7, f32[4,64,256]{2,1,0:T(8,128)S(1)} %shard_map.209.own.p_ref.wave_ref, f32[4,32,128]{2,1,0:T(8,128)S(1)} %shard_map.208.prior, bf16[256,128]{1,0:T(8,128)(2,1)S(1)} %copy-done.1, bf16[2,32,256]{2,1,0:T(8,128)(2,1)S(1)} %copy-done.4), custom_call_target="tpu_custom_call" | custom-call | flops 67108864 | bytes 524288 | tf_op jit(solution)/shard_map/pallas_call | solution.py:551
  42.8 5.2 %collective-permute-start.18 = (bf16[2,4,32,128]{3,2,1,0:T(8,128)(2,1)S(1)}, bf16[2,4,32,128]{3,2,1,0:T(8,128)(2,1)S(1)}, u32[]{:S(2)}, u32[]{:S(2)}) collective-permute-start(bf16[2,4,32,128]{3,2,1,0:T(8,128)(2,1)S(1)} %get-tuple-element.71), channel_id=1, source_target_pairs={{0,1},{1,0},{2,3},{3,2},{4,5},{5,4},{6,7},{7,6},{8,9},{9,8},{10,11... | collective-permute-start | bytes 196616 | tf_op jit(solution)/shard_map/ppermute | solution.py:508
  48.1 0.7 collective-permute-done.18
  49.6 2.2 %shard_map.211 = (bf16[80,64]{1,0:T(8,128)(2,1)S(1)}, bf16[80,128]{1,0:T(8,128)(2,1)S(1)}, f32[24,8]{1,0:T(8,128)S(1)}, f32[80,1]{1,0:T(8,128)S(1)}) custom-call(f32[8]{0:T(128)S(1)} %copy-done.9, f32[8]{0:T(128)S(1)} %copy-done.11, f32[2,160,20]{2,1,0:T(8,128)S(1)} %reshape.12.mode_ref, f32[4,20]{1,0:T(4,128)S(1)} %copy-done.13, f32[1,20]{1,0:T(1,128)S(1)} %bitcast.2, ...), custom_call_target="tpu_custom_call" | custom-call | flops 2000000000 | bytes 4000000 | tf_op jit(solution)/shard_map/pallas_call | solution.py:487
  51.9 1.4 %collective-permute-done.19 = bf16[2,4,32,128]{3,2,1,0:T(8,128)(2,1)S(1)} collective-permute-done((bf16[2,4,32,128]{3,2,1,0:T(8,128)(2,1)S(1)}, bf16[2,4,32,128]{3,2,1,0:T(8,128)(2,1)S(1)}, u32[]{:S(2)}, u32[]{:S(2)}) %collective-permute-start.19) | collective-permute-done | bytes 65568 | tf_op jit(solution)/shard_map/ppermute | solution.py:511
  53.4 3.1 %collective-permute-start.20 = (bf16[2,4,32,128]{3,2,1,0:T(8,128)(2,1)S(1)}, bf16[2,4,32,128]{3,2,1,0:T(8,128)(2,1)S(1)}, u32[]{:S(2)}, u32[]{:S(2)}) collective-permute-start(bf16[2,4,32,128]{3,2,1,0:T(8,128)(2,1)S(1)} %fusion.2), channel_id=1, source_target_pairs={{0,4},{4,0},{8,12},{12,8},{1,5},{5,1},{9,13},{13,9},{2,6},{6,2},{1... | collective-permute-start | bytes 196616 | tf_op jit(solution)/shard_map/ppermute | solution.py:511
  56.4 3.3 %shard_map.212.local_low = f32[80,32,256]{2,1,0:T(8,128)S(1)} custom-call(f32[8]{0:T(128)S(1)} %copy-done.9, f32[8]{0:T(128)S(1)} %copy-done.11, f32[4,64,256]{2,1,0:T(8,128)S(1)} %shard_map.209.own.p_ref.wave_ref, f32[4,64,256]{2,1,0:T(8,128)S(1)} %get-tuple-element.63.own.refs_0_.q_ref, f32[4,64,256]{2,1,0:T(8,128)S(1)} %collective-permute-done.21.p_mate.wave_other, ...), custom_call_target="tpu_custom_call" | custom-call | flops 1310720000 | bytes 3276800 | tf_op jit(solution)/shard_map/pallas_call | solution.py:566
  60.3 3.3 %shard_map.213.local_high = f32[80,32,256]{2,1,0:T(8,128)S(1)} custom-call(f32[8]{0:T(128)S(1)} %copy-done.9, f32[8]{0:T(128)S(1)} %copy-done.11, f32[4,64,256]{2,1,0:T(8,128)S(1)} %shard_map.209.own.p_ref.wave_ref, f32[4,64,256]{2,1,0:T(8,128)S(1)} %get-tuple-element.63.own.refs_0_.q_ref, f32[4,64,256]{2,1,0:T(8,128)S(1)} %collective-permute-done.21.p_mate.wave_other, ...), custom_call_target="tpu_custom_call" | custom-call | flops 1310720000 | bytes 3276800 | tf_op jit(solution)/shard_map/pallas_call | solution.py:566
  63.6 2.1 %collective-permute-done.22 = bf16[2,4,32,128]{3,2,1,0:T(8,128)(2,1)S(1)} collective-permute-done((bf16[2,4,32,128]{3,2,1,0:T(8,128)(2,1)S(1)}, bf16[2,4,32,128]{3,2,1,0:T(8,128)(2,1)S(1)}, u32[]{:S(2)}, u32[]{:S(2)}) %collective-permute-start.22) | collective-permute-done | bytes 65568 | tf_op jit(solution)/shard_map/ppermute | solution.py:511
  65.9 1.2 %collective-permute-done.23.other = bf16[2,4,32,128]{3,2,1,0:T(8,128)(2,1)S(1)} collective-permute-done((bf16[2,4,32,128]{3,2,1,0:T(8,128)(2,1)S(1)}, bf16[2,4,32,128]{3,2,1,0:T(8,128)(2,1)S(1)}, u32[]{:S(2)}, u32[]{:S(2)}) %collective-permute-start.23) | collective-permute-done | bytes 65568 | tf_op jit(solution)/shard_map/ppermute | solution.py:508
  67.1 8.3 %shard_map.214 = (bf16[4,20,64,256]{3,2,1,0:T(8,128)(2,1)}, f32[8,64,128]{2,1,0:T(8,128)}) custom-call(f32[2,4,32,128]{3,2,1,0:T(8,128)S(1)} %get-tuple-element.89.mine, bf16[2,4,32,128]{3,2,1,0:T(8,128)(2,1)S(1)} %collective-permute-done.23.other, f32[2,4,32,128]{3,2,1,0:T(8,128)S(1)} %convert_add_fusion.4.mine_early, ...), custom_call_target="tpu_custom_call" | custom-call | flops 131072000 | bytes 3932160 | tf_op jit(solution)/shard_map/pallas_call | solution.py:592
  (85 shorter events, 8.3 us)
Async XLA Ops:
  0.6 1.9 %collective-permute-start = (f32[8,64,128]{2,1,0:T(8,128)}, f32[8,64,128]{2,1,0:T(8,128)S(1)}, u32[]{:S(2)}, u32[]{:S(2)}) collective-permute-start(f32[8,64,128]{2,1,0:T(8,128)} %refs_3_.1), channel_id=1, source_target_pairs={{0,1},{1,0},{2,3},{3,2},{4,5},{5,4},{6,7},{7,6},{8,9},{9,8},{10,11... | collective-permute-start | bytes 786440 | tf_op jit(solution)/shard_map/ppermute | solution.py:477
  1.1 1.7 %collective-permute-start.1 = (f32[8,64,128]{2,1,0:T(8,128)}, f32[8,64,128]{2,1,0:T(8,128)S(1)}, u32[]{:S(2)}, u32[]{:S(2)}) collective-permute-start(f32[8,64,128]{2,1,0:T(8,128)} %refs_4_.1), channel_id=1, source_target_pairs={{0,1},{1,0},{2,3},{3,2},{4,5},{5,4},{6,7},{7,6},{8,9},{9,8},{10,11... | collective-permute-start | bytes 786440 | tf_op jit(solution)/shard_map/ppermute | solution.py:477
  1.2 2.0 %collective-permute-start.2 = (s32[8,64,128]{2,1,0:T(8,128)}, s32[8,64,128]{2,1,0:T(8,128)S(1)}, u32[]{:S(2)}, u32[]{:S(2)}) collective-permute-start(s32[8,64,128]{2,1,0:T(8,128)} %refs_5_.1), channel_id=1, source_target_pairs={{0,1},{1,0},{2,3},{3,2},{4,5},{5,4},{6,7},{7,6},{8,9},{9,8},{10,11... | collective-permute-start | bytes 786440 | tf_op jit(solution)/shard_map/ppermute | solution.py:477
  4.7 9.5 %collective-permute-start.3 = (f32[4,64,256]{2,1,0:T(8,128)S(1)}, f32[4,64,256]{2,1,0:T(8,128)S(1)}, u32[]{:S(2)}, u32[]{:S(2)}) collective-permute-start(f32[4,64,256]{2,1,0:T(8,128)S(1)} %get-tuple-element.45.refs_0_.refs_1_), channel_id=1, source_target_pairs={{0,1},{1,0},{2,3},{3,2},{4,5},{5,4},{6,7},{7,6},{8,9},{9,8},{10,11... | collective-permute-start | bytes 786440 | tf_op jit(solution)/shard_map/ppermute | solution.py:508
  5.2 9.1 %collective-permute-start.4 = (bf16[4,64,256]{2,1,0:T(8,128)(2,1)S(1)}, bf16[4,64,256]{2,1,0:T(8,128)(2,1)S(1)}, u32[]{:S(2)}, u32[]{:S(2)}) collective-permute-start(bf16[4,64,256]{2,1,0:T(8,128)(2,1)S(1)} %get-tuple-element.49), channel_id=1, source_target_pairs={{1,5},{4,8},{9,13},{5,1},{8,4},{13,9},{3,7},{6,10},{11,15},{7,3},{... | collective-permute-start | bytes 393224 | tf_op jit(solution)/shard_map/ppermute | solution.py:524
  5.9 8.3 %collective-permute-start.5 = (f32[4,8,256]{2,1,0:T(8,128)S(1)}, f32[4,8,256]{2,1,0:T(8,128)S(1)}, u32[]{:S(2)}, u32[]{:S(2)}) collective-permute-start(f32[4,8,256]{2,1,0:T(8,128)S(1)} %get-tuple-element.50), channel_id=1, source_target_pairs={{0,2},{2,0},{1,3},{3,1},{4,6},{6,4},{5,7},{7,5},{8,10},{10,8},{9,1... | collective-permute-start | bytes 98312 | tf_op jit(solution)/shard_map/ppermute | solution.py:526
  14.2 7.3 %collective-permute-start.9 = (bf16[2,4,32,128]{3,2,1,0:T(8,128)(2,1)S(1)}, bf16[2,4,32,128]{3,2,1,0:T(8,128)(2,1)S(1)}, u32[]{:S(2)}, u32[]{:S(2)}) collective-permute-start(bf16[2,4,32,128]{3,2,1,0:T(8,128)(2,1)S(1)} %convert_element_type.45), channel_id=1, source_target_pairs={{0,2},{2,0},{1,3},{3,1},{4,6},{6,4},{5,7},{7,5},{8,10},{10,8},{9,1... | collective-permute-start | bytes 196616 | tf_op jit(solution)/shard_map/ppermute | solution.py:511
  14.3 25.0 %copy-start.1 = (bf16[256,128]{1,0:T(8,128)(2,1)S(1)}, bf16[256,128]{1,0:T(8,128)(2,1)}, u32[]{:S(2)}) copy-start(bf16[256,128]{1,0:T(8,128)(2,1)} %constant.26.clone.table_z) | copy-start | bytes 196612
  14.3 25.0 %copy-start.4 = (bf16[2,32,256]{2,1,0:T(8,128)(2,1)S(1)}, bf16[2,32,256]{2,1,0:T(8,128)(2,1)}, u32[]{:S(2)}) copy-start(bf16[2,32,256]{2,1,0:T(8,128)(2,1)} %constant.27.clone.table_y) | copy-start | bytes 98308
  14.3 25.0 %copy-start.7 = (f32[512]{0:T(512)S(1)}, f32[512]{0:T(512)}, u32[]{:S(2)}) copy-start(f32[512]{0:T(512)} %constant.25.clone.twiddle_x) | copy-start | bytes 6148
  15.3 6.3 %collective-permute-start.8 = (f32[4,8,256]{2,1,0:T(8,128)S(1)}, f32[4,8,256]{2,1,0:T(8,128)S(1)}, u32[]{:S(2)}, u32[]{:S(2)}) collective-permute-start(f32[4,8,256]{2,1,0:T(8,128)S(1)} %get-tuple-element.55), channel_id=1, source_target_pairs={{0,2},{2,0},{1,3},{3,1},{4,6},{6,4},{5,7},{7,5},{8,10},{10,8},{9,1... | collective-permute-start | bytes 98312 | tf_op jit(solution)/shard_map/ppermute | solution.py:526
  17.3 7.0 %collective-permute-start.7 = (bf16[4,64,256]{2,1,0:T(8,128)(2,1)S(1)}, bf16[4,64,256]{2,1,0:T(8,128)(2,1)S(1)}, u32[]{:S(2)}, u32[]{:S(2)}) collective-permute-start(bf16[4,64,256]{2,1,0:T(8,128)(2,1)S(1)} %get-tuple-element.54), channel_id=1, source_target_pairs={{1,5},{4,8},{9,13},{5,1},{8,4},{13,9},{3,7},{6,10},{11,15},{7,3},{... | collective-permute-start | bytes 393224 | tf_op jit(solution)/shard_map/ppermute | solution.py:524
  18.0 6.3 %collective-permute-start.6 = (f32[4,64,256]{2,1,0:T(8,128)S(1)}, f32[4,64,256]{2,1,0:T(8,128)S(1)}, u32[]{:S(2)}, u32[]{:S(2)}) collective-permute-start(f32[4,64,256]{2,1,0:T(8,128)S(1)} %get-tuple-element.53.refs_0_.refs_1_), channel_id=1, source_target_pairs={{0,1},{1,0},{2,3},{3,2},{4,5},{5,4},{6,7},{7,6},{8,9},{9,8},{10,11... | collective-permute-start | bytes 786440 | tf_op jit(solution)/shard_map/ppermute | solution.py:508
  21.6 7.2 %collective-permute-start.13 = (bf16[2,4,32,128]{3,2,1,0:T(8,128)(2,1)S(1)}, bf16[2,4,32,128]{3,2,1,0:T(8,128)(2,1)S(1)}, u32[]{:S(2)}, u32[]{:S(2)}) collective-permute-start(bf16[2,4,32,128]{3,2,1,0:T(8,128)(2,1)S(1)} %convert_element_type.47), channel_id=1, source_target_pairs={{0,4},{4,0},{8,12},{12,8},{1,5},{5,1},{9,13},{13,9},{2,6},{6,2},{1... | collective-permute-start | bytes 196616 | tf_op jit(solution)/shard_map/ppermute | solution.py:511
  25.2 22.8 %copy-start.20 = (f32[2,8,20,20]{3,1,2,0:T(8,128)S(1)}, f32[2,8,20,20]{3,1,2,0:T(8,128)}, u32[]{:S(2)}) copy-start(f32[2,8,20,20]{3,1,2,0:T(8,128)} %param.28) | copy-start | bytes 76804
  25.2 4.2 %collective-permute-start.12 = (f32[4,8,256]{2,1,0:T(8,128)S(1)}, f32[4,8,256]{2,1,0:T(8,128)S(1)}, u32[]{:S(2)}, u32[]{:S(2)}) collective-permute-start(f32[4,8,256]{2,1,0:T(8,128)S(1)} %get-tuple-element.60), channel_id=1, source_target_pairs={{0,2},{2,0},{1,3},{3,1},{4,6},{6,4},{5,7},{7,5},{8,10},{10,8},{9,1... | collective-permute-start | bytes 98312 | tf_op jit(solution)/shard_map/ppermute | solution.py:526
  26.7 7.1 %collective-permute-start.11 = (bf16[4,64,256]{2,1,0:T(8,128)(2,1)S(1)}, bf16[4,64,256]{2,1,0:T(8,128)(2,1)S(1)}, u32[]{:S(2)}, u32[]{:S(2)}) collective-permute-start(bf16[4,64,256]{2,1,0:T(8,128)(2,1)S(1)} %get-tuple-element.59), channel_id=1, source_target_pairs={{1,5},{4,8},{9,13},{5,1},{8,4},{13,9},{3,7},{6,10},{11,15},{7,3},{... | collective-permute-start | bytes 393224 | tf_op jit(solution)/shard_map/ppermute | solution.py:524
  27.4 6.4 %collective-permute-start.10 = (f32[4,64,256]{2,1,0:T(8,128)S(1)}, f32[4,64,256]{2,1,0:T(8,128)S(1)}, u32[]{:S(2)}, u32[]{:S(2)}) collective-permute-start(f32[4,64,256]{2,1,0:T(8,128)S(1)} %get-tuple-element.58.refs_0_.refs_1_), channel_id=1, source_target_pairs={{0,1},{1,0},{2,3},{3,2},{4,5},{5,4},{6,7},{7,6},{8,9},{9,8},{10,11... | collective-permute-start | bytes 786440 | tf_op jit(solution)/shard_map/ppermute | solution.py:508
  29.4 20.1 %copy-start.9 = (f32[8]{0:T(128)S(1)}, f32[8]{0:T(128)}, u32[]{:S(2)}) copy-start(f32[8]{0:T(128)} %stiffness.7) | copy-start | bytes 100
  29.4 20.1 %copy-start.11 = (f32[8]{0:T(128)S(1)}, f32[8]{0:T(128)}, u32[]{:S(2)}) copy-start(f32[8]{0:T(128)} %density.7) | copy-start | bytes 100
  29.4 20.1 %copy-start.12 = (bf16[20,20]{1,0:T(8,128)(2,1)S(1)}, bf16[20,20]{1,0:T(8,128)(2,1)}, u32[]{:S(2)}) copy-start(bf16[20,20]{1,0:T(8,128)(2,1)} %local_ref.1) | copy-start | bytes 2404
  29.5 9.7 %collective-permute-start.17 = (bf16[2,4,32,128]{3,2,1,0:T(8,128)(2,1)S(1)}, bf16[2,4,32,128]{3,2,1,0:T(8,128)(2,1)S(1)}, u32[]{:S(2)}, u32[]{:S(2)}) collective-permute-start(bf16[2,4,32,128]{3,2,1,0:T(8,128)(2,1)S(1)} %convert_element_type.49), channel_id=1, source_target_pairs={{0,8},{4,12},{8,0},{12,4},{1,9},{5,13},{9,1},{13,5},{2,10},{6,14},... | collective-permute-start | bytes 196616 | tf_op jit(solution)/shard_map/ppermute | solution.py:511
  34.8 4.5 %collective-permute-start.14 = (f32[4,64,256]{2,1,0:T(8,128)S(1)}, f32[4,64,256]{2,1,0:T(8,128)S(1)}, u32[]{:S(2)}, u32[]{:S(2)}) collective-permute-start(f32[4,64,256]{2,1,0:T(8,128)S(1)} %get-tuple-element.63.own.refs_0_.q_ref), channel_id=1, source_target_pairs={{0,1},{1,0},{2,3},{3,2},{4,5},{5,4},{6,7},{7,6},{8,9},{9,8},{10,11... | collective-permute-start | bytes 786440 | tf_op jit(solution)/shard_map/ppermute | solution.py:508
  35.0 4.2 %collective-permute-start.16 = (f32[4,8,256]{2,1,0:T(8,128)S(1)}, f32[4,8,256]{2,1,0:T(8,128)S(1)}, u32[]{:S(2)}, u32[]{:S(2)}) collective-permute-start(f32[4,8,256]{2,1,0:T(8,128)S(1)} %get-tuple-element.66), channel_id=1, source_target_pairs={{0,2},{2,0},{1,3},{3,1},{4,6},{6,4},{5,7},{7,5},{8,10},{10,8},{9,1... | collective-permute-start | bytes 98312 | tf_op jit(solution)/shard_map/ppermute | solution.py:526
  36.5 4.1 %collective-permute-start.15 = (bf16[4,64,256]{2,1,0:T(8,128)(2,1)S(1)}, bf16[4,64,256]{2,1,0:T(8,128)(2,1)S(1)}, u32[]{:S(2)}, u32[]{:S(2)}) collective-permute-start(bf16[4,64,256]{2,1,0:T(8,128)(2,1)S(1)} %get-tuple-element.64), channel_id=1, source_target_pairs={{1,5},{4,8},{9,13},{5,1},{8,4},{13,9},{3,7},{6,10},{11,15},{7,3},{... | collective-permute-start | bytes 393224 | tf_op jit(solution)/shard_map/ppermute | solution.py:524
  42.8 6.1 %collective-permute-start.18 = (bf16[2,4,32,128]{3,2,1,0:T(8,128)(2,1)S(1)}, bf16[2,4,32,128]{3,2,1,0:T(8,128)(2,1)S(1)}, u32[]{:S(2)}, u32[]{:S(2)}) collective-permute-start(bf16[2,4,32,128]{3,2,1,0:T(8,128)(2,1)S(1)} %get-tuple-element.71), channel_id=1, source_target_pairs={{0,1},{1,0},{2,3},{3,2},{4,5},{5,4},{6,7},{7,6},{8,9},{9,8},{10,11... | collective-permute-start | bytes 196616 | tf_op jit(solution)/shard_map/ppermute | solution.py:508
  48.0 8.4 %collective-permute-start.21 = (f32[4,64,256]{2,1,0:T(8,128)S(1)}, f32[4,64,256]{2,1,0:T(8,128)S(1)}, u32[]{:S(2)}, u32[]{:S(2)}) collective-permute-start(f32[4,64,256]{2,1,0:T(8,128)S(1)} %shard_map.209.own.p_ref.wave_ref), channel_id=1, source_target_pairs={{0,1},{1,0},{2,3},{3,2},{4,5},{5,4},{6,7},{7,6},{8,9},{9,8},{10,11... | collective-permute-start | bytes 786440 | tf_op jit(solution)/shard_map/ppermute | solution.py:508
  48.9 4.4 %collective-permute-start.19 = (bf16[2,4,32,128]{3,2,1,0:T(8,128)(2,1)S(1)}, bf16[2,4,32,128]{3,2,1,0:T(8,128)(2,1)S(1)}, u32[]{:S(2)}, u32[]{:S(2)}) collective-permute-start(bf16[2,4,32,128]{3,2,1,0:T(8,128)(2,1)S(1)} %fusion), channel_id=1, source_target_pairs={{0,2},{2,0},{1,3},{3,1},{4,6},{6,4},{5,7},{7,5},{8,10},{10,8},{9,1... | collective-permute-start | bytes 196616 | tf_op jit(solution)/shard_map/ppermute | solution.py:511
  51.8 14.1 %collective-permute-start.24 = (bf16[2,4,32,128]{3,2,1,0:T(8,128)(2,1)S(1)}, bf16[2,4,32,128]{3,2,1,0:T(8,128)(2,1)S(1)}, u32[]{:S(2)}, u32[]{:S(2)}) collective-permute-start(bf16[2,4,32,128]{3,2,1,0:T(8,128)(2,1)S(1)} %convert_element_type.59), channel_id=1, source_target_pairs={{0,1},{1,0},{2,3},{3,2},{4,5},{5,4},{6,7},{7,6},{8,9},{9,8},{10,11... | collective-permute-start | bytes 196616 | tf_op jit(solution)/shard_map/ppermute | solution.py:508
  53.4 6.4 %collective-permute-start.20 = (bf16[2,4,32,128]{3,2,1,0:T(8,128)(2,1)S(1)}, bf16[2,4,32,128]{3,2,1,0:T(8,128)(2,1)S(1)}, u32[]{:S(2)}, u32[]{:S(2)}) collective-permute-start(bf16[2,4,32,128]{3,2,1,0:T(8,128)(2,1)S(1)} %fusion.2), channel_id=1, source_target_pairs={{0,4},{4,0},{8,12},{12,8},{1,5},{5,1},{9,13},{13,9},{2,6},{6,2},{1... | collective-permute-start | bytes 196616 | tf_op jit(solution)/shard_map/ppermute | solution.py:511
  59.8 5.9 %collective-permute-start.22 = (bf16[2,4,32,128]{3,2,1,0:T(8,128)(2,1)S(1)}, bf16[2,4,32,128]{3,2,1,0:T(8,128)(2,1)S(1)}, u32[]{:S(2)}, u32[]{:S(2)}) collective-permute-start(bf16[2,4,32,128]{3,2,1,0:T(8,128)(2,1)S(1)} %fusion.1), channel_id=1, source_target_pairs={{0,8},{4,12},{8,0},{12,4},{1,9},{5,13},{9,1},{13,5},{2,10},{6,14},... | collective-permute-start | bytes 196616 | tf_op jit(solution)/shard_map/ppermute | solution.py:511
  65.8 1.3 %collective-permute-start.23 = (bf16[2,4,32,128]{3,2,1,0:T(8,128)(2,1)S(1)}, bf16[2,4,32,128]{3,2,1,0:T(8,128)(2,1)S(1)}, u32[]{:S(2)}, u32[]{:S(2)}) collective-permute-start(bf16[2,4,32,128]{3,2,1,0:T(8,128)(2,1)S(1)} %get-tuple-element.88), channel_id=1, source_target_pairs={{0,1},{1,0},{2,3},{3,2},{4,5},{5,4},{6,7},{7,6},{8,9},{9,8},{10,11... | collective-permute-start | bytes 196616 | tf_op jit(solution)/shard_map/ppermute | solution.py:508
  (14 other events, 158.5 us)

commit v5 on v4

--- a/solution.py
+++ b/solution.py
@@ -207,7 +207,18 @@
     return at_mode
 
 
-def materials_body(twiddle_x, stiffness, density, cells, table_z, table_y, keep, lines, grid):
+def materials_body(*refs):
+    sources, cells, keep, lines, grid = refs[:5], refs[5], refs[6], refs[7], refs[8]
+    targets, semaphores = refs[9:14], refs[14]
+    copies = [
+        pltpu.make_async_copy(source, target, semaphores.at[index])
+        for index, (source, target) in enumerate(zip(sources, targets))
+    ]
+    for copy in copies:
+        copy.start()
+    for copy in copies:
+        copy.wait()
+    twiddle_x, stiffness, density, table_z, table_y = targets
     half_x = keep.shape[1]
     entries = stiffness.shape[0]
     rows = cells.shape[0]
@@ -244,7 +255,7 @@
         keep[mode] = summed(core * half_x + mode)
 
 
-def wave_body(twiddle_x, own, prior, table_z, table_y, keep, send, lines, grid):
+def wave_body(twiddle_x, own, prior, early, table_z, table_y, keep, send, lines, grid):
     half_x = keep.shape[1]
     rows = own.shape[0]
     first = (lax.axis_index("gx") * 2 + slot()) * rows
@@ -253,7 +264,7 @@
     core = lax.axis_index("gz")
     summed = at_mode(0, 2 * half_x)
     keep[1] = prior[...]
-    send[1] = jnp.zeros_like(send[1])
+    keep[2:4] = early[...]
 
     @pl.loop(0, half_x)
     def _(mode):
@@ -329,7 +340,7 @@
 
 
 def output_body(
-    mine, other, mine_early, other_early, local_low, local_high, left, table_y, table_z, wave_ref, wave_other,
+    mine, other, local_low, local_high, left, table_y, table_z, wave_ref, wave_other,
     features, wave_out, modes, right, sums,
 ):
     step = pl.program_id(0)
@@ -345,12 +356,11 @@
         chunk = 4
         left_y = table_y[column]
         for field in range(FIELDS):
-            own, far = ((mine, other), (mine_early, other_early))[field // 2]
             for start in range(0, modes_x, chunk):
                 parts = [[], []]
                 for mode in range(start, start + chunk):
-                    at = (field % 2, mode % half_x)
-                    value = jnp.where(core == mode // half_x, own[at], far[at].astype(F32))
+                    at = (field, mode % half_x)
+                    value = jnp.where(core == mode // half_x, mine[at], other[at].astype(F32))
                     parts[0].append(value.astype(BF16))
                     parts[1].append(turned(value, half, -1.0).astype(BF16))
                 stacked = jnp.concatenate([jnp.concatenate(part, axis=1) for part in parts], axis=0)
@@ -494,12 +504,12 @@
         lift_bias.reshape(1, channels), local_weight, spread, place, owner, turn, wide,
     )
 
-    part = [shape(2, modes_x // 2, modes_y, width, dtype=dtype) for dtype in (F32, BF16)]
-
-    def spectrum(body, outs, inputs, lines, extra=0):
+    part = lambda fields, dtype: shape(fields, modes_x // 2, modes_y, width, dtype=dtype)
+
+    def spectrum(body, outs, inputs, lines, specs=None, scratch=()):
         return call(
-            body, outs, [SMEM] * (1 + extra) + [VMEM] * (inputs + 2),
-            [pltpu.VMEM((4 * brick_y, lines * width), BF16), pltpu.VMEM((modes_y, lines * width), F32)],
+            body, outs, specs or [SMEM] + [VMEM] * (inputs + 2),
+            [pltpu.VMEM((4 * brick_y, lines * width), BF16), pltpu.VMEM((modes_y, lines * width), F32), *scratch],
             flops=cells_count * 256 * lines, moved=cells_count * 2 * lines,
         )
 
@@ -510,14 +520,12 @@
     def exchange(value, axis, count, distance):
         return lax.ppermute(value.astype(BF16), axis, xor_pairs(count, distance))
 
-    early = spectrum(materials_body, part[0], 1, 2 * brick_x, 2)(
-        twiddle_x, stiffness, density, cells, forward_z, forward_y
-    )
-    moves = list(stages)
-    pending = early_other = None
-
-    def settle(value):
-        return value if pending is None else value + pending.astype(F32)
+    tables = (twiddle_x, stiffness, density, forward_z, forward_y)
+    early = spectrum(
+        materials_body, part(2, F32), 1, 2 * brick_x, [HBM] * 5 + [VMEM],
+        [(pltpu.SMEM if table.ndim == 1 else pltpu.VMEM)(table.shape, table.dtype) for table in tables]
+        + [pltpu.SemaphoreType.DMA((5,))],
+    )(*here(*[jnp.asarray(table) for table in tables]), cells)
 
     for repeat in range(STEPS):
         last = repeat == STEPS - 1
@@ -526,12 +534,12 @@
         halos = [lax.ppermute(edge_values[0], "gy", xor_pairs(column_count, 1))]
         if two_sided:
             halos.append(lax.ppermute(edge_values[1], "gy", odd_pairs(column_count)))
-        early, pending = settle(early), None
-        halos[0], early = lax.optimization_barrier((halos[0], early))
-        if moves:
-            pending = exchange(early, *moves.pop(0))
-        elif early_other is None:
-            early_other = swap(early.astype(BF16))
+        if repeat == 0:
+            far, early = lax.optimization_barrier((far, early))
+        if repeat == 1:
+            far, mixing, pointwise, lift_table, offset = lax.optimization_barrier(
+                (far, mixing, pointwise, lift_table, offset)
+            )
         if last:
             prior = spectrum(prior_body, shape(modes_x // 2, modes_y, width), 2, brick_x)(
                 twiddle_x, current, mate, forward_z, forward_y
@@ -548,15 +556,11 @@
             sent, *edge_values = others
         current, before = new, current
 
-    total, sent = spectrum(wave_body, part, 2, rows)(twiddle_x, current, prior, forward_z, forward_y)
-    total = total + swap(sent).astype(F32)
+    total, sent = spectrum(wave_body, [part(FIELDS, F32), part(1, BF16)], 3, rows)(
+        twiddle_x, current, prior, early, forward_z, forward_y
+    )
+    total = total + jnp.pad(swap(sent).astype(F32), ((0, FIELDS - 1), (0, 0), (0, 0), (0, 0)))
     wave_other = swap(current)
-    while moves or pending is not None:
-        early, pending = settle(early), None
-        if moves:
-            pending = exchange(early, *moves.pop(0))
-    if early_other is None:
-        early_other = swap(early.astype(BF16))
     group = 8
     steps = brick_y // group
     whole = lambda array: pl.BlockSpec(array.shape, lambda i: (0,) * len(array.shape))
@@ -576,10 +580,6 @@
 
     for index, stage in enumerate(stages):
         arrived = exchange(total, *stage)
-        if index == 0:
-            arrived, mixing, pointwise, lift_table, offset = lax.optimization_barrier(
-                (arrived, mixing, pointwise, lift_table, offset)
-            )
         if index == len(stages) - 2:
             local_low = pointwise_part(0)
             arrived, local_low = lax.optimization_barrier((arrived, local_low))
@@ -593,8 +593,8 @@
         output_body,
         grid=(steps,),
         out_shape=[shape(rows, channels, brick_y, total_z, dtype=BF16), shape(*pressure.shape)],
-        in_specs=[whole(part[0]), whole(part[1])] * 2
-        + [pl.BlockSpec((height, group, total_z), lambda i: (0, jnp.minimum(i, steps // 2 - 1), 0)),
+        in_specs=[whole(part(FIELDS, F32)), whole(part(FIELDS, BF16)),
+           pl.BlockSpec((height, group, total_z), lambda i: (0, jnp.minimum(i, steps // 2 - 1), 0)),
            pl.BlockSpec((height, group, total_z), lambda i: (0, jnp.maximum(i - steps // 2, 0), 0)),
            whole(mixing), whole(inverse_y), whole(inverse_z),
                   whole(field), whole(field)],
@@ -606,7 +606,7 @@
         ],
         compiler_params=pltpu.CompilerParams(vmem_limit_bytes=scoped),
         cost_estimate=pl.CostEstimate(flops=cells_count * 2000, bytes_accessed=cells_count * 60, transcendentals=cells_count * 20),
-    )(total, other, early, early_other, local_low, local_high, mixing, inverse_y, inverse_z, current, wave_other)
+    )(total, other, local_low, local_high, mixing, inverse_y, inverse_z, current, wave_other)
     features = features.transpose(0, 2, 1, 3)
     return (wave, features)
 

time: 75.7 us -> 71.8 us (0.948)
  starting transfers between devices: 33.9 us -> 26.1 us
  waiting for transfers between devices: 9.66 us -> 17.1 us
  local copies, waits for them, and re-layouts: 3.74 us -> 0.15 us
    ppermute x6 -> x3, starting transfers between devices: 11.2 us -> 5.32 us  [exchange(): return lax.ppermute(value.astype(BF16), axis, xor_pairs(count, distance))]
    ppermute x4, waiting for transfers between devices: 0.63 us -> 5.66 us  [per_device(): halos = [lax.ppermute(edge_values[0], 'gy', xor_pairs(column_count, 1))]]
    unnamed x42 -> x32, local copies, waits for them, and re-layouts: 3.69 us -> 0.1 us
    ppermute x4, starting transfers between devices: 7.73 us -> 4.62 us  [per_device(): halos = [lax.ppermute(edge_values[0], 'gy', xor_pairs(column_count, 1))]]
    ppermute x6 -> x3, waiting for transfers between devices: 5.42 us -> 7.57 us  [exchange(): return lax.ppermute(value.astype(BF16), axis, xor_pairs(count, distance))]
    ppermute x8 -> x7, starting transfers between devices: 11.1 us -> 12.3 us  [per_device(): swap = lambda value: lax.ppermute(value, 'gz', swap_core)]
    ppermute x8 -> x7, waiting for transfers between devices: 1.99 us -> 2.21 us  [per_device(): swap = lambda value: lax.ppermute(value, 'gz', swap_core)]
  transfers between devices with their start and end apart: 25 -> 21, of which waited for: 9 -> 10; matrix products, arithmetic and copies ran while one was open for 0% -> 0% of each run, Pallas kernels for 20% -> 17%
where the time goes in v5:
time: 71.8 us; the launch traced here: 71.6 us
  Pallas kernels  27.1 us (38%)
  starting transfers between devices  26.1 us (36%)
  waiting for transfers between devices  17.1 us (24%)
  between operations  1.07 us (1%)
    ppermute x7, starting transfers between devices, per_device(): swap = lambda value: lax.ppermute(value, 'gz', swap_core)  12.3 us
    pallas_call x1, Pallas kernels, per_device(): pl.pallas_call(output_body, grid=(steps,), out_shape=[shape(rows, channel...  8.26 us
    ppermute x3, waiting for transfers between devices, exchange(): return lax.ppermute(value.astype(BF16), axis, xor_pairs(count, distance))  7.57 us
    pallas_call x2, Pallas kernels, pointwise_part(): pl.pallas_call(pointwise_body, grid=(steps // 2,), out_shape=shape(height...  6.59 us
    ppermute x4, waiting for transfers between devices, per_device(): halos = [lax.ppermute(edge_values[0], 'gy', xor_pairs(column_count, 1))]  5.66 us
    ppermute x3, starting transfers between devices, exchange(): return lax.ppermute(value.astype(BF16), axis, xor_pairs(count, distance))  5.32 us
    ppermute x4, starting transfers between devices, per_device(): halos = [lax.ppermute(edge_values[0], 'gy', xor_pairs(column_count, 1))]  4.62 us
    pallas_call x4, Pallas kernels, per_device(): call(body, outs, [VMEM] * (6 + len(halos)), [pltpu.VMEM((brick_y + 2 * ED...  3.72 us
  transfers between devices with their start and end apart: 21, of which 10 were waited for; matrix products, arithmetic and copies ran while one was open for 0% of the time, Pallas kernels for 17%

profile of v5, /device:TPU:0, one launch (start us, length us, event | category | flops | bytes accessed | tf_op | source)
XLA Modules:
  0.0 71.6 jit_solution(5683144862976793085)
XLA Ops:
  1.8 0.9 %collective-permute-done.refs_6_ = f32[8,64,128]{2,1,0:T(8,128)S(1)} collective-permute-done((f32[8,64,128]{2,1,0:T(8,128)}, f32[8,64,128]{2,1,0:T(8,128)S(1)}, u32[]{:S(2)}, u32[]{:S(2)}) %collective-permute-start) | collective-permute-done | bytes 262176 | tf_op jit(solution)/shard_map/ppermute | solution.py:487
  3.4 1.5 %shard_map.203 = (f32[4,64,256]{2,1,0:T(8,128)S(1)}, f32[4,64,256]{2,1,0:T(8,128)S(1)}, f32[4,64,256]{2,1,0:T(8,128)S(1)}, f32[4,64,256]{2,1,0:T(8,128)S(1)}, bf...) custom-call(f32[8]{0:T(128)} %stiffness.5, f32[8]{0:T(128)} %density.5, ...), custom_call_target="tpu_custom_call" | custom-call | bytes 2359296 | tf_op jit(solution)/shard_map/pallas_call | solution.py:490
  5.3 0.7 collective-permute-start.4
  6.0 2.7 %collective-permute-start.5 = (f32[4,8,256]{2,1,0:T(8,128)S(1)}, f32[4,8,256]{2,1,0:T(8,128)S(1)}, u32[]{:S(2)}, u32[]{:S(2)}) collective-permute-start(f32[4,8,256]{2,1,0:T(8,128)S(1)} %get-tuple-element.46), channel_id=1, source_target_pairs={{0,2},{2,0},{1,3},{3,1},{4,6},{6,4},{5,7},{7,5},{8,10},{10,8},{9,1... | collective-permute-start | bytes 98312 | tf_op jit(solution)/shard_map/ppermute | solution.py:534
  8.7 2.3 %shard_map.204.early = f32[2,4,32,128]{3,2,1,0:T(8,128)S(1)} custom-call(f32[512]{0:T(512)} %constant.29.clone.refs_0_.twiddle_x, f32[8]{0:T(128)} %stiffness.5, f32[8]{0:T(128)} %density.5, bf16[256,128]{1,0:T(8,128)(2,1)} %constant.30.clone.refs_3_.table_z, bf16[2,32,256]{2,1,0:T(8,128)(2,1)} %constant.31.clone.refs_4_.table_y, ...), custom_call_target="tpu_custom_call" | custom-call | flops 268435456 | bytes 2097152 | tf_op jit(solution)/shard_map/pallas_call | solution.py:524
  11.1 0.9 %shard_map.205 = (f32[4,64,256]{2,1,0:T(8,128)S(1)}, bf16[4,64,256]{2,1,0:T(8,128)(2,1)S(1)}, f32[4,8,256]{2,1,0:T(8,128)S(1)}) custom-call(f32[4,64,256]{2,1,0:T(8,128)S(1)} %get-tuple-element.39.refs_0_.refs_1_, f32[4,64,256]{2,1,0:T(8,128)S(1)} %get-tuple-element.40.refs_1_, f32[4,64,256]{2,1,0:T(8,128)S(1)} %get-tuple-element.41.refs_2_, ...), custom_call_target="tpu_custom_call" | custom-call | flops 3932160 | bytes 1835008 | tf_op jit(solution)/shard_map/pallas_call | solution.py:551
  12.0 2.7 %collective-permute-start.6 = (f32[4,64,256]{2,1,0:T(8,128)S(1)}, f32[4,64,256]{2,1,0:T(8,128)S(1)}, u32[]{:S(2)}, u32[]{:S(2)}) collective-permute-start(f32[4,64,256]{2,1,0:T(8,128)S(1)} %get-tuple-element.47.refs_0_.refs_1_), channel_id=1, source_target_pairs={{0,1},{1,0},{2,3},{3,2},{4,5},{5,4},{6,7},{7,6},{8,9},{9,8},{10,11... | collective-permute-start | bytes 786440 | tf_op jit(solution)/shard_map/ppermute | solution.py:518
  14.7 0.7 %collective-permute-start.8 = (f32[4,8,256]{2,1,0:T(8,128)S(1)}, f32[4,8,256]{2,1,0:T(8,128)S(1)}, u32[]{:S(2)}, u32[]{:S(2)}) collective-permute-start(f32[4,8,256]{2,1,0:T(8,128)S(1)} %get-tuple-element.54), channel_id=1, source_target_pairs={{0,2},{2,0},{1,3},{3,1},{4,6},{6,4},{5,7},{7,5},{8,10},{10,8},{9,1... | collective-permute-start | bytes 98312 | tf_op jit(solution)/shard_map/ppermute | solution.py:534
  15.5 0.7 collective-permute-start.7
  16.2 2.2 %shard_map.206 = (bf16[80,64]{1,0:T(8,128)(2,1)S(1)}, bf16[80,128]{1,0:T(8,128)(2,1)S(1)}, f32[24,8]{1,0:T(8,128)S(1)}, f32[80,1]{1,0:T(8,128)S(1)}) custom-call(f32[8]{0:T(128)S(1)} %copy-done.5, f32[8]{0:T(128)S(1)} %copy-done.6, f32[2,160,20]{2,1,0:T(8,128)S(1)} %reshape.12.mode_ref, f32[4,20]{1,0:T(4,128)S(1)} %copy-done.8, f32[1,20]{1,0:T(1,128)S(1)} %bitcast.2, ...), custom_call_target="tpu_custom_call" | custom-call | flops 2000000000 | bytes 4000000 | tf_op jit(solution)/shard_map/pallas_call | solution.py:497
  18.7 0.9 %shard_map.207 = (f32[4,64,256]{2,1,0:T(8,128)S(1)}, bf16[4,64,256]{2,1,0:T(8,128)(2,1)S(1)}, f32[4,8,256]{2,1,0:T(8,128)S(1)}) custom-call(f32[4,64,256]{2,1,0:T(8,128)S(1)} %get-tuple-element.47.refs_0_.refs_1_, f32[4,64,256]{2,1,0:T(8,128)S(1)} %get-tuple-element.39.refs_0_.refs_1_, f32[4,64,256]{2,1,0:T(8,128)S(1)} %get-tuple-element.41.refs_2_, ...), custom_call_target="tpu_custom_call" | custom-call | flops 3932160 | bytes 1835008 | tf_op jit(solution)/shard_map/pallas_call | solution.py:551
  19.7 3.6 %collective-permute-start.9 = (f32[4,64,256]{2,1,0:T(8,128)S(1)}, f32[4,64,256]{2,1,0:T(8,128)S(1)}, u32[]{:S(2)}, u32[]{:S(2)}) collective-permute-start(f32[4,64,256]{2,1,0:T(8,128)S(1)} %get-tuple-element.55.refs_0_.refs_1_), channel_id=1, source_target_pairs={{0,1},{1,0},{2,3},{3,2},{4,5},{5,4},{6,7},{7,6},{8,9},{9,8},{10,11... | collective-permute-start | bytes 786440 | tf_op jit(solution)/shard_map/ppermute | solution.py:518
  23.3 0.7 collective-permute-start.10
  24.6 3.4 %collective-permute-done.11.refs_6_ = f32[4,8,256]{2,1,0:T(8,128)S(1)} collective-permute-done((f32[4,8,256]{2,1,0:T(8,128)S(1)}, f32[4,8,256]{2,1,0:T(8,128)S(1)}, u32[]{:S(2)}, u32[]{:S(2)}) %collective-permute-start.11) | collective-permute-done | bytes 32800 | tf_op jit(solution)/shard_map/ppermute | solution.py:534
  28.0 0.9 %shard_map.208 = (f32[4,64,256]{2,1,0:T(8,128)S(1)}, bf16[4,64,256]{2,1,0:T(8,128)(2,1)S(1)}, f32[4,8,256]{2,1,0:T(8,128)S(1)}) custom-call(f32[4,64,256]{2,1,0:T(8,128)S(1)} %get-tuple-element.55.refs_0_.refs_1_, f32[4,64,256]{2,1,0:T(8,128)S(1)} %get-tuple-element.47.refs_0_.refs_1_, f32[4,64,256]{2,1,0:T(8,128)S(1)} %get-tuple-element.41.refs_2_, ...), custom_call_target="tpu_custom_call" | custom-call | flops 3932160 | bytes 1835008 | tf_op jit(solution)/shard_map/pallas_call | solution.py:551
  28.9 3.1 %collective-permute-start.12 = (f32[4,64,256]{2,1,0:T(8,128)S(1)}, f32[4,64,256]{2,1,0:T(8,128)S(1)}, u32[]{:S(2)}, u32[]{:S(2)}) collective-permute-start(f32[4,64,256]{2,1,0:T(8,128)S(1)} %get-tuple-element.58.own.refs_0_.q_ref), channel_id=1, source_target_pairs={{0,1},{1,0},{2,3},{3,2},{4,5},{5,4},{6,7},{7,6},{8,9},{9,8},{10,11... | collective-permute-start | bytes 786440 | tf_op jit(solution)/shard_map/ppermute | solution.py:518
  32.0 0.8 %collective-permute-start.13 = (bf16[4,64,256]{2,1,0:T(8,128)(2,1)S(1)}, bf16[4,64,256]{2,1,0:T(8,128)(2,1)S(1)}, u32[]{:S(2)}, u32[]{:S(2)}) collective-permute-start(bf16[4,64,256]{2,1,0:T(8,128)(2,1)S(1)} %get-tuple-element.59), channel_id=1, source_target_pairs={{1,5},{4,8},{9,13},{5,1},{8,4},{13,9},{3,7},{6,10},{11,15},{7,3},{... | collective-permute-start | bytes 393224 | tf_op jit(solution)/shard_map/ppermute | solution.py:532
  33.4 1.3 %shard_map.209.prior = f32[4,32,128]{2,1,0:T(8,128)S(1)} custom-call(f32[512]{0:T(512)S(1)} %copy-done.4, f32[4,64,256]{2,1,0:T(8,128)S(1)} %get-tuple-element.58.own.refs_0_.q_ref, f32[4,64,256]{2,1,0:T(8,128)S(1)} %collective-permute-done.12.mate.refs_4_.q_mate, bf16[256,128]{1,0:T(8,128)(2,1)S(1)} %copy-done, bf16[2,32,256]{2,1,0:T(8,128)(2,1)S(1)} %copy-done.2), custom_call_target="tpu_custom_call" | custom-call | flops 134217728 | bytes 1048576 | tf_op jit(solution)/shard_map/pallas_call | solution.py:544
  34.8 2.0 %collective-permute-done.14.refs_6_ = f32[4,8,256]{2,1,0:T(8,128)S(1)} collective-permute-done((f32[4,8,256]{2,1,0:T(8,128)S(1)}, f32[4,8,256]{2,1,0:T(8,128)S(1)}, u32[]{:S(2)}, u32[]{:S(2)}) %collective-permute-start.14) | collective-permute-done | bytes 32800 | tf_op jit(solution)/shard_map/ppermute | solution.py:534
  36.8 0.9 %shard_map.210.own.p_ref.wave_ref = f32[4,64,256]{2,1,0:T(8,128)S(1)} custom-call(f32[4,64,256]{2,1,0:T(8,128)S(1)} %get-tuple-element.58.own.refs_0_.q_ref, f32[4,64,256]{2,1,0:T(8,128)S(1)} %get-tuple-element.55.refs_0_.refs_1_, f32[4,64,256]{2,1,0:T(8,128)S(1)} %get-tuple-element.41.refs_2_, f32[4,64,256]{2,1,0:T(8,128)S(1)} %get-tuple-element.42.refs_3_, ...), custom_call_target="tpu_custom_call" | custom-call | flops 3932160 | bytes 1835008 | tf_op jit(solution)/shard_map/pallas_call | solution.py:551
  37.7 1.2 %shard_map.211 = (f32[4,4,32,128]{3,2,1,0:T(8,128)S(1)}, bf16[1,4,32,128]{3,2,1,0:T(8,128)(2,1)S(1)}) custom-call(f32[512]{0:T(512)S(1)} %copy-done.4, f32[4,64,256]{2,1,0:T(8,128)S(1)} %shard_map.210.own.p_ref.wave_ref, f32[4,32,128]{2,1,0:T(8,128)S(1)} %shard_map.209.prior, f32[2,4,32,128]{3,2,1,0:T(8,128)S(1)} %shard_map.204.early, ...), custom_call_target="tpu_custom_call" | custom-call | flops 67108864 | bytes 524288 | tf_op jit(solution)/shard_map/pallas_call | solution.py:559
  38.9 2.3 %collective-permute-start.15 = (bf16[1,4,32,128]{3,2,1,0:T(8,128)(2,1)S(1)}, bf16[1,4,32,128]{3,2,1,0:T(8,128)(2,1)S(1)}, u32[]{:S(2)}, u32[]{:S(2)}) collective-permute-start(bf16[1,4,32,128]{3,2,1,0:T(8,128)(2,1)S(1)} %get-tuple-element.65), channel_id=1, source_target_pairs={{0,1},{1,0},{2,3},{3,2},{4,5},{5,4},{6,7},{7,6},{8,9},{9,8},{10,11... | collective-permute-start | bytes 98312 | tf_op jit(solution)/shard_map/ppermute | solution.py:518
  41.2 0.9 %collective-permute-done.15 = bf16[1,4,32,128]{3,2,1,0:T(8,128)(2,1)S(1)} collective-permute-done((bf16[1,4,32,128]{3,2,1,0:T(8,128)(2,1)S(1)}, bf16[1,4,32,128]{3,2,1,0:T(8,128)(2,1)S(1)}, u32[]{:S(2)}, u32[]{:S(2)}) %collective-permute-start.15) | collective-permute-done | bytes 32800 | tf_op jit(solution)/shard_map/ppermute | solution.py:518
  42.1 1.0 %collective-permute-start.16 = (bf16[4,4,32,128]{3,2,1,0:T(8,128)(2,1)S(1)}, bf16[4,4,32,128]{3,2,1,0:T(8,128)(2,1)S(1)}, u32[]{:S(2)}, u32[]{:S(2)}) collective-permute-start(bf16[4,4,32,128]{3,2,1,0:T(8,128)(2,1)S(1)} %fusion), channel_id=1, source_target_pairs={{0,2},{2,0},{1,3},{3,1},{4,6},{6,4},{5,7},{7,5},{8,10},{10,8},{9,1... | collective-permute-start | bytes 393224 | tf_op jit(solution)/shard_map/ppermute | solution.py:521
  43.1 4.8 %collective-permute-done.16 = bf16[4,4,32,128]{3,2,1,0:T(8,128)(2,1)S(1)} collective-permute-done((bf16[4,4,32,128]{3,2,1,0:T(8,128)(2,1)S(1)}, bf16[4,4,32,128]{3,2,1,0:T(8,128)(2,1)S(1)}, u32[]{:S(2)}, u32[]{:S(2)}) %collective-permute-start.16) | collective-permute-done | bytes 131104 | tf_op jit(solution)/shard_map/ppermute | solution.py:521
  48.0 2.2 %collective-permute-start.17 = (bf16[4,4,32,128]{3,2,1,0:T(8,128)(2,1)S(1)}, bf16[4,4,32,128]{3,2,1,0:T(8,128)(2,1)S(1)}, u32[]{:S(2)}, u32[]{:S(2)}) collective-permute-start(bf16[4,4,32,128]{3,2,1,0:T(8,128)(2,1)S(1)} %fusion.2), channel_id=1, source_target_pairs={{0,4},{4,0},{8,12},{12,8},{1,5},{5,1},{9,13},{13,9},{2,6},{6,2},{1... | collective-permute-start | bytes 393224 | tf_op jit(solution)/shard_map/ppermute | solution.py:521
  50.2 3.3 %shard_map.212.local_low = f32[80,32,256]{2,1,0:T(8,128)S(1)} custom-call(f32[8]{0:T(128)S(1)} %copy-done.5, f32[8]{0:T(128)S(1)} %copy-done.6, f32[4,64,256]{2,1,0:T(8,128)S(1)} %shard_map.210.own.p_ref.wave_ref, f32[4,64,256]{2,1,0:T(8,128)S(1)} %get-tuple-element.58.own.refs_0_.q_ref, f32[4,64,256]{2,1,0:T(8,128)S(1)} %collective-permute-done.18.p_mate.wave_other, ...), custom_call_target="tpu_custom_call" | custom-call | flops 1310720000 | bytes 3276800 | tf_op jit(solution)/shard_map/pallas_call | solution.py:570
  53.6 2.1 %collective-permute-start.19 = (bf16[4,4,32,128]{3,2,1,0:T(8,128)(2,1)S(1)}, bf16[4,4,32,128]{3,2,1,0:T(8,128)(2,1)S(1)}, u32[]{:S(2)}, u32[]{:S(2)}) collective-permute-start(bf16[4,4,32,128]{3,2,1,0:T(8,128)(2,1)S(1)} %fusion.1), channel_id=1, source_target_pairs={{0,8},{4,12},{8,0},{12,4},{1,9},{5,13},{9,1},{13,5},{2,10},{6,14},... | collective-permute-start | bytes 393224 | tf_op jit(solution)/shard_map/ppermute | solution.py:521
  55.7 3.3 %shard_map.213.local_high = f32[80,32,256]{2,1,0:T(8,128)S(1)} custom-call(f32[8]{0:T(128)S(1)} %copy-done.5, f32[8]{0:T(128)S(1)} %copy-done.6, f32[4,64,256]{2,1,0:T(8,128)S(1)} %shard_map.210.own.p_ref.wave_ref, f32[4,64,256]{2,1,0:T(8,128)S(1)} %get-tuple-element.58.own.refs_0_.q_ref, f32[4,64,256]{2,1,0:T(8,128)S(1)} %collective-permute-done.18.p_mate.wave_other, ...), custom_call_target="tpu_custom_call" | custom-call | flops 1310720000 | bytes 3276800 | tf_op jit(solution)/shard_map/pallas_call | solution.py:570
  59.1 2.8 %collective-permute-done.19 = bf16[4,4,32,128]{3,2,1,0:T(8,128)(2,1)S(1)} collective-permute-done((bf16[4,4,32,128]{3,2,1,0:T(8,128)(2,1)S(1)}, bf16[4,4,32,128]{3,2,1,0:T(8,128)(2,1)S(1)}, u32[]{:S(2)}, u32[]{:S(2)}) %collective-permute-start.19) | collective-permute-done | bytes 131104 | tf_op jit(solution)/shard_map/ppermute | solution.py:521
  62.0 1.3 %collective-permute-done.20.other = bf16[4,4,32,128]{3,2,1,0:T(8,128)(2,1)S(1)} collective-permute-done((bf16[4,4,32,128]{3,2,1,0:T(8,128)(2,1)S(1)}, bf16[4,4,32,128]{3,2,1,0:T(8,128)(2,1)S(1)}, u32[]{:S(2)}, u32[]{:S(2)}) %collective-permute-start.20) | collective-permute-done | bytes 131104 | tf_op jit(solution)/shard_map/ppermute | solution.py:518
  63.3 8.3 %shard_map.214 = (bf16[4,20,64,256]{3,2,1,0:T(8,128)(2,1)}, f32[8,64,128]{2,1,0:T(8,128)}) custom-call(f32[4,4,32,128]{3,2,1,0:T(8,128)S(1)} %get-tuple-element.77.mine, bf16[4,4,32,128]{3,2,1,0:T(8,128)(2,1)S(1)} %collective-permute-done.20.other, f32[80,32,256]{2,1,0:T(8,128)S(1)} %shard_map.212.local_low, f32[80,32,256]{2,1,0:T(8,128)S(1)} %shard_map.213.local_high, ...), custom_call_target="tpu_custom_call" | custom-call | flops 131072000 | bytes 3932160 | tf_op jit(solution)/shard_map/pallas_call | solution.py:592
  (60 shorter events, 4.2 us)
Async XLA Ops:
  0.6 15.5 %copy-start.12 = (f32[124,128]{1,0:T(8,128)S(1)}, f32[124,128]{1,0:T(8,128)}, u32[]{:S(2)}) copy-start(f32[124,128]{1,0:T(8,128)} %constant.28.clone.wide_ref) | copy-start | bytes 190468
  0.6 15.5 %copy-start.10 = (f32[8,2,80,32]{3,2,1,0:T(8,128)S(1)}, f32[8,2,80,32]{3,2,1,0:T(8,128)}, u32[]{:S(2)}) copy-start(f32[8,2,80,32]{3,2,1,0:T(8,128)} %constant.27.clone.turn_ref) | copy-start | bytes 491524
  0.7 15.5 %copy-start.13 = (f32[80,20]{1,0:T(8,128)S(1)}, f32[80,20]{1,0:T(8,128)}, u32[]{:S(2)}) copy-start(f32[80,20]{1,0:T(8,128)} %constant.26.clone.owner_ref) | copy-start | bytes 19204
  0.7 15.5 %copy-start.14 = (f32[4,32]{1,0:T(4,128)S(1)}, f32[4,32]{1,0:T(4,128)}, u32[]{:S(2)}) copy-start(f32[4,32]{1,0:T(4,128)} %constant.25.clone.place_ref) | copy-start | bytes 1540
  0.7 15.5 %copy-start.11 = (f32[160,52]{1,0:T(8,128)S(1)}, f32[160,52]{1,0:T(8,128)}, u32[]{:S(2)}) copy-start(f32[160,52]{1,0:T(8,128)} %constant.24.clone.spread_ref) | copy-start | bytes 99844
  0.7 15.5 %copy-start.6 = (f32[8]{0:T(128)S(1)}, f32[8]{0:T(128)}, u32[]{:S(2)}) copy-start(f32[8]{0:T(128)} %density.5) | copy-start | bytes 100
  0.7 15.5 %copy-start.5 = (f32[8]{0:T(128)S(1)}, f32[8]{0:T(128)}, u32[]{:S(2)}) copy-start(f32[8]{0:T(128)} %stiffness.5) | copy-start | bytes 100
  0.7 15.5 %copy-start.7 = (bf16[20,20]{1,0:T(8,128)(2,1)S(1)}, bf16[20,20]{1,0:T(8,128)(2,1)}, u32[]{:S(2)}) copy-start(bf16[20,20]{1,0:T(8,128)(2,1)} %local_ref.1) | copy-start | bytes 2404
  0.7 15.5 %copy-start.9 = (f32[20]{0:T(128)S(1)}, f32[20]{0:T(128)}, u32[]{:S(2)}) copy-start(f32[20]{0:T(128)} %param.27) | copy-start | bytes 244
  0.7 15.5 %copy-start.8 = (f32[4,20]{1,0:T(4,128)S(1)}, f32[4,20]{1,0:T(4,128)}, u32[]{:S(2)}) copy-start(f32[4,20]{1,0:T(4,128)} %lift_ref.1) | copy-start | bytes 964
  0.8 1.9 %collective-permute-start = (f32[8,64,128]{2,1,0:T(8,128)}, f32[8,64,128]{2,1,0:T(8,128)S(1)}, u32[]{:S(2)}, u32[]{:S(2)}) collective-permute-start(f32[8,64,128]{2,1,0:T(8,128)} %refs_3_.2), channel_id=1, source_target_pairs={{0,1},{1,0},{2,3},{3,2},{4,5},{5,4},{6,7},{7,6},{8,9},{9,8},{10,11... | collective-permute-start | bytes 786440 | tf_op jit(solution)/shard_map/ppermute | solution.py:487
  1.3 1.7 %collective-permute-start.1 = (f32[8,64,128]{2,1,0:T(8,128)}, f32[8,64,128]{2,1,0:T(8,128)S(1)}, u32[]{:S(2)}, u32[]{:S(2)}) collective-permute-start(f32[8,64,128]{2,1,0:T(8,128)} %refs_4_.2), channel_id=1, source_target_pairs={{0,1},{1,0},{2,3},{3,2},{4,5},{5,4},{6,7},{7,6},{8,9},{9,8},{10,11... | collective-permute-start | bytes 786440 | tf_op jit(solution)/shard_map/ppermute | solution.py:487
  1.4 2.0 %collective-permute-start.2 = (s32[8,64,128]{2,1,0:T(8,128)}, s32[8,64,128]{2,1,0:T(8,128)S(1)}, u32[]{:S(2)}, u32[]{:S(2)}) collective-permute-start(s32[8,64,128]{2,1,0:T(8,128)} %refs_5_.1), channel_id=1, source_target_pairs={{0,1},{1,0},{2,3},{3,2},{4,5},{5,4},{6,7},{7,6},{8,9},{9,8},{10,11... | collective-permute-start | bytes 786440 | tf_op jit(solution)/shard_map/ppermute | solution.py:487
  4.9 6.2 %collective-permute-start.3 = (f32[4,64,256]{2,1,0:T(8,128)S(1)}, f32[4,64,256]{2,1,0:T(8,128)S(1)}, u32[]{:S(2)}, u32[]{:S(2)}) collective-permute-start(f32[4,64,256]{2,1,0:T(8,128)S(1)} %get-tuple-element.39.refs_0_.refs_1_), channel_id=1, source_target_pairs={{0,1},{1,0},{2,3},{3,2},{4,5},{5,4},{6,7},{7,6},{8,9},{9,8},{10,11... | collective-permute-start | bytes 786440 | tf_op jit(solution)/shard_map/ppermute | solution.py:518
  5.3 5.7 %collective-permute-start.4 = (bf16[4,64,256]{2,1,0:T(8,128)(2,1)S(1)}, bf16[4,64,256]{2,1,0:T(8,128)(2,1)S(1)}, u32[]{:S(2)}, u32[]{:S(2)}) collective-permute-start(bf16[4,64,256]{2,1,0:T(8,128)(2,1)S(1)} %get-tuple-element.43), channel_id=1, source_target_pairs={{1,5},{4,8},{9,13},{5,1},{8,4},{13,9},{3,7},{6,10},{11,15},{7,3},{... | collective-permute-start | bytes 393224 | tf_op jit(solution)/shard_map/ppermute | solution.py:532
  6.0 5.1 %collective-permute-start.5 = (f32[4,8,256]{2,1,0:T(8,128)S(1)}, f32[4,8,256]{2,1,0:T(8,128)S(1)}, u32[]{:S(2)}, u32[]{:S(2)}) collective-permute-start(f32[4,8,256]{2,1,0:T(8,128)S(1)} %get-tuple-element.46), channel_id=1, source_target_pairs={{0,2},{2,0},{1,3},{3,1},{4,6},{6,4},{5,7},{7,5},{8,10},{10,8},{9,1... | collective-permute-start | bytes 98312 | tf_op jit(solution)/shard_map/ppermute | solution.py:534
  12.0 6.7 %collective-permute-start.6 = (f32[4,64,256]{2,1,0:T(8,128)S(1)}, f32[4,64,256]{2,1,0:T(8,128)S(1)}, u32[]{:S(2)}, u32[]{:S(2)}) collective-permute-start(f32[4,64,256]{2,1,0:T(8,128)S(1)} %get-tuple-element.47.refs_0_.refs_1_), channel_id=1, source_target_pairs={{0,1},{1,0},{2,3},{3,2},{4,5},{5,4},{6,7},{7,6},{8,9},{9,8},{10,11... | collective-permute-start | bytes 786440 | tf_op jit(solution)/shard_map/ppermute | solution.py:518
  14.7 4.0 %collective-permute-start.8 = (f32[4,8,256]{2,1,0:T(8,128)S(1)}, f32[4,8,256]{2,1,0:T(8,128)S(1)}, u32[]{:S(2)}, u32[]{:S(2)}) collective-permute-start(f32[4,8,256]{2,1,0:T(8,128)S(1)} %get-tuple-element.54), channel_id=1, source_target_pairs={{0,2},{2,0},{1,3},{3,1},{4,6},{6,4},{5,7},{7,5},{8,10},{10,8},{9,1... | collective-permute-start | bytes 98312 | tf_op jit(solution)/shard_map/ppermute | solution.py:534
  15.5 3.0 %collective-permute-start.7 = (bf16[4,64,256]{2,1,0:T(8,128)(2,1)S(1)}, bf16[4,64,256]{2,1,0:T(8,128)(2,1)S(1)}, u32[]{:S(2)}, u32[]{:S(2)}) collective-permute-start(bf16[4,64,256]{2,1,0:T(8,128)(2,1)S(1)} %get-tuple-element.48), channel_id=1, source_target_pairs={{1,5},{4,8},{9,13},{5,1},{8,4},{13,9},{3,7},{6,10},{11,15},{7,3},{... | collective-permute-start | bytes 393224 | tf_op jit(solution)/shard_map/ppermute | solution.py:532
  18.4 15.0 %copy-start = (bf16[256,128]{1,0:T(8,128)(2,1)S(1)}, bf16[256,128]{1,0:T(8,128)(2,1)}, u32[]{:S(2)}) copy-start(bf16[256,128]{1,0:T(8,128)(2,1)} %constant.30.clone.refs_3_.table_z) | copy-start | bytes 196612
  19.7 8.3 %collective-permute-start.9 = (f32[4,64,256]{2,1,0:T(8,128)S(1)}, f32[4,64,256]{2,1,0:T(8,128)S(1)}, u32[]{:S(2)}, u32[]{:S(2)}) collective-permute-start(f32[4,64,256]{2,1,0:T(8,128)S(1)} %get-tuple-element.55.refs_0_.refs_1_), channel_id=1, source_target_pairs={{0,1},{1,0},{2,3},{3,2},{4,5},{5,4},{6,7},{7,6},{8,9},{9,8},{10,11... | collective-permute-start | bytes 786440 | tf_op jit(solution)/shard_map/ppermute | solution.py:518
  23.3 4.6 %collective-permute-start.10 = (bf16[4,64,256]{2,1,0:T(8,128)(2,1)S(1)}, bf16[4,64,256]{2,1,0:T(8,128)(2,1)S(1)}, u32[]{:S(2)}, u32[]{:S(2)}) collective-permute-start(bf16[4,64,256]{2,1,0:T(8,128)(2,1)S(1)} %get-tuple-element.56), channel_id=1, source_target_pairs={{1,5},{4,8},{9,13},{5,1},{8,4},{13,9},{3,7},{6,10},{11,15},{7,3},{... | collective-permute-start | bytes 393224 | tf_op jit(solution)/shard_map/ppermute | solution.py:532
  24.0 4.0 %collective-permute-start.11 = (f32[4,8,256]{2,1,0:T(8,128)S(1)}, f32[4,8,256]{2,1,0:T(8,128)S(1)}, u32[]{:S(2)}, u32[]{:S(2)}) collective-permute-start(f32[4,8,256]{2,1,0:T(8,128)S(1)} %get-tuple-element.57), channel_id=1, source_target_pairs={{0,2},{2,0},{1,3},{3,1},{4,6},{6,4},{5,7},{7,5},{8,10},{10,8},{9,1... | collective-permute-start | bytes 98312 | tf_op jit(solution)/shard_map/ppermute | solution.py:534
  28.9 4.5 %collective-permute-start.12 = (f32[4,64,256]{2,1,0:T(8,128)S(1)}, f32[4,64,256]{2,1,0:T(8,128)S(1)}, u32[]{:S(2)}, u32[]{:S(2)}) collective-permute-start(f32[4,64,256]{2,1,0:T(8,128)S(1)} %get-tuple-element.58.own.refs_0_.q_ref), channel_id=1, source_target_pairs={{0,1},{1,0},{2,3},{3,2},{4,5},{5,4},{6,7},{7,6},{8,9},{9,8},{10,11... | collective-permute-start | bytes 786440 | tf_op jit(solution)/shard_map/ppermute | solution.py:518
  32.0 2.8 %collective-permute-start.13 = (bf16[4,64,256]{2,1,0:T(8,128)(2,1)S(1)}, bf16[4,64,256]{2,1,0:T(8,128)(2,1)S(1)}, u32[]{:S(2)}, u32[]{:S(2)}) collective-permute-start(bf16[4,64,256]{2,1,0:T(8,128)(2,1)S(1)} %get-tuple-element.59), channel_id=1, source_target_pairs={{1,5},{4,8},{9,13},{5,1},{8,4},{13,9},{3,7},{6,10},{11,15},{7,3},{... | collective-permute-start | bytes 393224 | tf_op jit(solution)/shard_map/ppermute | solution.py:532
  32.8 4.0 %collective-permute-start.14 = (f32[4,8,256]{2,1,0:T(8,128)S(1)}, f32[4,8,256]{2,1,0:T(8,128)S(1)}, u32[]{:S(2)}, u32[]{:S(2)}) collective-permute-start(f32[4,8,256]{2,1,0:T(8,128)S(1)} %get-tuple-element.61), channel_id=1, source_target_pairs={{0,2},{2,0},{1,3},{3,1},{4,6},{6,4},{5,7},{7,5},{8,10},{10,8},{9,1... | collective-permute-start | bytes 98312 | tf_op jit(solution)/shard_map/ppermute | solution.py:534
  38.9 3.2 %collective-permute-start.15 = (bf16[1,4,32,128]{3,2,1,0:T(8,128)(2,1)S(1)}, bf16[1,4,32,128]{3,2,1,0:T(8,128)(2,1)S(1)}, u32[]{:S(2)}, u32[]{:S(2)}) collective-permute-start(bf16[1,4,32,128]{3,2,1,0:T(8,128)(2,1)S(1)} %get-tuple-element.65), channel_id=1, source_target_pairs={{0,1},{1,0},{2,3},{3,2},{4,5},{5,4},{6,7},{7,6},{8,9},{9,8},{10,11... | collective-permute-start | bytes 98312 | tf_op jit(solution)/shard_map/ppermute | solution.py:518
  42.1 5.8 %collective-permute-start.16 = (bf16[4,4,32,128]{3,2,1,0:T(8,128)(2,1)S(1)}, bf16[4,4,32,128]{3,2,1,0:T(8,128)(2,1)S(1)}, u32[]{:S(2)}, u32[]{:S(2)}) collective-permute-start(bf16[4,4,32,128]{3,2,1,0:T(8,128)(2,1)S(1)} %fusion), channel_id=1, source_target_pairs={{0,2},{2,0},{1,3},{3,1},{4,6},{6,4},{5,7},{7,5},{8,10},{10,8},{9,1... | collective-permute-start | bytes 393224 | tf_op jit(solution)/shard_map/ppermute | solution.py:521
  43.1 7.1 %collective-permute-start.18 = (f32[4,64,256]{2,1,0:T(8,128)S(1)}, f32[4,64,256]{2,1,0:T(8,128)S(1)}, u32[]{:S(2)}, u32[]{:S(2)}) collective-permute-start(f32[4,64,256]{2,1,0:T(8,128)S(1)} %shard_map.210.own.p_ref.wave_ref), channel_id=1, source_target_pairs={{0,1},{1,0},{2,3},{3,2},{4,5},{5,4},{6,7},{7,6},{8,9},{9,8},{10,11... | collective-permute-start | bytes 786440 | tf_op jit(solution)/shard_map/ppermute | solution.py:518
  48.0 5.5 %collective-permute-start.17 = (bf16[4,4,32,128]{3,2,1,0:T(8,128)(2,1)S(1)}, bf16[4,4,32,128]{3,2,1,0:T(8,128)(2,1)S(1)}, u32[]{:S(2)}, u32[]{:S(2)}) collective-permute-start(bf16[4,4,32,128]{3,2,1,0:T(8,128)(2,1)S(1)} %fusion.2), channel_id=1, source_target_pairs={{0,4},{4,0},{8,12},{12,8},{1,5},{5,1},{9,13},{13,9},{2,6},{6,2},{1... | collective-permute-start | bytes 393224 | tf_op jit(solution)/shard_map/ppermute | solution.py:521
  53.6 8.2 %collective-permute-start.19 = (bf16[4,4,32,128]{3,2,1,0:T(8,128)(2,1)S(1)}, bf16[4,4,32,128]{3,2,1,0:T(8,128)(2,1)S(1)}, u32[]{:S(2)}, u32[]{:S(2)}) collective-permute-start(bf16[4,4,32,128]{3,2,1,0:T(8,128)(2,1)S(1)} %fusion.1), channel_id=1, source_target_pairs={{0,8},{4,12},{8,0},{12,4},{1,9},{5,13},{9,1},{13,5},{2,10},{6,14},... | collective-permute-start | bytes 393224 | tf_op jit(solution)/shard_map/ppermute | solution.py:521
  61.9 1.4 %collective-permute-start.20 = (bf16[4,4,32,128]{3,2,1,0:T(8,128)(2,1)S(1)}, bf16[4,4,32,128]{3,2,1,0:T(8,128)(2,1)S(1)}, u32[]{:S(2)}, u32[]{:S(2)}) collective-permute-start(bf16[4,4,32,128]{3,2,1,0:T(8,128)(2,1)S(1)} %get-tuple-element.76), channel_id=1, source_target_pairs={{0,1},{1,0},{2,3},{3,2},{4,5},{5,4},{6,7},{7,6},{8,9},{9,8},{10,11... | collective-permute-start | bytes 393224 | tf_op jit(solution)/shard_map/ppermute | solution.py:518
  (5 other events, 63.5 us)

commit v6 on v5

--- a/solution.py
+++ b/solution.py
@@ -12,7 +12,8 @@
 STEPS = 4
 FIELDS = 4
 REACH = 4
-EDGE = 8
+PAD = 8
+EDGE = STEPS * REACH
 stencil_taps = (-205.0 / 72.0, 8.0 / 5.0, -1.0 / 5.0, 8.0 / 315.0, -1.0 / 560.0)
 F32 = jnp.float32
 BF16 = jnp.bfloat16
@@ -75,23 +76,46 @@
     return total * (1.0 / table.shape[0])
 
 
-def edges(value_of, outs, row_parity, brick_y):
-    for position, out in enumerate(outs):
-        upper = row_parity == position
-        out[...] = jnp.where(upper, value_of(brick_y - EDGE, brick_y), value_of(0, EDGE))
-
-
 def slot():
     return (lax.axis_index("gz") + lax.axis_index("gx")) % 2
 
 
-def assemble_body(count, *refs):
-    tables_in, own_in, got = refs[:3], refs[3:6], refs[6:9]
-    p_out, q_out, ratio, bend, sent, cells = refs[9:15]
-    edge_outs = refs[15 : 15 + count]
-    tables, own, semaphores = refs[15 + count : 18 + count], refs[18 + count : 21 + count], refs[21 + count]
+def own_start(sides):
+    return EDGE if sides == 2 else pl.multiple_of(EDGE * (lax.axis_index("gy") % 2), EDGE)
+
+
+def pack_body(sides, *refs):
+    own_in, sends, buffer, kinds, semaphores = refs[:3], refs[3 : 3 + 2 * sides], refs[-3], refs[-2], refs[-1]
+    rows, brick_y = sends[0].shape[1], own_in[0].shape[1]
+    parity = lax.axis_index("gy") % 2
+    copies = []
+    for position in range(sides):
+        edge = pl.multiple_of(jnp.where(parity == position, brick_y - EDGE, 0), EDGE)
+        for index in range(2):
+            block = slot() if index == 0 else 1 - slot()
+            for array, source in enumerate(own_in):
+                at = (position * 2 + index) * 3 + array
+                target = kinds.at[position * 2 + index] if array == 2 else buffer.at[(position * 2 + index) * 2 + array]
+                copies.append(pltpu.make_async_copy(
+                    source.at[pl.ds(block * rows, rows), pl.ds(edge, EDGE)], target, semaphores.at[at]
+                ))
+    for copy in copies:
+        copy.start()
+    for copy in copies:
+        copy.wait()
+    for index, send in enumerate(sends):
+        send[0:2] = buffer[2 * index : 2 * index + 2].astype(BF16)
+        send[2] = kinds[index].astype(F32).astype(BF16)
+
+
+def assemble_body(sides, last_column, *refs):
+    tables_in, own_in, got, borders = refs[:3], refs[3:6], refs[6:9], refs[9 : 9 + 2 * sides]
+    refs = refs[9 + 2 * sides :]
+    p_out, q_out, ratio, bend, sent, cells = refs[:6]
+    tables, own, semaphores = refs[6:9], refs[9:12], refs[12]
     core, column = lax.axis_index("gz"), lax.axis_index("gy")
-    rows, brick_y = p_out.shape[:2]
+    rows = p_out.shape[0]
+    brick_y = cells.shape[1]
     start = slot() * rows
     sources = [source.at[pl.ds(start, rows)] for source in own_in[:2]] + [own_in[2]]
     copies = [
@@ -110,31 +134,37 @@
             [jnp.where(core == 0, mine, other), jnp.where(core == 0, other, mine)], axis=-1
         )
 
+    def place(row, at, length, current, before, cell, inside):
+        lines = pl.ds(at, length)
+        p_out[row, lines, :] = current
+        sent[row, lines, :] = current.astype(BF16)
+        q_out[row, lines, :] = before
+        ratio[row, lines, :] = inside * looked_up(cell, lambda e: stiffness[e] / density[e], entries)
+        bend[row, lines, :] = inside * looked_up(cell, lambda e: nonlinear[e], entries)
+
     for row in range(cells.shape[0]):
         cells[row] = whole(own[2][row], got[2][row])
+    first = own_start(sides)
     for row in range(rows):
-        value = whole(own[0][row], got[0][start + row])
-        p_out[row] = value
-        sent[row] = value.astype(BF16)
-        q_out[row] = whole(own[1][row], got[1][start + row])
-        cell = cells[start + row]
-        ratio[row] = looked_up(cell, lambda e: stiffness[e] / density[e], entries)
-        bend[row] = looked_up(cell, lambda e: nonlinear[e], entries)
-    edges(lambda a, b: p_out[:, a:b, :], edge_outs, column % 2, brick_y)
-
-
-def step_body(two_sided, last, p_ref, q_ref, ratio, bend, mate, far, *rest):
-    count = 2 if two_sided else 1
-    halos = rest[:count]
-    new_ref = rest[count]
-    sent = None if last else rest[count + 1]
-    edge_outs = rest[count + 2 : -1]
-    padded = rest[-1]
+        current = whole(own[0][row], got[0][start + row])
+        before = whole(own[1][row], got[1][start + row])
+        place(row, first, brick_y, current, before, cells[start + row], 1.0)
+        for position in range(sides):
+            same, cross = borders[2 * position : 2 * position + 2]
+            above = column % 2 == position
+            at = pl.multiple_of(jnp.where(above, first + brick_y, 0), EDGE)
+            inside = jnp.where(column == jnp.where(above, last_column, 0), 0.0, 1.0) if sides == 2 else 1.0
+            current, before, cell = [whole(same[array, row].astype(F32), cross[array, row].astype(F32)) for array in range(3)]
+            place(row, at, EDGE, current, before, cell.astype(jnp.int32), inside)
+
+
+def step_body(sides, last, p_ref, q_ref, ratio, bend, mate, far, *outs):
+    padded = outs[-1]
     place = slot()
-    parity = lax.axis_index("gy") % 2
-    rows, brick_y, depth = p_ref.shape
-    lane = lax.broadcasted_iota(jnp.int32, (brick_y, depth), 1)
-    zero_edge = jnp.zeros((EDGE, depth), F32)
+    rows, length, depth = p_ref.shape
+    lane = lax.broadcasted_iota(jnp.int32, (length, depth), 1)
+    padded[0:PAD, :] = jnp.zeros((PAD, depth), F32)
+    padded[PAD + length :, :] = jnp.zeros((PAD, depth), F32)
 
     def line(index):
         if 0 <= index < rows:
@@ -144,16 +174,12 @@
         return jnp.where(place == 0, mate[index - rows], far[index - rows].astype(F32))
 
     for row in range(rows):
-        first = halos[0][row]
-        second = halos[1][row] if two_sided else zero_edge
         center = p_ref[row]
-        padded[0:EDGE, :] = jnp.where(parity == 0, second, first)
-        padded[EDGE : EDGE + brick_y, :] = center
-        padded[EDGE + brick_y :, :] = jnp.where(parity == 0, first, second)
+        padded[PAD : PAD + length, :] = center
         total = (3.0 * stencil_taps[0]) * center
         for offset in range(1, REACH + 1):
-            low, high = EDGE - offset, EDGE + offset
-            pair = padded[low : low + brick_y, :] + padded[high : high + brick_y, :]
+            low, high = PAD - offset, PAD + offset
+            pair = padded[low : low + length, :] + padded[high : high + length, :]
             pair = pair + (line(row - offset) + line(row + offset))
             pair = pair + jnp.where(lane >= offset, pltpu.roll(center, offset, 1), 0.0)
             pair = pair + jnp.where(
@@ -162,11 +188,17 @@
             total = total + stencil_taps[offset] * pair
         change = center - q_ref[row]
         value = (center + change) + ratio[row] * total + bend[row] * change * change
-        new_ref[row] = value
-        if not last:
-            sent[row] = value.astype(BF16)
-    if not last:
-        edges(lambda a, b: new_ref[:, a:b, :], edge_outs, parity, brick_y)
+        if last:
+            new_ref, prior, prior_mate = outs[:3]
+            brick_y = new_ref.shape[1]
+            first = own_start(sides)
+            padded[PAD : PAD + length, :] = value
+            new_ref[row] = padded[pl.ds(first + PAD, brick_y), :]
+            prior[row] = p_ref[row, pl.ds(first, brick_y), :]
+            prior_mate[row] = mate[row, pl.ds(first, brick_y), :]
+        else:
+            outs[0][row] = value
+            outs[1][row] = value.astype(BF16)
 
 
 def transformed(sources, first, twiddle_x, table_z, table_y, lines, grid):
@@ -239,13 +271,14 @@
             keep[field, mode] = summed(core * half_x + mode)
 
 
-def prior_body(twiddle_x, own, mate, table_z, table_y, keep, lines, grid):
+def prior_body(sides, twiddle_x, own, mate, table_z, table_y, keep, lines, grid):
     half_x = keep.shape[0]
     rows = own.shape[0]
     place = slot()
+    inner = pl.ds(own_start(sides), lines.shape[0] // 4)
     sources = [
-        (lambda row=row: jnp.where(place == 0, own[row], mate[row])) for row in range(rows)
-    ] + [(lambda row=row: jnp.where(place == 0, mate[row], own[row])) for row in range(rows)]
+        (lambda row=row: jnp.where(place == 0, own[row, inner, :], mate[row, inner, :])) for row in range(rows)
+    ] + [(lambda row=row: jnp.where(place == 0, mate[row, inner, :], own[row, inner, :])) for row in range(rows)]
     at_mode = transformed([sources], lax.axis_index("gx") * (2 * rows), twiddle_x, table_z, table_y, lines, grid)
     core = lax.axis_index("gz")
     summed = at_mode(0, 2 * half_x)
@@ -436,7 +469,8 @@
     height = rows * channels
     coupled = FIELDS * modes_x
     right_depth = -(-rows * padded_channels // 128) * 128
-    two_sided = column_count > 2
+    sides = 2 if column_count > 2 else 1
+    assert brick_y >= EDGE
 
     kept_first = kept_modes(total_x, modes_x)
     kept_second = kept_modes(total_y, modes_y)
@@ -481,18 +515,33 @@
 
     cells_count = rows * brick_y * total_z
     field = shape(rows, brick_y, total_z)
-    edge = [shape(rows, EDGE, total_z)] * (2 if two_sided else 1)
+    longer = brick_y + sides * EDGE
+    wider = shape(rows, longer, total_z)
+    border = shape(3, rows, EDGE, brick_z, dtype=BF16)
 
     swap_core = xor_pairs(core_count, 1)
     got = [lax.ppermute(array, "gz", swap_core) for array in (pressure, previous, material)]
-    sending = shape(rows, brick_y, total_z, dtype=BF16)
     here = lambda *arrays: [pltpu.with_memory_space_constraint(array, pltpu.HBM) for array in arrays]
-    current, before, ratio, bend, sent, cells, *edge_values = call(
-        lambda *refs: assemble_body(len(edge), *refs),
-        [field] * 4 + [sending, shape(brick_x, brick_y, total_z, dtype=jnp.int32)] + edge, [HBM] * 6 + [VMEM] * 3,
+    sends = call(
+        lambda *refs: pack_body(sides, *refs), [border] * (2 * sides), [HBM] * 3,
+        [pltpu.VMEM((4 * sides, rows, EDGE, brick_z), F32), pltpu.VMEM((2 * sides, rows, EDGE, brick_z), jnp.int32),
+         pltpu.SemaphoreType.DMA((6 * sides,))],
+        moved=cells_count * 8,
+    )(*here(pressure, previous, material))
+    borders = []
+    for position in range(sides):
+        pairs = (xor_pairs if position == 0 else lambda count, _: odd_pairs(count))(column_count, 1)
+        crossed = [(source * 2 + core, target * 2 + 1 - core) for source, target in pairs for core in range(2)]
+        borders.append(lax.ppermute(sends[2 * position], "gy", pairs))
+        borders.append(lax.ppermute(sends[2 * position + 1], ("gy", "gz"), crossed))
+    sending = shape(rows, longer, total_z, dtype=BF16)
+    current, before, ratio, bend, sent, cells = call(
+        lambda *refs: assemble_body(sides, column_count - 1, *refs),
+        [wider] * 4 + [sending, shape(brick_x, brick_y, total_z, dtype=jnp.int32)],
+        [HBM] * 6 + [VMEM] * (3 + 2 * sides),
         [pltpu.SMEM(stiffness.shape, F32)] * 3 + [pltpu.VMEM((rows, brick_y, brick_z), F32)] * 2
         + [pltpu.VMEM((brick_x, brick_y, brick_z), jnp.int32), pltpu.SemaphoreType.DMA((6,))], moved=cells_count * 36
-    )(*here(stiffness, density, nonlinear, pressure, previous, material), *got)
+    )(*here(stiffness, density, nonlinear, pressure, previous, material), *got, *borders)
 
     mixing, pointwise, lift_table, offset = call(
         prepare_body,
@@ -531,9 +580,6 @@
         last = repeat == STEPS - 1
         far = lax.ppermute(sent, ("gx", "gz"), like_core_pairs(cycle_count))
         mate = swap(current)
-        halos = [lax.ppermute(edge_values[0], "gy", xor_pairs(column_count, 1))]
-        if two_sided:
-            halos.append(lax.ppermute(edge_values[1], "gy", odd_pairs(column_count)))
         if repeat == 0:
             far, early = lax.optimization_barrier((far, early))
         if repeat == 1:
@@ -541,20 +587,20 @@
                 (far, mixing, pointwise, lift_table, offset)
             )
         if last:
-            prior = spectrum(prior_body, shape(modes_x // 2, modes_y, width), 2, brick_x)(
+            prior = spectrum(lambda *refs: prior_body(sides, *refs), shape(modes_x // 2, modes_y, width), 2, brick_x)(
                 twiddle_x, current, mate, forward_z, forward_y
             )
             far, prior = lax.optimization_barrier((far, prior))
-            prior_mate = mate
-        outs = [field] + ([] if last else [sending] + edge)
-        body = lambda *refs, last=last: step_body(two_sided, last, *refs)
+        body = lambda *refs, last=last: step_body(sides, last, *refs)
         new, *others = call(
-            body, outs, [VMEM] * (6 + len(halos)),
-            [pltpu.VMEM((brick_y + 2 * EDGE, total_z), F32)], flops=cells_count * 60, moved=cells_count * 28,
-        )(current, before, ratio, bend, mate, far, *halos)
-        if not last:
-            sent, *edge_values = others
-        current, before = new, current
+            body, [field] * 3 if last else [wider, sending], [VMEM] * 6,
+            [pltpu.VMEM((longer + 2 * PAD, total_z), F32)], flops=cells_count * 60, moved=cells_count * 28,
+        )(current, before, ratio, bend, mate, far)
+        if last:
+            before, prior_mate = others
+        else:
+            before, sent = current, others[0]
+        current = new
 
     total, sent = spectrum(wave_body, [part(FIELDS, F32), part(1, BF16)], 3, rows)(
         twiddle_x, current, prior, early, forward_z, forward_y

time: 71.8 us -> 78.1 us (1.088)
  starting transfers between devices: 26.1 us -> 31.9 us
  waiting for transfers between devices: 17.1 us -> 13.5 us
  Pallas kernels: 27.1 us -> 29.4 us
  local copies, waits for them, and re-layouts: 0.15 us -> 1.75 us
    ppermute x7, starting transfers between devices: 12.3 us -> 18.8 us  [per_device(): swap = lambda value: lax.ppermute(value, 'gz', swap_core)]
    pallas_call x6 -> x7, Pallas kernels: 6.53 us -> 8.78 us  [the longest x4 4.98 us: per_device(): call(body, [field] * 3 if last else [wider, sending], [VMEM] * 6, [pltpu....]
    ppermute x4 -> x2, waiting for transfers between devices: 5.66 us -> 3.57 us  [the longest x1 2.21 us: per_device(): borders.append(lax.ppermute(sends[2 * position], 'gy', pairs))]
    ppermute x4 -> x2, starting transfers between devices: 4.62 us -> 2.76 us  [the longest x1 2.63 us: per_device(): borders.append(lax.ppermute(sends[2 * position], 'gy', pairs))]
    ppermute x3, waiting for transfers between devices: 1.61 us -> 0.01 us  [per_device(): lax.ppermute(array, 'gz', swap_core)]
    reshape x2, local copies, waits for them, and re-layouts: 0.05 us -> 1.65 us  [per_device(): mode_weight.reshape(2, modes_x * channels, channels)]
    ppermute x3, starting transfers between devices: 5.32 us -> 6.53 us  [exchange(): return lax.ppermute(value.astype(BF16), axis, xor_pairs(count, distance))]
    ppermute x7, waiting for transfers between devices: 2.21 us -> 3.19 us  [per_device(): swap = lambda value: lax.ppermute(value, 'gz', swap_core)]
  transfers between devices with their start and end apart: 21 -> 19, of which waited for: 10 -> 8; matrix products, arithmetic and copies ran while one was open for 0% -> 2% of each run, Pallas kernels for 17% -> 17%
where the time goes in v6:
time: 78.1 us; the launch traced here: 77.8 us
  starting transfers between devices  31.9 us (41%)
  Pallas kernels  29.4 us (38%)
  waiting for transfers between devices  13.5 us (17%)
  local copies, waits for them, and re-layouts  1.75 us (2%)
  between operations  1.06 us (1%)
    ppermute x7, starting transfers between devices, per_device(): swap = lambda value: lax.ppermute(value, 'gz', swap_core)  18.8 us
    pallas_call x1, Pallas kernels, per_device(): pl.pallas_call(output_body, grid=(steps,), out_shape=[shape(rows, channel...  8.26 us
    ppermute x3, waiting for transfers between devices, exchange(): return lax.ppermute(value.astype(BF16), axis, xor_pairs(count, distance))  6.75 us
    pallas_call x2, Pallas kernels, pointwise_part(): pl.pallas_call(pointwise_body, grid=(steps // 2,), out_shape=shape(height...  6.6 us
    ppermute x3, starting transfers between devices, exchange(): return lax.ppermute(value.astype(BF16), axis, xor_pairs(count, distance))  6.53 us
    pallas_call x4, Pallas kernels, per_device(): call(body, [field] * 3 if last else [wider, sending], [VMEM] * 6, [pltpu....  4.98 us
    ppermute x7, waiting for transfers between devices, per_device(): swap = lambda value: lax.ppermute(value, 'gz', swap_core)  3.19 us
    ppermute x4, starting transfers between devices, per_device(): far = lax.ppermute(sent, ('gx', 'gz'), like_core_pairs(cycle_count))  2.83 us
  transfers between devices with their start and end apart: 19, of which 8 were waited for; matrix products, arithmetic and copies ran while one was open for 2% of the time, Pallas kernels for 17%

profile of v6, /device:TPU:0, one launch (start us, length us, event | category | flops | bytes accessed | tf_op | source)
XLA Modules:
  0.0 77.8 jit_solution(11298163197832280177)
XLA Ops:
  1.7 0.9 %shard_map.203 = (bf16[3,4,16,128]{3,2,1,0:T(8,128)(2,1)S(1)}, bf16[3,4,16,128]{3,2,1,0:T(8,128)(2,1)S(1)}) custom-call(f32[8,64,128]{2,1,0:T(8,128)} %refs_3_.3, f32[8,64,128]{2,1,0:T(8,128)} %refs_4_.3, s32[8,64,128]{2,1,0:T(8,128)} %refs_5_.1), custom_call_target="tpu_custom_call" | custom-call | bytes 524288 | tf_op jit(solution)/shard_map/pallas_call | solution.py:525
  2.7 2.6 %collective-permute-start.3 = (bf16[3,4,16,128]{3,2,1,0:T(8,128)(2,1)S(1)}, bf16[3,4,16,128]{3,2,1,0:T(8,128)(2,1)S(1)}, u32[]{:S(2)}, u32[]{:S(2)}) collective-permute-start(bf16[3,4,16,128]{3,2,1,0:T(8,128)(2,1)S(1)} %get-tuple-element.40), channel_id=1, source_target_pairs={{0,2},{2,0},{1,3},{3,1},{4,6},{6,4},{5,7},{7,5},{8,10},{10,8},{9,1... | collective-permute-start | bytes 147464 | tf_op jit(solution)/shard_map/ppermute | solution.py:535
  5.5 2.2 %collective-permute-done.3.refs_9_ = bf16[3,4,16,128]{3,2,1,0:T(8,128)(2,1)S(1)} collective-permute-done((bf16[3,4,16,128]{3,2,1,0:T(8,128)(2,1)S(1)}, bf16[3,4,16,128]{3,2,1,0:T(8,128)(2,1)S(1)}, u32[]{:S(2)}, u32[]{:S(2)}) %collective-permute-start.3) | collective-permute-done | bytes 49184 | tf_op jit(solution)/shard_map/ppermute | solution.py:535
  7.7 1.4 %collective-permute-done.4.refs_10_ = bf16[3,4,16,128]{3,2,1,0:T(8,128)(2,1)S(1)} collective-permute-done((bf16[3,4,16,128]{3,2,1,0:T(8,128)(2,1)S(1)}, bf16[3,4,16,128]{3,2,1,0:T(8,128)(2,1)S(1)}, u32[]{:S(2)}, u32[]{:S(2)}) %collective-permute-start.4) | collective-permute-done | bytes 49184 | tf_op jit(solution)/shard_map/ppermute | solution.py:536
  9.0 1.6 %shard_map.204 = (f32[4,80,256]{2,1,0:T(8,128)S(1)}, f32[4,80,256]{2,1,0:T(8,128)S(1)}, f32[4,80,256]{2,1,0:T(8,128)S(1)}, f32[4,80,256]{2,1,0:T(8,128)S(1)}, bf...) custom-call(f32[8]{0:T(128)} %stiffness.5, f32[8]{0:T(128)} %density.5, f32[8]{0:T(128)} %refs_2_.4, ...), custom_call_target="tpu_custom_call" | custom-call | bytes 2359296 | tf_op jit(solution)/shard_map/pallas_call | solution.py:538
  10.8 0.7 collective-permute-start.6
  11.5 2.4 %shard_map.205.early = f32[2,4,32,128]{3,2,1,0:T(8,128)S(1)} custom-call(f32[512]{0:T(512)} %constant.29.clone.refs_0_.twiddle_x, f32[8]{0:T(128)} %stiffness.5, f32[8]{0:T(128)} %density.5, bf16[256,128]{1,0:T(8,128)(2,1)} %constant.30.clone.refs_3_.table_z, bf16[2,32,256]{2,1,0:T(8,128)(2,1)} %constant.31.clone.refs_4_.table_y, ...), custom_call_target="tpu_custom_call" | custom-call | flops 268435456 | bytes 2097152 | tf_op jit(solution)/shard_map/pallas_call | solution.py:573
  13.9 1.2 %shard_map.206 = (f32[4,80,256]{2,1,0:T(8,128)S(1)}, bf16[4,80,256]{2,1,0:T(8,128)(2,1)S(1)}) custom-call(f32[4,80,256]{2,1,0:T(8,128)S(1)} %get-tuple-element.42.refs_0_.refs_1_, f32[4,80,256]{2,1,0:T(8,128)S(1)} %get-tuple-element.43.refs_1_, f32[4,80,256]{2,1,0:T(8,128)S(1)} %get-tuple-element.44.refs_2_, f32[4,80,256]{2,1,0:T(8,128)S(1)} %get-tuple-element.45.refs_3_, ...), custom_call_target="tpu_custom_call" | custom-call | flops 3932160 | bytes 1835008 | tf_op jit(solution)/shard_map/pallas_call | solution.py:595
  15.1 3.4 %collective-permute-start.7 = (f32[4,80,256]{2,1,0:T(8,128)S(1)}, f32[4,80,256]{2,1,0:T(8,128)S(1)}, u32[]{:S(2)}, u32[]{:S(2)}) collective-permute-start(f32[4,80,256]{2,1,0:T(8,128)S(1)} %get-tuple-element.49.refs_0_.refs_1_), channel_id=1, source_target_pairs={{0,1},{1,0},{2,3},{3,2},{4,5},{5,4},{6,7},{7,6},{8,9},{9,8},{10,11... | collective-permute-start | bytes 983048 | tf_op jit(solution)/shard_map/ppermute | solution.py:567
  18.5 0.7 copy.25
  19.3 0.9 %reshape.12.mode_ref = f32[2,160,20]{2,1,0:T(8,128)S(1)} reshape(f32[2,8,20,20]{3,2,1,0:T(8,128)} %copy.25) | data formatting | bytes 51200 | tf_op jit(solution)/shard_map/reshape | solution.py:552
  20.2 0.7 collective-permute-start.8
  21.0 2.2 %shard_map.207 = (bf16[80,64]{1,0:T(8,128)(2,1)S(1)}, bf16[80,128]{1,0:T(8,128)(2,1)S(1)}, f32[24,8]{1,0:T(8,128)S(1)}, f32[80,1]{1,0:T(8,128)S(1)}) custom-call(f32[8]{0:T(128)S(1)} %copy-done.5, f32[8]{0:T(128)S(1)} %copy-done.6, f32[2,160,20]{2,1,0:T(8,128)S(1)} %reshape.12.mode_ref, f32[4,20]{1,0:T(4,128)S(1)} %copy-done.8, f32[1,20]{1,0:T(1,128)S(1)} %bitcast.2, ...), custom_call_target="tpu_custom_call" | custom-call | flops 2000000000 | bytes 4000000 | tf_op jit(solution)/shard_map/pallas_call | solution.py:546
  23.2 1.2 %shard_map.208 = (f32[4,80,256]{2,1,0:T(8,128)S(1)}, bf16[4,80,256]{2,1,0:T(8,128)(2,1)S(1)}) custom-call(f32[4,80,256]{2,1,0:T(8,128)S(1)} %get-tuple-element.49.refs_0_.refs_1_, f32[4,80,256]{2,1,0:T(8,128)S(1)} %get-tuple-element.42.refs_0_.refs_1_, f32[4,80,256]{2,1,0:T(8,128)S(1)} %get-tuple-element.44.refs_2_, ...), custom_call_target="tpu_custom_call" | custom-call | flops 3932160 | bytes 1835008 | tf_op jit(solution)/shard_map/pallas_call | solution.py:595
  24.4 4.3 %collective-permute-start.9 = (f32[4,80,256]{2,1,0:T(8,128)S(1)}, f32[4,80,256]{2,1,0:T(8,128)S(1)}, u32[]{:S(2)}, u32[]{:S(2)}) collective-permute-start(f32[4,80,256]{2,1,0:T(8,128)S(1)} %get-tuple-element.56.refs_0_.refs_1_), channel_id=1, source_target_pairs={{0,1},{1,0},{2,3},{3,2},{4,5},{5,4},{6,7},{7,6},{8,9},{9,8},{10,11... | collective-permute-start | bytes 983048 | tf_op jit(solution)/shard_map/ppermute | solution.py:567
  30.0 1.2 %shard_map.209 = (f32[4,80,256]{2,1,0:T(8,128)S(1)}, bf16[4,80,256]{2,1,0:T(8,128)(2,1)S(1)}) custom-call(f32[4,80,256]{2,1,0:T(8,128)S(1)} %get-tuple-element.56.refs_0_.refs_1_, f32[4,80,256]{2,1,0:T(8,128)S(1)} %get-tuple-element.49.refs_0_.refs_1_, f32[4,80,256]{2,1,0:T(8,128)S(1)} %get-tuple-element.44.refs_2_, ...), custom_call_target="tpu_custom_call" | custom-call | flops 3932160 | bytes 1835008 | tf_op jit(solution)/shard_map/pallas_call | solution.py:595
  31.2 6.0 %collective-permute-start.11 = (f32[4,80,256]{2,1,0:T(8,128)S(1)}, f32[4,80,256]{2,1,0:T(8,128)S(1)}, u32[]{:S(2)}, u32[]{:S(2)}) collective-permute-start(f32[4,80,256]{2,1,0:T(8,128)S(1)} %get-tuple-element.58.refs_1_.refs_0_), channel_id=1, source_target_pairs={{0,1},{1,0},{2,3},{3,2},{4,5},{5,4},{6,7},{7,6},{8,9},{9,8},{10,11... | collective-permute-start | bytes 983048 | tf_op jit(solution)/shard_map/ppermute | solution.py:567
  37.2 0.8 %collective-permute-start.12 = (bf16[4,80,256]{2,1,0:T(8,128)(2,1)S(1)}, bf16[4,80,256]{2,1,0:T(8,128)(2,1)S(1)}, u32[]{:S(2)}, u32[]{:S(2)}) collective-permute-start(bf16[4,80,256]{2,1,0:T(8,128)(2,1)S(1)} %get-tuple-element.59), channel_id=1, source_target_pairs={{1,5},{4,8},{9,13},{5,1},{8,4},{13,9},{3,7},{6,10},{11,15},{7,3},{... | collective-permute-start | bytes 491528 | tf_op jit(solution)/shard_map/ppermute | solution.py:581
  38.5 1.3 %shard_map.210.prior = f32[4,32,128]{2,1,0:T(8,128)S(1)} custom-call(f32[512]{0:T(512)S(1)} %copy-done.4, f32[4,80,256]{2,1,0:T(8,128)S(1)} %get-tuple-element.58.refs_1_.refs_0_, f32[4,80,256]{2,1,0:T(8,128)S(1)} %collective-permute-done.11.refs_2_.refs_4_, bf16[256,128]{1,0:T(8,128)(2,1)S(1)} %copy-done, bf16[2,32,256]{2,1,0:T(8,128)(2,1)S(1)} %copy-done.2), custom_call_target="tpu_custom_call" | custom-call | flops 134217728 | bytes 1048576 | tf_op jit(solution)/shard_map/pallas_call | solution.py:590
  39.9 1.3 %shard_map.211 = (f32[4,64,256]{2,1,0:T(8,128)S(1)}, f32[4,64,256]{2,1,0:T(8,128)S(1)}, f32[4,64,256]{2,1,0:T(8,128)S(1)}) custom-call(f32[4,80,256]{2,1,0:T(8,128)S(1)} %get-tuple-element.58.refs_1_.refs_0_, f32[4,80,256]{2,1,0:T(8,128)S(1)} %get-tuple-element.56.refs_0_.refs_1_, f32[4,80,256]{2,1,0:T(8,128)S(1)} %get-tuple-element.44.refs_2_, ...), custom_call_target="tpu_custom_call" | custom-call | flops 3932160 | bytes 1835008 | tf_op jit(solution)/shard_map/pallas_call | solution.py:595
  41.2 1.2 %shard_map.212 = (f32[4,4,32,128]{3,2,1,0:T(8,128)S(1)}, bf16[1,4,32,128]{3,2,1,0:T(8,128)(2,1)S(1)}) custom-call(f32[512]{0:T(512)S(1)} %copy-done.4, f32[4,64,256]{2,1,0:T(8,128)S(1)} %get-tuple-element.61.own.p_ref.wave_ref, f32[4,32,128]{2,1,0:T(8,128)S(1)} %shard_map.210.prior, f32[2,4,32,128]{3,2,1,0:T(8,128)S(1)} %shard_map.205.early, ...), custom_call_target="tpu_custom_call" | custom-call | flops 67108864 | bytes 524288 | tf_op jit(solution)/shard_map/pallas_call | solution.py:605
  42.4 4.7 %collective-permute-start.13 = (bf16[1,4,32,128]{3,2,1,0:T(8,128)(2,1)S(1)}, bf16[1,4,32,128]{3,2,1,0:T(8,128)(2,1)S(1)}, u32[]{:S(2)}, u32[]{:S(2)}) collective-permute-start(bf16[1,4,32,128]{3,2,1,0:T(8,128)(2,1)S(1)} %get-tuple-element.65), channel_id=1, source_target_pairs={{0,1},{1,0},{2,3},{3,2},{4,5},{5,4},{6,7},{7,6},{8,9},{9,8},{10,11... | collective-permute-start | bytes 98312 | tf_op jit(solution)/shard_map/ppermute | solution.py:567
  47.0 0.9 %collective-permute-done.13 = bf16[1,4,32,128]{3,2,1,0:T(8,128)(2,1)S(1)} collective-permute-done((bf16[1,4,32,128]{3,2,1,0:T(8,128)(2,1)S(1)}, bf16[1,4,32,128]{3,2,1,0:T(8,128)(2,1)S(1)}, u32[]{:S(2)}, u32[]{:S(2)}) %collective-permute-start.13) | collective-permute-done | bytes 32800 | tf_op jit(solution)/shard_map/ppermute | solution.py:567
  47.9 1.2 %collective-permute-start.14 = (bf16[4,4,32,128]{3,2,1,0:T(8,128)(2,1)S(1)}, bf16[4,4,32,128]{3,2,1,0:T(8,128)(2,1)S(1)}, u32[]{:S(2)}, u32[]{:S(2)}) collective-permute-start(bf16[4,4,32,128]{3,2,1,0:T(8,128)(2,1)S(1)} %fusion), channel_id=1, source_target_pairs={{0,2},{2,0},{1,3},{3,1},{4,6},{6,4},{5,7},{7,5},{8,10},{10,8},{9,1... | collective-permute-start | bytes 393224 | tf_op jit(solution)/shard_map/ppermute | solution.py:570
  49.2 4.6 %collective-permute-done.14 = bf16[4,4,32,128]{3,2,1,0:T(8,128)(2,1)S(1)} collective-permute-done((bf16[4,4,32,128]{3,2,1,0:T(8,128)(2,1)S(1)}, bf16[4,4,32,128]{3,2,1,0:T(8,128)(2,1)S(1)}, u32[]{:S(2)}, u32[]{:S(2)}) %collective-permute-start.14) | collective-permute-done | bytes 131104 | tf_op jit(solution)/shard_map/ppermute | solution.py:570
  53.8 2.6 %collective-permute-start.15 = (bf16[4,4,32,128]{3,2,1,0:T(8,128)(2,1)S(1)}, bf16[4,4,32,128]{3,2,1,0:T(8,128)(2,1)S(1)}, u32[]{:S(2)}, u32[]{:S(2)}) collective-permute-start(bf16[4,4,32,128]{3,2,1,0:T(8,128)(2,1)S(1)} %fusion.2), channel_id=1, source_target_pairs={{0,4},{4,0},{8,12},{12,8},{1,5},{5,1},{9,13},{13,9},{2,6},{6,2},{1... | collective-permute-start | bytes 393224 | tf_op jit(solution)/shard_map/ppermute | solution.py:570
  56.4 3.3 %shard_map.213.local_low = f32[80,32,256]{2,1,0:T(8,128)S(1)} custom-call(f32[8]{0:T(128)S(1)} %copy-done.5, f32[8]{0:T(128)S(1)} %copy-done.6, f32[4,64,256]{2,1,0:T(8,128)S(1)} %get-tuple-element.61.own.p_ref.wave_ref, f32[4,64,256]{2,1,0:T(8,128)S(1)} %get-tuple-element.66.q_ref, f32[4,64,256]{2,1,0:T(8,128)S(1)} %collective-permute-done.16.p_mate.wave_other, ...), custom_call_target="tpu_custom_call" | custom-call | flops 1310720000 | bytes 3276800 | tf_op jit(solution)/shard_map/pallas_call | solution.py:616
  59.8 2.7 %collective-permute-start.17 = (bf16[4,4,32,128]{3,2,1,0:T(8,128)(2,1)S(1)}, bf16[4,4,32,128]{3,2,1,0:T(8,128)(2,1)S(1)}, u32[]{:S(2)}, u32[]{:S(2)}) collective-permute-start(bf16[4,4,32,128]{3,2,1,0:T(8,128)(2,1)S(1)} %fusion.1), channel_id=1, source_target_pairs={{0,8},{4,12},{8,0},{12,4},{1,9},{5,13},{9,1},{13,5},{2,10},{6,14},... | collective-permute-start | bytes 393224 | tf_op jit(solution)/shard_map/ppermute | solution.py:570
  62.5 3.3 %shard_map.214.local_high = f32[80,32,256]{2,1,0:T(8,128)S(1)} custom-call(f32[8]{0:T(128)S(1)} %copy-done.5, f32[8]{0:T(128)S(1)} %copy-done.6, f32[4,64,256]{2,1,0:T(8,128)S(1)} %get-tuple-element.61.own.p_ref.wave_ref, f32[4,64,256]{2,1,0:T(8,128)S(1)} %get-tuple-element.66.q_ref, f32[4,64,256]{2,1,0:T(8,128)S(1)} %collective-permute-done.16.p_mate.wave_other, ...), custom_call_target="tpu_custom_call" | custom-call | flops 1310720000 | bytes 3276800 | tf_op jit(solution)/shard_map/pallas_call | solution.py:616
  65.9 2.2 %collective-permute-done.17 = bf16[4,4,32,128]{3,2,1,0:T(8,128)(2,1)S(1)} collective-permute-done((bf16[4,4,32,128]{3,2,1,0:T(8,128)(2,1)S(1)}, bf16[4,4,32,128]{3,2,1,0:T(8,128)(2,1)S(1)}, u32[]{:S(2)}, u32[]{:S(2)}) %collective-permute-start.17) | collective-permute-done | bytes 131104 | tf_op jit(solution)/shard_map/ppermute | solution.py:570
  68.2 1.3 %collective-permute-done.18.other = bf16[4,4,32,128]{3,2,1,0:T(8,128)(2,1)S(1)} collective-permute-done((bf16[4,4,32,128]{3,2,1,0:T(8,128)(2,1)S(1)}, bf16[4,4,32,128]{3,2,1,0:T(8,128)(2,1)S(1)}, u32[]{:S(2)}, u32[]{:S(2)}) %collective-permute-start.18) | collective-permute-done | bytes 131104 | tf_op jit(solution)/shard_map/ppermute | solution.py:567
  69.5 8.3 %shard_map.215 = (bf16[4,20,64,256]{3,2,1,0:T(8,128)(2,1)}, f32[8,64,128]{2,1,0:T(8,128)}) custom-call(f32[4,4,32,128]{3,2,1,0:T(8,128)S(1)} %get-tuple-element.79.mine, bf16[4,4,32,128]{3,2,1,0:T(8,128)(2,1)S(1)} %collective-permute-done.18.other, f32[80,32,256]{2,1,0:T(8,128)S(1)} %shard_map.213.local_low, f32[80,32,256]{2,1,0:T(8,128)S(1)} %shard_map.214.local_high, ...), custom_call_target="tpu_custom_call" | custom-call | flops 131072000 | bytes 3932160 | tf_op jit(solution)/shard_map/pallas_call | solution.py:638
  (57 shorter events, 3.5 us)
Async XLA Ops:
  0.6 17.9 %copy-start.15 = (f32[2,8,20,20]{3,1,2,0:T(8,128)S(1)}, f32[2,8,20,20]{3,1,2,0:T(8,128)}, u32[]{:S(2)}) copy-start(f32[2,8,20,20]{3,1,2,0:T(8,128)} %param.28) | copy-start | bytes 76804
  0.6 8.4 %collective-permute-start = (f32[8,64,128]{2,1,0:T(8,128)}, f32[8,64,128]{2,1,0:T(8,128)S(1)}, u32[]{:S(2)}, u32[]{:S(2)}) collective-permute-start(f32[8,64,128]{2,1,0:T(8,128)} %refs_3_.3), channel_id=1, source_target_pairs={{0,1},{1,0},{2,3},{3,2},{4,5},{5,4},{6,7},{7,6},{8,9},{9,8},{10,11... | collective-permute-start | bytes 786440 | tf_op jit(solution)/shard_map/ppermute | solution.py:523
  1.2 7.9 %collective-permute-start.1 = (f32[8,64,128]{2,1,0:T(8,128)}, f32[8,64,128]{2,1,0:T(8,128)S(1)}, u32[]{:S(2)}, u32[]{:S(2)}) collective-permute-start(f32[8,64,128]{2,1,0:T(8,128)} %refs_4_.3), channel_id=1, source_target_pairs={{0,1},{1,0},{2,3},{3,2},{4,5},{5,4},{6,7},{7,6},{8,9},{9,8},{10,11... | collective-permute-start | bytes 786440 | tf_op jit(solution)/shard_map/ppermute | solution.py:523
  1.2 7.8 %collective-permute-start.2 = (s32[8,64,128]{2,1,0:T(8,128)}, s32[8,64,128]{2,1,0:T(8,128)S(1)}, u32[]{:S(2)}, u32[]{:S(2)}) collective-permute-start(s32[8,64,128]{2,1,0:T(8,128)} %refs_5_.1), channel_id=1, source_target_pairs={{0,1},{1,0},{2,3},{3,2},{4,5},{5,4},{6,7},{7,6},{8,9},{9,8},{10,11... | collective-permute-start | bytes 786440 | tf_op jit(solution)/shard_map/ppermute | solution.py:523
  2.6 18.3 %copy-start.5 = (f32[8]{0:T(128)S(1)}, f32[8]{0:T(128)}, u32[]{:S(2)}) copy-start(f32[8]{0:T(128)} %stiffness.5) | copy-start | bytes 100
  2.6 18.3 %copy-start.6 = (f32[8]{0:T(128)S(1)}, f32[8]{0:T(128)}, u32[]{:S(2)}) copy-start(f32[8]{0:T(128)} %density.5) | copy-start | bytes 100
  2.6 18.3 %copy-start.7 = (bf16[20,20]{1,0:T(8,128)(2,1)S(1)}, bf16[20,20]{1,0:T(8,128)(2,1)}, u32[]{:S(2)}) copy-start(bf16[20,20]{1,0:T(8,128)(2,1)} %local_ref.1) | copy-start | bytes 2404
  2.6 18.3 %copy-start.8 = (f32[4,20]{1,0:T(4,128)S(1)}, f32[4,20]{1,0:T(4,128)}, u32[]{:S(2)}) copy-start(f32[4,20]{1,0:T(4,128)} %lift_ref.1) | copy-start | bytes 964
  2.6 18.3 %copy-start.9 = (f32[20]{0:T(128)S(1)}, f32[20]{0:T(128)}, u32[]{:S(2)}) copy-start(f32[20]{0:T(128)} %param.27) | copy-start | bytes 244
  2.6 18.3 %copy-start.10 = (f32[8,2,80,32]{3,2,1,0:T(8,128)S(1)}, f32[8,2,80,32]{3,2,1,0:T(8,128)}, u32[]{:S(2)}) copy-start(f32[8,2,80,32]{3,2,1,0:T(8,128)} %constant.27.clone.turn_ref) | copy-start | bytes 491524
  2.7 18.3 %copy-start.11 = (f32[160,52]{1,0:T(8,128)S(1)}, f32[160,52]{1,0:T(8,128)}, u32[]{:S(2)}) copy-start(f32[160,52]{1,0:T(8,128)} %constant.24.clone.spread_ref) | copy-start | bytes 99844
  2.7 18.3 %copy-start.12 = (f32[124,128]{1,0:T(8,128)S(1)}, f32[124,128]{1,0:T(8,128)}, u32[]{:S(2)}) copy-start(f32[124,128]{1,0:T(8,128)} %constant.28.clone.wide_ref) | copy-start | bytes 190468
  2.7 18.3 %copy-start.13 = (f32[80,20]{1,0:T(8,128)S(1)}, f32[80,20]{1,0:T(8,128)}, u32[]{:S(2)}) copy-start(f32[80,20]{1,0:T(8,128)} %constant.26.clone.owner_ref) | copy-start | bytes 19204
  2.7 18.3 %copy-start.14 = (f32[4,32]{1,0:T(4,128)S(1)}, f32[4,32]{1,0:T(4,128)}, u32[]{:S(2)}) copy-start(f32[4,32]{1,0:T(4,128)} %constant.25.clone.place_ref) | copy-start | bytes 1540
  2.7 5.0 %collective-permute-start.3 = (bf16[3,4,16,128]{3,2,1,0:T(8,128)(2,1)S(1)}, bf16[3,4,16,128]{3,2,1,0:T(8,128)(2,1)S(1)}, u32[]{:S(2)}, u32[]{:S(2)}) collective-permute-start(bf16[3,4,16,128]{3,2,1,0:T(8,128)(2,1)S(1)} %get-tuple-element.40), channel_id=1, source_target_pairs={{0,2},{2,0},{1,3},{3,1},{4,6},{6,4},{5,7},{7,5},{8,10},{10,8},{9,1... | collective-permute-start | bytes 147464 | tf_op jit(solution)/shard_map/ppermute | solution.py:535
  5.3 3.7 %collective-permute-start.4 = (bf16[3,4,16,128]{3,2,1,0:T(8,128)(2,1)S(1)}, bf16[3,4,16,128]{3,2,1,0:T(8,128)(2,1)S(1)}, u32[]{:S(2)}, u32[]{:S(2)}) collective-permute-start(bf16[3,4,16,128]{3,2,1,0:T(8,128)(2,1)S(1)} %get-tuple-element.41), channel_id=1, source_target_pairs={{0,3},{1,2},{2,1},{3,0},{4,7},{5,6},{6,5},{7,4},{8,11},{9,10},{10,... | collective-permute-start | bytes 147464 | tf_op jit(solution)/shard_map/ppermute | solution.py:536
  10.6 3.3 %collective-permute-start.5 = (f32[4,80,256]{2,1,0:T(8,128)S(1)}, f32[4,80,256]{2,1,0:T(8,128)S(1)}, u32[]{:S(2)}, u32[]{:S(2)}) collective-permute-start(f32[4,80,256]{2,1,0:T(8,128)S(1)} %get-tuple-element.42.refs_0_.refs_1_), channel_id=1, source_target_pairs={{0,1},{1,0},{2,3},{3,2},{4,5},{5,4},{6,7},{7,6},{8,9},{9,8},{10,11... | collective-permute-start | bytes 983048 | tf_op jit(solution)/shard_map/ppermute | solution.py:567
  10.8 3.0 %collective-permute-start.6 = (bf16[4,80,256]{2,1,0:T(8,128)(2,1)S(1)}, bf16[4,80,256]{2,1,0:T(8,128)(2,1)S(1)}, u32[]{:S(2)}, u32[]{:S(2)}) collective-permute-start(bf16[4,80,256]{2,1,0:T(8,128)(2,1)S(1)} %get-tuple-element.46), channel_id=1, source_target_pairs={{1,5},{4,8},{9,13},{5,1},{8,4},{13,9},{3,7},{6,10},{11,15},{7,3},{... | collective-permute-start | bytes 491528 | tf_op jit(solution)/shard_map/ppermute | solution.py:581
  15.1 8.1 %collective-permute-start.7 = (f32[4,80,256]{2,1,0:T(8,128)S(1)}, f32[4,80,256]{2,1,0:T(8,128)S(1)}, u32[]{:S(2)}, u32[]{:S(2)}) collective-permute-start(f32[4,80,256]{2,1,0:T(8,128)S(1)} %get-tuple-element.49.refs_0_.refs_1_), channel_id=1, source_target_pairs={{0,1},{1,0},{2,3},{3,2},{4,5},{5,4},{6,7},{7,6},{8,9},{9,8},{10,11... | collective-permute-start | bytes 983048 | tf_op jit(solution)/shard_map/ppermute | solution.py:567
  20.2 3.0 %collective-permute-start.8 = (bf16[4,80,256]{2,1,0:T(8,128)(2,1)S(1)}, bf16[4,80,256]{2,1,0:T(8,128)(2,1)S(1)}, u32[]{:S(2)}, u32[]{:S(2)}) collective-permute-start(bf16[4,80,256]{2,1,0:T(8,128)(2,1)S(1)} %get-tuple-element.50), channel_id=1, source_target_pairs={{1,5},{4,8},{9,13},{5,1},{8,4},{13,9},{3,7},{6,10},{11,15},{7,3},{... | collective-permute-start | bytes 491528 | tf_op jit(solution)/shard_map/ppermute | solution.py:581
  23.1 15.4 %copy-start = (bf16[256,128]{1,0:T(8,128)(2,1)S(1)}, bf16[256,128]{1,0:T(8,128)(2,1)}, u32[]{:S(2)}) copy-start(bf16[256,128]{1,0:T(8,128)(2,1)} %constant.30.clone.refs_3_.table_z) | copy-start | bytes 196612
  23.2 15.3 %copy-start.2 = (bf16[2,32,256]{2,1,0:T(8,128)(2,1)S(1)}, bf16[2,32,256]{2,1,0:T(8,128)(2,1)}, u32[]{:S(2)}) copy-start(bf16[2,32,256]{2,1,0:T(8,128)(2,1)} %constant.31.clone.refs_4_.table_y) | copy-start | bytes 98308
  24.4 5.5 %collective-permute-start.9 = (f32[4,80,256]{2,1,0:T(8,128)S(1)}, f32[4,80,256]{2,1,0:T(8,128)S(1)}, u32[]{:S(2)}, u32[]{:S(2)}) collective-permute-start(f32[4,80,256]{2,1,0:T(8,128)S(1)} %get-tuple-element.56.refs_0_.refs_1_), channel_id=1, source_target_pairs={{0,1},{1,0},{2,3},{3,2},{4,5},{5,4},{6,7},{7,6},{8,9},{9,8},{10,11... | collective-permute-start | bytes 983048 | tf_op jit(solution)/shard_map/ppermute | solution.py:567
  28.7 0.7 collective-permute-start.10
  31.2 7.3 %collective-permute-start.11 = (f32[4,80,256]{2,1,0:T(8,128)S(1)}, f32[4,80,256]{2,1,0:T(8,128)S(1)}, u32[]{:S(2)}, u32[]{:S(2)}) collective-permute-start(f32[4,80,256]{2,1,0:T(8,128)S(1)} %get-tuple-element.58.refs_1_.refs_0_), channel_id=1, source_target_pairs={{0,1},{1,0},{2,3},{3,2},{4,5},{5,4},{6,7},{7,6},{8,9},{9,8},{10,11... | collective-permute-start | bytes 983048 | tf_op jit(solution)/shard_map/ppermute | solution.py:567
  37.2 2.6 %collective-permute-start.12 = (bf16[4,80,256]{2,1,0:T(8,128)(2,1)S(1)}, bf16[4,80,256]{2,1,0:T(8,128)(2,1)S(1)}, u32[]{:S(2)}, u32[]{:S(2)}) collective-permute-start(bf16[4,80,256]{2,1,0:T(8,128)(2,1)S(1)} %get-tuple-element.59), channel_id=1, source_target_pairs={{1,5},{4,8},{9,13},{5,1},{8,4},{13,9},{3,7},{6,10},{11,15},{7,3},{... | collective-permute-start | bytes 491528 | tf_op jit(solution)/shard_map/ppermute | solution.py:581
  42.4 5.5 %collective-permute-start.13 = (bf16[1,4,32,128]{3,2,1,0:T(8,128)(2,1)S(1)}, bf16[1,4,32,128]{3,2,1,0:T(8,128)(2,1)S(1)}, u32[]{:S(2)}, u32[]{:S(2)}) collective-permute-start(bf16[1,4,32,128]{3,2,1,0:T(8,128)(2,1)S(1)} %get-tuple-element.65), channel_id=1, source_target_pairs={{0,1},{1,0},{2,3},{3,2},{4,5},{5,4},{6,7},{7,6},{8,9},{9,8},{10,11... | collective-permute-start | bytes 98312 | tf_op jit(solution)/shard_map/ppermute | solution.py:567
  47.9 5.8 %collective-permute-start.14 = (bf16[4,4,32,128]{3,2,1,0:T(8,128)(2,1)S(1)}, bf16[4,4,32,128]{3,2,1,0:T(8,128)(2,1)S(1)}, u32[]{:S(2)}, u32[]{:S(2)}) collective-permute-start(bf16[4,4,32,128]{3,2,1,0:T(8,128)(2,1)S(1)} %fusion), channel_id=1, source_target_pairs={{0,2},{2,0},{1,3},{3,1},{4,6},{6,4},{5,7},{7,5},{8,10},{10,8},{9,1... | collective-permute-start | bytes 393224 | tf_op jit(solution)/shard_map/ppermute | solution.py:570
  49.1 7.3 %collective-permute-start.16 = (f32[4,64,256]{2,1,0:T(8,128)S(1)}, f32[4,64,256]{2,1,0:T(8,128)S(1)}, u32[]{:S(2)}, u32[]{:S(2)}) collective-permute-start(f32[4,64,256]{2,1,0:T(8,128)S(1)} %get-tuple-element.61.own.p_ref.wave_ref), channel_id=1, source_target_pairs={{0,1},{1,0},{2,3},{3,2},{4,5},{5,4},{6,7},{7,6},{8,9},{9,8},{10,11... | collective-permute-start | bytes 786440 | tf_op jit(solution)/shard_map/ppermute | solution.py:567
  53.8 5.9 %collective-permute-start.15 = (bf16[4,4,32,128]{3,2,1,0:T(8,128)(2,1)S(1)}, bf16[4,4,32,128]{3,2,1,0:T(8,128)(2,1)S(1)}, u32[]{:S(2)}, u32[]{:S(2)}) collective-permute-start(bf16[4,4,32,128]{3,2,1,0:T(8,128)(2,1)S(1)} %fusion.2), channel_id=1, source_target_pairs={{0,4},{4,0},{8,12},{12,8},{1,5},{5,1},{9,13},{13,9},{2,6},{6,2},{1... | collective-permute-start | bytes 393224 | tf_op jit(solution)/shard_map/ppermute | solution.py:570
  59.8 8.2 %collective-permute-start.17 = (bf16[4,4,32,128]{3,2,1,0:T(8,128)(2,1)S(1)}, bf16[4,4,32,128]{3,2,1,0:T(8,128)(2,1)S(1)}, u32[]{:S(2)}, u32[]{:S(2)}) collective-permute-start(bf16[4,4,32,128]{3,2,1,0:T(8,128)(2,1)S(1)} %fusion.1), channel_id=1, source_target_pairs={{0,8},{4,12},{8,0},{12,4},{1,9},{5,13},{9,1},{13,5},{2,10},{6,14},... | collective-permute-start | bytes 393224 | tf_op jit(solution)/shard_map/ppermute | solution.py:570
  68.1 1.4 %collective-permute-start.18 = (bf16[4,4,32,128]{3,2,1,0:T(8,128)(2,1)S(1)}, bf16[4,4,32,128]{3,2,1,0:T(8,128)(2,1)S(1)}, u32[]{:S(2)}, u32[]{:S(2)}) collective-permute-start(bf16[4,4,32,128]{3,2,1,0:T(8,128)(2,1)S(1)} %get-tuple-element.78), channel_id=1, source_target_pairs={{0,1},{1,0},{2,3},{3,2},{4,5},{5,4},{6,7},{7,6},{8,9},{9,8},{10,11... | collective-permute-start | bytes 393224 | tf_op jit(solution)/shard_map/ppermute | solution.py:567
  (3 other events, 34.8 us)

commit v7 on v5

--- a/solution.py
+++ b/solution.py
@@ -136,12 +136,15 @@
     lane = lax.broadcasted_iota(jnp.int32, (brick_y, depth), 1)
     zero_edge = jnp.zeros((EDGE, depth), F32)
 
+    cycle = lax.axis_index("gx")
+    outside = cycle == jnp.where(place == 0, 0, lax.axis_size("gx") - 1)
+
     def line(index):
         if 0 <= index < rows:
             return p_ref[index]
-        if index < 0:
-            return jnp.where(place == 0, far[index + rows].astype(F32), mate[index + rows])
-        return jnp.where(place == 0, mate[index - rows], far[index - rows].astype(F32))
+        at = index % rows
+        beyond = jnp.where(outside, 0.0, far[at].astype(F32))
+        return jnp.where(place == (0 if index < 0 else 1), beyond, mate[at])
 
     for row in range(rows):
         first = halos[0][row]
@@ -400,9 +403,16 @@
     return pairs + [(target, source) for source, target in pairs]
 
 
-def like_core_pairs(count):
-    pairs = [(2 * chip + 1 - chip % 2, 2 * chip + 3 - chip % 2) for chip in range(count - 1)]
-    return pairs + [(target, source) for source, target in pairs]
+def row_pairs(cycles, columns):
+    place = lambda cycle, column, core: (cycle * columns + column) * 2 + core
+    pairs = []
+    for column in range(columns):
+        for cycle in range(cycles - 1):
+            one, two = place(cycle, column, 1 - cycle % 2), place(cycle + 1, column, 1 - cycle % 2)
+            pairs += [(one, two), (two, one)]
+        for cycle, core in ((0, 0), (cycles - 1, 1 - (cycles - 1) % 2)):
+            pairs.append((place(cycle, column, core), place(cycle, column ^ 1, core)))
+    return pairs
 
 
 def per_device(
@@ -513,7 +523,7 @@
             flops=cells_count * 256 * lines, moved=cells_count * 2 * lines,
         )
 
-    stages = [(axis, count, 2**bit) for axis, count in (("gy", column_count), ("gx", cycle_count))
+    stages = [(axis, count, 2 ** (bit + 1) - 1) for axis, count in (("gy", column_count), ("gx", cycle_count))
               for bit in range((count - 1).bit_length())]
     swap = lambda value: lax.ppermute(value, "gz", swap_core)
 
@@ -529,7 +539,7 @@
 
     for repeat in range(STEPS):
         last = repeat == STEPS - 1
-        far = lax.ppermute(sent, ("gx", "gz"), like_core_pairs(cycle_count))
+        far = lax.ppermute(sent, ("gx", "gy", "gz"), row_pairs(cycle_count, column_count))
         mate = swap(current)
         halos = [lax.ppermute(edge_values[0], "gy", xor_pairs(column_count, 1))]
         if two_sided:

time: 71.8 us -> 64.4 us (0.90)
  starting transfers between devices: 26.1 us -> 14.4 us
  waiting for transfers between devices: 17.1 us -> 21.3 us
    ppermute x7, starting transfers between devices: 12.3 us -> 0.8 us  [per_device(): swap = lambda value: lax.ppermute(value, 'gz', swap_core)]
    ppermute x4, waiting for transfers between devices: 0.01 us -> 4.93 us  [per_device(): lax.ppermute(sent, ('gx', 'gy', 'gz'), row_pairs(cycle_count, column_count))]
    ppermute x3, starting transfers between devices: 5.32 us -> 3.61 us  [exchange(): return lax.ppermute(value.astype(BF16), axis, xor_pairs(count, distance))]
    ppermute x4, starting transfers between devices: 2.81 us -> 3.72 us  [per_device(): lax.ppermute(sent, ('gx', 'gy', 'gz'), row_pairs(cycle_count, column_count))]
    ppermute x4, waiting for transfers between devices: 5.66 us -> 4.83 us  [per_device(): halos = [lax.ppermute(edge_values[0], 'gy', xor_pairs(column_count, 1))]]
  transfers between devices with their start and end apart: 21 -> 21, of which waited for: 10 -> 14; matrix products, arithmetic and copies ran while one was open for 0% -> 0% of each run, Pallas kernels for 17% -> 19%
where the time goes in v7:
time: 64.4 us; the launch traced here: 64.2 us
  Pallas kernels  27.2 us (42%)
  waiting for transfers between devices  21.3 us (33%)
  starting transfers between devices  14.4 us (22%)
  between operations  1.01 us (2%)
    pallas_call x1, Pallas kernels, per_device(): pl.pallas_call(output_body, grid=(steps,), out_shape=[shape(rows, channel...  8.26 us
    ppermute x3, waiting for transfers between devices, exchange(): return lax.ppermute(value.astype(BF16), axis, xor_pairs(count, distance))  7.37 us
    pallas_call x2, Pallas kernels, pointwise_part(): pl.pallas_call(pointwise_body, grid=(steps // 2,), out_shape=shape(height...  6.59 us
    ppermute x4, starting transfers between devices, per_device(): halos = [lax.ppermute(edge_values[0], 'gy', xor_pairs(column_count, 1))]  5.2 us
    ppermute x4, waiting for transfers between devices, per_device(): lax.ppermute(sent, ('gx', 'gy', 'gz'), row_pairs(cycle_count, column_count))  4.93 us
    ppermute x4, waiting for transfers between devices, per_device(): halos = [lax.ppermute(edge_values[0], 'gy', xor_pairs(column_count, 1))]  4.83 us
    pallas_call x4, Pallas kernels, per_device(): call(body, outs, [VMEM] * (6 + len(halos)), [pltpu.VMEM((brick_y + 2 * ED...  3.89 us
    ppermute x4, starting transfers between devices, per_device(): lax.ppermute(sent, ('gx', 'gy', 'gz'), row_pairs(cycle_count, column_count))  3.72 us
  transfers between devices with their start and end apart: 21, of which 14 were waited for; matrix products, arithmetic and copies ran while one was open for 0% of the time, Pallas kernels for 19%

profile of v7, /device:TPU:0, one launch (start us, length us, event | category | flops | bytes accessed | tf_op | source)
XLA Modules:
  0.0 64.2 jit_solution(8976650340395284347)
XLA Ops:
  0.8 0.5 collective-permute-start
  1.4 0.4 collective-permute-start.2
  1.8 0.9 %collective-permute-done.refs_6_ = f32[8,64,128]{2,1,0:T(8,128)S(1)} collective-permute-done((f32[8,64,128]{2,1,0:T(8,128)}, f32[8,64,128]{2,1,0:T(8,128)S(1)}, u32[]{:S(2)}, u32[]{:S(2)}) %collective-permute-start) | collective-permute-done | bytes 262176 | tf_op jit(solution)/shard_map/ppermute | solution.py:497
  3.4 1.5 %shard_map.203 = (f32[4,64,256]{2,1,0:T(8,128)S(1)}, f32[4,64,256]{2,1,0:T(8,128)S(1)}, f32[4,64,256]{2,1,0:T(8,128)S(1)}, f32[4,64,256]{2,1,0:T(8,128)S(1)}, bf...) custom-call(f32[8]{0:T(128)} %stiffness.5, f32[8]{0:T(128)} %density.5, ...), custom_call_target="tpu_custom_call" | custom-call | bytes 2359296 | tf_op jit(solution)/shard_map/pallas_call | solution.py:500
  4.9 0.4 collective-permute-start.3
  5.3 2.6 %collective-permute-start.4 = (bf16[4,64,256]{2,1,0:T(8,128)(2,1)S(1)}, bf16[4,64,256]{2,1,0:T(8,128)(2,1)S(1)}, u32[]{:S(2)}, u32[]{:S(2)}) collective-permute-start(bf16[4,64,256]{2,1,0:T(8,128)(2,1)S(1)} %get-tuple-element.43), channel_id=1, source_target_pairs={{1,5},{5,1},{4,8},{8,4},{9,13},{13,9},{0,2},{12,14},{3,7},{7,3},{6... | collective-permute-start | bytes 393224 | tf_op jit(solution)/shard_map/ppermute | solution.py:542
  8.0 2.3 %shard_map.204.early = f32[2,4,32,128]{3,2,1,0:T(8,128)S(1)} custom-call(f32[512]{0:T(512)} %constant.29.clone.refs_0_.twiddle_x, f32[8]{0:T(128)} %stiffness.5, f32[8]{0:T(128)} %density.5, bf16[256,128]{1,0:T(8,128)(2,1)} %constant.30.clone.refs_3_.table_z, bf16[2,32,256]{2,1,0:T(8,128)(2,1)} %constant.31.clone.refs_4_.table_y, ...), custom_call_target="tpu_custom_call" | custom-call | flops 268435456 | bytes 2097152 | tf_op jit(solution)/shard_map/pallas_call | solution.py:534
  10.3 0.7 %collective-permute-done.4.refs_5_ = bf16[4,64,256]{2,1,0:T(8,128)(2,1)S(1)} collective-permute-done((bf16[4,64,256]{2,1,0:T(8,128)(2,1)S(1)}, bf16[4,64,256]{2,1,0:T(8,128)(2,1)S(1)}, u32[]{:S(2)}, u32[]{:S(2)}) %collective-permute-start.4) | collective-permute-done | bytes 131104 | tf_op jit(solution)/shard_map/ppermute | solution.py:542
  11.0 0.8 %collective-permute-done.5.refs_6_ = f32[4,8,256]{2,1,0:T(8,128)S(1)} collective-permute-done((f32[4,8,256]{2,1,0:T(8,128)S(1)}, f32[4,8,256]{2,1,0:T(8,128)S(1)}, u32[]{:S(2)}, u32[]{:S(2)}) %collective-permute-start.5) | collective-permute-done | bytes 32800 | tf_op jit(solution)/shard_map/ppermute | solution.py:544
  11.9 1.0 %shard_map.205 = (f32[4,64,256]{2,1,0:T(8,128)S(1)}, bf16[4,64,256]{2,1,0:T(8,128)(2,1)S(1)}, f32[4,8,256]{2,1,0:T(8,128)S(1)}) custom-call(f32[4,64,256]{2,1,0:T(8,128)S(1)} %get-tuple-element.39.refs_0_.refs_1_, f32[4,64,256]{2,1,0:T(8,128)S(1)} %get-tuple-element.40.refs_1_, f32[4,64,256]{2,1,0:T(8,128)S(1)} %get-tuple-element.41.refs_2_, ...), custom_call_target="tpu_custom_call" | custom-call | flops 3932160 | bytes 1835008 | tf_op jit(solution)/shard_map/pallas_call | solution.py:561
  13.0 1.8 %collective-permute-start.8 = (f32[4,8,256]{2,1,0:T(8,128)S(1)}, f32[4,8,256]{2,1,0:T(8,128)S(1)}, u32[]{:S(2)}, u32[]{:S(2)}) collective-permute-start(f32[4,8,256]{2,1,0:T(8,128)S(1)} %get-tuple-element.54), channel_id=1, source_target_pairs={{0,2},{2,0},{1,3},{3,1},{4,6},{6,4},{5,7},{7,5},{8,10},{10,8},{9,1... | collective-permute-start | bytes 98312 | tf_op jit(solution)/shard_map/ppermute | solution.py:544
  15.1 2.2 %shard_map.206 = (bf16[80,64]{1,0:T(8,128)(2,1)S(1)}, bf16[80,128]{1,0:T(8,128)(2,1)S(1)}, f32[24,8]{1,0:T(8,128)S(1)}, f32[80,1]{1,0:T(8,128)S(1)}) custom-call(f32[8]{0:T(128)S(1)} %copy-done.5, f32[8]{0:T(128)S(1)} %copy-done.6, f32[2,160,20]{2,1,0:T(8,128)S(1)} %reshape.12.mode_ref, f32[4,20]{1,0:T(4,128)S(1)} %copy-done.8, f32[1,20]{1,0:T(1,128)S(1)} %bitcast.2, ...), custom_call_target="tpu_custom_call" | custom-call | flops 2000000000 | bytes 4000000 | tf_op jit(solution)/shard_map/pallas_call | solution.py:507
  17.4 2.4 %collective-permute-done.7.refs_5_ = bf16[4,64,256]{2,1,0:T(8,128)(2,1)S(1)} collective-permute-done((bf16[4,64,256]{2,1,0:T(8,128)(2,1)S(1)}, bf16[4,64,256]{2,1,0:T(8,128)(2,1)S(1)}, u32[]{:S(2)}, u32[]{:S(2)}) %collective-permute-start.7) | collective-permute-done | bytes 131104 | tf_op jit(solution)/shard_map/ppermute | solution.py:542
  19.8 1.0 %shard_map.207 = (f32[4,64,256]{2,1,0:T(8,128)S(1)}, bf16[4,64,256]{2,1,0:T(8,128)(2,1)S(1)}, f32[4,8,256]{2,1,0:T(8,128)S(1)}) custom-call(f32[4,64,256]{2,1,0:T(8,128)S(1)} %get-tuple-element.47.refs_0_.refs_1_, f32[4,64,256]{2,1,0:T(8,128)S(1)} %get-tuple-element.39.refs_0_.refs_1_, f32[4,64,256]{2,1,0:T(8,128)S(1)} %get-tuple-element.41.refs_2_, ...), custom_call_target="tpu_custom_call" | custom-call | flops 3932160 | bytes 1835008 | tf_op jit(solution)/shard_map/pallas_call | solution.py:561
  21.3 1.7 %collective-permute-start.11 = (f32[4,8,256]{2,1,0:T(8,128)S(1)}, f32[4,8,256]{2,1,0:T(8,128)S(1)}, u32[]{:S(2)}, u32[]{:S(2)}) collective-permute-start(f32[4,8,256]{2,1,0:T(8,128)S(1)} %get-tuple-element.57), channel_id=1, source_target_pairs={{0,2},{2,0},{1,3},{3,1},{4,6},{6,4},{5,7},{7,5},{8,10},{10,8},{9,1... | collective-permute-start | bytes 98312 | tf_op jit(solution)/shard_map/ppermute | solution.py:544
  22.9 3.6 %collective-permute-done.11.refs_6_ = f32[4,8,256]{2,1,0:T(8,128)S(1)} collective-permute-done((f32[4,8,256]{2,1,0:T(8,128)S(1)}, f32[4,8,256]{2,1,0:T(8,128)S(1)}, u32[]{:S(2)}, u32[]{:S(2)}) %collective-permute-start.11) | collective-permute-done | bytes 32800 | tf_op jit(solution)/shard_map/ppermute | solution.py:544
  26.6 1.0 %shard_map.208 = (f32[4,64,256]{2,1,0:T(8,128)S(1)}, bf16[4,64,256]{2,1,0:T(8,128)(2,1)S(1)}, f32[4,8,256]{2,1,0:T(8,128)S(1)}) custom-call(f32[4,64,256]{2,1,0:T(8,128)S(1)} %get-tuple-element.55.refs_0_.refs_1_, f32[4,64,256]{2,1,0:T(8,128)S(1)} %get-tuple-element.47.refs_0_.refs_1_, f32[4,64,256]{2,1,0:T(8,128)S(1)} %get-tuple-element.41.refs_2_, ...), custom_call_target="tpu_custom_call" | custom-call | flops 3932160 | bytes 1835008 | tf_op jit(solution)/shard_map/pallas_call | solution.py:561
  28.1 1.7 %collective-permute-start.14 = (f32[4,8,256]{2,1,0:T(8,128)S(1)}, f32[4,8,256]{2,1,0:T(8,128)S(1)}, u32[]{:S(2)}, u32[]{:S(2)}) collective-permute-start(f32[4,8,256]{2,1,0:T(8,128)S(1)} %get-tuple-element.61), channel_id=1, source_target_pairs={{0,2},{2,0},{1,3},{3,1},{4,6},{6,4},{5,7},{7,5},{8,10},{10,8},{9,1... | collective-permute-start | bytes 98312 | tf_op jit(solution)/shard_map/ppermute | solution.py:544
  29.8 1.3 %shard_map.209.prior = f32[4,32,128]{2,1,0:T(8,128)S(1)} custom-call(f32[512]{0:T(512)S(1)} %copy-done.4, f32[4,64,256]{2,1,0:T(8,128)S(1)} %get-tuple-element.58.own.refs_0_.q_ref, f32[4,64,256]{2,1,0:T(8,128)S(1)} %collective-permute-done.12.mate.refs_4_.q_mate, bf16[256,128]{1,0:T(8,128)(2,1)S(1)} %copy-done, bf16[2,32,256]{2,1,0:T(8,128)(2,1)S(1)} %copy-done.2), custom_call_target="tpu_custom_call" | custom-call | flops 134217728 | bytes 1048576 | tf_op jit(solution)/shard_map/pallas_call | solution.py:554
  31.1 1.8 %collective-permute-done.13.refs_5_ = bf16[4,64,256]{2,1,0:T(8,128)(2,1)S(1)} collective-permute-done((bf16[4,64,256]{2,1,0:T(8,128)(2,1)S(1)}, bf16[4,64,256]{2,1,0:T(8,128)(2,1)S(1)}, u32[]{:S(2)}, u32[]{:S(2)}) %collective-permute-start.13) | collective-permute-done | bytes 131104 | tf_op jit(solution)/shard_map/ppermute | solution.py:542
  33.3 1.0 %shard_map.210.own.p_ref.wave_ref = f32[4,64,256]{2,1,0:T(8,128)S(1)} custom-call(f32[4,64,256]{2,1,0:T(8,128)S(1)} %get-tuple-element.58.own.refs_0_.q_ref, f32[4,64,256]{2,1,0:T(8,128)S(1)} %get-tuple-element.55.refs_0_.refs_1_, f32[4,64,256]{2,1,0:T(8,128)S(1)} %get-tuple-element.41.refs_2_, f32[4,64,256]{2,1,0:T(8,128)S(1)} %get-tuple-element.42.refs_3_, ...), custom_call_target="tpu_custom_call" | custom-call | flops 3932160 | bytes 1835008 | tf_op jit(solution)/shard_map/pallas_call | solution.py:561
  34.2 1.2 %shard_map.211 = (f32[4,4,32,128]{3,2,1,0:T(8,128)S(1)}, bf16[1,4,32,128]{3,2,1,0:T(8,128)(2,1)S(1)}) custom-call(f32[512]{0:T(512)S(1)} %copy-done.4, f32[4,64,256]{2,1,0:T(8,128)S(1)} %shard_map.210.own.p_ref.wave_ref, f32[4,32,128]{2,1,0:T(8,128)S(1)} %shard_map.209.prior, f32[2,4,32,128]{3,2,1,0:T(8,128)S(1)} %shard_map.204.early, ...), custom_call_target="tpu_custom_call" | custom-call | flops 67108864 | bytes 524288 | tf_op jit(solution)/shard_map/pallas_call | solution.py:569
  35.5 1.2 %collective-permute-done.15 = bf16[1,4,32,128]{3,2,1,0:T(8,128)(2,1)S(1)} collective-permute-done((bf16[1,4,32,128]{3,2,1,0:T(8,128)(2,1)S(1)}, bf16[1,4,32,128]{3,2,1,0:T(8,128)(2,1)S(1)}, u32[]{:S(2)}, u32[]{:S(2)}) %collective-permute-start.15) | collective-permute-done | bytes 32800 | tf_op jit(solution)/shard_map/ppermute | solution.py:528
  36.7 0.5 collective-permute-start.16
  37.3 5.1 %collective-permute-done.16 = bf16[4,4,32,128]{3,2,1,0:T(8,128)(2,1)S(1)} collective-permute-done((bf16[4,4,32,128]{3,2,1,0:T(8,128)(2,1)S(1)}, bf16[4,4,32,128]{3,2,1,0:T(8,128)(2,1)S(1)}, u32[]{:S(2)}, u32[]{:S(2)}) %collective-permute-start.16) | collective-permute-done | bytes 131104 | tf_op jit(solution)/shard_map/ppermute | solution.py:531
  42.8 3.3 %shard_map.212.local_low = f32[80,32,256]{2,1,0:T(8,128)S(1)} custom-call(f32[8]{0:T(128)S(1)} %copy-done.5, f32[8]{0:T(128)S(1)} %copy-done.6, f32[4,64,256]{2,1,0:T(8,128)S(1)} %shard_map.210.own.p_ref.wave_ref, f32[4,64,256]{2,1,0:T(8,128)S(1)} %get-tuple-element.58.own.refs_0_.q_ref, f32[4,64,256]{2,1,0:T(8,128)S(1)} %collective-permute-done.18.p_mate.wave_other, ...), custom_call_target="tpu_custom_call" | custom-call | flops 1310720000 | bytes 3276800 | tf_op jit(solution)/shard_map/pallas_call | solution.py:580
  46.1 1.4 %collective-permute-done.17 = bf16[4,4,32,128]{3,2,1,0:T(8,128)(2,1)S(1)} collective-permute-done((bf16[4,4,32,128]{3,2,1,0:T(8,128)(2,1)S(1)}, bf16[4,4,32,128]{3,2,1,0:T(8,128)(2,1)S(1)}, u32[]{:S(2)}, u32[]{:S(2)}) %collective-permute-start.17) | collective-permute-done | bytes 131104 | tf_op jit(solution)/shard_map/ppermute | solution.py:531
  47.5 2.7 %collective-permute-start.19 = (bf16[4,4,32,128]{3,2,1,0:T(8,128)(2,1)S(1)}, bf16[4,4,32,128]{3,2,1,0:T(8,128)(2,1)S(1)}, u32[]{:S(2)}, u32[]{:S(2)}) collective-permute-start(bf16[4,4,32,128]{3,2,1,0:T(8,128)(2,1)S(1)} %fusion.1), channel_id=1, source_target_pairs={{0,12},{4,8},{8,4},{12,0},{1,13},{5,9},{9,5},{13,1},{2,14},{6,10},... | collective-permute-start | bytes 393224 | tf_op jit(solution)/shard_map/ppermute | solution.py:531
  50.3 3.3 %shard_map.213.local_high = f32[80,32,256]{2,1,0:T(8,128)S(1)} custom-call(f32[8]{0:T(128)S(1)} %copy-done.5, f32[8]{0:T(128)S(1)} %copy-done.6, f32[4,64,256]{2,1,0:T(8,128)S(1)} %shard_map.210.own.p_ref.wave_ref, f32[4,64,256]{2,1,0:T(8,128)S(1)} %get-tuple-element.58.own.refs_0_.q_ref, f32[4,64,256]{2,1,0:T(8,128)S(1)} %collective-permute-done.18.p_mate.wave_other, ...), custom_call_target="tpu_custom_call" | custom-call | flops 1310720000 | bytes 3276800 | tf_op jit(solution)/shard_map/pallas_call | solution.py:580
  53.6 0.9 %collective-permute-done.19 = bf16[4,4,32,128]{3,2,1,0:T(8,128)(2,1)S(1)} collective-permute-done((bf16[4,4,32,128]{3,2,1,0:T(8,128)(2,1)S(1)}, bf16[4,4,32,128]{3,2,1,0:T(8,128)(2,1)S(1)}, u32[]{:S(2)}, u32[]{:S(2)}) %collective-permute-start.19) | collective-permute-done | bytes 131104 | tf_op jit(solution)/shard_map/ppermute | solution.py:531
  54.6 1.3 %collective-permute-done.20.other = bf16[4,4,32,128]{3,2,1,0:T(8,128)(2,1)S(1)} collective-permute-done((bf16[4,4,32,128]{3,2,1,0:T(8,128)(2,1)S(1)}, bf16[4,4,32,128]{3,2,1,0:T(8,128)(2,1)S(1)}, u32[]{:S(2)}, u32[]{:S(2)}) %collective-permute-start.20) | collective-permute-done | bytes 131104 | tf_op jit(solution)/shard_map/ppermute | solution.py:528
  56.0 8.3 %shard_map.214 = (bf16[4,20,64,256]{3,2,1,0:T(8,128)(2,1)}, f32[8,64,128]{2,1,0:T(8,128)}) custom-call(f32[4,4,32,128]{3,2,1,0:T(8,128)S(1)} %get-tuple-element.77.mine, bf16[4,4,32,128]{3,2,1,0:T(8,128)(2,1)S(1)} %collective-permute-done.20.other, f32[80,32,256]{2,1,0:T(8,128)S(1)} %shard_map.212.local_low, f32[80,32,256]{2,1,0:T(8,128)S(1)} %shard_map.213.local_high, ...), custom_call_target="tpu_custom_call" | custom-call | flops 131072000 | bytes 3932160 | tf_op jit(solution)/shard_map/pallas_call | solution.py:602
  (60 shorter events, 3.4 us)
Async XLA Ops:
  0.6 14.4 %copy-start.12 = (f32[124,128]{1,0:T(8,128)S(1)}, f32[124,128]{1,0:T(8,128)}, u32[]{:S(2)}) copy-start(f32[124,128]{1,0:T(8,128)} %constant.28.clone.wide_ref) | copy-start | bytes 190468
  0.6 14.4 %copy-start.10 = (f32[8,2,80,32]{3,2,1,0:T(8,128)S(1)}, f32[8,2,80,32]{3,2,1,0:T(8,128)}, u32[]{:S(2)}) copy-start(f32[8,2,80,32]{3,2,1,0:T(8,128)} %constant.27.clone.turn_ref) | copy-start | bytes 491524
  0.7 14.4 %copy-start.13 = (f32[80,20]{1,0:T(8,128)S(1)}, f32[80,20]{1,0:T(8,128)}, u32[]{:S(2)}) copy-start(f32[80,20]{1,0:T(8,128)} %constant.26.clone.owner_ref) | copy-start | bytes 19204
  0.7 14.4 %copy-start.14 = (f32[4,32]{1,0:T(4,128)S(1)}, f32[4,32]{1,0:T(4,128)}, u32[]{:S(2)}) copy-start(f32[4,32]{1,0:T(4,128)} %constant.25.clone.place_ref) | copy-start | bytes 1540
  0.7 14.4 %copy-start.11 = (f32[160,52]{1,0:T(8,128)S(1)}, f32[160,52]{1,0:T(8,128)}, u32[]{:S(2)}) copy-start(f32[160,52]{1,0:T(8,128)} %constant.24.clone.spread_ref) | copy-start | bytes 99844
  0.7 14.4 %copy-start.6 = (f32[8]{0:T(128)S(1)}, f32[8]{0:T(128)}, u32[]{:S(2)}) copy-start(f32[8]{0:T(128)} %density.5) | copy-start | bytes 100
  0.7 14.4 %copy-start.5 = (f32[8]{0:T(128)S(1)}, f32[8]{0:T(128)}, u32[]{:S(2)}) copy-start(f32[8]{0:T(128)} %stiffness.5) | copy-start | bytes 100
  0.7 14.4 %copy-start.7 = (bf16[20,20]{1,0:T(8,128)(2,1)S(1)}, bf16[20,20]{1,0:T(8,128)(2,1)}, u32[]{:S(2)}) copy-start(bf16[20,20]{1,0:T(8,128)(2,1)} %local_ref.1) | copy-start | bytes 2404
  0.7 14.4 %copy-start.9 = (f32[20]{0:T(128)S(1)}, f32[20]{0:T(128)}, u32[]{:S(2)}) copy-start(f32[20]{0:T(128)} %param.27) | copy-start | bytes 244
  0.7 14.4 %copy-start.8 = (f32[4,20]{1,0:T(4,128)S(1)}, f32[4,20]{1,0:T(4,128)}, u32[]{:S(2)}) copy-start(f32[4,20]{1,0:T(4,128)} %lift_ref.1) | copy-start | bytes 964
  0.8 1.9 %collective-permute-start = (f32[8,64,128]{2,1,0:T(8,128)}, f32[8,64,128]{2,1,0:T(8,128)S(1)}, u32[]{:S(2)}, u32[]{:S(2)}) collective-permute-start(f32[8,64,128]{2,1,0:T(8,128)} %refs_3_.2), channel_id=1, source_target_pairs={{0,1},{1,0},{2,3},{3,2},{4,5},{5,4},{6,7},{7,6},{8,9},{9,8},{10,11... | collective-permute-start | bytes 786440 | tf_op jit(solution)/shard_map/ppermute | solution.py:497
  1.3 1.7 %collective-permute-start.1 = (f32[8,64,128]{2,1,0:T(8,128)}, f32[8,64,128]{2,1,0:T(8,128)S(1)}, u32[]{:S(2)}, u32[]{:S(2)}) collective-permute-start(f32[8,64,128]{2,1,0:T(8,128)} %refs_4_.2), channel_id=1, source_target_pairs={{0,1},{1,0},{2,3},{3,2},{4,5},{5,4},{6,7},{7,6},{8,9},{9,8},{10,11... | collective-permute-start | bytes 786440 | tf_op jit(solution)/shard_map/ppermute | solution.py:497
  1.4 2.0 %collective-permute-start.2 = (s32[8,64,128]{2,1,0:T(8,128)}, s32[8,64,128]{2,1,0:T(8,128)S(1)}, u32[]{:S(2)}, u32[]{:S(2)}) collective-permute-start(s32[8,64,128]{2,1,0:T(8,128)} %refs_5_.1), channel_id=1, source_target_pairs={{0,1},{1,0},{2,3},{3,2},{4,5},{5,4},{6,7},{7,6},{8,9},{9,8},{10,11... | collective-permute-start | bytes 786440 | tf_op jit(solution)/shard_map/ppermute | solution.py:497
  4.9 7.0 %collective-permute-start.3 = (f32[4,64,256]{2,1,0:T(8,128)S(1)}, f32[4,64,256]{2,1,0:T(8,128)S(1)}, u32[]{:S(2)}, u32[]{:S(2)}) collective-permute-start(f32[4,64,256]{2,1,0:T(8,128)S(1)} %get-tuple-element.39.refs_0_.refs_1_), channel_id=1, source_target_pairs={{0,1},{1,0},{2,3},{3,2},{4,5},{5,4},{6,7},{7,6},{8,9},{9,8},{10,11... | collective-permute-start | bytes 786440 | tf_op jit(solution)/shard_map/ppermute | solution.py:528
  5.3 5.7 %collective-permute-start.4 = (bf16[4,64,256]{2,1,0:T(8,128)(2,1)S(1)}, bf16[4,64,256]{2,1,0:T(8,128)(2,1)S(1)}, u32[]{:S(2)}, u32[]{:S(2)}) collective-permute-start(bf16[4,64,256]{2,1,0:T(8,128)(2,1)S(1)} %get-tuple-element.43), channel_id=1, source_target_pairs={{1,5},{5,1},{4,8},{8,4},{9,13},{13,9},{0,2},{12,14},{3,7},{7,3},{6... | collective-permute-start | bytes 393224 | tf_op jit(solution)/shard_map/ppermute | solution.py:542
  7.9 3.9 %collective-permute-start.5 = (f32[4,8,256]{2,1,0:T(8,128)S(1)}, f32[4,8,256]{2,1,0:T(8,128)S(1)}, u32[]{:S(2)}, u32[]{:S(2)}) collective-permute-start(f32[4,8,256]{2,1,0:T(8,128)S(1)} %get-tuple-element.46), channel_id=1, source_target_pairs={{0,2},{2,0},{1,3},{3,1},{4,6},{6,4},{5,7},{7,5},{8,10},{10,8},{9,1... | collective-permute-start | bytes 98312 | tf_op jit(solution)/shard_map/ppermute | solution.py:544
  12.8 6.9 %collective-permute-start.6 = (f32[4,64,256]{2,1,0:T(8,128)S(1)}, f32[4,64,256]{2,1,0:T(8,128)S(1)}, u32[]{:S(2)}, u32[]{:S(2)}) collective-permute-start(f32[4,64,256]{2,1,0:T(8,128)S(1)} %get-tuple-element.47.refs_0_.refs_1_), channel_id=1, source_target_pairs={{0,1},{1,0},{2,3},{3,2},{4,5},{5,4},{6,7},{7,6},{8,9},{9,8},{10,11... | collective-permute-start | bytes 786440 | tf_op jit(solution)/shard_map/ppermute | solution.py:528
  13.0 6.8 %collective-permute-start.8 = (f32[4,8,256]{2,1,0:T(8,128)S(1)}, f32[4,8,256]{2,1,0:T(8,128)S(1)}, u32[]{:S(2)}, u32[]{:S(2)}) collective-permute-start(f32[4,8,256]{2,1,0:T(8,128)S(1)} %get-tuple-element.54), channel_id=1, source_target_pairs={{0,2},{2,0},{1,3},{3,1},{4,6},{6,4},{5,7},{7,5},{8,10},{10,8},{9,1... | collective-permute-start | bytes 98312 | tf_op jit(solution)/shard_map/ppermute | solution.py:544
  14.8 5.0 %collective-permute-start.7 = (bf16[4,64,256]{2,1,0:T(8,128)(2,1)S(1)}, bf16[4,64,256]{2,1,0:T(8,128)(2,1)S(1)}, u32[]{:S(2)}, u32[]{:S(2)}) collective-permute-start(bf16[4,64,256]{2,1,0:T(8,128)(2,1)S(1)} %get-tuple-element.48), channel_id=1, source_target_pairs={{1,5},{5,1},{4,8},{8,4},{9,13},{13,9},{0,2},{12,14},{3,7},{7,3},{6... | collective-permute-start | bytes 393224 | tf_op jit(solution)/shard_map/ppermute | solution.py:542
  17.3 12.4 %copy-start = (bf16[256,128]{1,0:T(8,128)(2,1)S(1)}, bf16[256,128]{1,0:T(8,128)(2,1)}, u32[]{:S(2)}) copy-start(bf16[256,128]{1,0:T(8,128)(2,1)} %constant.30.clone.refs_3_.table_z) | copy-start | bytes 196612
  20.8 5.8 %collective-permute-start.9 = (f32[4,64,256]{2,1,0:T(8,128)S(1)}, f32[4,64,256]{2,1,0:T(8,128)S(1)}, u32[]{:S(2)}, u32[]{:S(2)}) collective-permute-start(f32[4,64,256]{2,1,0:T(8,128)S(1)} %get-tuple-element.55.refs_0_.refs_1_), channel_id=1, source_target_pairs={{0,1},{1,0},{2,3},{3,2},{4,5},{5,4},{6,7},{7,6},{8,9},{9,8},{10,11... | collective-permute-start | bytes 786440 | tf_op jit(solution)/shard_map/ppermute | solution.py:528
  20.8 5.7 %collective-permute-start.10 = (bf16[4,64,256]{2,1,0:T(8,128)(2,1)S(1)}, bf16[4,64,256]{2,1,0:T(8,128)(2,1)S(1)}, u32[]{:S(2)}, u32[]{:S(2)}) collective-permute-start(bf16[4,64,256]{2,1,0:T(8,128)(2,1)S(1)} %get-tuple-element.56), channel_id=1, source_target_pairs={{1,5},{5,1},{4,8},{8,4},{9,13},{13,9},{0,2},{12,14},{3,7},{7,3},{6... | collective-permute-start | bytes 393224 | tf_op jit(solution)/shard_map/ppermute | solution.py:542
  21.3 5.3 %collective-permute-start.11 = (f32[4,8,256]{2,1,0:T(8,128)S(1)}, f32[4,8,256]{2,1,0:T(8,128)S(1)}, u32[]{:S(2)}, u32[]{:S(2)}) collective-permute-start(f32[4,8,256]{2,1,0:T(8,128)S(1)} %get-tuple-element.57), channel_id=1, source_target_pairs={{0,2},{2,0},{1,3},{3,1},{4,6},{6,4},{5,7},{7,5},{8,10},{10,8},{9,1... | collective-permute-start | bytes 98312 | tf_op jit(solution)/shard_map/ppermute | solution.py:544
  27.6 2.2 %collective-permute-start.12 = (f32[4,64,256]{2,1,0:T(8,128)S(1)}, f32[4,64,256]{2,1,0:T(8,128)S(1)}, u32[]{:S(2)}, u32[]{:S(2)}) collective-permute-start(f32[4,64,256]{2,1,0:T(8,128)S(1)} %get-tuple-element.58.own.refs_0_.q_ref), channel_id=1, source_target_pairs={{0,1},{1,0},{2,3},{3,2},{4,5},{5,4},{6,7},{7,6},{8,9},{9,8},{10,11... | collective-permute-start | bytes 786440 | tf_op jit(solution)/shard_map/ppermute | solution.py:528
  27.6 5.3 %collective-permute-start.13 = (bf16[4,64,256]{2,1,0:T(8,128)(2,1)S(1)}, bf16[4,64,256]{2,1,0:T(8,128)(2,1)S(1)}, u32[]{:S(2)}, u32[]{:S(2)}) collective-permute-start(bf16[4,64,256]{2,1,0:T(8,128)(2,1)S(1)} %get-tuple-element.59), channel_id=1, source_target_pairs={{1,5},{5,1},{4,8},{8,4},{9,13},{13,9},{0,2},{12,14},{3,7},{7,3},{6... | collective-permute-start | bytes 393224 | tf_op jit(solution)/shard_map/ppermute | solution.py:542
  28.1 5.2 %collective-permute-start.14 = (f32[4,8,256]{2,1,0:T(8,128)S(1)}, f32[4,8,256]{2,1,0:T(8,128)S(1)}, u32[]{:S(2)}, u32[]{:S(2)}) collective-permute-start(f32[4,8,256]{2,1,0:T(8,128)S(1)} %get-tuple-element.61), channel_id=1, source_target_pairs={{0,2},{2,0},{1,3},{3,1},{4,6},{6,4},{5,7},{7,5},{8,10},{10,8},{9,1... | collective-permute-start | bytes 98312 | tf_op jit(solution)/shard_map/ppermute | solution.py:544
  35.4 1.3 %collective-permute-start.15 = (bf16[1,4,32,128]{3,2,1,0:T(8,128)(2,1)S(1)}, bf16[1,4,32,128]{3,2,1,0:T(8,128)(2,1)S(1)}, u32[]{:S(2)}, u32[]{:S(2)}) collective-permute-start(bf16[1,4,32,128]{3,2,1,0:T(8,128)(2,1)S(1)} %get-tuple-element.65), channel_id=1, source_target_pairs={{0,1},{1,0},{2,3},{3,2},{4,5},{5,4},{6,7},{7,6},{8,9},{9,8},{10,11... | collective-permute-start | bytes 98312 | tf_op jit(solution)/shard_map/ppermute | solution.py:528
  36.7 5.6 %collective-permute-start.16 = (bf16[4,4,32,128]{3,2,1,0:T(8,128)(2,1)S(1)}, bf16[4,4,32,128]{3,2,1,0:T(8,128)(2,1)S(1)}, u32[]{:S(2)}, u32[]{:S(2)}) collective-permute-start(bf16[4,4,32,128]{3,2,1,0:T(8,128)(2,1)S(1)} %fusion), channel_id=1, source_target_pairs={{0,2},{2,0},{1,3},{3,1},{4,6},{6,4},{5,7},{7,5},{8,10},{10,8},{9,1... | collective-permute-start | bytes 393224 | tf_op jit(solution)/shard_map/ppermute | solution.py:531
  37.3 5.5 %collective-permute-start.18 = (f32[4,64,256]{2,1,0:T(8,128)S(1)}, f32[4,64,256]{2,1,0:T(8,128)S(1)}, u32[]{:S(2)}, u32[]{:S(2)}) collective-permute-start(f32[4,64,256]{2,1,0:T(8,128)S(1)} %shard_map.210.own.p_ref.wave_ref), channel_id=1, source_target_pairs={{0,1},{1,0},{2,3},{3,2},{4,5},{5,4},{6,7},{7,6},{8,9},{9,8},{10,11... | collective-permute-start | bytes 786440 | tf_op jit(solution)/shard_map/ppermute | solution.py:528
  42.4 5.0 %collective-permute-start.17 = (bf16[4,4,32,128]{3,2,1,0:T(8,128)(2,1)S(1)}, bf16[4,4,32,128]{3,2,1,0:T(8,128)(2,1)S(1)}, u32[]{:S(2)}, u32[]{:S(2)}) collective-permute-start(bf16[4,4,32,128]{3,2,1,0:T(8,128)(2,1)S(1)} %fusion.2), channel_id=1, source_target_pairs={{0,4},{4,0},{8,12},{12,8},{1,5},{5,1},{9,13},{13,9},{2,6},{6,2},{1... | collective-permute-start | bytes 393224 | tf_op jit(solution)/shard_map/ppermute | solution.py:531
  47.5 6.9 %collective-permute-start.19 = (bf16[4,4,32,128]{3,2,1,0:T(8,128)(2,1)S(1)}, bf16[4,4,32,128]{3,2,1,0:T(8,128)(2,1)S(1)}, u32[]{:S(2)}, u32[]{:S(2)}) collective-permute-start(bf16[4,4,32,128]{3,2,1,0:T(8,128)(2,1)S(1)} %fusion.1), channel_id=1, source_target_pairs={{0,12},{4,8},{8,4},{12,0},{1,13},{5,9},{9,5},{13,1},{2,14},{6,10},... | collective-permute-start | bytes 393224 | tf_op jit(solution)/shard_map/ppermute | solution.py:531
  54.6 1.4 %collective-permute-start.20 = (bf16[4,4,32,128]{3,2,1,0:T(8,128)(2,1)S(1)}, bf16[4,4,32,128]{3,2,1,0:T(8,128)(2,1)S(1)}, u32[]{:S(2)}, u32[]{:S(2)}) collective-permute-start(bf16[4,4,32,128]{3,2,1,0:T(8,128)(2,1)S(1)} %get-tuple-element.76), channel_id=1, source_target_pairs={{0,1},{1,0},{2,3},{3,2},{4,5},{5,4},{6,7},{7,6},{8,9},{9,8},{10,11... | collective-permute-start | bytes 393224 | tf_op jit(solution)/shard_map/ppermute | solution.py:528
  (5 other events, 53.9 us)

commit v8 on v7

--- a/solution.py
+++ b/solution.py
@@ -48,6 +48,26 @@
         compiler_params=pltpu.CompilerParams(vmem_limit_bytes=16 * 1024 * 1024),
         cost_estimate=pl.CostEstimate(flops=flops, bytes_accessed=moved, transcendentals=0),
     )
+
+
+def begin(sources, targets, semaphores):
+    copies = [
+        pltpu.make_async_copy(source, target, semaphores.at[index])
+        for index, (source, target) in enumerate(zip(sources, targets))
+    ]
+    for copy in copies:
+        copy.start()
+    return copies
+
+
+def here(*arrays):
+    return [pltpu.with_memory_space_constraint(jnp.asarray(array), pltpu.HBM) for array in arrays]
+
+
+def room(*arrays):
+    return [(pltpu.SMEM if array.ndim == 1 else pltpu.VMEM)(array.shape, array.dtype) for array in arrays] + [
+        pltpu.SemaphoreType.DMA((len(arrays),))
+    ]
 
 
 def high_low(value):
@@ -172,7 +192,7 @@
         edges(lambda a, b: new_ref[:, a:b, :], edge_outs, parity, brick_y)
 
 
-def transformed(sources, first, twiddle_x, table_z, table_y, lines, grid):
+def transformed(sources, first, twiddle_x, table_z, table_y, lines, grid, late=()):
     column = lax.axis_index("gy")
     brick_y = lines.shape[0] // 4
     modes_y = grid.shape[0]
@@ -190,6 +210,8 @@
             for index, part in enumerate((high, back_high, low, back_low)):
                 lines[index * brick_y : (index + 1) * brick_y, lanes] = part
     grid[...] = jnp.dot(table_y[column], lines[...], preferred_element_type=F32)
+    for copy in late:
+        copy.wait()
 
     def at_mode(field, modes_x):
         count = len(sources[field])
@@ -211,17 +233,11 @@
 
 
 def materials_body(*refs):
-    sources, cells, keep, lines, grid = refs[:5], refs[5], refs[6], refs[7], refs[8]
-    targets, semaphores = refs[9:14], refs[14]
-    copies = [
-        pltpu.make_async_copy(source, target, semaphores.at[index])
-        for index, (source, target) in enumerate(zip(sources, targets))
-    ]
-    for copy in copies:
-        copy.start()
+    sources, cells, keep, table_z, table_y, lines, grid = refs[:5], *refs[5:11]
+    twiddle_x, stiffness, density, semaphores = refs[11:15]
+    copies = begin(sources, (twiddle_x, stiffness, density, table_z, table_y), semaphores)
     for copy in copies:
         copy.wait()
-    twiddle_x, stiffness, density, table_z, table_y = targets
     half_x = keep.shape[1]
     entries = stiffness.shape[0]
     rows = cells.shape[0]
@@ -242,14 +258,15 @@
             keep[field, mode] = summed(core * half_x + mode)
 
 
-def prior_body(twiddle_x, own, mate, table_z, table_y, keep, lines, grid):
+def prior_body(twiddles, own, mate, table_z, table_y, keep, lines, grid, twiddle_x, semaphores):
+    copies = begin((twiddles,), (twiddle_x,), semaphores)
     half_x = keep.shape[0]
     rows = own.shape[0]
     place = slot()
     sources = [
         (lambda row=row: jnp.where(place == 0, own[row], mate[row])) for row in range(rows)
     ] + [(lambda row=row: jnp.where(place == 0, mate[row], own[row])) for row in range(rows)]
-    at_mode = transformed([sources], lax.axis_index("gx") * (2 * rows), twiddle_x, table_z, table_y, lines, grid)
+    at_mode = transformed([sources], lax.axis_index("gx") * (2 * rows), twiddle_x, table_z, table_y, lines, grid, copies)
     core = lax.axis_index("gz")
     summed = at_mode(0, 2 * half_x)
 
@@ -258,12 +275,13 @@
         keep[mode] = summed(core * half_x + mode)
 
 
-def wave_body(twiddle_x, own, prior, early, table_z, table_y, keep, send, lines, grid):
+def wave_body(twiddles, own, prior, early, table_z, table_y, keep, send, lines, grid, twiddle_x, semaphores):
+    copies = begin((twiddles,), (twiddle_x,), semaphores)
     half_x = keep.shape[1]
     rows = own.shape[0]
     first = (lax.axis_index("gx") * 2 + slot()) * rows
     sources = [(lambda row=row: own[row]) for row in range(rows)]
-    at_mode = transformed([sources], first, twiddle_x, table_z, table_y, lines, grid)
+    at_mode = transformed([sources], first, twiddle_x, table_z, table_y, lines, grid, copies)
     core = lax.axis_index("gz")
     summed = at_mode(0, 2 * half_x)
     keep[1] = prior[...]
@@ -275,11 +293,14 @@
         send[0, mode] = summed((1 - core) * half_x + mode).astype(BF16)
 
 
-def prepare_body(
-    stiffness, density, mode_ref, lift_ref, bias_ref, local_ref, spread_ref, place_ref, owner_ref, turn_ref,
-    wide_ref, mixing, pointwise, lift_table, offset,
-):
+def prepare_body(*refs):
+    sources, outs, targets, semaphores = refs[:11], refs[11:15], refs[15:26], refs[26]
+    mixing, pointwise, lift_table, offset = outs
     block = lax.axis_index("gx") * 2 + lax.axis_index("gz")
+    copies = begin([*sources[:9], sources[9].at[block], sources[10]], targets, semaphores)
+    for copy in copies:
+        copy.wait()
+    stiffness, density, mode_ref, lift_ref, bias_ref, local_ref, spread_ref, place_ref, owner_ref, turn_ref, wide_ref = targets
     half = place_ref.shape[1]
     channels = lift_ref.shape[1]
     spread = owner_ref[...]
@@ -290,13 +311,19 @@
     across = ((1,), (1,))
     lifted = dot(dot(spread_ref[:, :channels], lift_ref[...], across), place_ref[...])
     lifted = lifted * spread_ref[:, channels : channels + half]
-    real = dot(dot(spread, mode_ref[0], across), lifted)
-    imag = dot(dot(spread, mode_ref[1], across), lifted)
-    cosine = turn_ref[block, 0]
-    sine = turn_ref[block, 1]
+    flat = [mode_ref[index].reshape(-1, channels) for index in range(2)]
+    real, imag = [dot(dot(spread, values, across), lifted) for values in flat]
+    cosine = turn_ref[0]
+    sine = turn_ref[1]
     coupled = jnp.concatenate([cosine * real - sine * imag, -(cosine * imag + sine * real)], axis=1)
-    mixing[...] = coupled.astype(BF16)
-    constant = dot(spread, mode_ref[0, 0:channels, :], across)
+    width = 2 * half
+    blocks = mixing.shape[0]
+    for index in range(blocks):
+        parts = [jnp.zeros((coupled.shape[0], width * index), F32)] * (index > 0) + [coupled]
+        parts += [jnp.zeros((coupled.shape[0], width * (blocks - 1 - index)), F32)] * (index < blocks - 1)
+        line = jnp.concatenate(parts, axis=1) if blocks > 1 else coupled
+        mixing[index] = line.astype(BF16)
+    constant = dot(spread, mode_ref[0, :, 0, :], across)
     bias = bias_ref[...] + middle(stiffness) * lift_ref[2:3, :] + middle(density) * lift_ref[3:4, :]
     offset[...] = jnp.sum(constant * bias, axis=1, keepdims=True)
     height = spread.shape[0]
@@ -309,7 +336,8 @@
     lift_table[:, FIELDS + 1 :] = jnp.zeros_like(lift_table[:, FIELDS + 1 :])
 
 
-def pointwise_body(stiffness, density, p_ref, q_ref, p_mate, q_mate, cells, lift_ref, left, offset, out, right):
+def pointwise_body(stiffness_in, density_in, p_ref, q_ref, p_mate, q_mate, cells, lift_ref, left, offset, *rest):
+    out, right, stiffness, density, semaphores = rest[-5:]
     rows, group, depth = p_ref.shape
     padded_channels = lift_ref.shape[0]
     height = rows * padded_channels
@@ -320,6 +348,8 @@
     @pl.when(pl.program_id(0) == 0)
     def _():
         right[...] = jnp.zeros_like(right)
+        for copy in begin((stiffness_in, density_in), (stiffness, density), semaphores):
+            copy.wait()
 
     weights = [lift_ref[:, index : index + 1] for index in range(FIELDS + 1)]
     values = []
@@ -342,9 +372,18 @@
         out[:, y, :] = jnp.dot(left[...], right[y], preferred_element_type=F32) + offset[...]
 
 
+def join_body(own, other, wave_out):
+    core = lax.axis_index("gz")
+    rows, _, depth = own.shape
+    half = depth // 2
+    place = slot()
+    for row in range(rows):
+        for ref, start in ((own, place * rows), (other, (1 - place) * rows)):
+            wave_out[start + row] = jnp.where(core == 0, ref[row, :, :half], ref[row, :, half:])
+
+
 def output_body(
-    mine, other, local_low, local_high, left, table_y, table_z, wave_ref, wave_other,
-    features, wave_out, modes, right, sums,
+    mine, other, local, left, table_y, table_z, features, modes, right, sums,
 ):
     step = pl.program_id(0)
     core, column = lax.axis_index("gz"), lax.axis_index("gy")
@@ -356,7 +395,7 @@
 
     @pl.when(step == 0)
     def _():
-        chunk = 4
+        chunk = min(8, modes_x)
         left_y = table_y[column]
         for field in range(FIELDS):
             for start in range(0, modes_x, chunk):
@@ -371,26 +410,31 @@
                 for mode in range(start, start + chunk):
                     lanes = slice((mode - start) * width, (mode - start + 1) * width)
                     modes[:, mode * FIELDS + field, :] = result[:, lanes]
-        z_half = depth // 2
-        place = slot()
-        for row in range(rows):
-            for ref, start in ((wave_ref, place * rows), (wave_other, (1 - place) * rows)):
-                wave_out[start + row] = jnp.where(core == 0, ref[row, :, :z_half], ref[row, :, z_half:])
 
     base = pl.multiple_of(step * group, group)
     lines = modes[pl.ds(base, group)].reshape(group * coupled, width).astype(BF16)
     waves = jnp.dot(lines, table_z[...], preferred_element_type=F32).astype(BF16)
+    joined, height = left.shape[:2]
     for y in range(group):
         lines = slice(y * coupled, (y + 1) * coupled)
-        right[y, 0:coupled, :] = waves[lines, :depth]
-        right[y, coupled:, :] = waves[lines, depth:]
-        sums[:, y, :] = jnp.dot(left[...], right[y], preferred_element_type=F32)
+        start = y * 2 * coupled
+        right[start : start + coupled, :] = waves[lines, :depth]
+        right[start + coupled : start + 2 * coupled, :] = waves[lines, depth:]
+    span = joined * 2 * coupled
+    every = left[...].reshape(joined * height, span)
+    for first in range(0, group, joined):
+        start = first * 2 * coupled
+        result = jnp.dot(every, right[start : start + span, :], preferred_element_type=F32)
+        for index in range(joined):
+            sums[:, first + index, :] = result[index * height : (index + 1) * height]
     for row in range(rows):
         for channel in range(channels):
             at = row * channels + channel
-            total = sums[at] + jnp.where(step < pl.num_programs(0) // 2, local_low[at], local_high[at])
-            inner = math.sqrt(2.0 / math.pi) * (total + 0.044715 * (total * total * total))
-            total = (0.5 * total) * (1.0 + jnp.tanh(inner))
+            total = sums[at] + local[at, pl.ds(base, group), :]
+            scale = math.sqrt(2.0 / math.pi)
+            inner = total * (scale + (scale * 0.044715) * (total * total))
+            part = 0.5 * total
+            total = part + part * jnp.tanh(inner)
             features[row, channel] = total.astype(BF16)
 
 
@@ -445,6 +489,7 @@
     padded_channels = -(-channels // 8) * 8
     height = rows * channels
     coupled = FIELDS * modes_x
+    joined = max(1, 256 // (2 * coupled))
     right_depth = -(-rows * padded_channels // 128) * 128
     two_sided = column_count > 2
 
@@ -479,10 +524,8 @@
         np.eye(rows), np.ones((channels, padded_channels))
     )
     wide[channels + height :, :channels] = padded_eye.T
-    spread = np.tile(np.eye(channels, dtype=np.float32), (modes_x, 1))
-    same = np.repeat(
-        np.repeat(np.eye(modes_x, dtype=np.float32), channels, 0), FIELDS, 1
-    )
+    spread = np.repeat(np.eye(channels, dtype=np.float32), modes_x, 0)
+    same = np.tile(np.repeat(np.eye(modes_x, dtype=np.float32), FIELDS, 1), (channels, 1))
     spread = np.concatenate([spread, same], 1)
     place = np.tile(np.eye(FIELDS, dtype=np.float32), (1, modes_x))
 
@@ -496,7 +539,6 @@
     swap_core = xor_pairs(core_count, 1)
     got = [lax.ppermute(array, "gz", swap_core) for array in (pressure, previous, material)]
     sending = shape(rows, brick_y, total_z, dtype=BF16)
-    here = lambda *arrays: [pltpu.with_memory_space_constraint(array, pltpu.HBM) for array in arrays]
     current, before, ratio, bend, sent, cells, *edge_values = call(
         lambda *refs: assemble_body(len(edge), *refs),
         [field] * 4 + [sending, shape(brick_x, brick_y, total_z, dtype=jnp.int32)] + edge, [HBM] * 6 + [VMEM] * 3,
@@ -504,21 +546,22 @@
         + [pltpu.VMEM((brick_x, brick_y, brick_z), jnp.int32), pltpu.SemaphoreType.DMA((6,))], moved=cells_count * 36
     )(*here(stiffness, density, nonlinear, pressure, previous, material), *got)
 
+    weights = (
+        stiffness, density, mode_weight.transpose(0, 2, 1, 3), lift_weight, lift_bias.reshape(1, channels),
+        local_weight, spread, place, owner, turn, wide,
+    )
     mixing, pointwise, lift_table, offset = call(
         prepare_body,
-        [shape(height, 2 * coupled, dtype=BF16), shape(height, right_depth, dtype=BF16),
+        [shape(joined, height, joined * 2 * coupled, dtype=BF16), shape(height, right_depth, dtype=BF16),
          shape(padded_channels, 8), shape(height, 1)],
-        [SMEM] * 2 + [VMEM] * 9, flops=2_000_000_000, moved=4_000_000,
-    )(
-        stiffness, density, mode_weight.reshape(2, modes_x * channels, channels), lift_weight,
-        lift_bias.reshape(1, channels), local_weight, spread, place, owner, turn, wide,
-    )
+        [HBM] * 11, room(*weights[:9], turn[0], wide), flops=2_000_000_000, moved=4_000_000,
+    )(*here(*weights))
 
     part = lambda fields, dtype: shape(fields, modes_x // 2, modes_y, width, dtype=dtype)
 
     def spectrum(body, outs, inputs, lines, specs=None, scratch=()):
         return call(
-            body, outs, specs or [SMEM] + [VMEM] * (inputs + 2),
+            body, outs, specs or [HBM] + [VMEM] * (inputs + 2),
             [pltpu.VMEM((4 * brick_y, lines * width), BF16), pltpu.VMEM((modes_y, lines * width), F32), *scratch],
             flops=cells_count * 256 * lines, moved=cells_count * 2 * lines,
         )
@@ -531,11 +574,13 @@
         return lax.ppermute(value.astype(BF16), axis, xor_pairs(count, distance))
 
     tables = (twiddle_x, stiffness, density, forward_z, forward_y)
-    early = spectrum(
-        materials_body, part(2, F32), 1, 2 * brick_x, [HBM] * 5 + [VMEM],
-        [(pltpu.SMEM if table.ndim == 1 else pltpu.VMEM)(table.shape, table.dtype) for table in tables]
-        + [pltpu.SemaphoreType.DMA((5,))],
-    )(*here(*[jnp.asarray(table) for table in tables]), cells)
+    early, forward_z, forward_y = spectrum(
+        materials_body,
+        [part(2, F32)] + [jax.ShapeDtypeStruct(table.shape, table.dtype) for table in (forward_z, forward_y)],
+        1, 2 * brick_x, [HBM] * 5 + [VMEM], room(*tables[:3])[:3] + [pltpu.SemaphoreType.DMA((5,))],
+    )(*here(*tables), cells)
+    twiddles = here(twiddle_x)
+    twiddle_room = room(twiddle_x)
 
     for repeat in range(STEPS):
         last = repeat == STEPS - 1
@@ -551,8 +596,8 @@
                 (far, mixing, pointwise, lift_table, offset)
             )
         if last:
-            prior = spectrum(prior_body, shape(modes_x // 2, modes_y, width), 2, brick_x)(
-                twiddle_x, current, mate, forward_z, forward_y
+            prior = spectrum(prior_body, shape(modes_x // 2, modes_y, width), 2, brick_x, None, twiddle_room)(
+                *twiddles, current, mate, forward_z, forward_y
             )
             far, prior = lax.optimization_barrier((far, prior))
             prior_mate = mate
@@ -566,8 +611,8 @@
             sent, *edge_values = others
         current, before = new, current
 
-    total, sent = spectrum(wave_body, [part(FIELDS, F32), part(1, BF16)], 3, rows)(
-        twiddle_x, current, prior, early, forward_z, forward_y
+    total, sent = spectrum(wave_body, [part(FIELDS, F32), part(1, BF16)], 3, rows, None, twiddle_room)(
+        *twiddles, current, prior, early, forward_z, forward_y
     )
     total = total + jnp.pad(swap(sent).astype(F32), ((0, FIELDS - 1), (0, 0), (0, 0), (0, 0)))
     wave_other = swap(current)
@@ -575,48 +620,49 @@
     steps = brick_y // group
     whole = lambda array: pl.BlockSpec(array.shape, lambda i: (0,) * len(array.shape))
 
-    def pointwise_part(start):
+    def pointwise_part(start, held=()):
         slab = lambda count: pl.BlockSpec((count, group, total_z), lambda i: (0, i + start, 0))
         return pl.pallas_call(
             pointwise_body,
             grid=(steps // 2,),
-            out_shape=shape(height, brick_y // 2, total_z),
-            in_specs=[SMEM] * 2 + [slab(rows)] * 4 + [slab(brick_x), whole(lift_table), whole(pointwise), whole(offset)],
-            out_specs=pl.BlockSpec((height, group, total_z), lambda i: (0, i, 0)),
-            scratch_shapes=[pltpu.VMEM((group, right_depth, total_z), BF16)],
+            out_shape=shape(height, brick_y, total_z),
+            in_specs=[HBM] * 2 + [slab(rows)] * 4 + [slab(brick_x), whole(lift_table), whole(pointwise), whole(offset)]
+            + [pl.BlockSpec(memory_space=pl.ANY)] * len(held),
+            out_specs=pl.BlockSpec((height, group, total_z), lambda i: (0, i + start, 0)),
+            input_output_aliases={10: 0} if held else {},
+            scratch_shapes=[pltpu.VMEM((group, right_depth, total_z), BF16)] + room(stiffness, density),
             compiler_params=pltpu.CompilerParams(vmem_limit_bytes=16 * 1024 * 1024),
             cost_estimate=pl.CostEstimate(flops=cells_count * 20000, bytes_accessed=cells_count * 50, transcendentals=0),
-        )(stiffness, density, current, before, wave_other, prior_mate, cells, lift_table, pointwise, offset)
+        )(*here(stiffness, density), current, before, wave_other, prior_mate, cells, lift_table, pointwise, offset, *held)
 
     for index, stage in enumerate(stages):
         arrived = exchange(total, *stage)
         if index == len(stages) - 2:
-            local_low = pointwise_part(0)
-            arrived, local_low = lax.optimization_barrier((arrived, local_low))
+            local = pointwise_part(0)
+            wave = call(join_body, shape(*pressure.shape), [VMEM] * 2, moved=cells_count * 12)(current, wave_other)
+            arrived, local, wave = lax.optimization_barrier((arrived, local, wave))
         if index == len(stages) - 1:
-            local_high = pointwise_part(steps // 2)
-            arrived, local_high = lax.optimization_barrier((arrived, local_high))
+            local = pointwise_part(steps // 2, (local,))
+            arrived, local = lax.optimization_barrier((arrived, local))
         total = total + arrived.astype(F32)
     other = swap(total.astype(BF16))
-    scoped = 12 * 2**20 + 4 * (6 * 2 * modes_x * modes_y * width + brick_y * coupled * width + 6 * group * coupled * total_z)
-    features, wave = pl.pallas_call(
+    batch = min(32, brick_y)
+    scoped = 14 * 2**20 + 4 * (brick_y * coupled * width + 6 * batch * coupled * total_z)
+    features = pl.pallas_call(
         output_body,
-        grid=(steps,),
-        out_shape=[shape(rows, channels, brick_y, total_z, dtype=BF16), shape(*pressure.shape)],
-        in_specs=[whole(part(FIELDS, F32)), whole(part(FIELDS, BF16)),
-           pl.BlockSpec((height, group, total_z), lambda i: (0, jnp.minimum(i, steps // 2 - 1), 0)),
-           pl.BlockSpec((height, group, total_z), lambda i: (0, jnp.maximum(i - steps // 2, 0), 0)),
-           whole(mixing), whole(inverse_y), whole(inverse_z),
-                  whole(field), whole(field)],
-        out_specs=[pl.BlockSpec((rows, channels, group, total_z), lambda i: (0, 0, i, 0)), whole(pressure)],
+        grid=(brick_y // batch,),
+        out_shape=shape(rows, channels, brick_y, total_z, dtype=BF16),
+        in_specs=[VMEM, VMEM,
+                  VMEM, VMEM, VMEM, VMEM],
+        out_specs=pl.BlockSpec((rows, channels, batch, total_z), lambda i: (0, 0, i, 0)),
         scratch_shapes=[
             pltpu.VMEM((brick_y, coupled, width), F32),
-            pltpu.VMEM((group, 2 * coupled, total_z), BF16),
-            pltpu.VMEM((height, group, total_z), F32),
+            pltpu.VMEM((batch * 2 * coupled, total_z), BF16),
+            pltpu.VMEM((height, batch, total_z), F32),
         ],
         compiler_params=pltpu.CompilerParams(vmem_limit_bytes=scoped),
         cost_estimate=pl.CostEstimate(flops=cells_count * 2000, bytes_accessed=cells_count * 60, transcendentals=cells_count * 20),
-    )(total, other, local_low, local_high, mixing, inverse_y, inverse_z, current, wave_other)
+    )(total, other, local, mixing, inverse_y, inverse_z)
     features = features.transpose(0, 2, 1, 3)
     return (wave, features)
 

time: 64.4 us -> 61.5 us (0.955)
  waiting for transfers between devices: 21.3 us -> 18.4 us
  starting transfers between devices: 14.4 us -> 15.2 us
    ppermute x4, starting transfers between devices: 5.2 us -> 1.26 us  [per_device(): halos = [lax.ppermute(edge_values[0], 'gy', xor_pairs(column_count, 1))]]
    ppermute x4, starting transfers between devices: 3.72 us -> 7.6 us  [per_device(): lax.ppermute(sent, ('gx', 'gy', 'gz'), row_pairs(cycle_count, column_count))]
    ppermute x4, waiting for transfers between devices: 4.93 us -> 3.31 us  [per_device(): lax.ppermute(sent, ('gx', 'gy', 'gz'), row_pairs(cycle_count, column_count))]
    ppermute x3, waiting for transfers between devices: 7.37 us -> 5.8 us  [exchange(): return lax.ppermute(value.astype(BF16), axis, xor_pairs(count, distance))]
    pallas_call x5 -> x6, Pallas kernels: 15.3 us -> 14.5 us  [the longest x1 6.5 us: per_device(): pl.pallas_call(output_body, grid=(brick_y // batch,), out_shape=shape(row...]
  transfers between devices with their start and end apart: 21 -> 21, of which waited for: 14 -> 15; matrix products, arithmetic and copies ran while one was open for 0% -> 0% of each run, Pallas kernels for 19% -> 23%
where the time goes in v8:
time: 61.5 us; the launch traced here: 61.2 us
  Pallas kernels  26.6 us (43%)
  waiting for transfers between devices  18.4 us (30%)
  starting transfers between devices  15.2 us (25%)
  between operations  0.8 us (1%)
    ppermute x4, starting transfers between devices, per_device(): lax.ppermute(sent, ('gx', 'gy', 'gz'), row_pairs(cycle_count, column_count))  7.6 us
    pallas_call x2, Pallas kernels, pointwise_part(): pl.pallas_call(pointwise_body, grid=(steps // 2,), out_shape=shape(height...  6.78 us
    pallas_call x1, Pallas kernels, per_device(): pl.pallas_call(output_body, grid=(brick_y // batch,), out_shape=shape(row...  6.5 us
    ppermute x3, waiting for transfers between devices, exchange(): return lax.ppermute(value.astype(BF16), axis, xor_pairs(count, distance))  5.8 us
    ppermute x4, waiting for transfers between devices, per_device(): halos = [lax.ppermute(edge_values[0], 'gy', xor_pairs(column_count, 1))]  5.18 us
    ppermute x3, starting transfers between devices, exchange(): return lax.ppermute(value.astype(BF16), axis, xor_pairs(count, distance))  4.25 us
    pallas_call x4, Pallas kernels, per_device(): call(body, outs, [VMEM] * (6 + len(halos)), [pltpu.VMEM((brick_y + 2 * ED...  3.89 us
    ppermute x4, waiting for transfers between devices, per_device(): lax.ppermute(sent, ('gx', 'gy', 'gz'), row_pairs(cycle_count, column_count))  3.31 us
  transfers between devices with their start and end apart: 21, of which 15 were waited for; matrix products, arithmetic and copies ran while one was open for 0% of the time, Pallas kernels for 23%

profile of v8, /device:TPU:0, one launch (start us, length us, event | category | flops | bytes accessed | tf_op | source)
XLA Modules:
  0.0 61.2 jit_solution(2207910955985847136)
XLA Ops:
  0.6 0.5 collective-permute-start
  1.7 0.9 %collective-permute-done.refs_6_ = f32[8,64,128]{2,1,0:T(8,128)S(1)} collective-permute-done((f32[8,64,128]{2,1,0:T(8,128)}, f32[8,64,128]{2,1,0:T(8,128)S(1)}, u32[]{:S(2)}, u32[]{:S(2)}) %collective-permute-start) | collective-permute-done | bytes 262176 | tf_op jit(solution)/shard_map/ppermute | solution.py:540
  3.3 1.5 %shard_map.203 = (f32[4,64,256]{2,1,0:T(8,128)S(1)}, f32[4,64,256]{2,1,0:T(8,128)S(1)}, f32[4,64,256]{2,1,0:T(8,128)S(1)}, f32[4,64,256]{2,1,0:T(8,128)S(1)}, bf...) custom-call(f32[8]{0:T(128)} %stiffness_in.3, f32[8]{0:T(128)} %density_in.3, ...), custom_call_target="tpu_custom_call" | custom-call | bytes 2359296 | tf_op jit(solution)/shard_map/pallas_call | solution.py:542
  4.7 0.4 collective-permute-start.3
  5.2 2.6 %collective-permute-start.4 = (bf16[4,64,256]{2,1,0:T(8,128)(2,1)S(1)}, bf16[4,64,256]{2,1,0:T(8,128)(2,1)S(1)}, u32[]{:S(2)}, u32[]{:S(2)}) collective-permute-start(bf16[4,64,256]{2,1,0:T(8,128)(2,1)S(1)} %get-tuple-element.45), channel_id=1, source_target_pairs={{1,5},{5,1},{4,8},{8,4},{9,13},{13,9},{0,2},{12,14},{3,7},{7,3},{6... | collective-permute-start | bytes 393224 | tf_op jit(solution)/shard_map/ppermute | solution.py:587
  7.8 2.3 %shard_map.204 = (f32[2,4,32,128]{3,2,1,0:T(8,128)S(1)}, bf16[256,128]{1,0:T(8,128)(2,1)S(1)}, bf16[2,32,256]{2,1,0:T(8,128)(2,1)S(1)}) custom-call(f32[512]{0:T(512)} %constant.29.clone.refs_0_.twiddles, f32[8]{0:T(128)} %stiffness_in.3, f32[8]{0:T(128)} %density_in.3, bf16[256,128]{1,0:T(8,128)(2,1)} %constant.30.clone.refs_3_, ...), custom_call_target="tpu_custom_call" | custom-call | flops 268435456 | bytes 2097152 | tf_op jit(solution)/shard_map/pallas_call | solution.py:577
  10.2 0.7 %collective-permute-done.4.refs_5_ = bf16[4,64,256]{2,1,0:T(8,128)(2,1)S(1)} collective-permute-done((bf16[4,64,256]{2,1,0:T(8,128)(2,1)S(1)}, bf16[4,64,256]{2,1,0:T(8,128)(2,1)S(1)}, u32[]{:S(2)}, u32[]{:S(2)}) %collective-permute-start.4) | collective-permute-done | bytes 131104 | tf_op jit(solution)/shard_map/ppermute | solution.py:587
  10.9 0.8 %collective-permute-done.5.refs_6_ = f32[4,8,256]{2,1,0:T(8,128)S(1)} collective-permute-done((f32[4,8,256]{2,1,0:T(8,128)S(1)}, f32[4,8,256]{2,1,0:T(8,128)S(1)}, u32[]{:S(2)}, u32[]{:S(2)}) %collective-permute-start.5) | collective-permute-done | bytes 32800 | tf_op jit(solution)/shard_map/ppermute | solution.py:589
  11.7 1.0 %shard_map.205 = (f32[4,64,256]{2,1,0:T(8,128)S(1)}, bf16[4,64,256]{2,1,0:T(8,128)(2,1)S(1)}, f32[4,8,256]{2,1,0:T(8,128)S(1)}) custom-call(f32[4,64,256]{2,1,0:T(8,128)S(1)} %get-tuple-element.41.refs_0_.refs_1_, f32[4,64,256]{2,1,0:T(8,128)S(1)} %get-tuple-element.42.refs_1_, f32[4,64,256]{2,1,0:T(8,128)S(1)} %get-tuple-element.43.refs_2_, ...), custom_call_target="tpu_custom_call" | custom-call | flops 3932160 | bytes 1835008 | tf_op jit(solution)/shard_map/pallas_call | solution.py:606
  12.8 1.8 %collective-permute-start.7 = (bf16[4,64,256]{2,1,0:T(8,128)(2,1)S(1)}, bf16[4,64,256]{2,1,0:T(8,128)(2,1)S(1)}, u32[]{:S(2)}, u32[]{:S(2)}) collective-permute-start(bf16[4,64,256]{2,1,0:T(8,128)(2,1)S(1)} %get-tuple-element.51), channel_id=1, source_target_pairs={{1,5},{5,1},{4,8},{8,4},{9,13},{13,9},{0,2},{12,14},{3,7},{7,3},{6... | collective-permute-start | bytes 393224 | tf_op jit(solution)/shard_map/ppermute | solution.py:587
  14.9 2.8 %shard_map.206 = (bf16[4,80,256]{2,1,0:T(8,128)(2,1)S(1)}, bf16[80,128]{1,0:T(8,128)(2,1)S(1)}, f32[24,8]{1,0:T(8,128)S(1)}, f32[80,1]{1,0:T(8,128)S(1)}) custom-call(f32[8]{0:T(128)} %stiffness_in.3, f32[8]{0:T(128)} %density_in.3, f32[2,20,8,20]{3,2,1,0:T(8,128)} %bitcast.4, f32[4,20]{1,0:T(4,128)} %refs_3_.4, f32[1,20]{1,0:T(1,128)} %bitcast.5, ...), custom_call_target="tpu_custom_call" | custom-call | flops 2000000000 | bytes 4000000 | tf_op jit(solution)/shard_map/pallas_call | solution.py:553
  18.5 1.0 %shard_map.207 = (f32[4,64,256]{2,1,0:T(8,128)S(1)}, bf16[4,64,256]{2,1,0:T(8,128)(2,1)S(1)}, f32[4,8,256]{2,1,0:T(8,128)S(1)}) custom-call(f32[4,64,256]{2,1,0:T(8,128)S(1)} %get-tuple-element.50.refs_0_.refs_1_, f32[4,64,256]{2,1,0:T(8,128)S(1)} %get-tuple-element.41.refs_0_.refs_1_, f32[4,64,256]{2,1,0:T(8,128)S(1)} %get-tuple-element.43.refs_2_, ...), custom_call_target="tpu_custom_call" | custom-call | flops 3932160 | bytes 1835008 | tf_op jit(solution)/shard_map/pallas_call | solution.py:606
  19.8 1.6 %collective-permute-start.10 = (bf16[4,64,256]{2,1,0:T(8,128)(2,1)S(1)}, bf16[4,64,256]{2,1,0:T(8,128)(2,1)S(1)}, u32[]{:S(2)}, u32[]{:S(2)}) collective-permute-start(bf16[4,64,256]{2,1,0:T(8,128)(2,1)S(1)} %get-tuple-element.59), channel_id=1, source_target_pairs={{1,5},{5,1},{4,8},{8,4},{9,13},{13,9},{0,2},{12,14},{3,7},{7,3},{6... | collective-permute-start | bytes 393224 | tf_op jit(solution)/shard_map/ppermute | solution.py:587
  21.8 3.6 %collective-permute-done.11.refs_6_ = f32[4,8,256]{2,1,0:T(8,128)S(1)} collective-permute-done((f32[4,8,256]{2,1,0:T(8,128)S(1)}, f32[4,8,256]{2,1,0:T(8,128)S(1)}, u32[]{:S(2)}, u32[]{:S(2)}) %collective-permute-start.11) | collective-permute-done | bytes 32800 | tf_op jit(solution)/shard_map/ppermute | solution.py:589
  25.5 1.0 %shard_map.208 = (f32[4,64,256]{2,1,0:T(8,128)S(1)}, bf16[4,64,256]{2,1,0:T(8,128)(2,1)S(1)}, f32[4,8,256]{2,1,0:T(8,128)S(1)}) custom-call(f32[4,64,256]{2,1,0:T(8,128)S(1)} %get-tuple-element.58.refs_0_.refs_1_, f32[4,64,256]{2,1,0:T(8,128)S(1)} %get-tuple-element.50.refs_0_.refs_1_, f32[4,64,256]{2,1,0:T(8,128)S(1)} %get-tuple-element.43.refs_2_, ...), custom_call_target="tpu_custom_call" | custom-call | flops 3932160 | bytes 1835008 | tf_op jit(solution)/shard_map/pallas_call | solution.py:606
  26.5 1.6 %collective-permute-start.13 = (bf16[4,64,256]{2,1,0:T(8,128)(2,1)S(1)}, bf16[4,64,256]{2,1,0:T(8,128)(2,1)S(1)}, u32[]{:S(2)}, u32[]{:S(2)}) collective-permute-start(bf16[4,64,256]{2,1,0:T(8,128)(2,1)S(1)} %get-tuple-element.62), channel_id=1, source_target_pairs={{1,5},{5,1},{4,8},{8,4},{9,13},{13,9},{0,2},{12,14},{3,7},{7,3},{6... | collective-permute-start | bytes 393224 | tf_op jit(solution)/shard_map/ppermute | solution.py:587
  28.1 0.5 collective-permute-start.14
  28.6 1.1 %shard_map.209.prior = f32[4,32,128]{2,1,0:T(8,128)S(1)} custom-call(f32[512]{0:T(512)} %constant.29.clone.refs_0_.twiddles, f32[4,64,256]{2,1,0:T(8,128)S(1)} %get-tuple-element.61.own.refs_0_.q_ref, f32[4,64,256]{2,1,0:T(8,128)S(1)} %collective-permute-done.12.mate.refs_4_.q_mate, bf16[256,128]{1,0:T(8,128)(2,1)S(1)} %get-tuple-element.63.table_z, ...), custom_call_target="tpu_custom_call" | custom-call | flops 134217728 | bytes 1048576 | tf_op jit(solution)/shard_map/pallas_call | solution.py:599
  29.7 2.2 %collective-permute-done.13.refs_5_ = bf16[4,64,256]{2,1,0:T(8,128)(2,1)S(1)} collective-permute-done((bf16[4,64,256]{2,1,0:T(8,128)(2,1)S(1)}, bf16[4,64,256]{2,1,0:T(8,128)(2,1)S(1)}, u32[]{:S(2)}, u32[]{:S(2)}) %collective-permute-start.13) | collective-permute-done | bytes 131104 | tf_op jit(solution)/shard_map/ppermute | solution.py:587
  32.3 1.0 %shard_map.210.own.p_ref = f32[4,64,256]{2,1,0:T(8,128)S(1)} custom-call(f32[4,64,256]{2,1,0:T(8,128)S(1)} %get-tuple-element.61.own.refs_0_.q_ref, f32[4,64,256]{2,1,0:T(8,128)S(1)} %get-tuple-element.58.refs_0_.refs_1_, f32[4,64,256]{2,1,0:T(8,128)S(1)} %get-tuple-element.43.refs_2_, f32[4,64,256]{2,1,0:T(8,128)S(1)} %get-tuple-element.44.refs_3_, ...), custom_call_target="tpu_custom_call" | custom-call | flops 3932160 | bytes 1835008 | tf_op jit(solution)/shard_map/pallas_call | solution.py:606
  33.3 0.9 %shard_map.211 = (f32[4,4,32,128]{3,2,1,0:T(8,128)S(1)}, bf16[1,4,32,128]{3,2,1,0:T(8,128)(2,1)S(1)}) custom-call(f32[512]{0:T(512)} %constant.29.clone.refs_0_.twiddles, f32[4,64,256]{2,1,0:T(8,128)S(1)} %shard_map.210.own.p_ref, f32[4,32,128]{2,1,0:T(8,128)S(1)} %shard_map.209.prior, f32[2,4,32,128]{3,2,1,0:T(8,128)S(1)} %get-tuple-element.68.early, ...), custom_call_target="tpu_custom_call" | custom-call | flops 67108864 | bytes 524288 | tf_op jit(solution)/shard_map/pallas_call | solution.py:614
  34.3 1.2 %collective-permute-done.15 = bf16[1,4,32,128]{3,2,1,0:T(8,128)(2,1)S(1)} collective-permute-done((bf16[1,4,32,128]{3,2,1,0:T(8,128)(2,1)S(1)}, bf16[1,4,32,128]{3,2,1,0:T(8,128)(2,1)S(1)}, u32[]{:S(2)}, u32[]{:S(2)}) %collective-permute-start.15) | collective-permute-done | bytes 32800 | tf_op jit(solution)/shard_map/ppermute | solution.py:571
  35.5 1.2 %collective-permute-start.16 = (bf16[4,4,32,128]{3,2,1,0:T(8,128)(2,1)S(1)}, bf16[4,4,32,128]{3,2,1,0:T(8,128)(2,1)S(1)}, u32[]{:S(2)}, u32[]{:S(2)}) collective-permute-start(bf16[4,4,32,128]{3,2,1,0:T(8,128)(2,1)S(1)} %fusion), channel_id=1, source_target_pairs={{0,2},{2,0},{1,3},{3,1},{4,6},{6,4},{5,7},{7,5},{8,10},{10,8},{9,1... | collective-permute-start | bytes 393224 | tf_op jit(solution)/shard_map/ppermute | solution.py:574
  36.7 4.4 %collective-permute-done.16 = bf16[4,4,32,128]{3,2,1,0:T(8,128)(2,1)S(1)} collective-permute-done((bf16[4,4,32,128]{3,2,1,0:T(8,128)(2,1)S(1)}, bf16[4,4,32,128]{3,2,1,0:T(8,128)(2,1)S(1)}, u32[]{:S(2)}, u32[]{:S(2)}) %collective-permute-start.16) | collective-permute-done | bytes 131104 | tf_op jit(solution)/shard_map/ppermute | solution.py:574
  41.2 0.6 collective-permute-start.17
  41.7 0.7 %shard_map.213 = f32[8,64,128]{2,1,0:T(8,128)} custom-call(f32[4,64,256]{2,1,0:T(8,128)S(1)} %shard_map.210.own.p_ref, f32[4,64,256]{2,1,0:T(8,128)S(1)} %collective-permute-done.18.p_mate.other), custom_call_target="tpu_custom_call" | custom-call | bytes 786432 | tf_op jit(solution)/shard_map/pallas_call | solution.py:642
  42.5 3.4 %shard_map.212.rest_0_ = f32[80,64,256]{2,1,0:T(8,128)S(1)} custom-call(f32[8]{0:T(128)} %stiffness_in.3, f32[8]{0:T(128)} %density_in.3, f32[4,64,256]{2,1,0:T(8,128)S(1)} %shard_map.210.own.p_ref, f32[4,64,256]{2,1,0:T(8,128)S(1)} %get-tuple-element.61.own.refs_0_.q_ref, f32[4,64,256]{2,1,0:T(8,128)S(1)} %collective-permute-done.18.p_mate.other, ...), custom_call_target="tpu_custom_call" | custom-call | flops 1310720000 | bytes 3276800 | tf_op jit(solution)/shard_map/pallas_call | solution.py:625
  46.3 2.5 %collective-permute-start.19 = (bf16[4,4,32,128]{3,2,1,0:T(8,128)(2,1)S(1)}, bf16[4,4,32,128]{3,2,1,0:T(8,128)(2,1)S(1)}, u32[]{:S(2)}, u32[]{:S(2)}) collective-permute-start(bf16[4,4,32,128]{3,2,1,0:T(8,128)(2,1)S(1)} %fusion.1), channel_id=1, source_target_pairs={{0,12},{4,8},{8,4},{12,0},{1,13},{5,9},{9,5},{13,1},{2,14},{6,10},... | collective-permute-start | bytes 393224 | tf_op jit(solution)/shard_map/ppermute | solution.py:574
  48.7 3.4 %shard_map.214.local = f32[80,64,256]{2,1,0:T(8,128)S(1)} custom-call(f32[8]{0:T(128)} %stiffness_in.3, f32[8]{0:T(128)} %density_in.3, f32[4,64,256]{2,1,0:T(8,128)S(1)} %shard_map.210.own.p_ref, f32[4,64,256]{2,1,0:T(8,128)S(1)} %get-tuple-element.61.own.refs_0_.q_ref, ...), custom_call_target="tpu_custom_call", output_to_operand_aliasing={{}: (10, {})} | custom-call | flops 1310720000 | bytes 3276800 | tf_op jit(solution)/shard_map/pallas_call | solution.py:625
  52.1 1.1 %collective-permute-done.19 = bf16[4,4,32,128]{3,2,1,0:T(8,128)(2,1)S(1)} collective-permute-done((bf16[4,4,32,128]{3,2,1,0:T(8,128)(2,1)S(1)}, bf16[4,4,32,128]{3,2,1,0:T(8,128)(2,1)S(1)}, u32[]{:S(2)}, u32[]{:S(2)}) %collective-permute-start.19) | collective-permute-done | bytes 131104 | tf_op jit(solution)/shard_map/ppermute | solution.py:574
  53.4 1.3 %collective-permute-done.20.other = bf16[4,4,32,128]{3,2,1,0:T(8,128)(2,1)S(1)} collective-permute-done((bf16[4,4,32,128]{3,2,1,0:T(8,128)(2,1)S(1)}, bf16[4,4,32,128]{3,2,1,0:T(8,128)(2,1)S(1)}, u32[]{:S(2)}, u32[]{:S(2)}) %collective-permute-start.20) | collective-permute-done | bytes 131104 | tf_op jit(solution)/shard_map/ppermute | solution.py:571
  54.7 6.5 %shard_map.215 = bf16[4,20,64,256]{3,2,1,0:T(8,128)(2,1)} custom-call(f32[4,4,32,128]{3,2,1,0:T(8,128)S(1)} %get-tuple-element.81.mine, bf16[4,4,32,128]{3,2,1,0:T(8,128)(2,1)S(1)} %collective-permute-done.20.other, f32[80,64,256]{2,1,0:T(8,128)S(1)} %shard_map.214.local, bf16[4,80,256]{2,1,0:T(8,128)(2,1)S(1)} %get-tuple-element.79.left, ...), custom_call_target="tpu_custom_call" | custom-call | flops 131072000 | bytes 3932160 | tf_op jit(solution)/shard_map/pallas_call | solution.py:651
  (31 shorter events, 4.2 us)
Async XLA Ops:
  0.6 1.9 %collective-permute-start = (f32[8,64,128]{2,1,0:T(8,128)}, f32[8,64,128]{2,1,0:T(8,128)S(1)}, u32[]{:S(2)}, u32[]{:S(2)}) collective-permute-start(f32[8,64,128]{2,1,0:T(8,128)} %refs_3_.3), channel_id=1, source_target_pairs={{0,1},{1,0},{2,3},{3,2},{4,5},{5,4},{6,7},{7,6},{8,9},{9,8},{10,11... | collective-permute-start | bytes 786440 | tf_op jit(solution)/shard_map/ppermute | solution.py:540
  1.1 1.7 %collective-permute-start.1 = (f32[8,64,128]{2,1,0:T(8,128)}, f32[8,64,128]{2,1,0:T(8,128)S(1)}, u32[]{:S(2)}, u32[]{:S(2)}) collective-permute-start(f32[8,64,128]{2,1,0:T(8,128)} %refs_4_.2), channel_id=1, source_target_pairs={{0,1},{1,0},{2,3},{3,2},{4,5},{5,4},{6,7},{7,6},{8,9},{9,8},{10,11... | collective-permute-start | bytes 786440 | tf_op jit(solution)/shard_map/ppermute | solution.py:540
  1.2 2.0 %collective-permute-start.2 = (s32[8,64,128]{2,1,0:T(8,128)}, s32[8,64,128]{2,1,0:T(8,128)S(1)}, u32[]{:S(2)}, u32[]{:S(2)}) collective-permute-start(s32[8,64,128]{2,1,0:T(8,128)} %refs_5_.2), channel_id=1, source_target_pairs={{0,1},{1,0},{2,3},{3,2},{4,5},{5,4},{6,7},{7,6},{8,9},{9,8},{10,11... | collective-permute-start | bytes 786440 | tf_op jit(solution)/shard_map/ppermute | solution.py:540
  4.7 7.0 %collective-permute-start.3 = (f32[4,64,256]{2,1,0:T(8,128)S(1)}, f32[4,64,256]{2,1,0:T(8,128)S(1)}, u32[]{:S(2)}, u32[]{:S(2)}) collective-permute-start(f32[4,64,256]{2,1,0:T(8,128)S(1)} %get-tuple-element.41.refs_0_.refs_1_), channel_id=1, source_target_pairs={{0,1},{1,0},{2,3},{3,2},{4,5},{5,4},{6,7},{7,6},{8,9},{9,8},{10,11... | collective-permute-start | bytes 786440 | tf_op jit(solution)/shard_map/ppermute | solution.py:571
  5.2 5.7 %collective-permute-start.4 = (bf16[4,64,256]{2,1,0:T(8,128)(2,1)S(1)}, bf16[4,64,256]{2,1,0:T(8,128)(2,1)S(1)}, u32[]{:S(2)}, u32[]{:S(2)}) collective-permute-start(bf16[4,64,256]{2,1,0:T(8,128)(2,1)S(1)} %get-tuple-element.45), channel_id=1, source_target_pairs={{1,5},{5,1},{4,8},{8,4},{9,13},{13,9},{0,2},{12,14},{3,7},{7,3},{6... | collective-permute-start | bytes 393224 | tf_op jit(solution)/shard_map/ppermute | solution.py:587
  7.8 3.9 %collective-permute-start.5 = (f32[4,8,256]{2,1,0:T(8,128)S(1)}, f32[4,8,256]{2,1,0:T(8,128)S(1)}, u32[]{:S(2)}, u32[]{:S(2)}) collective-permute-start(f32[4,8,256]{2,1,0:T(8,128)S(1)} %get-tuple-element.49), channel_id=1, source_target_pairs={{0,2},{2,0},{1,3},{3,1},{4,6},{6,4},{5,7},{7,5},{8,10},{10,8},{9,1... | collective-permute-start | bytes 98312 | tf_op jit(solution)/shard_map/ppermute | solution.py:589
  12.7 5.8 %collective-permute-start.6 = (f32[4,64,256]{2,1,0:T(8,128)S(1)}, f32[4,64,256]{2,1,0:T(8,128)S(1)}, u32[]{:S(2)}, u32[]{:S(2)}) collective-permute-start(f32[4,64,256]{2,1,0:T(8,128)S(1)} %get-tuple-element.50.refs_0_.refs_1_), channel_id=1, source_target_pairs={{0,1},{1,0},{2,3},{3,2},{4,5},{5,4},{6,7},{7,6},{8,9},{9,8},{10,11... | collective-permute-start | bytes 786440 | tf_op jit(solution)/shard_map/ppermute | solution.py:571
  12.8 5.4 %collective-permute-start.7 = (bf16[4,64,256]{2,1,0:T(8,128)(2,1)S(1)}, bf16[4,64,256]{2,1,0:T(8,128)(2,1)S(1)}, u32[]{:S(2)}, u32[]{:S(2)}) collective-permute-start(bf16[4,64,256]{2,1,0:T(8,128)(2,1)S(1)} %get-tuple-element.51), channel_id=1, source_target_pairs={{1,5},{5,1},{4,8},{8,4},{9,13},{13,9},{0,2},{12,14},{3,7},{7,3},{6... | collective-permute-start | bytes 393224 | tf_op jit(solution)/shard_map/ppermute | solution.py:587
  14.6 3.9 %collective-permute-start.8 = (f32[4,8,256]{2,1,0:T(8,128)S(1)}, f32[4,8,256]{2,1,0:T(8,128)S(1)}, u32[]{:S(2)}, u32[]{:S(2)}) collective-permute-start(f32[4,8,256]{2,1,0:T(8,128)S(1)} %get-tuple-element.57), channel_id=1, source_target_pairs={{0,2},{2,0},{1,3},{3,1},{4,6},{6,4},{5,7},{7,5},{8,10},{10,8},{9,1... | collective-permute-start | bytes 98312 | tf_op jit(solution)/shard_map/ppermute | solution.py:589
  19.5 6.0 %collective-permute-start.9 = (f32[4,64,256]{2,1,0:T(8,128)S(1)}, f32[4,64,256]{2,1,0:T(8,128)S(1)}, u32[]{:S(2)}, u32[]{:S(2)}) collective-permute-start(f32[4,64,256]{2,1,0:T(8,128)S(1)} %get-tuple-element.58.refs_0_.refs_1_), channel_id=1, source_target_pairs={{0,1},{1,0},{2,3},{3,2},{4,5},{5,4},{6,7},{7,6},{8,9},{9,8},{10,11... | collective-permute-start | bytes 786440 | tf_op jit(solution)/shard_map/ppermute | solution.py:571
  19.8 5.7 %collective-permute-start.10 = (bf16[4,64,256]{2,1,0:T(8,128)(2,1)S(1)}, bf16[4,64,256]{2,1,0:T(8,128)(2,1)S(1)}, u32[]{:S(2)}, u32[]{:S(2)}) collective-permute-start(bf16[4,64,256]{2,1,0:T(8,128)(2,1)S(1)} %get-tuple-element.59), channel_id=1, source_target_pairs={{1,5},{5,1},{4,8},{8,4},{9,13},{13,9},{0,2},{12,14},{3,7},{7,3},{6... | collective-permute-start | bytes 393224 | tf_op jit(solution)/shard_map/ppermute | solution.py:587
  21.4 4.1 %collective-permute-start.11 = (f32[4,8,256]{2,1,0:T(8,128)S(1)}, f32[4,8,256]{2,1,0:T(8,128)S(1)}, u32[]{:S(2)}, u32[]{:S(2)}) collective-permute-start(f32[4,8,256]{2,1,0:T(8,128)S(1)} %get-tuple-element.60), channel_id=1, source_target_pairs={{0,2},{2,0},{1,3},{3,1},{4,6},{6,4},{5,7},{7,5},{8,10},{10,8},{9,1... | collective-permute-start | bytes 98312 | tf_op jit(solution)/shard_map/ppermute | solution.py:589
  26.4 2.2 %collective-permute-start.12 = (f32[4,64,256]{2,1,0:T(8,128)S(1)}, f32[4,64,256]{2,1,0:T(8,128)S(1)}, u32[]{:S(2)}, u32[]{:S(2)}) collective-permute-start(f32[4,64,256]{2,1,0:T(8,128)S(1)} %get-tuple-element.61.own.refs_0_.q_ref), channel_id=1, source_target_pairs={{0,1},{1,0},{2,3},{3,2},{4,5},{5,4},{6,7},{7,6},{8,9},{9,8},{10,11... | collective-permute-start | bytes 786440 | tf_op jit(solution)/shard_map/ppermute | solution.py:571
  26.5 5.4 %collective-permute-start.13 = (bf16[4,64,256]{2,1,0:T(8,128)(2,1)S(1)}, bf16[4,64,256]{2,1,0:T(8,128)(2,1)S(1)}, u32[]{:S(2)}, u32[]{:S(2)}) collective-permute-start(bf16[4,64,256]{2,1,0:T(8,128)(2,1)S(1)} %get-tuple-element.62), channel_id=1, source_target_pairs={{1,5},{5,1},{4,8},{8,4},{9,13},{13,9},{0,2},{12,14},{3,7},{7,3},{6... | collective-permute-start | bytes 393224 | tf_op jit(solution)/shard_map/ppermute | solution.py:587
  28.1 4.2 %collective-permute-start.14 = (f32[4,8,256]{2,1,0:T(8,128)S(1)}, f32[4,8,256]{2,1,0:T(8,128)S(1)}, u32[]{:S(2)}, u32[]{:S(2)}) collective-permute-start(f32[4,8,256]{2,1,0:T(8,128)S(1)} %get-tuple-element.66), channel_id=1, source_target_pairs={{0,2},{2,0},{1,3},{3,1},{4,6},{6,4},{5,7},{7,5},{8,10},{10,8},{9,1... | collective-permute-start | bytes 98312 | tf_op jit(solution)/shard_map/ppermute | solution.py:589
  34.2 1.3 %collective-permute-start.15 = (bf16[1,4,32,128]{3,2,1,0:T(8,128)(2,1)S(1)}, bf16[1,4,32,128]{3,2,1,0:T(8,128)(2,1)S(1)}, u32[]{:S(2)}, u32[]{:S(2)}) collective-permute-start(bf16[1,4,32,128]{3,2,1,0:T(8,128)(2,1)S(1)} %get-tuple-element.70), channel_id=1, source_target_pairs={{0,1},{1,0},{2,3},{3,2},{4,5},{5,4},{6,7},{7,6},{8,9},{9,8},{10,11... | collective-permute-start | bytes 98312 | tf_op jit(solution)/shard_map/ppermute | solution.py:571
  35.5 5.6 %collective-permute-start.16 = (bf16[4,4,32,128]{3,2,1,0:T(8,128)(2,1)S(1)}, bf16[4,4,32,128]{3,2,1,0:T(8,128)(2,1)S(1)}, u32[]{:S(2)}, u32[]{:S(2)}) collective-permute-start(bf16[4,4,32,128]{3,2,1,0:T(8,128)(2,1)S(1)} %fusion), channel_id=1, source_target_pairs={{0,2},{2,0},{1,3},{3,1},{4,6},{6,4},{5,7},{7,5},{8,10},{10,8},{9,1... | collective-permute-start | bytes 393224 | tf_op jit(solution)/shard_map/ppermute | solution.py:574
  36.7 5.1 %collective-permute-start.18 = (f32[4,64,256]{2,1,0:T(8,128)S(1)}, f32[4,64,256]{2,1,0:T(8,128)S(1)}, u32[]{:S(2)}, u32[]{:S(2)}) collective-permute-start(f32[4,64,256]{2,1,0:T(8,128)S(1)} %shard_map.210.own.p_ref), channel_id=1, source_target_pairs={{0,1},{1,0},{2,3},{3,2},{4,5},{5,4},{6,7},{7,6},{8,9},{9,8},{10,11... | collective-permute-start | bytes 786440 | tf_op jit(solution)/shard_map/ppermute | solution.py:571
  41.2 5.0 %collective-permute-start.17 = (bf16[4,4,32,128]{3,2,1,0:T(8,128)(2,1)S(1)}, bf16[4,4,32,128]{3,2,1,0:T(8,128)(2,1)S(1)}, u32[]{:S(2)}, u32[]{:S(2)}) collective-permute-start(bf16[4,4,32,128]{3,2,1,0:T(8,128)(2,1)S(1)} %fusion.2), channel_id=1, source_target_pairs={{0,4},{4,0},{8,12},{12,8},{1,5},{5,1},{9,13},{13,9},{2,6},{6,2},{1... | collective-permute-start | bytes 393224 | tf_op jit(solution)/shard_map/ppermute | solution.py:574
  46.2 8.5 %copy-start = (bf16[128,512]{1,0:T(8,128)(2,1)S(1)}, bf16[128,512]{1,0:T(8,128)(2,1)}, u32[]{:S(2)}) copy-start(bf16[128,512]{1,0:T(8,128)(2,1)} %constant.33.clone.table_z) | copy-start | bytes 393220
  46.3 8.4 %copy-start.1 = (bf16[2,64,64]{2,1,0:T(8,128)(2,1)S(1)}, bf16[2,64,64]{2,1,0:T(8,128)(2,1)}, u32[]{:S(2)}) copy-start(bf16[2,64,64]{2,1,0:T(8,128)(2,1)} %constant.32.clone.table_y) | copy-start | bytes 49156
  46.3 6.9 %collective-permute-start.19 = (bf16[4,4,32,128]{3,2,1,0:T(8,128)(2,1)S(1)}, bf16[4,4,32,128]{3,2,1,0:T(8,128)(2,1)S(1)}, u32[]{:S(2)}, u32[]{:S(2)}) collective-permute-start(bf16[4,4,32,128]{3,2,1,0:T(8,128)(2,1)S(1)} %fusion.1), channel_id=1, source_target_pairs={{0,12},{4,8},{8,4},{12,0},{1,13},{5,9},{9,5},{13,1},{2,14},{6,10},... | collective-permute-start | bytes 393224 | tf_op jit(solution)/shard_map/ppermute | solution.py:574
  53.3 1.4 %collective-permute-start.20 = (bf16[4,4,32,128]{3,2,1,0:T(8,128)(2,1)S(1)}, bf16[4,4,32,128]{3,2,1,0:T(8,128)(2,1)S(1)}, u32[]{:S(2)}, u32[]{:S(2)}) collective-permute-start(bf16[4,4,32,128]{3,2,1,0:T(8,128)(2,1)S(1)} %get-tuple-element.80), channel_id=1, source_target_pairs={{0,1},{1,0},{2,3},{3,2},{4,5},{5,4},{6,7},{7,6},{8,9},{9,8},{10,11... | collective-permute-start | bytes 393224 | tf_op jit(solution)/shard_map/ppermute | solution.py:571

commit v9 on v8

--- a/solution.py
+++ b/solution.py
@@ -316,13 +316,7 @@
     cosine = turn_ref[0]
     sine = turn_ref[1]
     coupled = jnp.concatenate([cosine * real - sine * imag, -(cosine * imag + sine * real)], axis=1)
-    width = 2 * half
-    blocks = mixing.shape[0]
-    for index in range(blocks):
-        parts = [jnp.zeros((coupled.shape[0], width * index), F32)] * (index > 0) + [coupled]
-        parts += [jnp.zeros((coupled.shape[0], width * (blocks - 1 - index)), F32)] * (index < blocks - 1)
-        line = jnp.concatenate(parts, axis=1) if blocks > 1 else coupled
-        mixing[index] = line.astype(BF16)
+    mixing[...] = coupled.astype(BF16)
     constant = dot(spread, mode_ref[0, :, 0, :], across)
     bias = bias_ref[...] + middle(stiffness) * lift_ref[2:3, :] + middle(density) * lift_ref[3:4, :]
     offset[...] = jnp.sum(constant * bias, axis=1, keepdims=True)
@@ -334,6 +328,15 @@
     lift_table[:, 0:FIELDS] = dot(padded, lift_ref[...], across)
     lift_table[:, FIELDS : FIELDS + 1] = dot(padded, bias_ref[...], across)
     lift_table[:, FIELDS + 1 :] = jnp.zeros_like(lift_table[:, FIELDS + 1 :])
+
+
+def widen_body(mixing, repeat_ref, out):
+    rows, span = repeat_ref.shape[0], mixing.shape[1]
+    count = rows // mixing.shape[0]
+    values = jnp.dot(repeat_ref[...], mixing[...], preferred_element_type=F32)
+    column = lax.broadcasted_iota(jnp.int32, (rows, span), 0) % count
+    parts = [jnp.where(column == index, values, 0.0) for index in range(count)]
+    out[...] = jnp.concatenate(parts, axis=1).astype(BF16)
 
 
 def pointwise_body(stiffness_in, density_in, p_ref, q_ref, p_mate, q_mate, cells, lift_ref, left, offset, *rest):
@@ -383,7 +386,7 @@
 
 
 def output_body(
-    mine, other, local, left, table_y, table_z, features, modes, right, sums,
+    mine, other, local, left, table_y, table_z, features, modes, right,
 ):
     step = pl.program_id(0)
     core, column = lax.axis_index("gz"), lax.axis_index("gy")
@@ -414,28 +417,28 @@
     base = pl.multiple_of(step * group, group)
     lines = modes[pl.ds(base, group)].reshape(group * coupled, width).astype(BF16)
     waves = jnp.dot(lines, table_z[...], preferred_element_type=F32).astype(BF16)
-    joined, height = left.shape[:2]
+    count = left.shape[1] // (2 * coupled)
     for y in range(group):
         lines = slice(y * coupled, (y + 1) * coupled)
         start = y * 2 * coupled
         right[start : start + coupled, :] = waves[lines, :depth]
         right[start + coupled : start + 2 * coupled, :] = waves[lines, depth:]
-    span = joined * 2 * coupled
-    every = left[...].reshape(joined * height, span)
-    for first in range(0, group, joined):
-        start = first * 2 * coupled
-        result = jnp.dot(every, right[start : start + span, :], preferred_element_type=F32)
-        for index in range(joined):
-            sums[:, first + index, :] = result[index * height : (index + 1) * height]
-    for row in range(rows):
-        for channel in range(channels):
-            at = row * channels + channel
-            total = sums[at] + local[at, pl.ds(base, group), :]
-            scale = math.sqrt(2.0 / math.pi)
-            inner = total * (scale + (scale * 0.044715) * (total * total))
-            part = 0.5 * total
-            total = part + part * jnp.tanh(inner)
-            features[row, channel] = total.astype(BF16)
+    for first in range(0, group, 2 * count):
+        results = []
+        for start in (first * 2 * coupled, (first + count) * 2 * coupled):
+            results.append(jnp.dot(
+                left[...], right[start : start + count * 2 * coupled, :], preferred_element_type=F32
+            ))
+        for row in range(rows):
+            for channel in range(channels):
+                at = row * channels + channel
+                total = jnp.concatenate([result[at * count : (at + 1) * count] for result in results], axis=0)
+                total = total + local[at, pl.ds(base + first, 2 * count), :]
+                scale = math.sqrt(2.0 / math.pi)
+                inner = total * (scale + (scale * 0.044715) * (total * total))
+                part = 0.5 * total
+                total = part + part * jnp.tanh(inner)
+                features[row, channel, first : first + 2 * count, :] = total.astype(BF16)
 
 
 def xor_pairs(count, distance):
@@ -489,7 +492,6 @@
     padded_channels = -(-channels // 8) * 8
     height = rows * channels
     coupled = FIELDS * modes_x
-    joined = max(1, 256 // (2 * coupled))
     right_depth = -(-rows * padded_channels // 128) * 128
     two_sided = column_count > 2
 
@@ -552,7 +554,7 @@
     )
     mixing, pointwise, lift_table, offset = call(
         prepare_body,
-        [shape(joined, height, joined * 2 * coupled, dtype=BF16), shape(height, right_depth, dtype=BF16),
+        [shape(height, 2 * coupled, dtype=BF16), shape(height, right_depth, dtype=BF16),
          shape(padded_channels, 8), shape(height, 1)],
         [HBM] * 11, room(*weights[:9], turn[0], wide), flops=2_000_000_000, moved=4_000_000,
     )(*here(*weights))
@@ -591,6 +593,12 @@
             halos.append(lax.ppermute(edge_values[1], "gy", odd_pairs(column_count)))
         if repeat == 0:
             far, early = lax.optimization_barrier((far, early))
+        if repeat == 2:
+            repeats = np.repeat(np.eye(height), 8, 0).astype(ml_dtypes.bfloat16)
+            wide_mixing = call(
+                widen_body, shape(height * 8, 16 * coupled, dtype=BF16), [VMEM] * 2, flops=1_000_000_000, moved=2_000_000
+            )(mixing, repeats)
+            far, wide_mixing = lax.optimization_barrier((far, wide_mixing))
         if repeat == 1:
             far, mixing, pointwise, lift_table, offset = lax.optimization_barrier(
                 (far, mixing, pointwise, lift_table, offset)
@@ -647,7 +655,7 @@
         total = total + arrived.astype(F32)
     other = swap(total.astype(BF16))
     batch = min(32, brick_y)
-    scoped = 14 * 2**20 + 4 * (brick_y * coupled * width + 6 * batch * coupled * total_z)
+    scoped = 10 * 2**20 + 20 * height * 16 * coupled + 4 * (brick_y * coupled * width + 6 * batch * coupled * total_z)
     features = pl.pallas_call(
         output_body,
         grid=(brick_y // batch,),
@@ -658,11 +666,10 @@
         scratch_shapes=[
             pltpu.VMEM((brick_y, coupled, width), F32),
             pltpu.VMEM((batch * 2 * coupled, total_z), BF16),
-            pltpu.VMEM((height, batch, total_z), F32),
         ],
         compiler_params=pltpu.CompilerParams(vmem_limit_bytes=scoped),
         cost_estimate=pl.CostEstimate(flops=cells_count * 2000, bytes_accessed=cells_count * 60, transcendentals=cells_count * 20),
-    )(total, other, local, mixing, inverse_y, inverse_z)
+    )(total, other, local, wide_mixing, inverse_y, inverse_z)
     features = features.transpose(0, 2, 1, 3)
     return (wave, features)
 

time: 61.5 us -> 60 us (0.976)
  Pallas kernels: 26.6 us -> 25.5 us
    ppermute x4, waiting for transfers between devices: 5.18 us -> 1.88 us  [per_device(): halos = [lax.ppermute(edge_values[0], 'gy', xor_pairs(column_count, 1))]]
    ppermute x4, waiting for transfers between devices: 3.31 us -> 6.17 us  [per_device(): lax.ppermute(sent, ('gx', 'gy', 'gz'), row_pairs(cycle_count, column_count))]
    pallas_call x1, Pallas kernels: 6.5 us -> 5.03 us  [per_device(): pl.pallas_call(output_body, grid=(brick_y // batch,), out_shape=shape(row...]
    pallas_call x1 -> x2, Pallas kernels: 2.84 us -> 3.25 us  [the longest x1 2.81 us: per_device(): call(prepare_body, [shape(height, 2 * coupled, dtype=BF16), shape(height,...]
  transfers between devices with their start and end apart: 21 -> 21, of which waited for: 15 -> 16; matrix products, arithmetic and copies ran while one was open for 0% -> 0% of each run, Pallas kernels for 23% -> 24%
where the time goes in v9:
time: 60 us; the launch traced here: 59.7 us
  Pallas kernels  25.5 us (42%)
  waiting for transfers between devices  18 us (30%)
  starting transfers between devices  15.2 us (25%)
  between operations  0.82 us (1%)
    ppermute x4, starting transfers between devices, per_device(): lax.ppermute(sent, ('gx', 'gy', 'gz'), row_pairs(cycle_count, column_count))  7.66 us
    pallas_call x2, Pallas kernels, pointwise_part(): pl.pallas_call(pointwise_body, grid=(steps // 2,), out_shape=shape(height...  6.76 us
    ppermute x4, waiting for transfers between devices, per_device(): lax.ppermute(sent, ('gx', 'gy', 'gz'), row_pairs(cycle_count, column_count))  6.17 us
    ppermute x3, waiting for transfers between devices, exchange(): return lax.ppermute(value.astype(BF16), axis, xor_pairs(count, distance))  5.76 us
    pallas_call x1, Pallas kernels, per_device(): pl.pallas_call(output_body, grid=(brick_y // batch,), out_shape=shape(row...  5.03 us
    ppermute x3, starting transfers between devices, exchange(): return lax.ppermute(value.astype(BF16), axis, xor_pairs(count, distance))  4.31 us
    pallas_call x4, Pallas kernels, per_device(): call(body, outs, [VMEM] * (6 + len(halos)), [pltpu.VMEM((brick_y + 2 * ED...  3.92 us
    pallas_call x1, Pallas kernels, per_device(): call(prepare_body, [shape(height, 2 * coupled, dtype=BF16), shape(height,...  2.81 us
  transfers between devices with their start and end apart: 21, of which 16 were waited for; matrix products, arithmetic and copies ran while one was open for 0% of the time, Pallas kernels for 24%

profile of v9, /device:TPU:0, one launch (start us, length us, event | category | flops | bytes accessed | tf_op | source)
XLA Modules:
  0.0 59.7 jit_solution(11856507130595645854)
XLA Ops:
  0.6 0.5 collective-permute-start
  1.7 0.9 %collective-permute-done.refs_6_ = f32[8,64,128]{2,1,0:T(8,128)S(1)} collective-permute-done((f32[8,64,128]{2,1,0:T(8,128)}, f32[8,64,128]{2,1,0:T(8,128)S(1)}, u32[]{:S(2)}, u32[]{:S(2)}) %collective-permute-start) | collective-permute-done | bytes 262176 | tf_op jit(solution)/shard_map/ppermute | solution.py:542
  3.3 1.5 %shard_map.212 = (f32[4,64,256]{2,1,0:T(8,128)S(1)}, f32[4,64,256]{2,1,0:T(8,128)S(1)}, f32[4,64,256]{2,1,0:T(8,128)S(1)}, f32[4,64,256]{2,1,0:T(8,128)S(1)}, bf...) custom-call(f32[8]{0:T(128)} %stiffness_in.3, f32[8]{0:T(128)} %density_in.3, ...), custom_call_target="tpu_custom_call" | custom-call | bytes 2359296 | tf_op jit(solution)/shard_map/pallas_call | solution.py:544
  5.2 2.6 %collective-permute-start.4 = (bf16[4,64,256]{2,1,0:T(8,128)(2,1)S(1)}, bf16[4,64,256]{2,1,0:T(8,128)(2,1)S(1)}, u32[]{:S(2)}, u32[]{:S(2)}) collective-permute-start(bf16[4,64,256]{2,1,0:T(8,128)(2,1)S(1)} %get-tuple-element.47), channel_id=1, source_target_pairs={{1,5},{5,1},{4,8},{8,4},{9,13},{13,9},{0,2},{12,14},{3,7},{7,3},{6... | collective-permute-start | bytes 393224 | tf_op jit(solution)/shard_map/ppermute | solution.py:589
  7.8 2.3 %shard_map.213 = (f32[2,4,32,128]{3,2,1,0:T(8,128)S(1)}, bf16[256,128]{1,0:T(8,128)(2,1)S(1)}, bf16[2,32,256]{2,1,0:T(8,128)(2,1)S(1)}) custom-call(f32[512]{0:T(512)} %constant.31.clone.refs_0_.twiddles, f32[8]{0:T(128)} %stiffness_in.3, f32[8]{0:T(128)} %density_in.3, bf16[256,128]{1,0:T(8,128)(2,1)} %constant.32.clone.refs_3_, ...), custom_call_target="tpu_custom_call" | custom-call | flops 268435456 | bytes 2097152 | tf_op jit(solution)/shard_map/pallas_call | solution.py:579
  10.2 0.7 %collective-permute-done.4.refs_5_ = bf16[4,64,256]{2,1,0:T(8,128)(2,1)S(1)} collective-permute-done((bf16[4,64,256]{2,1,0:T(8,128)(2,1)S(1)}, bf16[4,64,256]{2,1,0:T(8,128)(2,1)S(1)}, u32[]{:S(2)}, u32[]{:S(2)}) %collective-permute-start.4) | collective-permute-done | bytes 131104 | tf_op jit(solution)/shard_map/ppermute | solution.py:589
  10.9 0.8 %collective-permute-done.5.refs_6_ = f32[4,8,256]{2,1,0:T(8,128)S(1)} collective-permute-done((f32[4,8,256]{2,1,0:T(8,128)S(1)}, f32[4,8,256]{2,1,0:T(8,128)S(1)}, u32[]{:S(2)}, u32[]{:S(2)}) %collective-permute-start.5) | collective-permute-done | bytes 32800 | tf_op jit(solution)/shard_map/ppermute | solution.py:591
  11.7 1.0 %shard_map.214 = (f32[4,64,256]{2,1,0:T(8,128)S(1)}, bf16[4,64,256]{2,1,0:T(8,128)(2,1)S(1)}, f32[4,8,256]{2,1,0:T(8,128)S(1)}) custom-call(f32[4,64,256]{2,1,0:T(8,128)S(1)} %get-tuple-element.43.refs_0_.refs_1_, f32[4,64,256]{2,1,0:T(8,128)S(1)} %get-tuple-element.44.refs_1_, f32[4,64,256]{2,1,0:T(8,128)S(1)} %get-tuple-element.45.refs_2_, ...), custom_call_target="tpu_custom_call" | custom-call | flops 3932160 | bytes 1835008 | tf_op jit(solution)/shard_map/pallas_call | solution.py:614
  12.8 1.8 %collective-permute-start.7 = (bf16[4,64,256]{2,1,0:T(8,128)(2,1)S(1)}, bf16[4,64,256]{2,1,0:T(8,128)(2,1)S(1)}, u32[]{:S(2)}, u32[]{:S(2)}) collective-permute-start(bf16[4,64,256]{2,1,0:T(8,128)(2,1)S(1)} %get-tuple-element.53), channel_id=1, source_target_pairs={{1,5},{5,1},{4,8},{8,4},{9,13},{13,9},{0,2},{12,14},{3,7},{7,3},{6... | collective-permute-start | bytes 393224 | tf_op jit(solution)/shard_map/ppermute | solution.py:589
  14.9 2.8 %shard_map.215 = (bf16[80,64]{1,0:T(8,128)(2,1)S(1)}, bf16[80,128]{1,0:T(8,128)(2,1)S(1)}, f32[24,8]{1,0:T(8,128)S(1)}, f32[80,1]{1,0:T(8,128)S(1)}) custom-call(f32[8]{0:T(128)} %stiffness_in.3, f32[8]{0:T(128)} %density_in.3, f32[2,20,8,20]{3,2,1,0:T(8,128)} %bitcast.4, f32[4,20]{1,0:T(4,128)} %refs_3_.4, f32[1,20]{1,0:T(1,128)} %bitcast.5, ...), custom_call_target="tpu_custom_call" | custom-call | flops 2000000000 | bytes 4000000 | tf_op jit(solution)/shard_map/pallas_call | solution.py:555
  17.7 0.5 collective-permute-done.7.refs_5_
  18.5 1.0 %shard_map.216 = (f32[4,64,256]{2,1,0:T(8,128)S(1)}, bf16[4,64,256]{2,1,0:T(8,128)(2,1)S(1)}, f32[4,8,256]{2,1,0:T(8,128)S(1)}) custom-call(f32[4,64,256]{2,1,0:T(8,128)S(1)} %get-tuple-element.52.refs_0_.refs_1_, f32[4,64,256]{2,1,0:T(8,128)S(1)} %get-tuple-element.43.refs_0_.refs_1_, f32[4,64,256]{2,1,0:T(8,128)S(1)} %get-tuple-element.45.refs_2_, ...), custom_call_target="tpu_custom_call" | custom-call | flops 3932160 | bytes 1835008 | tf_op jit(solution)/shard_map/pallas_call | solution.py:614
  19.8 1.6 %collective-permute-start.10 = (bf16[4,64,256]{2,1,0:T(8,128)(2,1)S(1)}, bf16[4,64,256]{2,1,0:T(8,128)(2,1)S(1)}, u32[]{:S(2)}, u32[]{:S(2)}) collective-permute-start(bf16[4,64,256]{2,1,0:T(8,128)(2,1)S(1)} %get-tuple-element.61), channel_id=1, source_target_pairs={{1,5},{5,1},{4,8},{8,4},{9,13},{13,9},{0,2},{12,14},{3,7},{7,3},{6... | collective-permute-start | bytes 393224 | tf_op jit(solution)/shard_map/ppermute | solution.py:589
  22.3 2.8 %collective-permute-done.10.refs_5_ = bf16[4,64,256]{2,1,0:T(8,128)(2,1)S(1)} collective-permute-done((bf16[4,64,256]{2,1,0:T(8,128)(2,1)S(1)}, bf16[4,64,256]{2,1,0:T(8,128)(2,1)S(1)}, u32[]{:S(2)}, u32[]{:S(2)}) %collective-permute-start.10) | collective-permute-done | bytes 131104 | tf_op jit(solution)/shard_map/ppermute | solution.py:589
  25.4 1.0 %shard_map.218 = (f32[4,64,256]{2,1,0:T(8,128)S(1)}, bf16[4,64,256]{2,1,0:T(8,128)(2,1)S(1)}, f32[4,8,256]{2,1,0:T(8,128)S(1)}) custom-call(f32[4,64,256]{2,1,0:T(8,128)S(1)} %get-tuple-element.60.refs_0_.refs_1_, f32[4,64,256]{2,1,0:T(8,128)S(1)} %get-tuple-element.52.refs_0_.refs_1_, f32[4,64,256]{2,1,0:T(8,128)S(1)} %get-tuple-element.45.refs_2_, ...), custom_call_target="tpu_custom_call" | custom-call | flops 3932160 | bytes 1835008 | tf_op jit(solution)/shard_map/pallas_call | solution.py:614
  26.5 1.6 %collective-permute-start.13 = (bf16[4,64,256]{2,1,0:T(8,128)(2,1)S(1)}, bf16[4,64,256]{2,1,0:T(8,128)(2,1)S(1)}, u32[]{:S(2)}, u32[]{:S(2)}) collective-permute-start(bf16[4,64,256]{2,1,0:T(8,128)(2,1)S(1)} %get-tuple-element.66), channel_id=1, source_target_pairs={{1,5},{5,1},{4,8},{8,4},{9,13},{13,9},{0,2},{12,14},{3,7},{7,3},{6... | collective-permute-start | bytes 393224 | tf_op jit(solution)/shard_map/ppermute | solution.py:589
  28.1 0.5 collective-permute-start.14
  28.6 1.1 %shard_map.219.prior = f32[4,32,128]{2,1,0:T(8,128)S(1)} custom-call(f32[512]{0:T(512)} %constant.31.clone.refs_0_.twiddles, f32[4,64,256]{2,1,0:T(8,128)S(1)} %get-tuple-element.65.own.refs_0_.q_ref, f32[4,64,256]{2,1,0:T(8,128)S(1)} %collective-permute-done.12.mate.refs_4_.q_mate, bf16[256,128]{1,0:T(8,128)(2,1)S(1)} %get-tuple-element.67.table_z, ...), custom_call_target="tpu_custom_call" | custom-call | flops 134217728 | bytes 1048576 | tf_op jit(solution)/shard_map/pallas_call | solution.py:607
  29.7 2.2 %collective-permute-done.13.refs_5_ = bf16[4,64,256]{2,1,0:T(8,128)(2,1)S(1)} collective-permute-done((bf16[4,64,256]{2,1,0:T(8,128)(2,1)S(1)}, bf16[4,64,256]{2,1,0:T(8,128)(2,1)S(1)}, u32[]{:S(2)}, u32[]{:S(2)}) %collective-permute-start.13) | collective-permute-done | bytes 131104 | tf_op jit(solution)/shard_map/ppermute | solution.py:589
  32.2 1.0 %shard_map.220.own.p_ref = f32[4,64,256]{2,1,0:T(8,128)S(1)} custom-call(f32[4,64,256]{2,1,0:T(8,128)S(1)} %get-tuple-element.65.own.refs_0_.q_ref, f32[4,64,256]{2,1,0:T(8,128)S(1)} %get-tuple-element.60.refs_0_.refs_1_, f32[4,64,256]{2,1,0:T(8,128)S(1)} %get-tuple-element.45.refs_2_, f32[4,64,256]{2,1,0:T(8,128)S(1)} %get-tuple-element.46.refs_3_, ...), custom_call_target="tpu_custom_call" | custom-call | flops 3932160 | bytes 1835008 | tf_op jit(solution)/shard_map/pallas_call | solution.py:614
  33.3 0.9 %shard_map.221 = (f32[4,4,32,128]{3,2,1,0:T(8,128)S(1)}, bf16[1,4,32,128]{3,2,1,0:T(8,128)(2,1)S(1)}) custom-call(f32[512]{0:T(512)} %constant.31.clone.refs_0_.twiddles, f32[4,64,256]{2,1,0:T(8,128)S(1)} %shard_map.220.own.p_ref, f32[4,32,128]{2,1,0:T(8,128)S(1)} %shard_map.219.prior, f32[2,4,32,128]{3,2,1,0:T(8,128)S(1)} %get-tuple-element.72.early, ...), custom_call_target="tpu_custom_call" | custom-call | flops 67108864 | bytes 524288 | tf_op jit(solution)/shard_map/pallas_call | solution.py:622
  34.2 1.2 %collective-permute-done.15 = bf16[1,4,32,128]{3,2,1,0:T(8,128)(2,1)S(1)} collective-permute-done((bf16[1,4,32,128]{3,2,1,0:T(8,128)(2,1)S(1)}, bf16[1,4,32,128]{3,2,1,0:T(8,128)(2,1)S(1)}, u32[]{:S(2)}, u32[]{:S(2)}) %collective-permute-start.15) | collective-permute-done | bytes 32800 | tf_op jit(solution)/shard_map/ppermute | solution.py:573
  35.5 1.2 %collective-permute-start.16 = (bf16[4,4,32,128]{3,2,1,0:T(8,128)(2,1)S(1)}, bf16[4,4,32,128]{3,2,1,0:T(8,128)(2,1)S(1)}, u32[]{:S(2)}, u32[]{:S(2)}) collective-permute-start(bf16[4,4,32,128]{3,2,1,0:T(8,128)(2,1)S(1)} %fusion), channel_id=1, source_target_pairs={{0,2},{2,0},{1,3},{3,1},{4,6},{6,4},{5,7},{7,5},{8,10},{10,8},{9,1... | collective-permute-start | bytes 393224 | tf_op jit(solution)/shard_map/ppermute | solution.py:576
  36.7 4.4 %collective-permute-done.16 = bf16[4,4,32,128]{3,2,1,0:T(8,128)(2,1)S(1)} collective-permute-done((bf16[4,4,32,128]{3,2,1,0:T(8,128)(2,1)S(1)}, bf16[4,4,32,128]{3,2,1,0:T(8,128)(2,1)S(1)}, u32[]{:S(2)}, u32[]{:S(2)}) %collective-permute-start.16) | collective-permute-done | bytes 131104 | tf_op jit(solution)/shard_map/ppermute | solution.py:576
  41.1 0.6 collective-permute-start.17
  41.7 0.7 %shard_map.223 = f32[8,64,128]{2,1,0:T(8,128)} custom-call(f32[4,64,256]{2,1,0:T(8,128)S(1)} %shard_map.220.own.p_ref, f32[4,64,256]{2,1,0:T(8,128)S(1)} %collective-permute-done.18.p_mate.other), custom_call_target="tpu_custom_call" | custom-call | bytes 786432 | tf_op jit(solution)/shard_map/pallas_call | solution.py:650
  42.5 3.4 %shard_map.222.rest_0_ = f32[80,64,256]{2,1,0:T(8,128)S(1)} custom-call(f32[8]{0:T(128)} %stiffness_in.3, f32[8]{0:T(128)} %density_in.3, f32[4,64,256]{2,1,0:T(8,128)S(1)} %shard_map.220.own.p_ref, f32[4,64,256]{2,1,0:T(8,128)S(1)} %get-tuple-element.65.own.refs_0_.q_ref, f32[4,64,256]{2,1,0:T(8,128)S(1)} %collective-permute-done.18.p_mate.other, ...), custom_call_target="tpu_custom_call" | custom-call | flops 1310720000 | bytes 3276800 | tf_op jit(solution)/shard_map/pallas_call | solution.py:633
  46.3 2.5 %collective-permute-start.19 = (bf16[4,4,32,128]{3,2,1,0:T(8,128)(2,1)S(1)}, bf16[4,4,32,128]{3,2,1,0:T(8,128)(2,1)S(1)}, u32[]{:S(2)}, u32[]{:S(2)}) collective-permute-start(bf16[4,4,32,128]{3,2,1,0:T(8,128)(2,1)S(1)} %fusion.1), channel_id=1, source_target_pairs={{0,12},{4,8},{8,4},{12,0},{1,13},{5,9},{9,5},{13,1},{2,14},{6,10},... | collective-permute-start | bytes 393224 | tf_op jit(solution)/shard_map/ppermute | solution.py:576
  48.7 3.4 %shard_map.224.local = f32[80,64,256]{2,1,0:T(8,128)S(1)} custom-call(f32[8]{0:T(128)} %stiffness_in.3, f32[8]{0:T(128)} %density_in.3, f32[4,64,256]{2,1,0:T(8,128)S(1)} %shard_map.220.own.p_ref, f32[4,64,256]{2,1,0:T(8,128)S(1)} %get-tuple-element.65.own.refs_0_.q_ref, ...), custom_call_target="tpu_custom_call", output_to_operand_aliasing={{}: (10, {})} | custom-call | flops 1310720000 | bytes 3276800 | tf_op jit(solution)/shard_map/pallas_call | solution.py:633
  52.1 1.1 %collective-permute-done.19 = bf16[4,4,32,128]{3,2,1,0:T(8,128)(2,1)S(1)} collective-permute-done((bf16[4,4,32,128]{3,2,1,0:T(8,128)(2,1)S(1)}, bf16[4,4,32,128]{3,2,1,0:T(8,128)(2,1)S(1)}, u32[]{:S(2)}, u32[]{:S(2)}) %collective-permute-start.19) | collective-permute-done | bytes 131104 | tf_op jit(solution)/shard_map/ppermute | solution.py:576
  53.3 1.3 %collective-permute-done.20.other = bf16[4,4,32,128]{3,2,1,0:T(8,128)(2,1)S(1)} collective-permute-done((bf16[4,4,32,128]{3,2,1,0:T(8,128)(2,1)S(1)}, bf16[4,4,32,128]{3,2,1,0:T(8,128)(2,1)S(1)}, u32[]{:S(2)}, u32[]{:S(2)}) %collective-permute-start.20) | collective-permute-done | bytes 131104 | tf_op jit(solution)/shard_map/ppermute | solution.py:573
  54.7 5.0 %shard_map.225 = bf16[4,20,64,256]{3,2,1,0:T(8,128)(2,1)} custom-call(f32[4,4,32,128]{3,2,1,0:T(8,128)S(1)} %get-tuple-element.85.mine, bf16[4,4,32,128]{3,2,1,0:T(8,128)(2,1)S(1)} %collective-permute-done.20.other, f32[80,64,256]{2,1,0:T(8,128)S(1)} %shard_map.224.local, bf16[640,512]{1,0:T(8,128)(2,1)S(1)} %shard_map.217.left, ...), custom_call_target="tpu_custom_call" | custom-call | flops 131072000 | bytes 3932160 | tf_op jit(solution)/shard_map/pallas_call | solution.py:659
  (34 shorter events, 5.0 us)
Async XLA Ops:
  0.6 1.9 %collective-permute-start = (f32[8,64,128]{2,1,0:T(8,128)}, f32[8,64,128]{2,1,0:T(8,128)S(1)}, u32[]{:S(2)}, u32[]{:S(2)}) collective-permute-start(f32[8,64,128]{2,1,0:T(8,128)} %refs_3_.3), channel_id=1, source_target_pairs={{0,1},{1,0},{2,3},{3,2},{4,5},{5,4},{6,7},{7,6},{8,9},{9,8},{10,11... | collective-permute-start | bytes 786440 | tf_op jit(solution)/shard_map/ppermute | solution.py:542
  1.1 1.7 %collective-permute-start.1 = (f32[8,64,128]{2,1,0:T(8,128)}, f32[8,64,128]{2,1,0:T(8,128)S(1)}, u32[]{:S(2)}, u32[]{:S(2)}) collective-permute-start(f32[8,64,128]{2,1,0:T(8,128)} %refs_4_.2), channel_id=1, source_target_pairs={{0,1},{1,0},{2,3},{3,2},{4,5},{5,4},{6,7},{7,6},{8,9},{9,8},{10,11... | collective-permute-start | bytes 786440 | tf_op jit(solution)/shard_map/ppermute | solution.py:542
  1.2 2.0 %collective-permute-start.2 = (s32[8,64,128]{2,1,0:T(8,128)}, s32[8,64,128]{2,1,0:T(8,128)S(1)}, u32[]{:S(2)}, u32[]{:S(2)}) collective-permute-start(s32[8,64,128]{2,1,0:T(8,128)} %refs_5_.2), channel_id=1, source_target_pairs={{0,1},{1,0},{2,3},{3,2},{4,5},{5,4},{6,7},{7,6},{8,9},{9,8},{10,11... | collective-permute-start | bytes 786440 | tf_op jit(solution)/shard_map/ppermute | solution.py:542
  4.7 7.0 %collective-permute-start.3 = (f32[4,64,256]{2,1,0:T(8,128)S(1)}, f32[4,64,256]{2,1,0:T(8,128)S(1)}, u32[]{:S(2)}, u32[]{:S(2)}) collective-permute-start(f32[4,64,256]{2,1,0:T(8,128)S(1)} %get-tuple-element.43.refs_0_.refs_1_), channel_id=1, source_target_pairs={{0,1},{1,0},{2,3},{3,2},{4,5},{5,4},{6,7},{7,6},{8,9},{9,8},{10,11... | collective-permute-start | bytes 786440 | tf_op jit(solution)/shard_map/ppermute | solution.py:573
  5.2 5.7 %collective-permute-start.4 = (bf16[4,64,256]{2,1,0:T(8,128)(2,1)S(1)}, bf16[4,64,256]{2,1,0:T(8,128)(2,1)S(1)}, u32[]{:S(2)}, u32[]{:S(2)}) collective-permute-start(bf16[4,64,256]{2,1,0:T(8,128)(2,1)S(1)} %get-tuple-element.47), channel_id=1, source_target_pairs={{1,5},{5,1},{4,8},{8,4},{9,13},{13,9},{0,2},{12,14},{3,7},{7,3},{6... | collective-permute-start | bytes 393224 | tf_op jit(solution)/shard_map/ppermute | solution.py:589
  7.8 3.9 %collective-permute-start.5 = (f32[4,8,256]{2,1,0:T(8,128)S(1)}, f32[4,8,256]{2,1,0:T(8,128)S(1)}, u32[]{:S(2)}, u32[]{:S(2)}) collective-permute-start(f32[4,8,256]{2,1,0:T(8,128)S(1)} %get-tuple-element.51), channel_id=1, source_target_pairs={{0,2},{2,0},{1,3},{3,1},{4,6},{6,4},{5,7},{7,5},{8,10},{10,8},{9,1... | collective-permute-start | bytes 98312 | tf_op jit(solution)/shard_map/ppermute | solution.py:591
  10.2 11.6 %copy-start.2 = (bf16[640,80]{1,0:T(8,128)(2,1)S(1)}, bf16[640,80]{1,0:T(8,128)(2,1)}, u32[]{:S(2)}) copy-start(bf16[640,80]{1,0:T(8,128)(2,1)} %constant.34.clone.repeat_ref) | copy-start | bytes 307204
  12.7 5.8 %collective-permute-start.6 = (f32[4,64,256]{2,1,0:T(8,128)S(1)}, f32[4,64,256]{2,1,0:T(8,128)S(1)}, u32[]{:S(2)}, u32[]{:S(2)}) collective-permute-start(f32[4,64,256]{2,1,0:T(8,128)S(1)} %get-tuple-element.52.refs_0_.refs_1_), channel_id=1, source_target_pairs={{0,1},{1,0},{2,3},{3,2},{4,5},{5,4},{6,7},{7,6},{8,9},{9,8},{10,11... | collective-permute-start | bytes 786440 | tf_op jit(solution)/shard_map/ppermute | solution.py:573
  12.8 5.4 %collective-permute-start.7 = (bf16[4,64,256]{2,1,0:T(8,128)(2,1)S(1)}, bf16[4,64,256]{2,1,0:T(8,128)(2,1)S(1)}, u32[]{:S(2)}, u32[]{:S(2)}) collective-permute-start(bf16[4,64,256]{2,1,0:T(8,128)(2,1)S(1)} %get-tuple-element.53), channel_id=1, source_target_pairs={{1,5},{5,1},{4,8},{8,4},{9,13},{13,9},{0,2},{12,14},{3,7},{7,3},{6... | collective-permute-start | bytes 393224 | tf_op jit(solution)/shard_map/ppermute | solution.py:589
  14.6 3.9 %collective-permute-start.8 = (f32[4,8,256]{2,1,0:T(8,128)S(1)}, f32[4,8,256]{2,1,0:T(8,128)S(1)}, u32[]{:S(2)}, u32[]{:S(2)}) collective-permute-start(f32[4,8,256]{2,1,0:T(8,128)S(1)} %get-tuple-element.59), channel_id=1, source_target_pairs={{0,2},{2,0},{1,3},{3,1},{4,6},{6,4},{5,7},{7,5},{8,10},{10,8},{9,1... | collective-permute-start | bytes 98312 | tf_op jit(solution)/shard_map/ppermute | solution.py:591
  19.5 5.9 %collective-permute-start.9 = (f32[4,64,256]{2,1,0:T(8,128)S(1)}, f32[4,64,256]{2,1,0:T(8,128)S(1)}, u32[]{:S(2)}, u32[]{:S(2)}) collective-permute-start(f32[4,64,256]{2,1,0:T(8,128)S(1)} %get-tuple-element.60.refs_0_.refs_1_), channel_id=1, source_target_pairs={{0,1},{1,0},{2,3},{3,2},{4,5},{5,4},{6,7},{7,6},{8,9},{9,8},{10,11... | collective-permute-start | bytes 786440 | tf_op jit(solution)/shard_map/ppermute | solution.py:573
  19.8 5.3 %collective-permute-start.10 = (bf16[4,64,256]{2,1,0:T(8,128)(2,1)S(1)}, bf16[4,64,256]{2,1,0:T(8,128)(2,1)S(1)}, u32[]{:S(2)}, u32[]{:S(2)}) collective-permute-start(bf16[4,64,256]{2,1,0:T(8,128)(2,1)S(1)} %get-tuple-element.61), channel_id=1, source_target_pairs={{1,5},{5,1},{4,8},{8,4},{9,13},{13,9},{0,2},{12,14},{3,7},{7,3},{6... | collective-permute-start | bytes 393224 | tf_op jit(solution)/shard_map/ppermute | solution.py:589
  21.4 4.0 %collective-permute-start.11 = (f32[4,8,256]{2,1,0:T(8,128)S(1)}, f32[4,8,256]{2,1,0:T(8,128)S(1)}, u32[]{:S(2)}, u32[]{:S(2)}) collective-permute-start(f32[4,8,256]{2,1,0:T(8,128)S(1)} %get-tuple-element.64), channel_id=1, source_target_pairs={{0,2},{2,0},{1,3},{3,1},{4,6},{6,4},{5,7},{7,5},{8,10},{10,8},{9,1... | collective-permute-start | bytes 98312 | tf_op jit(solution)/shard_map/ppermute | solution.py:591
  26.4 2.2 %collective-permute-start.12 = (f32[4,64,256]{2,1,0:T(8,128)S(1)}, f32[4,64,256]{2,1,0:T(8,128)S(1)}, u32[]{:S(2)}, u32[]{:S(2)}) collective-permute-start(f32[4,64,256]{2,1,0:T(8,128)S(1)} %get-tuple-element.65.own.refs_0_.q_ref), channel_id=1, source_target_pairs={{0,1},{1,0},{2,3},{3,2},{4,5},{5,4},{6,7},{7,6},{8,9},{9,8},{10,11... | collective-permute-start | bytes 786440 | tf_op jit(solution)/shard_map/ppermute | solution.py:573
  26.5 5.4 %collective-permute-start.13 = (bf16[4,64,256]{2,1,0:T(8,128)(2,1)S(1)}, bf16[4,64,256]{2,1,0:T(8,128)(2,1)S(1)}, u32[]{:S(2)}, u32[]{:S(2)}) collective-permute-start(bf16[4,64,256]{2,1,0:T(8,128)(2,1)S(1)} %get-tuple-element.66), channel_id=1, source_target_pairs={{1,5},{5,1},{4,8},{8,4},{9,13},{13,9},{0,2},{12,14},{3,7},{7,3},{6... | collective-permute-start | bytes 393224 | tf_op jit(solution)/shard_map/ppermute | solution.py:589
  28.1 4.2 %collective-permute-start.14 = (f32[4,8,256]{2,1,0:T(8,128)S(1)}, f32[4,8,256]{2,1,0:T(8,128)S(1)}, u32[]{:S(2)}, u32[]{:S(2)}) collective-permute-start(f32[4,8,256]{2,1,0:T(8,128)S(1)} %get-tuple-element.70), channel_id=1, source_target_pairs={{0,2},{2,0},{1,3},{3,1},{4,6},{6,4},{5,7},{7,5},{8,10},{10,8},{9,1... | collective-permute-start | bytes 98312 | tf_op jit(solution)/shard_map/ppermute | solution.py:591
  34.2 1.3 %collective-permute-start.15 = (bf16[1,4,32,128]{3,2,1,0:T(8,128)(2,1)S(1)}, bf16[1,4,32,128]{3,2,1,0:T(8,128)(2,1)S(1)}, u32[]{:S(2)}, u32[]{:S(2)}) collective-permute-start(bf16[1,4,32,128]{3,2,1,0:T(8,128)(2,1)S(1)} %get-tuple-element.74), channel_id=1, source_target_pairs={{0,1},{1,0},{2,3},{3,2},{4,5},{5,4},{6,7},{7,6},{8,9},{9,8},{10,11... | collective-permute-start | bytes 98312 | tf_op jit(solution)/shard_map/ppermute | solution.py:573
  35.5 5.6 %collective-permute-start.16 = (bf16[4,4,32,128]{3,2,1,0:T(8,128)(2,1)S(1)}, bf16[4,4,32,128]{3,2,1,0:T(8,128)(2,1)S(1)}, u32[]{:S(2)}, u32[]{:S(2)}) collective-permute-start(bf16[4,4,32,128]{3,2,1,0:T(8,128)(2,1)S(1)} %fusion), channel_id=1, source_target_pairs={{0,2},{2,0},{1,3},{3,1},{4,6},{6,4},{5,7},{7,5},{8,10},{10,8},{9,1... | collective-permute-start | bytes 393224 | tf_op jit(solution)/shard_map/ppermute | solution.py:576
  36.7 5.0 %collective-permute-start.18 = (f32[4,64,256]{2,1,0:T(8,128)S(1)}, f32[4,64,256]{2,1,0:T(8,128)S(1)}, u32[]{:S(2)}, u32[]{:S(2)}) collective-permute-start(f32[4,64,256]{2,1,0:T(8,128)S(1)} %shard_map.220.own.p_ref), channel_id=1, source_target_pairs={{0,1},{1,0},{2,3},{3,2},{4,5},{5,4},{6,7},{7,6},{8,9},{9,8},{10,11... | collective-permute-start | bytes 786440 | tf_op jit(solution)/shard_map/ppermute | solution.py:573
  41.1 5.0 %collective-permute-start.17 = (bf16[4,4,32,128]{3,2,1,0:T(8,128)(2,1)S(1)}, bf16[4,4,32,128]{3,2,1,0:T(8,128)(2,1)S(1)}, u32[]{:S(2)}, u32[]{:S(2)}) collective-permute-start(bf16[4,4,32,128]{3,2,1,0:T(8,128)(2,1)S(1)} %fusion.2), channel_id=1, source_target_pairs={{0,4},{4,0},{8,12},{12,8},{1,5},{5,1},{9,13},{13,9},{2,6},{6,2},{1... | collective-permute-start | bytes 393224 | tf_op jit(solution)/shard_map/ppermute | solution.py:576
  46.2 8.5 %copy-start = (bf16[128,512]{1,0:T(8,128)(2,1)S(1)}, bf16[128,512]{1,0:T(8,128)(2,1)}, u32[]{:S(2)}) copy-start(bf16[128,512]{1,0:T(8,128)(2,1)} %constant.36.clone.table_z) | copy-start | bytes 393220
  46.2 8.4 %copy-start.1 = (bf16[2,64,64]{2,1,0:T(8,128)(2,1)S(1)}, bf16[2,64,64]{2,1,0:T(8,128)(2,1)}, u32[]{:S(2)}) copy-start(bf16[2,64,64]{2,1,0:T(8,128)(2,1)} %constant.35.clone.table_y) | copy-start | bytes 49156
  46.3 6.9 %collective-permute-start.19 = (bf16[4,4,32,128]{3,2,1,0:T(8,128)(2,1)S(1)}, bf16[4,4,32,128]{3,2,1,0:T(8,128)(2,1)S(1)}, u32[]{:S(2)}, u32[]{:S(2)}) collective-permute-start(bf16[4,4,32,128]{3,2,1,0:T(8,128)(2,1)S(1)} %fusion.1), channel_id=1, source_target_pairs={{0,12},{4,8},{8,4},{12,0},{1,13},{5,9},{9,5},{13,1},{2,14},{6,10},... | collective-permute-start | bytes 393224 | tf_op jit(solution)/shard_map/ppermute | solution.py:576
  53.3 1.4 %collective-permute-start.20 = (bf16[4,4,32,128]{3,2,1,0:T(8,128)(2,1)S(1)}, bf16[4,4,32,128]{3,2,1,0:T(8,128)(2,1)S(1)}, u32[]{:S(2)}, u32[]{:S(2)}) collective-permute-start(bf16[4,4,32,128]{3,2,1,0:T(8,128)(2,1)S(1)} %get-tuple-element.84), channel_id=1, source_target_pairs={{0,1},{1,0},{2,3},{3,2},{4,5},{5,4},{6,7},{7,6},{8,9},{9,8},{10,11... | collective-permute-start | bytes 393224 | tf_op jit(solution)/shard_map/ppermute | solution.py:573

commit v10 on v9

--- a/solution.py
+++ b/solution.py
@@ -105,30 +105,42 @@
     return (lax.axis_index("gz") + lax.axis_index("gx")) % 2
 
 
-def assemble_body(count, *refs):
-    tables_in, own_in, got = refs[:3], refs[3:6], refs[6:9]
-    p_out, q_out, ratio, bend, sent, cells = refs[9:15]
-    edge_outs = refs[15 : 15 + count]
-    tables, own, semaphores = refs[15 + count : 18 + count], refs[18 + count : 21 + count], refs[21 + count]
-    core, column = lax.axis_index("gz"), lax.axis_index("gy")
-    rows, brick_y = p_out.shape[:2]
+def fetch_body(*refs):
+    tables_in, own_in = refs[:3], refs[3:6]
+    p_out, q_out, m_out = refs[6:9]
+    tables_out = refs[9]
+    tables, semaphores = refs[10:13], refs[13]
+    rows = p_out.shape[0]
     start = slot() * rows
     sources = [source.at[pl.ds(start, rows)] for source in own_in[:2]] + [own_in[2]]
-    copies = [
-        pltpu.make_async_copy(source, target, semaphores.at[index])
-        for index, (source, target) in enumerate(zip(list(tables_in) + sources, list(tables) + list(own)))
-    ]
-    for copy in copies:
-        copy.start()
+    copies = begin(list(tables_in) + sources, list(tables) + [p_out, q_out, m_out], semaphores)
     for copy in copies:
         copy.wait()
     stiffness, density, nonlinear = tables
-    entries = stiffness.shape[0]
+    for entry in range(stiffness.shape[0]):
+        tables_out[2 * entry] = jnp.full(tables_out.shape[1:], stiffness[entry] / density[entry], F32)
+        tables_out[2 * entry + 1] = jnp.full(tables_out.shape[1:], nonlinear[entry], F32)
+
+
+def assemble_body(count, *refs):
+    own, tables, got = refs[:3], refs[3], refs[4:7]
+    p_out, q_out, ratio, bend, sent, cells = refs[7:13]
+    edge_outs = refs[13 : 13 + count]
+    core, column = lax.axis_index("gz"), lax.axis_index("gy")
+    rows, brick_y, depth = p_out.shape
+    start = slot() * rows
+    entries = tables.shape[0] // 2
 
     def whole(mine, other):
         return jnp.concatenate(
             [jnp.where(core == 0, mine, other), jnp.where(core == 0, other, mine)], axis=-1
         )
+
+    def chosen(cell, place):
+        result = jnp.broadcast_to(tables[place, 0:1, 0:1], cell.shape)
+        for entry in range(1, entries):
+            result = jnp.where(cell == entry, jnp.broadcast_to(tables[2 * entry + place, 0:1, 0:1], cell.shape), result)
+        return result
 
     for row in range(cells.shape[0]):
         cells[row] = whole(own[2][row], got[2][row])
@@ -138,8 +150,8 @@
         sent[row] = value.astype(BF16)
         q_out[row] = whole(own[1][row], got[1][start + row])
         cell = cells[start + row]
-        ratio[row] = looked_up(cell, lambda e: stiffness[e] / density[e], entries)
-        bend[row] = looked_up(cell, lambda e: nonlinear[e], entries)
+        ratio[row] = chosen(cell, 0)
+        bend[row] = chosen(cell, 1)
     edges(lambda a, b: p_out[:, a:b, :], edge_outs, column % 2, brick_y)
 
 
@@ -541,12 +553,18 @@
     swap_core = xor_pairs(core_count, 1)
     got = [lax.ppermute(array, "gz", swap_core) for array in (pressure, previous, material)]
     sending = shape(rows, brick_y, total_z, dtype=BF16)
+    half = (rows, brick_y, brick_z)
+    fetched = call(
+        fetch_body,
+        [shape(*half), shape(*half), shape(brick_x, brick_y, brick_z, dtype=jnp.int32), shape(2 * stiffness.shape[0], 8, 128)],
+        [HBM] * 6, [pltpu.SMEM(stiffness.shape, F32)] * 3 + [pltpu.SemaphoreType.DMA((6,))], moved=cells_count * 8
+    )(*here(stiffness, density, nonlinear, pressure, previous, material))
+    fetched, got = lax.optimization_barrier((fetched, got))
     current, before, ratio, bend, sent, cells, *edge_values = call(
         lambda *refs: assemble_body(len(edge), *refs),
-        [field] * 4 + [sending, shape(brick_x, brick_y, total_z, dtype=jnp.int32)] + edge, [HBM] * 6 + [VMEM] * 3,
-        [pltpu.SMEM(stiffness.shape, F32)] * 3 + [pltpu.VMEM((rows, brick_y, brick_z), F32)] * 2
-        + [pltpu.VMEM((brick_x, brick_y, brick_z), jnp.int32), pltpu.SemaphoreType.DMA((6,))], moved=cells_count * 36
-    )(*here(stiffness, density, nonlinear, pressure, previous, material), *got)
+        [field] * 4 + [sending, shape(brick_x, brick_y, total_z, dtype=jnp.int32)] + edge, [VMEM] * 7,
+        moved=cells_count * 36
+    )(*fetched, *got)
 
     weights = (
         stiffness, density, mode_weight.transpose(0, 2, 1, 3), lift_weight, lift_bias.reshape(1, channels),
@@ -593,16 +611,6 @@
             halos.append(lax.ppermute(edge_values[1], "gy", odd_pairs(column_count)))
         if repeat == 0:
             far, early = lax.optimization_barrier((far, early))
-        if repeat == 2:
-            repeats = np.repeat(np.eye(height), 8, 0).astype(ml_dtypes.bfloat16)
-            wide_mixing = call(
-                widen_body, shape(height * 8, 16 * coupled, dtype=BF16), [VMEM] * 2, flops=1_000_000_000, moved=2_000_000
-            )(mixing, repeats)
-            far, wide_mixing = lax.optimization_barrier((far, wide_mixing))
-        if repeat == 1:
-            far, mixing, pointwise, lift_table, offset = lax.optimization_barrier(
-                (far, mixing, pointwise, lift_table, offset)
-            )
         if last:
             prior = spectrum(prior_body, shape(modes_x // 2, modes_y, width), 2, brick_x, None, twiddle_room)(
                 *twiddles, current, mate, forward_z, forward_y
@@ -645,13 +653,21 @@
 
     for index, stage in enumerate(stages):
         arrived = exchange(total, *stage)
+        if index == 0:
+            arrived, mixing, pointwise, lift_table, offset = lax.optimization_barrier(
+                (arrived, mixing, pointwise, lift_table, offset)
+            )
         if index == len(stages) - 2:
             local = pointwise_part(0)
             wave = call(join_body, shape(*pressure.shape), [VMEM] * 2, moved=cells_count * 12)(current, wave_other)
             arrived, local, wave = lax.optimization_barrier((arrived, local, wave))
         if index == len(stages) - 1:
             local = pointwise_part(steps // 2, (local,))
-            arrived, local = lax.optimization_barrier((arrived, local))
+            repeats = np.repeat(np.eye(height), 8, 0).astype(ml_dtypes.bfloat16)
+            wide_mixing = call(
+                widen_body, shape(height * 8, 16 * coupled, dtype=BF16), [VMEM] * 2, flops=1_000_000_000, moved=2_000_000
+            )(mixing, repeats)
+            arrived, local, wide_mixing = lax.optimization_barrier((arrived, local, wide_mixing))
         total = total + arrived.astype(F32)
     other = swap(total.astype(BF16))
     batch = min(32, brick_y)

time: 60 us -> 58.6 us (0.977)
  waiting for transfers between devices: 18 us -> 16.1 us
    ppermute x4, waiting for transfers between devices: 1.88 us -> 8.66 us  [per_device(): halos = [lax.ppermute(edge_values[0], 'gy', xor_pairs(column_count, 1))]]
    ppermute x4, waiting for transfers between devices: 6.17 us -> 2.56 us  [per_device(): lax.ppermute(sent, ('gx', 'gy', 'gz'), row_pairs(cycle_count, column_count))]
    ppermute x3, waiting for transfers between devices: 5.76 us -> 2.43 us  [exchange(): return lax.ppermute(value.astype(BF16), axis, xor_pairs(count, distance))]
    ppermute x3, waiting for transfers between devices: 1.61 us -> 0.41 us  [per_device(): lax.ppermute(array, 'gz', swap_core)]
    pallas_call x0 -> x1, Pallas kernels: none -> 1.18 us  [per_device(): call(fetch_body, [shape(*half), shape(*half), shape(brick_x, brick_y, bri...]
    pallas_call x1, Pallas kernels: 1.47 us -> 0.36 us  [per_device(): call(lambda *refs: assemble_body(len(edge), *refs), [field] * 4 + [sendin...]
  transfers between devices with their start and end apart: 21 -> 21, of which waited for: 16 -> 12; matrix products, arithmetic and copies ran while one was open for 0% -> 0% of each run, Pallas kernels for 24% -> 26%
where the time goes in v10:
time: 58.6 us; the launch traced here: 58.3 us
  Pallas kernels  25.6 us (44%)
  waiting for transfers between devices  16.1 us (27%)
  starting transfers between devices  15.5 us (26%)
  between operations  0.86 us (1%)
    ppermute x4, waiting for transfers between devices, per_device(): halos = [lax.ppermute(edge_values[0], 'gy', xor_pairs(column_count, 1))]  8.66 us
    ppermute x4, starting transfers between devices, per_device(): lax.ppermute(sent, ('gx', 'gy', 'gz'), row_pairs(cycle_count, column_count))  7.96 us
    pallas_call x2, Pallas kernels, pointwise_part(): pl.pallas_call(pointwise_body, grid=(steps // 2,), out_shape=shape(height...  6.81 us
    pallas_call x1, Pallas kernels, per_device(): pl.pallas_call(output_body, grid=(brick_y // batch,), out_shape=shape(row...  5.01 us
    ppermute x3, starting transfers between devices, exchange(): return lax.ppermute(value.astype(BF16), axis, xor_pairs(count, distance))  4.27 us
    pallas_call x4, Pallas kernels, per_device(): call(body, outs, [VMEM] * (6 + len(halos)), [pltpu.VMEM((brick_y + 2 * ED...  3.89 us
    pallas_call x1, Pallas kernels, per_device(): call(prepare_body, [shape(height, 2 * coupled, dtype=BF16), shape(height,...  2.81 us
    ppermute x4, waiting for transfers between devices, per_device(): lax.ppermute(sent, ('gx', 'gy', 'gz'), row_pairs(cycle_count, column_count))  2.56 us
  transfers between devices with their start and end apart: 21, of which 12 were waited for; matrix products, arithmetic and copies ran while one was open for 0% of the time, Pallas kernels for 26%

profile of v10, /device:TPU:0, one launch (start us, length us, event | category | flops | bytes accessed | tf_op | source)
XLA Modules:
  0.0 58.3 jit_solution(17251665675129683977)
XLA Ops:
  0.6 0.5 collective-permute-start
  1.7 1.2 %shard_map.212 = (f32[4,64,128]{2,1,0:T(8,128)S(1)}, f32[4,64,128]{2,1,0:T(8,128)S(1)}, s32[8,64,128]{2,1,0:T(8,128)S(1)}, f32[16,8,128]{2,1,0:T(8,128)S(1)}) custom-call(f32[8]{0:T(128)} %stiffness_in.3, f32[8]{0:T(128)} %density_in.3, f32[8]{0:T(128)} %refs_2_.2, f32[8,64,128]{2,1,0:T(8,128)} %refs_3_.3, f32[8,64,128]{2,1,0:T(8,128)} %refs_4_.2, ...), custom_call_target="tpu_custom_call" | custom-call | bytes 524288 | tf_op jit(solution)/shard_map/pallas_call | solution.py:557
  4.1 2.6 %collective-permute-start.4 = (bf16[4,64,256]{2,1,0:T(8,128)(2,1)S(1)}, bf16[4,64,256]{2,1,0:T(8,128)(2,1)S(1)}, u32[]{:S(2)}, u32[]{:S(2)}) collective-permute-start(bf16[4,64,256]{2,1,0:T(8,128)(2,1)S(1)} %get-tuple-element.68), channel_id=1, source_target_pairs={{1,5},{5,1},{4,8},{8,4},{9,13},{13,9},{0,2},{12,14},{3,7},{7,3},{6... | collective-permute-start | bytes 393224 | tf_op jit(solution)/shard_map/ppermute | solution.py:607
  6.7 2.3 %shard_map.214 = (f32[2,4,32,128]{3,2,1,0:T(8,128)S(1)}, bf16[256,128]{1,0:T(8,128)(2,1)S(1)}, bf16[2,32,256]{2,1,0:T(8,128)(2,1)S(1)}) custom-call(f32[512]{0:T(512)} %constant.31.clone.refs_0_.twiddles, f32[8]{0:T(128)} %stiffness_in.3, f32[8]{0:T(128)} %density_in.3, bf16[256,128]{1,0:T(8,128)(2,1)} %constant.32.clone.refs_3_, ...), custom_call_target="tpu_custom_call" | custom-call | flops 268435456 | bytes 2097152 | tf_op jit(solution)/shard_map/pallas_call | solution.py:597
  9.1 0.7 %collective-permute-done.4.refs_5_ = bf16[4,64,256]{2,1,0:T(8,128)(2,1)S(1)} collective-permute-done((bf16[4,64,256]{2,1,0:T(8,128)(2,1)S(1)}, bf16[4,64,256]{2,1,0:T(8,128)(2,1)S(1)}, u32[]{:S(2)}, u32[]{:S(2)}) %collective-permute-start.4) | collective-permute-done | bytes 131104 | tf_op jit(solution)/shard_map/ppermute | solution.py:607
  9.8 0.8 %collective-permute-done.5.refs_6_ = f32[4,8,256]{2,1,0:T(8,128)S(1)} collective-permute-done((f32[4,8,256]{2,1,0:T(8,128)S(1)}, f32[4,8,256]{2,1,0:T(8,128)S(1)}, u32[]{:S(2)}, u32[]{:S(2)}) %collective-permute-start.5) | collective-permute-done | bytes 32800 | tf_op jit(solution)/shard_map/ppermute | solution.py:609
  10.6 1.0 %shard_map.215 = (f32[4,64,256]{2,1,0:T(8,128)S(1)}, bf16[4,64,256]{2,1,0:T(8,128)(2,1)S(1)}, f32[4,8,256]{2,1,0:T(8,128)S(1)}) custom-call(f32[4,64,256]{2,1,0:T(8,128)S(1)} %get-tuple-element.64.refs_0_.refs_1_, f32[4,64,256]{2,1,0:T(8,128)S(1)} %get-tuple-element.65.refs_1_, f32[4,64,256]{2,1,0:T(8,128)S(1)} %get-tuple-element.66.refs_2_, ...), custom_call_target="tpu_custom_call" | custom-call | flops 3932160 | bytes 1835008 | tf_op jit(solution)/shard_map/pallas_call | solution.py:622
  11.7 1.8 %collective-permute-start.7 = (bf16[4,64,256]{2,1,0:T(8,128)(2,1)S(1)}, bf16[4,64,256]{2,1,0:T(8,128)(2,1)S(1)}, u32[]{:S(2)}, u32[]{:S(2)}) collective-permute-start(bf16[4,64,256]{2,1,0:T(8,128)(2,1)S(1)} %get-tuple-element.74), channel_id=1, source_target_pairs={{1,5},{5,1},{4,8},{8,4},{9,13},{13,9},{0,2},{12,14},{3,7},{7,3},{6... | collective-permute-start | bytes 393224 | tf_op jit(solution)/shard_map/ppermute | solution.py:607
  13.8 3.6 %collective-permute-done.8.refs_6_ = f32[4,8,256]{2,1,0:T(8,128)S(1)} collective-permute-done((f32[4,8,256]{2,1,0:T(8,128)S(1)}, f32[4,8,256]{2,1,0:T(8,128)S(1)}, u32[]{:S(2)}, u32[]{:S(2)}) %collective-permute-start.8) | collective-permute-done | bytes 32800 | tf_op jit(solution)/shard_map/ppermute | solution.py:609
  17.4 1.0 %shard_map.216 = (f32[4,64,256]{2,1,0:T(8,128)S(1)}, bf16[4,64,256]{2,1,0:T(8,128)(2,1)S(1)}, f32[4,8,256]{2,1,0:T(8,128)S(1)}) custom-call(f32[4,64,256]{2,1,0:T(8,128)S(1)} %get-tuple-element.73.refs_0_.refs_1_, f32[4,64,256]{2,1,0:T(8,128)S(1)} %get-tuple-element.64.refs_0_.refs_1_, f32[4,64,256]{2,1,0:T(8,128)S(1)} %get-tuple-element.66.refs_2_, ...), custom_call_target="tpu_custom_call" | custom-call | flops 3932160 | bytes 1835008 | tf_op jit(solution)/shard_map/pallas_call | solution.py:622
  18.5 1.8 %collective-permute-start.10 = (bf16[4,64,256]{2,1,0:T(8,128)(2,1)S(1)}, bf16[4,64,256]{2,1,0:T(8,128)(2,1)S(1)}, u32[]{:S(2)}, u32[]{:S(2)}) collective-permute-start(bf16[4,64,256]{2,1,0:T(8,128)(2,1)S(1)} %get-tuple-element.77), channel_id=1, source_target_pairs={{1,5},{5,1},{4,8},{8,4},{9,13},{13,9},{0,2},{12,14},{3,7},{7,3},{6... | collective-permute-start | bytes 393224 | tf_op jit(solution)/shard_map/ppermute | solution.py:607
  20.6 3.6 %collective-permute-done.11.refs_6_ = f32[4,8,256]{2,1,0:T(8,128)S(1)} collective-permute-done((f32[4,8,256]{2,1,0:T(8,128)S(1)}, f32[4,8,256]{2,1,0:T(8,128)S(1)}, u32[]{:S(2)}, u32[]{:S(2)}) %collective-permute-start.11) | collective-permute-done | bytes 32800 | tf_op jit(solution)/shard_map/ppermute | solution.py:609
  24.2 1.0 %shard_map.217 = (f32[4,64,256]{2,1,0:T(8,128)S(1)}, bf16[4,64,256]{2,1,0:T(8,128)(2,1)S(1)}, f32[4,8,256]{2,1,0:T(8,128)S(1)}) custom-call(f32[4,64,256]{2,1,0:T(8,128)S(1)} %get-tuple-element.76.refs_0_.refs_1_, f32[4,64,256]{2,1,0:T(8,128)S(1)} %get-tuple-element.73.refs_0_.refs_1_, f32[4,64,256]{2,1,0:T(8,128)S(1)} %get-tuple-element.66.refs_2_, ...), custom_call_target="tpu_custom_call" | custom-call | flops 3932160 | bytes 1835008 | tf_op jit(solution)/shard_map/pallas_call | solution.py:622
  25.3 1.7 %collective-permute-start.13 = (bf16[4,64,256]{2,1,0:T(8,128)(2,1)S(1)}, bf16[4,64,256]{2,1,0:T(8,128)(2,1)S(1)}, u32[]{:S(2)}, u32[]{:S(2)}) collective-permute-start(bf16[4,64,256]{2,1,0:T(8,128)(2,1)S(1)} %get-tuple-element.80), channel_id=1, source_target_pairs={{1,5},{5,1},{4,8},{8,4},{9,13},{13,9},{0,2},{12,14},{3,7},{7,3},{6... | collective-permute-start | bytes 393224 | tf_op jit(solution)/shard_map/ppermute | solution.py:607
  27.4 1.1 %shard_map.218.prior = f32[4,32,128]{2,1,0:T(8,128)S(1)} custom-call(f32[512]{0:T(512)} %constant.31.clone.refs_0_.twiddles, f32[4,64,256]{2,1,0:T(8,128)S(1)} %get-tuple-element.79.own.refs_0_.q_ref, f32[4,64,256]{2,1,0:T(8,128)S(1)} %collective-permute-done.12.mate.refs_4_.q_mate, bf16[256,128]{1,0:T(8,128)(2,1)S(1)} %get-tuple-element.81.table_z, ...), custom_call_target="tpu_custom_call" | custom-call | flops 134217728 | bytes 1048576 | tf_op jit(solution)/shard_map/pallas_call | solution.py:615
  28.5 1.9 %collective-permute-done.13.refs_5_ = bf16[4,64,256]{2,1,0:T(8,128)(2,1)S(1)} collective-permute-done((bf16[4,64,256]{2,1,0:T(8,128)(2,1)S(1)}, bf16[4,64,256]{2,1,0:T(8,128)(2,1)S(1)}, u32[]{:S(2)}, u32[]{:S(2)}) %collective-permute-start.13) | collective-permute-done | bytes 131104 | tf_op jit(solution)/shard_map/ppermute | solution.py:607
  30.3 0.5 collective-permute-done.14.refs_6_
  30.9 1.0 %shard_map.219.own.p_ref = f32[4,64,256]{2,1,0:T(8,128)S(1)} custom-call(f32[4,64,256]{2,1,0:T(8,128)S(1)} %get-tuple-element.79.own.refs_0_.q_ref, f32[4,64,256]{2,1,0:T(8,128)S(1)} %get-tuple-element.76.refs_0_.refs_1_, f32[4,64,256]{2,1,0:T(8,128)S(1)} %get-tuple-element.66.refs_2_, f32[4,64,256]{2,1,0:T(8,128)S(1)} %get-tuple-element.67.refs_3_, ...), custom_call_target="tpu_custom_call" | custom-call | flops 3932160 | bytes 1835008 | tf_op jit(solution)/shard_map/pallas_call | solution.py:622
  31.9 0.9 %shard_map.220 = (f32[4,4,32,128]{3,2,1,0:T(8,128)S(1)}, bf16[1,4,32,128]{3,2,1,0:T(8,128)(2,1)S(1)}) custom-call(f32[512]{0:T(512)} %constant.31.clone.refs_0_.twiddles, f32[4,64,256]{2,1,0:T(8,128)S(1)} %shard_map.219.own.p_ref, f32[4,32,128]{2,1,0:T(8,128)S(1)} %shard_map.218.prior, f32[2,4,32,128]{3,2,1,0:T(8,128)S(1)} %get-tuple-element.86.early, ...), custom_call_target="tpu_custom_call" | custom-call | flops 67108864 | bytes 524288 | tf_op jit(solution)/shard_map/pallas_call | solution.py:630
  32.9 0.5 collective-permute-start.18
  33.4 0.7 %collective-permute-done.15 = bf16[1,4,32,128]{3,2,1,0:T(8,128)(2,1)S(1)} collective-permute-done((bf16[1,4,32,128]{3,2,1,0:T(8,128)(2,1)S(1)}, bf16[1,4,32,128]{3,2,1,0:T(8,128)(2,1)S(1)}, u32[]{:S(2)}, u32[]{:S(2)}) %collective-permute-start.15) | collective-permute-done | bytes 32800 | tf_op jit(solution)/shard_map/ppermute | solution.py:591
  34.1 1.5 %collective-permute-start.16 = (bf16[4,4,32,128]{3,2,1,0:T(8,128)(2,1)S(1)}, bf16[4,4,32,128]{3,2,1,0:T(8,128)(2,1)S(1)}, u32[]{:S(2)}, u32[]{:S(2)}) collective-permute-start(bf16[4,4,32,128]{3,2,1,0:T(8,128)(2,1)S(1)} %fusion), channel_id=1, source_target_pairs={{0,2},{2,0},{1,3},{3,1},{4,6},{6,4},{5,7},{7,5},{8,10},{10,8},{9,1... | collective-permute-start | bytes 393224 | tf_op jit(solution)/shard_map/ppermute | solution.py:594
  35.6 2.8 %shard_map.221 = (bf16[80,64]{1,0:T(8,128)(2,1)S(1)}, bf16[80,128]{1,0:T(8,128)(2,1)S(1)}, f32[24,8]{1,0:T(8,128)S(1)}, f32[80,1]{1,0:T(8,128)S(1)}) custom-call(f32[8]{0:T(128)} %stiffness_in.3, f32[8]{0:T(128)} %density_in.3, f32[2,20,8,20]{3,2,1,0:T(8,128)} %bitcast.4, f32[4,20]{1,0:T(4,128)} %refs_3_.4, f32[1,20]{1,0:T(1,128)} %bitcast.5, ...), custom_call_target="tpu_custom_call" | custom-call | flops 2000000000 | bytes 4000000 | tf_op jit(solution)/shard_map/pallas_call | solution.py:573
  38.4 1.3 %collective-permute-done.16 = bf16[4,4,32,128]{3,2,1,0:T(8,128)(2,1)S(1)} collective-permute-done((bf16[4,4,32,128]{3,2,1,0:T(8,128)(2,1)S(1)}, bf16[4,4,32,128]{3,2,1,0:T(8,128)(2,1)S(1)}, u32[]{:S(2)}, u32[]{:S(2)}) %collective-permute-start.16) | collective-permute-done | bytes 131104 | tf_op jit(solution)/shard_map/ppermute | solution.py:594
  39.9 0.7 %shard_map.223 = f32[8,64,128]{2,1,0:T(8,128)} custom-call(f32[4,64,256]{2,1,0:T(8,128)S(1)} %shard_map.219.own.p_ref, f32[4,64,256]{2,1,0:T(8,128)S(1)} %collective-permute-done.18.p_mate.other), custom_call_target="tpu_custom_call" | custom-call | bytes 786432 | tf_op jit(solution)/shard_map/pallas_call | solution.py:662
  40.6 3.4 %shard_map.222.rest_0_ = f32[80,64,256]{2,1,0:T(8,128)S(1)} custom-call(f32[8]{0:T(128)} %stiffness_in.3, f32[8]{0:T(128)} %density_in.3, f32[4,64,256]{2,1,0:T(8,128)S(1)} %shard_map.219.own.p_ref, f32[4,64,256]{2,1,0:T(8,128)S(1)} %get-tuple-element.79.own.refs_0_.q_ref, f32[4,64,256]{2,1,0:T(8,128)S(1)} %collective-permute-done.18.p_mate.other, ...), custom_call_target="tpu_custom_call" | custom-call | flops 1310720000 | bytes 3276800 | tf_op jit(solution)/shard_map/pallas_call | solution.py:641
  44.0 0.8 %collective-permute-done.17 = bf16[4,4,32,128]{3,2,1,0:T(8,128)(2,1)S(1)} collective-permute-done((bf16[4,4,32,128]{3,2,1,0:T(8,128)(2,1)S(1)}, bf16[4,4,32,128]{3,2,1,0:T(8,128)(2,1)S(1)}, u32[]{:S(2)}, u32[]{:S(2)}) %collective-permute-start.17) | collective-permute-done | bytes 131104 | tf_op jit(solution)/shard_map/ppermute | solution.py:594
  44.9 2.7 %collective-permute-start.19 = (bf16[4,4,32,128]{3,2,1,0:T(8,128)(2,1)S(1)}, bf16[4,4,32,128]{3,2,1,0:T(8,128)(2,1)S(1)}, u32[]{:S(2)}, u32[]{:S(2)}) collective-permute-start(bf16[4,4,32,128]{3,2,1,0:T(8,128)(2,1)S(1)} %fusion.1), channel_id=1, source_target_pairs={{0,12},{4,8},{8,4},{12,0},{1,13},{5,9},{9,5},{13,1},{2,14},{6,10},... | collective-permute-start | bytes 393224 | tf_op jit(solution)/shard_map/ppermute | solution.py:594
  47.6 0.4 shard_map.225.left
  48.1 3.4 %shard_map.224.local = f32[80,64,256]{2,1,0:T(8,128)S(1)} custom-call(f32[8]{0:T(128)} %stiffness_in.3, f32[8]{0:T(128)} %density_in.3, f32[4,64,256]{2,1,0:T(8,128)S(1)} %shard_map.219.own.p_ref, f32[4,64,256]{2,1,0:T(8,128)S(1)} %get-tuple-element.79.own.refs_0_.q_ref, ...), custom_call_target="tpu_custom_call", output_to_operand_aliasing={{}: (10, {})} | custom-call | flops 1310720000 | bytes 3276800 | tf_op jit(solution)/shard_map/pallas_call | solution.py:641
  52.0 1.3 %collective-permute-done.20.other = bf16[4,4,32,128]{3,2,1,0:T(8,128)(2,1)S(1)} collective-permute-done((bf16[4,4,32,128]{3,2,1,0:T(8,128)(2,1)S(1)}, bf16[4,4,32,128]{3,2,1,0:T(8,128)(2,1)S(1)}, u32[]{:S(2)}, u32[]{:S(2)}) %collective-permute-start.20) | collective-permute-done | bytes 131104 | tf_op jit(solution)/shard_map/ppermute | solution.py:591
  53.3 5.0 %shard_map.226 = bf16[4,20,64,256]{3,2,1,0:T(8,128)(2,1)} custom-call(f32[4,4,32,128]{3,2,1,0:T(8,128)S(1)} %get-tuple-element.105.mine, bf16[4,4,32,128]{3,2,1,0:T(8,128)(2,1)S(1)} %collective-permute-done.20.other, f32[80,64,256]{2,1,0:T(8,128)S(1)} %shard_map.224.local, bf16[640,512]{1,0:T(8,128)(2,1)S(1)} %shard_map.225.left, ...), custom_call_target="tpu_custom_call" | custom-call | flops 131072000 | bytes 3932160 | tf_op jit(solution)/shard_map/pallas_call | solution.py:675
  (35 shorter events, 3.6 us)
Async XLA Ops:
  0.6 2.2 %collective-permute-start = (f32[8,64,128]{2,1,0:T(8,128)}, f32[8,64,128]{2,1,0:T(8,128)S(1)}, u32[]{:S(2)}, u32[]{:S(2)}) collective-permute-start(f32[8,64,128]{2,1,0:T(8,128)} %refs_3_.3), channel_id=1, source_target_pairs={{0,1},{1,0},{2,3},{3,2},{4,5},{5,4},{6,7},{7,6},{8,9},{9,8},{10,11... | collective-permute-start | bytes 786440 | tf_op jit(solution)/shard_map/ppermute | solution.py:554
  1.1 1.7 %collective-permute-start.1 = (f32[8,64,128]{2,1,0:T(8,128)}, f32[8,64,128]{2,1,0:T(8,128)S(1)}, u32[]{:S(2)}, u32[]{:S(2)}) collective-permute-start(f32[8,64,128]{2,1,0:T(8,128)} %refs_4_.2), channel_id=1, source_target_pairs={{0,1},{1,0},{2,3},{3,2},{4,5},{5,4},{6,7},{7,6},{8,9},{9,8},{10,11... | collective-permute-start | bytes 786440 | tf_op jit(solution)/shard_map/ppermute | solution.py:554
  1.2 2.0 %collective-permute-start.2 = (s32[8,64,128]{2,1,0:T(8,128)}, s32[8,64,128]{2,1,0:T(8,128)S(1)}, u32[]{:S(2)}, u32[]{:S(2)}) collective-permute-start(s32[8,64,128]{2,1,0:T(8,128)} %refs_5_.2), channel_id=1, source_target_pairs={{0,1},{1,0},{2,3},{3,2},{4,5},{5,4},{6,7},{7,6},{8,9},{9,8},{10,11... | collective-permute-start | bytes 786440 | tf_op jit(solution)/shard_map/ppermute | solution.py:554
  3.6 7.0 %collective-permute-start.3 = (f32[4,64,256]{2,1,0:T(8,128)S(1)}, f32[4,64,256]{2,1,0:T(8,128)S(1)}, u32[]{:S(2)}, u32[]{:S(2)}) collective-permute-start(f32[4,64,256]{2,1,0:T(8,128)S(1)} %get-tuple-element.64.refs_0_.refs_1_), channel_id=1, source_target_pairs={{0,1},{1,0},{2,3},{3,2},{4,5},{5,4},{6,7},{7,6},{8,9},{9,8},{10,11... | collective-permute-start | bytes 786440 | tf_op jit(solution)/shard_map/ppermute | solution.py:591
  4.1 5.7 %collective-permute-start.4 = (bf16[4,64,256]{2,1,0:T(8,128)(2,1)S(1)}, bf16[4,64,256]{2,1,0:T(8,128)(2,1)S(1)}, u32[]{:S(2)}, u32[]{:S(2)}) collective-permute-start(bf16[4,64,256]{2,1,0:T(8,128)(2,1)S(1)} %get-tuple-element.68), channel_id=1, source_target_pairs={{1,5},{5,1},{4,8},{8,4},{9,13},{13,9},{0,2},{12,14},{3,7},{7,3},{6... | collective-permute-start | bytes 393224 | tf_op jit(solution)/shard_map/ppermute | solution.py:607
  6.7 3.9 %collective-permute-start.5 = (f32[4,8,256]{2,1,0:T(8,128)S(1)}, f32[4,8,256]{2,1,0:T(8,128)S(1)}, u32[]{:S(2)}, u32[]{:S(2)}) collective-permute-start(f32[4,8,256]{2,1,0:T(8,128)S(1)} %get-tuple-element.72), channel_id=1, source_target_pairs={{0,2},{2,0},{1,3},{3,1},{4,6},{6,4},{5,7},{7,5},{8,10},{10,8},{9,1... | collective-permute-start | bytes 98312 | tf_op jit(solution)/shard_map/ppermute | solution.py:609
  11.6 5.8 %collective-permute-start.6 = (f32[4,64,256]{2,1,0:T(8,128)S(1)}, f32[4,64,256]{2,1,0:T(8,128)S(1)}, u32[]{:S(2)}, u32[]{:S(2)}) collective-permute-start(f32[4,64,256]{2,1,0:T(8,128)S(1)} %get-tuple-element.73.refs_0_.refs_1_), channel_id=1, source_target_pairs={{0,1},{1,0},{2,3},{3,2},{4,5},{5,4},{6,7},{7,6},{8,9},{9,8},{10,11... | collective-permute-start | bytes 786440 | tf_op jit(solution)/shard_map/ppermute | solution.py:591
  11.7 5.7 %collective-permute-start.7 = (bf16[4,64,256]{2,1,0:T(8,128)(2,1)S(1)}, bf16[4,64,256]{2,1,0:T(8,128)(2,1)S(1)}, u32[]{:S(2)}, u32[]{:S(2)}) collective-permute-start(bf16[4,64,256]{2,1,0:T(8,128)(2,1)S(1)} %get-tuple-element.74), channel_id=1, source_target_pairs={{1,5},{5,1},{4,8},{8,4},{9,13},{13,9},{0,2},{12,14},{3,7},{7,3},{6... | collective-permute-start | bytes 393224 | tf_op jit(solution)/shard_map/ppermute | solution.py:607
  13.5 3.9 %collective-permute-start.8 = (f32[4,8,256]{2,1,0:T(8,128)S(1)}, f32[4,8,256]{2,1,0:T(8,128)S(1)}, u32[]{:S(2)}, u32[]{:S(2)}) collective-permute-start(f32[4,8,256]{2,1,0:T(8,128)S(1)} %get-tuple-element.75), channel_id=1, source_target_pairs={{0,2},{2,0},{1,3},{3,1},{4,6},{6,4},{5,7},{7,5},{8,10},{10,8},{9,1... | collective-permute-start | bytes 98312 | tf_op jit(solution)/shard_map/ppermute | solution.py:609
  18.4 5.8 %collective-permute-start.9 = (f32[4,64,256]{2,1,0:T(8,128)S(1)}, f32[4,64,256]{2,1,0:T(8,128)S(1)}, u32[]{:S(2)}, u32[]{:S(2)}) collective-permute-start(f32[4,64,256]{2,1,0:T(8,128)S(1)} %get-tuple-element.76.refs_0_.refs_1_), channel_id=1, source_target_pairs={{0,1},{1,0},{2,3},{3,2},{4,5},{5,4},{6,7},{7,6},{8,9},{9,8},{10,11... | collective-permute-start | bytes 786440 | tf_op jit(solution)/shard_map/ppermute | solution.py:591
  18.5 5.7 %collective-permute-start.10 = (bf16[4,64,256]{2,1,0:T(8,128)(2,1)S(1)}, bf16[4,64,256]{2,1,0:T(8,128)(2,1)S(1)}, u32[]{:S(2)}, u32[]{:S(2)}) collective-permute-start(bf16[4,64,256]{2,1,0:T(8,128)(2,1)S(1)} %get-tuple-element.77), channel_id=1, source_target_pairs={{1,5},{5,1},{4,8},{8,4},{9,13},{13,9},{0,2},{12,14},{3,7},{7,3},{6... | collective-permute-start | bytes 393224 | tf_op jit(solution)/shard_map/ppermute | solution.py:607
  20.3 3.9 %collective-permute-start.11 = (f32[4,8,256]{2,1,0:T(8,128)S(1)}, f32[4,8,256]{2,1,0:T(8,128)S(1)}, u32[]{:S(2)}, u32[]{:S(2)}) collective-permute-start(f32[4,8,256]{2,1,0:T(8,128)S(1)} %get-tuple-element.78), channel_id=1, source_target_pairs={{0,2},{2,0},{1,3},{3,1},{4,6},{6,4},{5,7},{7,5},{8,10},{10,8},{9,1... | collective-permute-start | bytes 98312 | tf_op jit(solution)/shard_map/ppermute | solution.py:609
  25.2 2.2 %collective-permute-start.12 = (f32[4,64,256]{2,1,0:T(8,128)S(1)}, f32[4,64,256]{2,1,0:T(8,128)S(1)}, u32[]{:S(2)}, u32[]{:S(2)}) collective-permute-start(f32[4,64,256]{2,1,0:T(8,128)S(1)} %get-tuple-element.79.own.refs_0_.q_ref), channel_id=1, source_target_pairs={{0,1},{1,0},{2,3},{3,2},{4,5},{5,4},{6,7},{7,6},{8,9},{9,8},{10,11... | collective-permute-start | bytes 786440 | tf_op jit(solution)/shard_map/ppermute | solution.py:591
  25.3 5.1 %collective-permute-start.13 = (bf16[4,64,256]{2,1,0:T(8,128)(2,1)S(1)}, bf16[4,64,256]{2,1,0:T(8,128)(2,1)S(1)}, u32[]{:S(2)}, u32[]{:S(2)}) collective-permute-start(bf16[4,64,256]{2,1,0:T(8,128)(2,1)S(1)} %get-tuple-element.80), channel_id=1, source_target_pairs={{1,5},{5,1},{4,8},{8,4},{9,13},{13,9},{0,2},{12,14},{3,7},{7,3},{6... | collective-permute-start | bytes 393224 | tf_op jit(solution)/shard_map/ppermute | solution.py:607
  27.0 3.9 %collective-permute-start.14 = (f32[4,8,256]{2,1,0:T(8,128)S(1)}, f32[4,8,256]{2,1,0:T(8,128)S(1)}, u32[]{:S(2)}, u32[]{:S(2)}) collective-permute-start(f32[4,8,256]{2,1,0:T(8,128)S(1)} %get-tuple-element.84), channel_id=1, source_target_pairs={{0,2},{2,0},{1,3},{3,1},{4,6},{6,4},{5,7},{7,5},{8,10},{10,8},{9,1... | collective-permute-start | bytes 98312 | tf_op jit(solution)/shard_map/ppermute | solution.py:609
  32.8 1.3 %collective-permute-start.15 = (bf16[1,4,32,128]{3,2,1,0:T(8,128)(2,1)S(1)}, bf16[1,4,32,128]{3,2,1,0:T(8,128)(2,1)S(1)}, u32[]{:S(2)}, u32[]{:S(2)}) collective-permute-start(bf16[1,4,32,128]{3,2,1,0:T(8,128)(2,1)S(1)} %get-tuple-element.88), channel_id=1, source_target_pairs={{0,1},{1,0},{2,3},{3,2},{4,5},{5,4},{6,7},{7,6},{8,9},{9,8},{10,11... | collective-permute-start | bytes 98312 | tf_op jit(solution)/shard_map/ppermute | solution.py:591
  32.9 7.0 %collective-permute-start.18 = (f32[4,64,256]{2,1,0:T(8,128)S(1)}, f32[4,64,256]{2,1,0:T(8,128)S(1)}, u32[]{:S(2)}, u32[]{:S(2)}) collective-permute-start(f32[4,64,256]{2,1,0:T(8,128)S(1)} %shard_map.219.own.p_ref), channel_id=1, source_target_pairs={{0,1},{1,0},{2,3},{3,2},{4,5},{5,4},{6,7},{7,6},{8,9},{9,8},{10,11... | collective-permute-start | bytes 786440 | tf_op jit(solution)/shard_map/ppermute | solution.py:591
  34.1 5.6 %collective-permute-start.16 = (bf16[4,4,32,128]{3,2,1,0:T(8,128)(2,1)S(1)}, bf16[4,4,32,128]{3,2,1,0:T(8,128)(2,1)S(1)}, u32[]{:S(2)}, u32[]{:S(2)}) collective-permute-start(bf16[4,4,32,128]{3,2,1,0:T(8,128)(2,1)S(1)} %fusion), channel_id=1, source_target_pairs={{0,2},{2,0},{1,3},{3,1},{4,6},{6,4},{5,7},{7,5},{8,10},{10,8},{9,1... | collective-permute-start | bytes 393224 | tf_op jit(solution)/shard_map/ppermute | solution.py:594
  38.4 9.2 %copy-start.2 = (bf16[640,80]{1,0:T(8,128)(2,1)S(1)}, bf16[640,80]{1,0:T(8,128)(2,1)}, u32[]{:S(2)}) copy-start(bf16[640,80]{1,0:T(8,128)(2,1)} %constant.34.clone.repeat_ref) | copy-start | bytes 307204
  39.8 5.0 %collective-permute-start.17 = (bf16[4,4,32,128]{3,2,1,0:T(8,128)(2,1)S(1)}, bf16[4,4,32,128]{3,2,1,0:T(8,128)(2,1)S(1)}, u32[]{:S(2)}, u32[]{:S(2)}) collective-permute-start(bf16[4,4,32,128]{3,2,1,0:T(8,128)(2,1)S(1)} %fusion.2), channel_id=1, source_target_pairs={{0,4},{4,0},{8,12},{12,8},{1,5},{5,1},{9,13},{13,9},{2,6},{6,2},{1... | collective-permute-start | bytes 393224 | tf_op jit(solution)/shard_map/ppermute | solution.py:594
  44.9 6.9 %collective-permute-start.19 = (bf16[4,4,32,128]{3,2,1,0:T(8,128)(2,1)S(1)}, bf16[4,4,32,128]{3,2,1,0:T(8,128)(2,1)S(1)}, u32[]{:S(2)}, u32[]{:S(2)}) collective-permute-start(bf16[4,4,32,128]{3,2,1,0:T(8,128)(2,1)S(1)} %fusion.1), channel_id=1, source_target_pairs={{0,12},{4,8},{8,4},{12,0},{1,13},{5,9},{9,5},{13,1},{2,14},{6,10},... | collective-permute-start | bytes 393224 | tf_op jit(solution)/shard_map/ppermute | solution.py:594
  48.0 5.2 %copy-start = (bf16[128,512]{1,0:T(8,128)(2,1)S(1)}, bf16[128,512]{1,0:T(8,128)(2,1)}, u32[]{:S(2)}) copy-start(bf16[128,512]{1,0:T(8,128)(2,1)} %constant.36.clone.table_z) | copy-start | bytes 393220
  48.1 5.2 %copy-start.1 = (bf16[2,64,64]{2,1,0:T(8,128)(2,1)S(1)}, bf16[2,64,64]{2,1,0:T(8,128)(2,1)}, u32[]{:S(2)}) copy-start(bf16[2,64,64]{2,1,0:T(8,128)(2,1)} %constant.35.clone.table_y) | copy-start | bytes 49156
  51.9 1.4 %collective-permute-start.20 = (bf16[4,4,32,128]{3,2,1,0:T(8,128)(2,1)S(1)}, bf16[4,4,32,128]{3,2,1,0:T(8,128)(2,1)S(1)}, u32[]{:S(2)}, u32[]{:S(2)}) collective-permute-start(bf16[4,4,32,128]{3,2,1,0:T(8,128)(2,1)S(1)} %get-tuple-element.104), channel_id=1, source_target_pairs={{0,1},{1,0},{2,3},{3,2},{4,5},{5,4},{6,7},{7,6},{8,9},{9,8},{10,11... | collective-permute-start | bytes 393224 | tf_op jit(solution)/shard_map/ppermute | solution.py:591

commit v11 on v10

--- a/solution.py
+++ b/solution.py
@@ -38,14 +38,14 @@
     return rounded(np.cos(phases)), rounded(np.sin(phases))
 
 
-def call(body, outs, in_specs, scratch=(), flops=0, moved=0):
+def call(body, outs, in_specs, scratch=(), flops=0, moved=0, room_bytes=16 * 1024 * 1024):
     return pl.pallas_call(
         body,
         out_shape=outs,
         in_specs=in_specs,
         out_specs=jax.tree.map(lambda _: VMEM, outs),
         scratch_shapes=list(scratch),
-        compiler_params=pltpu.CompilerParams(vmem_limit_bytes=16 * 1024 * 1024),
+        compiler_params=pltpu.CompilerParams(vmem_limit_bytes=room_bytes),
         cost_estimate=pl.CostEstimate(flops=flops, bytes_accessed=moved, transcendentals=0),
     )
 
@@ -397,44 +397,53 @@
             wave_out[start + row] = jnp.where(core == 0, ref[row, :, :half], ref[row, :, half:])
 
 
+def back_columns(spectra, left_y, modes):
+    fields, half_x, _, width = spectra.shape
+    chunk = min(8, half_x)
+    for field in range(fields):
+        for start in range(0, half_x, chunk):
+            values = [spectra[field, mode].astype(F32) for mode in range(start, start + chunk)]
+            stacked = jnp.concatenate([
+                jnp.concatenate([value.astype(BF16) for value in values], axis=1),
+                jnp.concatenate([turned(value, width // 2, -1.0).astype(BF16) for value in values], axis=1),
+            ], axis=0)
+            result = jnp.dot(left_y, stacked, preferred_element_type=F32)
+            for mode in range(start, start + chunk):
+                lanes = slice((mode - start) * width, (mode - start + 1) * width)
+                modes[:, mode * fields + field, :] = result[:, lanes]
+
+
+def own_half_body(mine, table_y, table_z, out, modes):
+    back_columns(mine, table_y[lax.axis_index("gy")], modes)
+    lines = modes[...].reshape(out.shape[0], modes.shape[2]).astype(BF16)
+    out[...] = jnp.dot(lines, table_z[...], preferred_element_type=F32).astype(BF16)
+
+
 def output_body(
-    mine, other, local, left, table_y, table_z, features, modes, right,
+    waves_own, other, local, left, table_y, table_z, features, modes, right,
 ):
     step = pl.program_id(0)
     core, column = lax.axis_index("gz"), lax.axis_index("gy")
-    half_x, modes_y, width = mine.shape[1:]
-    modes_x = 2 * half_x
-    half = width // 2
+    half_x, modes_y, width = other.shape[1:]
     rows, channels, group, depth = features.shape
-    coupled = FIELDS * modes_x
+    coupled = 2 * FIELDS * half_x
+    half_rows = FIELDS * half_x
 
     @pl.when(step == 0)
     def _():
-        chunk = min(8, modes_x)
-        left_y = table_y[column]
-        for field in range(FIELDS):
-            for start in range(0, modes_x, chunk):
-                parts = [[], []]
-                for mode in range(start, start + chunk):
-                    at = (field, mode % half_x)
-                    value = jnp.where(core == mode // half_x, mine[at], other[at].astype(F32))
-                    parts[0].append(value.astype(BF16))
-                    parts[1].append(turned(value, half, -1.0).astype(BF16))
-                stacked = jnp.concatenate([jnp.concatenate(part, axis=1) for part in parts], axis=0)
-                result = jnp.dot(left_y, stacked, preferred_element_type=F32)
-                for mode in range(start, start + chunk):
-                    lanes = slice((mode - start) * width, (mode - start + 1) * width)
-                    modes[:, mode * FIELDS + field, :] = result[:, lanes]
+        back_columns(other, table_y[column], modes)
 
     base = pl.multiple_of(step * group, group)
-    lines = modes[pl.ds(base, group)].reshape(group * coupled, width).astype(BF16)
+    lines = modes[pl.ds(base, group)].reshape(group * half_rows, width).astype(BF16)
     waves = jnp.dot(lines, table_z[...], preferred_element_type=F32).astype(BF16)
+    own = waves_own[pl.ds(pl.multiple_of(base * half_rows, group * half_rows), group * half_rows), :]
     count = left.shape[1] // (2 * coupled)
     for y in range(group):
-        lines = slice(y * coupled, (y + 1) * coupled)
-        start = y * 2 * coupled
-        right[start : start + coupled, :] = waves[lines, :depth]
-        right[start + coupled : start + 2 * coupled, :] = waves[lines, depth:]
+        lines = slice(y * half_rows, (y + 1) * half_rows)
+        for values, place in ((own, core), (waves, 1 - core)):
+            for part in range(2):
+                at = pl.multiple_of(y * 2 * coupled + part * coupled + place * half_rows, half_rows)
+                right[pl.ds(at, half_rows), :] = values[lines, part * depth : (part + 1) * depth]
     for first in range(0, group, 2 * count):
         results = []
         for start in (first * 2 * coupled, (first + count) * 2 * coupled):
@@ -672,6 +681,11 @@
     other = swap(total.astype(BF16))
     batch = min(32, brick_y)
     scoped = 10 * 2**20 + 20 * height * 16 * coupled + 4 * (brick_y * coupled * width + 6 * batch * coupled * total_z)
+    waves_own = call(
+        own_half_body, shape(brick_y * coupled // 2, 2 * total_z, dtype=BF16), [VMEM] * 3,
+        [pltpu.VMEM((brick_y, coupled // 2, width), F32)], flops=1_000_000_000, moved=2_000_000, room_bytes=scoped,
+    )(total, inverse_y, inverse_z)
+    other, waves_own = lax.optimization_barrier((other, waves_own))
     features = pl.pallas_call(
         output_body,
         grid=(brick_y // batch,),
@@ -680,12 +694,12 @@
                   VMEM, VMEM, VMEM, VMEM],
         out_specs=pl.BlockSpec((rows, channels, batch, total_z), lambda i: (0, 0, i, 0)),
         scratch_shapes=[
-            pltpu.VMEM((brick_y, coupled, width), F32),
+            pltpu.VMEM((brick_y, coupled // 2, width), F32),
             pltpu.VMEM((batch * 2 * coupled, total_z), BF16),
         ],
         compiler_params=pltpu.CompilerParams(vmem_limit_bytes=scoped),
         cost_estimate=pl.CostEstimate(flops=cells_count * 2000, bytes_accessed=cells_count * 60, transcendentals=cells_count * 20),
-    )(total, other, local, wide_mixing, inverse_y, inverse_z)
+    )(waves_own, other, local, wide_mixing, inverse_y, inverse_z)
     features = features.transpose(0, 2, 1, 3)
     return (wave, features)
 

time: 58.6 us -> 58.3 us (level)
  waiting for transfers between devices: 16.1 us -> 15.2 us
  Pallas kernels: 25.6 us -> 26.2 us
    ppermute x7, waiting for transfers between devices: 2.04 us -> 1.14 us  [per_device(): swap = lambda value: lax.ppermute(value, 'gz', swap_core)]
    pallas_call x0 -> x1, Pallas kernels: none -> 0.88 us  [per_device(): call(own_half_body, shape(brick_y * coupled // 2, 2 * total_z, dtype=BF16...]
  transfers between devices with their start and end apart: 21 -> 21, of which waited for: 12 -> 12; matrix products, arithmetic and copies ran while one was open for 0% -> 0% of each run, Pallas kernels for 26% -> 28%
where the time goes in v11:
time: 58.3 us; the launch traced here: 58 us
  Pallas kernels  26.2 us (45%)
  starting transfers between devices  15.5 us (27%)
  waiting for transfers between devices  15.2 us (26%)
  between operations  0.88 us (2%)
    ppermute x4, waiting for transfers between devices, per_device(): halos = [lax.ppermute(edge_values[0], 'gy', xor_pairs(column_count, 1))]  8.66 us
    ppermute x4, starting transfers between devices, per_device(): lax.ppermute(sent, ('gx', 'gy', 'gz'), row_pairs(cycle_count, column_count))  7.96 us
    pallas_call x2, Pallas kernels, pointwise_part(): pl.pallas_call(pointwise_body, grid=(steps // 2,), out_shape=shape(height...  6.79 us
    pallas_call x1, Pallas kernels, per_device(): pl.pallas_call(output_body, grid=(brick_y // batch,), out_shape=shape(row...  4.73 us
    ppermute x3, starting transfers between devices, exchange(): return lax.ppermute(value.astype(BF16), axis, xor_pairs(count, distance))  4.27 us
    pallas_call x4, Pallas kernels, per_device(): call(body, outs, [VMEM] * (6 + len(halos)), [pltpu.VMEM((brick_y + 2 * ED...  3.89 us
    pallas_call x1, Pallas kernels, per_device(): call(prepare_body, [shape(height, 2 * coupled, dtype=BF16), shape(height,...  2.8 us
    ppermute x4, waiting for transfers between devices, per_device(): lax.ppermute(sent, ('gx', 'gy', 'gz'), row_pairs(cycle_count, column_count))  2.56 us
  transfers between devices with their start and end apart: 21, of which 12 were waited for; matrix products, arithmetic and copies ran while one was open for 0% of the time, Pallas kernels for 28%

profile of v11, /device:TPU:0, one launch (start us, length us, event | category | flops | bytes accessed | tf_op | source)
XLA Modules:
  0.0 58.0 jit_solution(8531941061980460898)
XLA Ops:
  0.6 0.5 collective-permute-start
  1.7 1.2 %shard_map.212 = (f32[4,64,128]{2,1,0:T(8,128)S(1)}, f32[4,64,128]{2,1,0:T(8,128)S(1)}, s32[8,64,128]{2,1,0:T(8,128)S(1)}, f32[16,8,128]{2,1,0:T(8,128)S(1)}) custom-call(f32[8]{0:T(128)} %stiffness_in.3, f32[8]{0:T(128)} %density_in.3, f32[8]{0:T(128)} %refs_2_.2, f32[8,64,128]{2,1,0:T(8,128)} %refs_3_.3, f32[8,64,128]{2,1,0:T(8,128)} %refs_4_.2, ...), custom_call_target="tpu_custom_call" | custom-call | bytes 524288 | tf_op jit(solution)/shard_map/pallas_call | solution.py:566
  4.1 2.6 %collective-permute-start.4 = (bf16[4,64,256]{2,1,0:T(8,128)(2,1)S(1)}, bf16[4,64,256]{2,1,0:T(8,128)(2,1)S(1)}, u32[]{:S(2)}, u32[]{:S(2)}) collective-permute-start(bf16[4,64,256]{2,1,0:T(8,128)(2,1)S(1)} %get-tuple-element.70), channel_id=1, source_target_pairs={{1,5},{5,1},{4,8},{8,4},{9,13},{13,9},{0,2},{12,14},{3,7},{7,3},{6... | collective-permute-start | bytes 393224 | tf_op jit(solution)/shard_map/ppermute | solution.py:616
  6.7 2.3 %shard_map.214 = (f32[2,4,32,128]{3,2,1,0:T(8,128)S(1)}, bf16[256,128]{1,0:T(8,128)(2,1)S(1)}, bf16[2,32,256]{2,1,0:T(8,128)(2,1)S(1)}) custom-call(f32[512]{0:T(512)} %constant.31.clone.refs_0_.twiddles, f32[8]{0:T(128)} %stiffness_in.3, f32[8]{0:T(128)} %density_in.3, bf16[256,128]{1,0:T(8,128)(2,1)} %constant.32.clone.refs_3_, ...), custom_call_target="tpu_custom_call" | custom-call | flops 268435456 | bytes 2097152 | tf_op jit(solution)/shard_map/pallas_call | solution.py:606
  9.1 0.7 %collective-permute-done.4.refs_5_ = bf16[4,64,256]{2,1,0:T(8,128)(2,1)S(1)} collective-permute-done((bf16[4,64,256]{2,1,0:T(8,128)(2,1)S(1)}, bf16[4,64,256]{2,1,0:T(8,128)(2,1)S(1)}, u32[]{:S(2)}, u32[]{:S(2)}) %collective-permute-start.4) | collective-permute-done | bytes 131104 | tf_op jit(solution)/shard_map/ppermute | solution.py:616
  9.8 0.8 %collective-permute-done.5.refs_6_ = f32[4,8,256]{2,1,0:T(8,128)S(1)} collective-permute-done((f32[4,8,256]{2,1,0:T(8,128)S(1)}, f32[4,8,256]{2,1,0:T(8,128)S(1)}, u32[]{:S(2)}, u32[]{:S(2)}) %collective-permute-start.5) | collective-permute-done | bytes 32800 | tf_op jit(solution)/shard_map/ppermute | solution.py:618
  10.6 1.0 %shard_map.215 = (f32[4,64,256]{2,1,0:T(8,128)S(1)}, bf16[4,64,256]{2,1,0:T(8,128)(2,1)S(1)}, f32[4,8,256]{2,1,0:T(8,128)S(1)}) custom-call(f32[4,64,256]{2,1,0:T(8,128)S(1)} %get-tuple-element.66.refs_0_.refs_1_, f32[4,64,256]{2,1,0:T(8,128)S(1)} %get-tuple-element.67.refs_1_, f32[4,64,256]{2,1,0:T(8,128)S(1)} %get-tuple-element.68.refs_2_, ...), custom_call_target="tpu_custom_call" | custom-call | flops 3932160 | bytes 1835008 | tf_op jit(solution)/shard_map/pallas_call | solution.py:631
  11.7 1.8 %collective-permute-start.7 = (bf16[4,64,256]{2,1,0:T(8,128)(2,1)S(1)}, bf16[4,64,256]{2,1,0:T(8,128)(2,1)S(1)}, u32[]{:S(2)}, u32[]{:S(2)}) collective-permute-start(bf16[4,64,256]{2,1,0:T(8,128)(2,1)S(1)} %get-tuple-element.76), channel_id=1, source_target_pairs={{1,5},{5,1},{4,8},{8,4},{9,13},{13,9},{0,2},{12,14},{3,7},{7,3},{6... | collective-permute-start | bytes 393224 | tf_op jit(solution)/shard_map/ppermute | solution.py:616
  13.8 3.6 %collective-permute-done.8.refs_6_ = f32[4,8,256]{2,1,0:T(8,128)S(1)} collective-permute-done((f32[4,8,256]{2,1,0:T(8,128)S(1)}, f32[4,8,256]{2,1,0:T(8,128)S(1)}, u32[]{:S(2)}, u32[]{:S(2)}) %collective-permute-start.8) | collective-permute-done | bytes 32800 | tf_op jit(solution)/shard_map/ppermute | solution.py:618
  17.4 1.0 %shard_map.216 = (f32[4,64,256]{2,1,0:T(8,128)S(1)}, bf16[4,64,256]{2,1,0:T(8,128)(2,1)S(1)}, f32[4,8,256]{2,1,0:T(8,128)S(1)}) custom-call(f32[4,64,256]{2,1,0:T(8,128)S(1)} %get-tuple-element.75.refs_0_.refs_1_, f32[4,64,256]{2,1,0:T(8,128)S(1)} %get-tuple-element.66.refs_0_.refs_1_, f32[4,64,256]{2,1,0:T(8,128)S(1)} %get-tuple-element.68.refs_2_, ...), custom_call_target="tpu_custom_call" | custom-call | flops 3932160 | bytes 1835008 | tf_op jit(solution)/shard_map/pallas_call | solution.py:631
  18.5 1.8 %collective-permute-start.10 = (bf16[4,64,256]{2,1,0:T(8,128)(2,1)S(1)}, bf16[4,64,256]{2,1,0:T(8,128)(2,1)S(1)}, u32[]{:S(2)}, u32[]{:S(2)}) collective-permute-start(bf16[4,64,256]{2,1,0:T(8,128)(2,1)S(1)} %get-tuple-element.79), channel_id=1, source_target_pairs={{1,5},{5,1},{4,8},{8,4},{9,13},{13,9},{0,2},{12,14},{3,7},{7,3},{6... | collective-permute-start | bytes 393224 | tf_op jit(solution)/shard_map/ppermute | solution.py:616
  20.6 3.6 %collective-permute-done.11.refs_6_ = f32[4,8,256]{2,1,0:T(8,128)S(1)} collective-permute-done((f32[4,8,256]{2,1,0:T(8,128)S(1)}, f32[4,8,256]{2,1,0:T(8,128)S(1)}, u32[]{:S(2)}, u32[]{:S(2)}) %collective-permute-start.11) | collective-permute-done | bytes 32800 | tf_op jit(solution)/shard_map/ppermute | solution.py:618
  24.2 1.0 %shard_map.217 = (f32[4,64,256]{2,1,0:T(8,128)S(1)}, bf16[4,64,256]{2,1,0:T(8,128)(2,1)S(1)}, f32[4,8,256]{2,1,0:T(8,128)S(1)}) custom-call(f32[4,64,256]{2,1,0:T(8,128)S(1)} %get-tuple-element.78.refs_0_.refs_1_, f32[4,64,256]{2,1,0:T(8,128)S(1)} %get-tuple-element.75.refs_0_.refs_1_, f32[4,64,256]{2,1,0:T(8,128)S(1)} %get-tuple-element.68.refs_2_, ...), custom_call_target="tpu_custom_call" | custom-call | flops 3932160 | bytes 1835008 | tf_op jit(solution)/shard_map/pallas_call | solution.py:631
  25.3 1.7 %collective-permute-start.13 = (bf16[4,64,256]{2,1,0:T(8,128)(2,1)S(1)}, bf16[4,64,256]{2,1,0:T(8,128)(2,1)S(1)}, u32[]{:S(2)}, u32[]{:S(2)}) collective-permute-start(bf16[4,64,256]{2,1,0:T(8,128)(2,1)S(1)} %get-tuple-element.82), channel_id=1, source_target_pairs={{1,5},{5,1},{4,8},{8,4},{9,13},{13,9},{0,2},{12,14},{3,7},{7,3},{6... | collective-permute-start | bytes 393224 | tf_op jit(solution)/shard_map/ppermute | solution.py:616
  27.4 1.1 %shard_map.218.prior = f32[4,32,128]{2,1,0:T(8,128)S(1)} custom-call(f32[512]{0:T(512)} %constant.31.clone.refs_0_.twiddles, f32[4,64,256]{2,1,0:T(8,128)S(1)} %get-tuple-element.81.own.refs_0_.q_ref, f32[4,64,256]{2,1,0:T(8,128)S(1)} %collective-permute-done.12.mate.refs_4_.q_mate, bf16[256,128]{1,0:T(8,128)(2,1)S(1)} %get-tuple-element.83.table_z, ...), custom_call_target="tpu_custom_call" | custom-call | flops 134217728 | bytes 1048576 | tf_op jit(solution)/shard_map/pallas_call | solution.py:624
  28.5 1.9 %collective-permute-done.13.refs_5_ = bf16[4,64,256]{2,1,0:T(8,128)(2,1)S(1)} collective-permute-done((bf16[4,64,256]{2,1,0:T(8,128)(2,1)S(1)}, bf16[4,64,256]{2,1,0:T(8,128)(2,1)S(1)}, u32[]{:S(2)}, u32[]{:S(2)}) %collective-permute-start.13) | collective-permute-done | bytes 131104 | tf_op jit(solution)/shard_map/ppermute | solution.py:616
  30.3 0.5 collective-permute-done.14.refs_6_
  30.9 1.0 %shard_map.219.own.p_ref = f32[4,64,256]{2,1,0:T(8,128)S(1)} custom-call(f32[4,64,256]{2,1,0:T(8,128)S(1)} %get-tuple-element.81.own.refs_0_.q_ref, f32[4,64,256]{2,1,0:T(8,128)S(1)} %get-tuple-element.78.refs_0_.refs_1_, f32[4,64,256]{2,1,0:T(8,128)S(1)} %get-tuple-element.68.refs_2_, f32[4,64,256]{2,1,0:T(8,128)S(1)} %get-tuple-element.69.refs_3_, ...), custom_call_target="tpu_custom_call" | custom-call | flops 3932160 | bytes 1835008 | tf_op jit(solution)/shard_map/pallas_call | solution.py:631
  31.9 0.9 %shard_map.220 = (f32[4,4,32,128]{3,2,1,0:T(8,128)S(1)}, bf16[1,4,32,128]{3,2,1,0:T(8,128)(2,1)S(1)}) custom-call(f32[512]{0:T(512)} %constant.31.clone.refs_0_.twiddles, f32[4,64,256]{2,1,0:T(8,128)S(1)} %shard_map.219.own.p_ref, f32[4,32,128]{2,1,0:T(8,128)S(1)} %shard_map.218.prior, f32[2,4,32,128]{3,2,1,0:T(8,128)S(1)} %get-tuple-element.88.early, ...), custom_call_target="tpu_custom_call" | custom-call | flops 67108864 | bytes 524288 | tf_op jit(solution)/shard_map/pallas_call | solution.py:639
  32.9 0.5 collective-permute-start.18
  33.4 0.7 %collective-permute-done.15 = bf16[1,4,32,128]{3,2,1,0:T(8,128)(2,1)S(1)} collective-permute-done((bf16[1,4,32,128]{3,2,1,0:T(8,128)(2,1)S(1)}, bf16[1,4,32,128]{3,2,1,0:T(8,128)(2,1)S(1)}, u32[]{:S(2)}, u32[]{:S(2)}) %collective-permute-start.15) | collective-permute-done | bytes 32800 | tf_op jit(solution)/shard_map/ppermute | solution.py:600
  34.1 1.5 %collective-permute-start.16 = (bf16[4,4,32,128]{3,2,1,0:T(8,128)(2,1)S(1)}, bf16[4,4,32,128]{3,2,1,0:T(8,128)(2,1)S(1)}, u32[]{:S(2)}, u32[]{:S(2)}) collective-permute-start(bf16[4,4,32,128]{3,2,1,0:T(8,128)(2,1)S(1)} %fusion), channel_id=1, source_target_pairs={{0,2},{2,0},{1,3},{3,1},{4,6},{6,4},{5,7},{7,5},{8,10},{10,8},{9,1... | collective-permute-start | bytes 393224 | tf_op jit(solution)/shard_map/ppermute | solution.py:603
  35.6 2.8 %shard_map.221 = (bf16[80,64]{1,0:T(8,128)(2,1)S(1)}, bf16[80,128]{1,0:T(8,128)(2,1)S(1)}, f32[24,8]{1,0:T(8,128)S(1)}, f32[80,1]{1,0:T(8,128)S(1)}) custom-call(f32[8]{0:T(128)} %stiffness_in.3, f32[8]{0:T(128)} %density_in.3, f32[2,20,8,20]{3,2,1,0:T(8,128)} %bitcast.4, f32[4,20]{1,0:T(4,128)} %refs_3_.4, f32[1,20]{1,0:T(1,128)} %bitcast.5, ...), custom_call_target="tpu_custom_call" | custom-call | flops 2000000000 | bytes 4000000 | tf_op jit(solution)/shard_map/pallas_call | solution.py:582
  38.4 1.3 %collective-permute-done.16 = bf16[4,4,32,128]{3,2,1,0:T(8,128)(2,1)S(1)} collective-permute-done((bf16[4,4,32,128]{3,2,1,0:T(8,128)(2,1)S(1)}, bf16[4,4,32,128]{3,2,1,0:T(8,128)(2,1)S(1)}, u32[]{:S(2)}, u32[]{:S(2)}) %collective-permute-start.16) | collective-permute-done | bytes 131104 | tf_op jit(solution)/shard_map/ppermute | solution.py:603
  39.9 0.7 %shard_map.223 = f32[8,64,128]{2,1,0:T(8,128)} custom-call(f32[4,64,256]{2,1,0:T(8,128)S(1)} %shard_map.219.own.p_ref, f32[4,64,256]{2,1,0:T(8,128)S(1)} %collective-permute-done.18.p_mate.other), custom_call_target="tpu_custom_call" | custom-call | bytes 786432 | tf_op jit(solution)/shard_map/pallas_call | solution.py:671
  40.6 3.4 %shard_map.222.rest_0_ = f32[80,64,256]{2,1,0:T(8,128)S(1)} custom-call(f32[8]{0:T(128)} %stiffness_in.3, f32[8]{0:T(128)} %density_in.3, f32[4,64,256]{2,1,0:T(8,128)S(1)} %shard_map.219.own.p_ref, f32[4,64,256]{2,1,0:T(8,128)S(1)} %get-tuple-element.81.own.refs_0_.q_ref, f32[4,64,256]{2,1,0:T(8,128)S(1)} %collective-permute-done.18.p_mate.other, ...), custom_call_target="tpu_custom_call" | custom-call | flops 1310720000 | bytes 3276800 | tf_op jit(solution)/shard_map/pallas_call | solution.py:650
  44.0 0.8 %collective-permute-done.17 = bf16[4,4,32,128]{3,2,1,0:T(8,128)(2,1)S(1)} collective-permute-done((bf16[4,4,32,128]{3,2,1,0:T(8,128)(2,1)S(1)}, bf16[4,4,32,128]{3,2,1,0:T(8,128)(2,1)S(1)}, u32[]{:S(2)}, u32[]{:S(2)}) %collective-permute-start.17) | collective-permute-done | bytes 131104 | tf_op jit(solution)/shard_map/ppermute | solution.py:603
  44.9 2.7 %collective-permute-start.19 = (bf16[4,4,32,128]{3,2,1,0:T(8,128)(2,1)S(1)}, bf16[4,4,32,128]{3,2,1,0:T(8,128)(2,1)S(1)}, u32[]{:S(2)}, u32[]{:S(2)}) collective-permute-start(bf16[4,4,32,128]{3,2,1,0:T(8,128)(2,1)S(1)} %fusion.1), channel_id=1, source_target_pairs={{0,12},{4,8},{8,4},{12,0},{1,13},{5,9},{9,5},{13,1},{2,14},{6,10},... | collective-permute-start | bytes 393224 | tf_op jit(solution)/shard_map/ppermute | solution.py:603
  47.6 0.4 shard_map.225.left
  48.1 3.4 %shard_map.224.local = f32[80,64,256]{2,1,0:T(8,128)S(1)} custom-call(f32[8]{0:T(128)} %stiffness_in.3, f32[8]{0:T(128)} %density_in.3, f32[4,64,256]{2,1,0:T(8,128)S(1)} %shard_map.219.own.p_ref, f32[4,64,256]{2,1,0:T(8,128)S(1)} %get-tuple-element.81.own.refs_0_.q_ref, ...), custom_call_target="tpu_custom_call", output_to_operand_aliasing={{}: (10, {})} | custom-call | flops 1310720000 | bytes 3276800 | tf_op jit(solution)/shard_map/pallas_call | solution.py:650
  52.0 0.9 %shard_map.226.waves_own = bf16[1024,512]{1,0:T(8,128)(2,1)S(1)} custom-call(f32[4,4,32,128]{3,2,1,0:T(8,128)S(1)} %get-tuple-element.109.mine, bf16[2,64,64]{2,1,0:T(8,128)(2,1)S(1)} %copy-done.1, bf16[128,512]{1,0:T(8,128)(2,1)S(1)} %copy-done), custom_call_target="tpu_custom_call" | custom-call | flops 1000000000 | bytes 2000000 | tf_op jit(solution)/shard_map/pallas_call | solution.py:684
  53.3 4.7 %shard_map.227 = bf16[4,20,64,256]{3,2,1,0:T(8,128)(2,1)} custom-call(bf16[1024,512]{1,0:T(8,128)(2,1)S(1)} %shard_map.226.waves_own, bf16[4,4,32,128]{3,2,1,0:T(8,128)(2,1)S(1)} %collective-permute-done.20.other, f32[80,64,256]{2,1,0:T(8,128)S(1)} %shard_map.224.local, bf16[640,512]{1,0:T(8,128)(2,1)S(1)} %shard_map.225.left, ...), custom_call_target="tpu_custom_call" | custom-call | flops 131072000 | bytes 3932160 | tf_op jit(solution)/shard_map/pallas_call | solution.py:689
  (36 shorter events, 4.1 us)
Async XLA Ops:
  0.6 2.2 %collective-permute-start = (f32[8,64,128]{2,1,0:T(8,128)}, f32[8,64,128]{2,1,0:T(8,128)S(1)}, u32[]{:S(2)}, u32[]{:S(2)}) collective-permute-start(f32[8,64,128]{2,1,0:T(8,128)} %refs_3_.3), channel_id=1, source_target_pairs={{0,1},{1,0},{2,3},{3,2},{4,5},{5,4},{6,7},{7,6},{8,9},{9,8},{10,11... | collective-permute-start | bytes 786440 | tf_op jit(solution)/shard_map/ppermute | solution.py:563
  1.1 1.7 %collective-permute-start.1 = (f32[8,64,128]{2,1,0:T(8,128)}, f32[8,64,128]{2,1,0:T(8,128)S(1)}, u32[]{:S(2)}, u32[]{:S(2)}) collective-permute-start(f32[8,64,128]{2,1,0:T(8,128)} %refs_4_.2), channel_id=1, source_target_pairs={{0,1},{1,0},{2,3},{3,2},{4,5},{5,4},{6,7},{7,6},{8,9},{9,8},{10,11... | collective-permute-start | bytes 786440 | tf_op jit(solution)/shard_map/ppermute | solution.py:563
  1.2 2.0 %collective-permute-start.2 = (s32[8,64,128]{2,1,0:T(8,128)}, s32[8,64,128]{2,1,0:T(8,128)S(1)}, u32[]{:S(2)}, u32[]{:S(2)}) collective-permute-start(s32[8,64,128]{2,1,0:T(8,128)} %refs_5_.2), channel_id=1, source_target_pairs={{0,1},{1,0},{2,3},{3,2},{4,5},{5,4},{6,7},{7,6},{8,9},{9,8},{10,11... | collective-permute-start | bytes 786440 | tf_op jit(solution)/shard_map/ppermute | solution.py:563
  3.6 7.0 %collective-permute-start.3 = (f32[4,64,256]{2,1,0:T(8,128)S(1)}, f32[4,64,256]{2,1,0:T(8,128)S(1)}, u32[]{:S(2)}, u32[]{:S(2)}) collective-permute-start(f32[4,64,256]{2,1,0:T(8,128)S(1)} %get-tuple-element.66.refs_0_.refs_1_), channel_id=1, source_target_pairs={{0,1},{1,0},{2,3},{3,2},{4,5},{5,4},{6,7},{7,6},{8,9},{9,8},{10,11... | collective-permute-start | bytes 786440 | tf_op jit(solution)/shard_map/ppermute | solution.py:600
  4.1 5.7 %collective-permute-start.4 = (bf16[4,64,256]{2,1,0:T(8,128)(2,1)S(1)}, bf16[4,64,256]{2,1,0:T(8,128)(2,1)S(1)}, u32[]{:S(2)}, u32[]{:S(2)}) collective-permute-start(bf16[4,64,256]{2,1,0:T(8,128)(2,1)S(1)} %get-tuple-element.70), channel_id=1, source_target_pairs={{1,5},{5,1},{4,8},{8,4},{9,13},{13,9},{0,2},{12,14},{3,7},{7,3},{6... | collective-permute-start | bytes 393224 | tf_op jit(solution)/shard_map/ppermute | solution.py:616
  6.7 3.9 %collective-permute-start.5 = (f32[4,8,256]{2,1,0:T(8,128)S(1)}, f32[4,8,256]{2,1,0:T(8,128)S(1)}, u32[]{:S(2)}, u32[]{:S(2)}) collective-permute-start(f32[4,8,256]{2,1,0:T(8,128)S(1)} %get-tuple-element.74), channel_id=1, source_target_pairs={{0,2},{2,0},{1,3},{3,1},{4,6},{6,4},{5,7},{7,5},{8,10},{10,8},{9,1... | collective-permute-start | bytes 98312 | tf_op jit(solution)/shard_map/ppermute | solution.py:618
  11.6 5.8 %collective-permute-start.6 = (f32[4,64,256]{2,1,0:T(8,128)S(1)}, f32[4,64,256]{2,1,0:T(8,128)S(1)}, u32[]{:S(2)}, u32[]{:S(2)}) collective-permute-start(f32[4,64,256]{2,1,0:T(8,128)S(1)} %get-tuple-element.75.refs_0_.refs_1_), channel_id=1, source_target_pairs={{0,1},{1,0},{2,3},{3,2},{4,5},{5,4},{6,7},{7,6},{8,9},{9,8},{10,11... | collective-permute-start | bytes 786440 | tf_op jit(solution)/shard_map/ppermute | solution.py:600
  11.7 5.7 %collective-permute-start.7 = (bf16[4,64,256]{2,1,0:T(8,128)(2,1)S(1)}, bf16[4,64,256]{2,1,0:T(8,128)(2,1)S(1)}, u32[]{:S(2)}, u32[]{:S(2)}) collective-permute-start(bf16[4,64,256]{2,1,0:T(8,128)(2,1)S(1)} %get-tuple-element.76), channel_id=1, source_target_pairs={{1,5},{5,1},{4,8},{8,4},{9,13},{13,9},{0,2},{12,14},{3,7},{7,3},{6... | collective-permute-start | bytes 393224 | tf_op jit(solution)/shard_map/ppermute | solution.py:616
  13.5 3.9 %collective-permute-start.8 = (f32[4,8,256]{2,1,0:T(8,128)S(1)}, f32[4,8,256]{2,1,0:T(8,128)S(1)}, u32[]{:S(2)}, u32[]{:S(2)}) collective-permute-start(f32[4,8,256]{2,1,0:T(8,128)S(1)} %get-tuple-element.77), channel_id=1, source_target_pairs={{0,2},{2,0},{1,3},{3,1},{4,6},{6,4},{5,7},{7,5},{8,10},{10,8},{9,1... | collective-permute-start | bytes 98312 | tf_op jit(solution)/shard_map/ppermute | solution.py:618
  18.4 5.8 %collective-permute-start.9 = (f32[4,64,256]{2,1,0:T(8,128)S(1)}, f32[4,64,256]{2,1,0:T(8,128)S(1)}, u32[]{:S(2)}, u32[]{:S(2)}) collective-permute-start(f32[4,64,256]{2,1,0:T(8,128)S(1)} %get-tuple-element.78.refs_0_.refs_1_), channel_id=1, source_target_pairs={{0,1},{1,0},{2,3},{3,2},{4,5},{5,4},{6,7},{7,6},{8,9},{9,8},{10,11... | collective-permute-start | bytes 786440 | tf_op jit(solution)/shard_map/ppermute | solution.py:600
  18.5 5.7 %collective-permute-start.10 = (bf16[4,64,256]{2,1,0:T(8,128)(2,1)S(1)}, bf16[4,64,256]{2,1,0:T(8,128)(2,1)S(1)}, u32[]{:S(2)}, u32[]{:S(2)}) collective-permute-start(bf16[4,64,256]{2,1,0:T(8,128)(2,1)S(1)} %get-tuple-element.79), channel_id=1, source_target_pairs={{1,5},{5,1},{4,8},{8,4},{9,13},{13,9},{0,2},{12,14},{3,7},{7,3},{6... | collective-permute-start | bytes 393224 | tf_op jit(solution)/shard_map/ppermute | solution.py:616
  20.3 3.9 %collective-permute-start.11 = (f32[4,8,256]{2,1,0:T(8,128)S(1)}, f32[4,8,256]{2,1,0:T(8,128)S(1)}, u32[]{:S(2)}, u32[]{:S(2)}) collective-permute-start(f32[4,8,256]{2,1,0:T(8,128)S(1)} %get-tuple-element.80), channel_id=1, source_target_pairs={{0,2},{2,0},{1,3},{3,1},{4,6},{6,4},{5,7},{7,5},{8,10},{10,8},{9,1... | collective-permute-start | bytes 98312 | tf_op jit(solution)/shard_map/ppermute | solution.py:618
  25.2 2.2 %collective-permute-start.12 = (f32[4,64,256]{2,1,0:T(8,128)S(1)}, f32[4,64,256]{2,1,0:T(8,128)S(1)}, u32[]{:S(2)}, u32[]{:S(2)}) collective-permute-start(f32[4,64,256]{2,1,0:T(8,128)S(1)} %get-tuple-element.81.own.refs_0_.q_ref), channel_id=1, source_target_pairs={{0,1},{1,0},{2,3},{3,2},{4,5},{5,4},{6,7},{7,6},{8,9},{9,8},{10,11... | collective-permute-start | bytes 786440 | tf_op jit(solution)/shard_map/ppermute | solution.py:600
  25.3 5.1 %collective-permute-start.13 = (bf16[4,64,256]{2,1,0:T(8,128)(2,1)S(1)}, bf16[4,64,256]{2,1,0:T(8,128)(2,1)S(1)}, u32[]{:S(2)}, u32[]{:S(2)}) collective-permute-start(bf16[4,64,256]{2,1,0:T(8,128)(2,1)S(1)} %get-tuple-element.82), channel_id=1, source_target_pairs={{1,5},{5,1},{4,8},{8,4},{9,13},{13,9},{0,2},{12,14},{3,7},{7,3},{6... | collective-permute-start | bytes 393224 | tf_op jit(solution)/shard_map/ppermute | solution.py:616
  27.0 3.9 %collective-permute-start.14 = (f32[4,8,256]{2,1,0:T(8,128)S(1)}, f32[4,8,256]{2,1,0:T(8,128)S(1)}, u32[]{:S(2)}, u32[]{:S(2)}) collective-permute-start(f32[4,8,256]{2,1,0:T(8,128)S(1)} %get-tuple-element.86), channel_id=1, source_target_pairs={{0,2},{2,0},{1,3},{3,1},{4,6},{6,4},{5,7},{7,5},{8,10},{10,8},{9,1... | collective-permute-start | bytes 98312 | tf_op jit(solution)/shard_map/ppermute | solution.py:618
  32.8 1.3 %collective-permute-start.15 = (bf16[1,4,32,128]{3,2,1,0:T(8,128)(2,1)S(1)}, bf16[1,4,32,128]{3,2,1,0:T(8,128)(2,1)S(1)}, u32[]{:S(2)}, u32[]{:S(2)}) collective-permute-start(bf16[1,4,32,128]{3,2,1,0:T(8,128)(2,1)S(1)} %get-tuple-element.90), channel_id=1, source_target_pairs={{0,1},{1,0},{2,3},{3,2},{4,5},{5,4},{6,7},{7,6},{8,9},{9,8},{10,11... | collective-permute-start | bytes 98312 | tf_op jit(solution)/shard_map/ppermute | solution.py:600
  32.9 7.0 %collective-permute-start.18 = (f32[4,64,256]{2,1,0:T(8,128)S(1)}, f32[4,64,256]{2,1,0:T(8,128)S(1)}, u32[]{:S(2)}, u32[]{:S(2)}) collective-permute-start(f32[4,64,256]{2,1,0:T(8,128)S(1)} %shard_map.219.own.p_ref), channel_id=1, source_target_pairs={{0,1},{1,0},{2,3},{3,2},{4,5},{5,4},{6,7},{7,6},{8,9},{9,8},{10,11... | collective-permute-start | bytes 786440 | tf_op jit(solution)/shard_map/ppermute | solution.py:600
  34.1 5.6 %collective-permute-start.16 = (bf16[4,4,32,128]{3,2,1,0:T(8,128)(2,1)S(1)}, bf16[4,4,32,128]{3,2,1,0:T(8,128)(2,1)S(1)}, u32[]{:S(2)}, u32[]{:S(2)}) collective-permute-start(bf16[4,4,32,128]{3,2,1,0:T(8,128)(2,1)S(1)} %fusion), channel_id=1, source_target_pairs={{0,2},{2,0},{1,3},{3,1},{4,6},{6,4},{5,7},{7,5},{8,10},{10,8},{9,1... | collective-permute-start | bytes 393224 | tf_op jit(solution)/shard_map/ppermute | solution.py:603
  38.4 9.2 %copy-start.2 = (bf16[640,80]{1,0:T(8,128)(2,1)S(1)}, bf16[640,80]{1,0:T(8,128)(2,1)}, u32[]{:S(2)}) copy-start(bf16[640,80]{1,0:T(8,128)(2,1)} %constant.34.clone.repeat_ref) | copy-start | bytes 307204
  39.8 5.0 %collective-permute-start.17 = (bf16[4,4,32,128]{3,2,1,0:T(8,128)(2,1)S(1)}, bf16[4,4,32,128]{3,2,1,0:T(8,128)(2,1)S(1)}, u32[]{:S(2)}, u32[]{:S(2)}) collective-permute-start(bf16[4,4,32,128]{3,2,1,0:T(8,128)(2,1)S(1)} %fusion.2), channel_id=1, source_target_pairs={{0,4},{4,0},{8,12},{12,8},{1,5},{5,1},{9,13},{13,9},{2,6},{6,2},{1... | collective-permute-start | bytes 393224 | tf_op jit(solution)/shard_map/ppermute | solution.py:603
  44.9 6.9 %collective-permute-start.19 = (bf16[4,4,32,128]{3,2,1,0:T(8,128)(2,1)S(1)}, bf16[4,4,32,128]{3,2,1,0:T(8,128)(2,1)S(1)}, u32[]{:S(2)}, u32[]{:S(2)}) collective-permute-start(bf16[4,4,32,128]{3,2,1,0:T(8,128)(2,1)S(1)} %fusion.1), channel_id=1, source_target_pairs={{0,12},{4,8},{8,4},{12,0},{1,13},{5,9},{9,5},{13,1},{2,14},{6,10},... | collective-permute-start | bytes 393224 | tf_op jit(solution)/shard_map/ppermute | solution.py:603
  48.0 3.9 %copy-start = (bf16[128,512]{1,0:T(8,128)(2,1)S(1)}, bf16[128,512]{1,0:T(8,128)(2,1)}, u32[]{:S(2)}) copy-start(bf16[128,512]{1,0:T(8,128)(2,1)} %constant.36.clone.table_z) | copy-start | bytes 393220
  48.1 3.9 %copy-start.1 = (bf16[2,64,64]{2,1,0:T(8,128)(2,1)S(1)}, bf16[2,64,64]{2,1,0:T(8,128)(2,1)}, u32[]{:S(2)}) copy-start(bf16[2,64,64]{2,1,0:T(8,128)(2,1)} %constant.35.clone.table_y) | copy-start | bytes 49156
  51.9 1.4 %collective-permute-start.20 = (bf16[4,4,32,128]{3,2,1,0:T(8,128)(2,1)S(1)}, bf16[4,4,32,128]{3,2,1,0:T(8,128)(2,1)S(1)}, u32[]{:S(2)}, u32[]{:S(2)}) collective-permute-start(bf16[4,4,32,128]{3,2,1,0:T(8,128)(2,1)S(1)} %get-tuple-element.108), channel_id=1, source_target_pairs={{0,1},{1,0},{2,3},{3,2},{4,5},{5,4},{6,7},{7,6},{8,9},{9,8},{10,11... | collective-permute-start | bytes 393224 | tf_op jit(solution)/shard_map/ppermute | solution.py:600

commit v12 on v11

--- a/solution.py
+++ b/solution.py
@@ -98,7 +98,7 @@
 def edges(value_of, outs, row_parity, brick_y):
     for position, out in enumerate(outs):
         upper = row_parity == position
-        out[...] = jnp.where(upper, value_of(brick_y - EDGE, brick_y), value_of(0, EDGE))
+        out[...] = jnp.where(upper, value_of(brick_y - EDGE, brick_y), value_of(0, EDGE)).astype(BF16)
 
 
 def slot():
@@ -179,8 +179,8 @@
         return jnp.where(place == (0 if index < 0 else 1), beyond, mate[at])
 
     for row in range(rows):
-        first = halos[0][row]
-        second = halos[1][row] if two_sided else zero_edge
+        first = halos[0][row].astype(F32)
+        second = halos[1][row].astype(F32) if two_sided else zero_edge
         center = p_ref[row]
         padded[0:EDGE, :] = jnp.where(parity == 0, second, first)
         padded[EDGE : EDGE + brick_y, :] = center
@@ -557,7 +557,7 @@
 
     cells_count = rows * brick_y * total_z
     field = shape(rows, brick_y, total_z)
-    edge = [shape(rows, EDGE, total_z)] * (2 if two_sided else 1)
+    edge = [shape(rows, EDGE, total_z, dtype=BF16)] * (2 if two_sided else 1)
 
     swap_core = xor_pairs(core_count, 1)
     got = [lax.ppermute(array, "gz", swap_core) for array in (pressure, previous, material)]

time: 58.3 us -> 57.3 us (0.983)
  waiting for transfers between devices: 15.2 us -> 12.9 us
  starting transfers between devices: 15.5 us -> 16.9 us
    ppermute x3, starting transfers between devices: 4.27 us -> 5.63 us  [exchange(): return lax.ppermute(value.astype(BF16), axis, xor_pairs(count, distance))]
    ppermute x3, waiting for transfers between devices: 2.46 us -> 1.21 us  [exchange(): return lax.ppermute(value.astype(BF16), axis, xor_pairs(count, distance))]
    ppermute x4, waiting for transfers between devices: 8.66 us -> 7.43 us  [per_device(): halos = [lax.ppermute(edge_values[0], 'gy', xor_pairs(column_count, 1))]]
  transfers between devices with their start and end apart: 21 -> 21, of which waited for: 12 -> 10; matrix products, arithmetic and copies ran while one was open for 0% -> 0% of each run, Pallas kernels for 28% -> 29%
where the time goes in v12:
time: 57.3 us; the launch traced here: 57 us
  Pallas kernels  26.2 us (46%)
  starting transfers between devices  16.9 us (29%)
  waiting for transfers between devices  12.9 us (23%)
  between operations  0.86 us (2%)
    ppermute x4, starting transfers between devices, per_device(): lax.ppermute(sent, ('gx', 'gy', 'gz'), row_pairs(cycle_count, column_count))  7.51 us
    ppermute x4, waiting for transfers between devices, per_device(): halos = [lax.ppermute(edge_values[0], 'gy', xor_pairs(column_count, 1))]  7.43 us
    pallas_call x2, Pallas kernels, pointwise_part(): pl.pallas_call(pointwise_body, grid=(steps // 2,), out_shape=shape(height...  6.79 us
    ppermute x3, starting transfers between devices, exchange(): return lax.ppermute(value.astype(BF16), axis, xor_pairs(count, distance))  5.63 us
    pallas_call x1, Pallas kernels, per_device(): pl.pallas_call(output_body, grid=(brick_y // batch,), out_shape=shape(row...  4.72 us
    pallas_call x4, Pallas kernels, per_device(): call(body, outs, [VMEM] * (6 + len(halos)), [pltpu.VMEM((brick_y + 2 * ED...  3.91 us
    pallas_call x1, Pallas kernels, per_device(): call(prepare_body, [shape(height, 2 * coupled, dtype=BF16), shape(height,...  2.8 us
    ppermute x4, waiting for transfers between devices, per_device(): lax.ppermute(sent, ('gx', 'gy', 'gz'), row_pairs(cycle_count, column_count))  2.7 us
  transfers between devices with their start and end apart: 21, of which 10 were waited for; matrix products, arithmetic and copies ran while one was open for 0% of the time, Pallas kernels for 29%

profile of v12, /device:TPU:0, one launch (start us, length us, event | category | flops | bytes accessed | tf_op | source)
XLA Modules:
  0.0 57.0 jit_solution(3567072661782412148)
XLA Ops:
  0.6 0.5 collective-permute-start
  1.7 1.2 %shard_map.212 = (f32[4,64,128]{2,1,0:T(8,128)S(1)}, f32[4,64,128]{2,1,0:T(8,128)S(1)}, s32[8,64,128]{2,1,0:T(8,128)S(1)}, f32[16,8,128]{2,1,0:T(8,128)S(1)}) custom-call(f32[8]{0:T(128)} %stiffness_in.3, f32[8]{0:T(128)} %density_in.3, f32[8]{0:T(128)} %refs_2_.2, f32[8,64,128]{2,1,0:T(8,128)} %refs_3_.3, f32[8,64,128]{2,1,0:T(8,128)} %refs_4_.2, ...), custom_call_target="tpu_custom_call" | custom-call | bytes 524288 | tf_op jit(solution)/shard_map/pallas_call | solution.py:566
  4.1 2.6 %collective-permute-start.4 = (bf16[4,64,256]{2,1,0:T(8,128)(2,1)S(1)}, bf16[4,64,256]{2,1,0:T(8,128)(2,1)S(1)}, u32[]{:S(2)}, u32[]{:S(2)}) collective-permute-start(bf16[4,64,256]{2,1,0:T(8,128)(2,1)S(1)} %get-tuple-element.70), channel_id=1, source_target_pairs={{1,5},{5,1},{4,8},{8,4},{9,13},{13,9},{0,2},{12,14},{3,7},{7,3},{6... | collective-permute-start | bytes 393224 | tf_op jit(solution)/shard_map/ppermute | solution.py:616
  6.7 2.3 %shard_map.214 = (f32[2,4,32,128]{3,2,1,0:T(8,128)S(1)}, bf16[256,128]{1,0:T(8,128)(2,1)S(1)}, bf16[2,32,256]{2,1,0:T(8,128)(2,1)S(1)}) custom-call(f32[512]{0:T(512)} %constant.31.clone.refs_0_.twiddles, f32[8]{0:T(128)} %stiffness_in.3, f32[8]{0:T(128)} %density_in.3, bf16[256,128]{1,0:T(8,128)(2,1)} %constant.32.clone.refs_3_, ...), custom_call_target="tpu_custom_call" | custom-call | flops 268435456 | bytes 2097152 | tf_op jit(solution)/shard_map/pallas_call | solution.py:606
  9.1 0.7 %collective-permute-done.4.refs_5_ = bf16[4,64,256]{2,1,0:T(8,128)(2,1)S(1)} collective-permute-done((bf16[4,64,256]{2,1,0:T(8,128)(2,1)S(1)}, bf16[4,64,256]{2,1,0:T(8,128)(2,1)S(1)}, u32[]{:S(2)}, u32[]{:S(2)}) %collective-permute-start.4) | collective-permute-done | bytes 131104 | tf_op jit(solution)/shard_map/ppermute | solution.py:616
  9.8 0.7 %collective-permute-done.5.refs_6_ = bf16[4,8,256]{2,1,0:T(8,128)(2,1)S(1)} collective-permute-done((bf16[4,8,256]{2,1,0:T(8,128)(2,1)S(1)}, bf16[4,8,256]{2,1,0:T(8,128)(2,1)S(1)}, u32[]{:S(2)}, u32[]{:S(2)}) %collective-permute-start.5) | collective-permute-done | bytes 16416 | tf_op jit(solution)/shard_map/ppermute | solution.py:618
  10.4 1.0 %shard_map.215 = (f32[4,64,256]{2,1,0:T(8,128)S(1)}, bf16[4,64,256]{2,1,0:T(8,128)(2,1)S(1)}, bf16[4,8,256]{2,1,0:T(8,128)(2,1)S(1)}) custom-call(f32[4,64,256]{2,1,0:T(8,128)S(1)} %get-tuple-element.66.refs_0_.refs_1_, f32[4,64,256]{2,1,0:T(8,128)S(1)} %get-tuple-element.67.refs_1_, f32[4,64,256]{2,1,0:T(8,128)S(1)} %get-tuple-element.68.refs_2_, ...), custom_call_target="tpu_custom_call" | custom-call | flops 3932160 | bytes 1835008 | tf_op jit(solution)/shard_map/pallas_call | solution.py:631
  11.5 1.6 %collective-permute-start.7 = (bf16[4,64,256]{2,1,0:T(8,128)(2,1)S(1)}, bf16[4,64,256]{2,1,0:T(8,128)(2,1)S(1)}, u32[]{:S(2)}, u32[]{:S(2)}) collective-permute-start(bf16[4,64,256]{2,1,0:T(8,128)(2,1)S(1)} %get-tuple-element.76), channel_id=1, source_target_pairs={{1,5},{5,1},{4,8},{8,4},{9,13},{13,9},{0,2},{12,14},{3,7},{7,3},{6... | collective-permute-start | bytes 393224 | tf_op jit(solution)/shard_map/ppermute | solution.py:616
  13.6 3.3 %collective-permute-done.8.refs_6_ = bf16[4,8,256]{2,1,0:T(8,128)(2,1)S(1)} collective-permute-done((bf16[4,8,256]{2,1,0:T(8,128)(2,1)S(1)}, bf16[4,8,256]{2,1,0:T(8,128)(2,1)S(1)}, u32[]{:S(2)}, u32[]{:S(2)}) %collective-permute-start.8) | collective-permute-done | bytes 16416 | tf_op jit(solution)/shard_map/ppermute | solution.py:618
  16.9 1.0 %shard_map.216 = (f32[4,64,256]{2,1,0:T(8,128)S(1)}, bf16[4,64,256]{2,1,0:T(8,128)(2,1)S(1)}, bf16[4,8,256]{2,1,0:T(8,128)(2,1)S(1)}) custom-call(f32[4,64,256]{2,1,0:T(8,128)S(1)} %get-tuple-element.75.refs_0_.refs_1_, f32[4,64,256]{2,1,0:T(8,128)S(1)} %get-tuple-element.66.refs_0_.refs_1_, f32[4,64,256]{2,1,0:T(8,128)S(1)} %get-tuple-element.68.refs_2_, ...), custom_call_target="tpu_custom_call" | custom-call | flops 3932160 | bytes 1835008 | tf_op jit(solution)/shard_map/pallas_call | solution.py:631
  18.0 1.6 %collective-permute-start.10 = (bf16[4,64,256]{2,1,0:T(8,128)(2,1)S(1)}, bf16[4,64,256]{2,1,0:T(8,128)(2,1)S(1)}, u32[]{:S(2)}, u32[]{:S(2)}) collective-permute-start(bf16[4,64,256]{2,1,0:T(8,128)(2,1)S(1)} %get-tuple-element.79), channel_id=1, source_target_pairs={{1,5},{5,1},{4,8},{8,4},{9,13},{13,9},{0,2},{12,14},{3,7},{7,3},{6... | collective-permute-start | bytes 393224 | tf_op jit(solution)/shard_map/ppermute | solution.py:616
  19.6 0.5 collective-permute-start.11
  20.0 3.3 %collective-permute-done.11.refs_6_ = bf16[4,8,256]{2,1,0:T(8,128)(2,1)S(1)} collective-permute-done((bf16[4,8,256]{2,1,0:T(8,128)(2,1)S(1)}, bf16[4,8,256]{2,1,0:T(8,128)(2,1)S(1)}, u32[]{:S(2)}, u32[]{:S(2)}) %collective-permute-start.11) | collective-permute-done | bytes 16416 | tf_op jit(solution)/shard_map/ppermute | solution.py:618
  23.3 1.0 %shard_map.217 = (f32[4,64,256]{2,1,0:T(8,128)S(1)}, bf16[4,64,256]{2,1,0:T(8,128)(2,1)S(1)}, bf16[4,8,256]{2,1,0:T(8,128)(2,1)S(1)}) custom-call(f32[4,64,256]{2,1,0:T(8,128)S(1)} %get-tuple-element.78.refs_0_.refs_1_, f32[4,64,256]{2,1,0:T(8,128)S(1)} %get-tuple-element.75.refs_0_.refs_1_, f32[4,64,256]{2,1,0:T(8,128)S(1)} %get-tuple-element.68.refs_2_, ...), custom_call_target="tpu_custom_call" | custom-call | flops 3932160 | bytes 1835008 | tf_op jit(solution)/shard_map/pallas_call | solution.py:631
  24.4 1.6 %collective-permute-start.13 = (bf16[4,64,256]{2,1,0:T(8,128)(2,1)S(1)}, bf16[4,64,256]{2,1,0:T(8,128)(2,1)S(1)}, u32[]{:S(2)}, u32[]{:S(2)}) collective-permute-start(bf16[4,64,256]{2,1,0:T(8,128)(2,1)S(1)} %get-tuple-element.82), channel_id=1, source_target_pairs={{1,5},{5,1},{4,8},{8,4},{9,13},{13,9},{0,2},{12,14},{3,7},{7,3},{6... | collective-permute-start | bytes 393224 | tf_op jit(solution)/shard_map/ppermute | solution.py:616
  26.0 0.5 collective-permute-start.14
  26.5 1.1 %shard_map.218.prior = f32[4,32,128]{2,1,0:T(8,128)S(1)} custom-call(f32[512]{0:T(512)} %constant.31.clone.refs_0_.twiddles, f32[4,64,256]{2,1,0:T(8,128)S(1)} %get-tuple-element.81.own.refs_0_.q_ref, f32[4,64,256]{2,1,0:T(8,128)S(1)} %collective-permute-done.12.mate.refs_4_.q_mate, bf16[256,128]{1,0:T(8,128)(2,1)S(1)} %get-tuple-element.83.table_z, ...), custom_call_target="tpu_custom_call" | custom-call | flops 134217728 | bytes 1048576 | tf_op jit(solution)/shard_map/pallas_call | solution.py:624
  27.6 2.0 %collective-permute-done.13.refs_5_ = bf16[4,64,256]{2,1,0:T(8,128)(2,1)S(1)} collective-permute-done((bf16[4,64,256]{2,1,0:T(8,128)(2,1)S(1)}, bf16[4,64,256]{2,1,0:T(8,128)(2,1)S(1)}, u32[]{:S(2)}, u32[]{:S(2)}) %collective-permute-start.13) | collective-permute-done | bytes 131104 | tf_op jit(solution)/shard_map/ppermute | solution.py:616
  29.8 1.0 %shard_map.219.own.p_ref = f32[4,64,256]{2,1,0:T(8,128)S(1)} custom-call(f32[4,64,256]{2,1,0:T(8,128)S(1)} %get-tuple-element.81.own.refs_0_.q_ref, f32[4,64,256]{2,1,0:T(8,128)S(1)} %get-tuple-element.78.refs_0_.refs_1_, f32[4,64,256]{2,1,0:T(8,128)S(1)} %get-tuple-element.68.refs_2_, f32[4,64,256]{2,1,0:T(8,128)S(1)} %get-tuple-element.69.refs_3_, ...), custom_call_target="tpu_custom_call" | custom-call | flops 3932160 | bytes 1835008 | tf_op jit(solution)/shard_map/pallas_call | solution.py:631
  30.8 0.9 %shard_map.220 = (f32[4,4,32,128]{3,2,1,0:T(8,128)S(1)}, bf16[1,4,32,128]{3,2,1,0:T(8,128)(2,1)S(1)}) custom-call(f32[512]{0:T(512)} %constant.31.clone.refs_0_.twiddles, f32[4,64,256]{2,1,0:T(8,128)S(1)} %shard_map.219.own.p_ref, f32[4,32,128]{2,1,0:T(8,128)S(1)} %shard_map.218.prior, f32[2,4,32,128]{3,2,1,0:T(8,128)S(1)} %get-tuple-element.88.early, ...), custom_call_target="tpu_custom_call" | custom-call | flops 67108864 | bytes 524288 | tf_op jit(solution)/shard_map/pallas_call | solution.py:639
  31.8 0.5 collective-permute-start.18
  32.3 0.7 %collective-permute-done.15 = bf16[1,4,32,128]{3,2,1,0:T(8,128)(2,1)S(1)} collective-permute-done((bf16[1,4,32,128]{3,2,1,0:T(8,128)(2,1)S(1)}, bf16[1,4,32,128]{3,2,1,0:T(8,128)(2,1)S(1)}, u32[]{:S(2)}, u32[]{:S(2)}) %collective-permute-start.15) | collective-permute-done | bytes 32800 | tf_op jit(solution)/shard_map/ppermute | solution.py:600
  33.0 1.6 %collective-permute-start.16 = (bf16[4,4,32,128]{3,2,1,0:T(8,128)(2,1)S(1)}, bf16[4,4,32,128]{3,2,1,0:T(8,128)(2,1)S(1)}, u32[]{:S(2)}, u32[]{:S(2)}) collective-permute-start(bf16[4,4,32,128]{3,2,1,0:T(8,128)(2,1)S(1)} %fusion), channel_id=1, source_target_pairs={{0,2},{2,0},{1,3},{3,1},{4,6},{6,4},{5,7},{7,5},{8,10},{10,8},{9,1... | collective-permute-start | bytes 393224 | tf_op jit(solution)/shard_map/ppermute | solution.py:603
  34.6 2.8 %shard_map.221 = (bf16[80,64]{1,0:T(8,128)(2,1)S(1)}, bf16[80,128]{1,0:T(8,128)(2,1)S(1)}, f32[24,8]{1,0:T(8,128)S(1)}, f32[80,1]{1,0:T(8,128)S(1)}) custom-call(f32[8]{0:T(128)} %stiffness_in.3, f32[8]{0:T(128)} %density_in.3, f32[2,20,8,20]{3,2,1,0:T(8,128)} %bitcast.4, f32[4,20]{1,0:T(4,128)} %refs_3_.4, f32[1,20]{1,0:T(1,128)} %bitcast.5, ...), custom_call_target="tpu_custom_call" | custom-call | flops 2000000000 | bytes 4000000 | tf_op jit(solution)/shard_map/pallas_call | solution.py:582
  37.5 1.2 %collective-permute-done.16 = bf16[4,4,32,128]{3,2,1,0:T(8,128)(2,1)S(1)} collective-permute-done((bf16[4,4,32,128]{3,2,1,0:T(8,128)(2,1)S(1)}, bf16[4,4,32,128]{3,2,1,0:T(8,128)(2,1)S(1)}, u32[]{:S(2)}, u32[]{:S(2)}) %collective-permute-start.16) | collective-permute-done | bytes 131104 | tf_op jit(solution)/shard_map/ppermute | solution.py:603
  38.7 0.9 %collective-permute-start.17 = (bf16[4,4,32,128]{3,2,1,0:T(8,128)(2,1)S(1)}, bf16[4,4,32,128]{3,2,1,0:T(8,128)(2,1)S(1)}, u32[]{:S(2)}, u32[]{:S(2)}) collective-permute-start(bf16[4,4,32,128]{3,2,1,0:T(8,128)(2,1)S(1)} %fusion.2), channel_id=1, source_target_pairs={{0,4},{4,0},{8,12},{12,8},{1,5},{5,1},{9,13},{13,9},{2,6},{6,2},{1... | collective-permute-start | bytes 393224 | tf_op jit(solution)/shard_map/ppermute | solution.py:603
  39.6 0.7 %shard_map.223 = f32[8,64,128]{2,1,0:T(8,128)} custom-call(f32[4,64,256]{2,1,0:T(8,128)S(1)} %shard_map.219.own.p_ref, f32[4,64,256]{2,1,0:T(8,128)S(1)} %collective-permute-done.18.p_mate.other), custom_call_target="tpu_custom_call" | custom-call | bytes 786432 | tf_op jit(solution)/shard_map/pallas_call | solution.py:671
  40.3 3.4 %shard_map.222.rest_0_ = f32[80,64,256]{2,1,0:T(8,128)S(1)} custom-call(f32[8]{0:T(128)} %stiffness_in.3, f32[8]{0:T(128)} %density_in.3, f32[4,64,256]{2,1,0:T(8,128)S(1)} %shard_map.219.own.p_ref, f32[4,64,256]{2,1,0:T(8,128)S(1)} %get-tuple-element.81.own.refs_0_.q_ref, f32[4,64,256]{2,1,0:T(8,128)S(1)} %collective-permute-done.18.p_mate.other, ...), custom_call_target="tpu_custom_call" | custom-call | flops 1310720000 | bytes 3276800 | tf_op jit(solution)/shard_map/pallas_call | solution.py:650
  43.8 3.1 %collective-permute-start.19 = (bf16[4,4,32,128]{3,2,1,0:T(8,128)(2,1)S(1)}, bf16[4,4,32,128]{3,2,1,0:T(8,128)(2,1)S(1)}, u32[]{:S(2)}, u32[]{:S(2)}) collective-permute-start(bf16[4,4,32,128]{3,2,1,0:T(8,128)(2,1)S(1)} %fusion.1), channel_id=1, source_target_pairs={{0,12},{4,8},{8,4},{12,0},{1,13},{5,9},{9,5},{13,1},{2,14},{6,10},... | collective-permute-start | bytes 393224 | tf_op jit(solution)/shard_map/ppermute | solution.py:603
  47.4 3.4 %shard_map.224.local = f32[80,64,256]{2,1,0:T(8,128)S(1)} custom-call(f32[8]{0:T(128)} %stiffness_in.3, f32[8]{0:T(128)} %density_in.3, f32[4,64,256]{2,1,0:T(8,128)S(1)} %shard_map.219.own.p_ref, f32[4,64,256]{2,1,0:T(8,128)S(1)} %get-tuple-element.81.own.refs_0_.q_ref, ...), custom_call_target="tpu_custom_call", output_to_operand_aliasing={{}: (10, {})} | custom-call | flops 1310720000 | bytes 3276800 | tf_op jit(solution)/shard_map/pallas_call | solution.py:650
  51.0 0.9 %shard_map.226.waves_own = bf16[1024,512]{1,0:T(8,128)(2,1)S(1)} custom-call(f32[4,4,32,128]{3,2,1,0:T(8,128)S(1)} %get-tuple-element.109.mine, bf16[2,64,64]{2,1,0:T(8,128)(2,1)S(1)} %copy-done.1, bf16[128,512]{1,0:T(8,128)(2,1)S(1)} %copy-done), custom_call_target="tpu_custom_call" | custom-call | flops 1000000000 | bytes 2000000 | tf_op jit(solution)/shard_map/pallas_call | solution.py:684
  52.3 4.7 %shard_map.227 = bf16[4,20,64,256]{3,2,1,0:T(8,128)(2,1)} custom-call(bf16[1024,512]{1,0:T(8,128)(2,1)S(1)} %shard_map.226.waves_own, bf16[4,4,32,128]{3,2,1,0:T(8,128)(2,1)S(1)} %collective-permute-done.20.other, f32[80,64,256]{2,1,0:T(8,128)S(1)} %shard_map.224.local, bf16[640,512]{1,0:T(8,128)(2,1)S(1)} %shard_map.225.left, ...), custom_call_target="tpu_custom_call" | custom-call | flops 131072000 | bytes 3932160 | tf_op jit(solution)/shard_map/pallas_call | solution.py:689
  (36 shorter events, 3.9 us)
Async XLA Ops:
  0.6 2.2 %collective-permute-start = (f32[8,64,128]{2,1,0:T(8,128)}, f32[8,64,128]{2,1,0:T(8,128)S(1)}, u32[]{:S(2)}, u32[]{:S(2)}) collective-permute-start(f32[8,64,128]{2,1,0:T(8,128)} %refs_3_.3), channel_id=1, source_target_pairs={{0,1},{1,0},{2,3},{3,2},{4,5},{5,4},{6,7},{7,6},{8,9},{9,8},{10,11... | collective-permute-start | bytes 786440 | tf_op jit(solution)/shard_map/ppermute | solution.py:563
  1.1 1.7 %collective-permute-start.1 = (f32[8,64,128]{2,1,0:T(8,128)}, f32[8,64,128]{2,1,0:T(8,128)S(1)}, u32[]{:S(2)}, u32[]{:S(2)}) collective-permute-start(f32[8,64,128]{2,1,0:T(8,128)} %refs_4_.2), channel_id=1, source_target_pairs={{0,1},{1,0},{2,3},{3,2},{4,5},{5,4},{6,7},{7,6},{8,9},{9,8},{10,11... | collective-permute-start | bytes 786440 | tf_op jit(solution)/shard_map/ppermute | solution.py:563
  1.2 2.0 %collective-permute-start.2 = (s32[8,64,128]{2,1,0:T(8,128)}, s32[8,64,128]{2,1,0:T(8,128)S(1)}, u32[]{:S(2)}, u32[]{:S(2)}) collective-permute-start(s32[8,64,128]{2,1,0:T(8,128)} %refs_5_.2), channel_id=1, source_target_pairs={{0,1},{1,0},{2,3},{3,2},{4,5},{5,4},{6,7},{7,6},{8,9},{9,8},{10,11... | collective-permute-start | bytes 786440 | tf_op jit(solution)/shard_map/ppermute | solution.py:563
  3.6 6.8 %collective-permute-start.3 = (f32[4,64,256]{2,1,0:T(8,128)S(1)}, f32[4,64,256]{2,1,0:T(8,128)S(1)}, u32[]{:S(2)}, u32[]{:S(2)}) collective-permute-start(f32[4,64,256]{2,1,0:T(8,128)S(1)} %get-tuple-element.66.refs_0_.refs_1_), channel_id=1, source_target_pairs={{0,1},{1,0},{2,3},{3,2},{4,5},{5,4},{6,7},{7,6},{8,9},{9,8},{10,11... | collective-permute-start | bytes 786440 | tf_op jit(solution)/shard_map/ppermute | solution.py:600
  4.1 5.7 %collective-permute-start.4 = (bf16[4,64,256]{2,1,0:T(8,128)(2,1)S(1)}, bf16[4,64,256]{2,1,0:T(8,128)(2,1)S(1)}, u32[]{:S(2)}, u32[]{:S(2)}) collective-permute-start(bf16[4,64,256]{2,1,0:T(8,128)(2,1)S(1)} %get-tuple-element.70), channel_id=1, source_target_pairs={{1,5},{5,1},{4,8},{8,4},{9,13},{13,9},{0,2},{12,14},{3,7},{7,3},{6... | collective-permute-start | bytes 393224 | tf_op jit(solution)/shard_map/ppermute | solution.py:616
  6.7 3.7 %collective-permute-start.5 = (bf16[4,8,256]{2,1,0:T(8,128)(2,1)S(1)}, bf16[4,8,256]{2,1,0:T(8,128)(2,1)S(1)}, u32[]{:S(2)}, u32[]{:S(2)}) collective-permute-start(bf16[4,8,256]{2,1,0:T(8,128)(2,1)S(1)} %get-tuple-element.74), channel_id=1, source_target_pairs={{0,2},{2,0},{1,3},{3,1},{4,6},{6,4},{5,7},{7,5},{8,10},{10,8},{9,1... | collective-permute-start | bytes 49160 | tf_op jit(solution)/shard_map/ppermute | solution.py:618
  11.4 5.5 %collective-permute-start.6 = (f32[4,64,256]{2,1,0:T(8,128)S(1)}, f32[4,64,256]{2,1,0:T(8,128)S(1)}, u32[]{:S(2)}, u32[]{:S(2)}) collective-permute-start(f32[4,64,256]{2,1,0:T(8,128)S(1)} %get-tuple-element.75.refs_0_.refs_1_), channel_id=1, source_target_pairs={{0,1},{1,0},{2,3},{3,2},{4,5},{5,4},{6,7},{7,6},{8,9},{9,8},{10,11... | collective-permute-start | bytes 786440 | tf_op jit(solution)/shard_map/ppermute | solution.py:600
  11.5 5.4 %collective-permute-start.7 = (bf16[4,64,256]{2,1,0:T(8,128)(2,1)S(1)}, bf16[4,64,256]{2,1,0:T(8,128)(2,1)S(1)}, u32[]{:S(2)}, u32[]{:S(2)}) collective-permute-start(bf16[4,64,256]{2,1,0:T(8,128)(2,1)S(1)} %get-tuple-element.76), channel_id=1, source_target_pairs={{1,5},{5,1},{4,8},{8,4},{9,13},{13,9},{0,2},{12,14},{3,7},{7,3},{6... | collective-permute-start | bytes 393224 | tf_op jit(solution)/shard_map/ppermute | solution.py:616
  13.1 3.8 %collective-permute-start.8 = (bf16[4,8,256]{2,1,0:T(8,128)(2,1)S(1)}, bf16[4,8,256]{2,1,0:T(8,128)(2,1)S(1)}, u32[]{:S(2)}, u32[]{:S(2)}) collective-permute-start(bf16[4,8,256]{2,1,0:T(8,128)(2,1)S(1)} %get-tuple-element.77), channel_id=1, source_target_pairs={{0,2},{2,0},{1,3},{3,1},{4,6},{6,4},{5,7},{7,5},{8,10},{10,8},{9,1... | collective-permute-start | bytes 49160 | tf_op jit(solution)/shard_map/ppermute | solution.py:618
  17.9 5.5 %collective-permute-start.9 = (f32[4,64,256]{2,1,0:T(8,128)S(1)}, f32[4,64,256]{2,1,0:T(8,128)S(1)}, u32[]{:S(2)}, u32[]{:S(2)}) collective-permute-start(f32[4,64,256]{2,1,0:T(8,128)S(1)} %get-tuple-element.78.refs_0_.refs_1_), channel_id=1, source_target_pairs={{0,1},{1,0},{2,3},{3,2},{4,5},{5,4},{6,7},{7,6},{8,9},{9,8},{10,11... | collective-permute-start | bytes 786440 | tf_op jit(solution)/shard_map/ppermute | solution.py:600
  18.0 5.4 %collective-permute-start.10 = (bf16[4,64,256]{2,1,0:T(8,128)(2,1)S(1)}, bf16[4,64,256]{2,1,0:T(8,128)(2,1)S(1)}, u32[]{:S(2)}, u32[]{:S(2)}) collective-permute-start(bf16[4,64,256]{2,1,0:T(8,128)(2,1)S(1)} %get-tuple-element.79), channel_id=1, source_target_pairs={{1,5},{5,1},{4,8},{8,4},{9,13},{13,9},{0,2},{12,14},{3,7},{7,3},{6... | collective-permute-start | bytes 393224 | tf_op jit(solution)/shard_map/ppermute | solution.py:616
  19.6 3.8 %collective-permute-start.11 = (bf16[4,8,256]{2,1,0:T(8,128)(2,1)S(1)}, bf16[4,8,256]{2,1,0:T(8,128)(2,1)S(1)}, u32[]{:S(2)}, u32[]{:S(2)}) collective-permute-start(bf16[4,8,256]{2,1,0:T(8,128)(2,1)S(1)} %get-tuple-element.80), channel_id=1, source_target_pairs={{0,2},{2,0},{1,3},{3,1},{4,6},{6,4},{5,7},{7,5},{8,10},{10,8},{9,1... | collective-permute-start | bytes 49160 | tf_op jit(solution)/shard_map/ppermute | solution.py:618
  24.3 2.2 %collective-permute-start.12 = (f32[4,64,256]{2,1,0:T(8,128)S(1)}, f32[4,64,256]{2,1,0:T(8,128)S(1)}, u32[]{:S(2)}, u32[]{:S(2)}) collective-permute-start(f32[4,64,256]{2,1,0:T(8,128)S(1)} %get-tuple-element.81.own.refs_0_.q_ref), channel_id=1, source_target_pairs={{0,1},{1,0},{2,3},{3,2},{4,5},{5,4},{6,7},{7,6},{8,9},{9,8},{10,11... | collective-permute-start | bytes 786440 | tf_op jit(solution)/shard_map/ppermute | solution.py:600
  24.4 5.2 %collective-permute-start.13 = (bf16[4,64,256]{2,1,0:T(8,128)(2,1)S(1)}, bf16[4,64,256]{2,1,0:T(8,128)(2,1)S(1)}, u32[]{:S(2)}, u32[]{:S(2)}) collective-permute-start(bf16[4,64,256]{2,1,0:T(8,128)(2,1)S(1)} %get-tuple-element.82), channel_id=1, source_target_pairs={{1,5},{5,1},{4,8},{8,4},{9,13},{13,9},{0,2},{12,14},{3,7},{7,3},{6... | collective-permute-start | bytes 393224 | tf_op jit(solution)/shard_map/ppermute | solution.py:616
  26.0 3.8 %collective-permute-start.14 = (bf16[4,8,256]{2,1,0:T(8,128)(2,1)S(1)}, bf16[4,8,256]{2,1,0:T(8,128)(2,1)S(1)}, u32[]{:S(2)}, u32[]{:S(2)}) collective-permute-start(bf16[4,8,256]{2,1,0:T(8,128)(2,1)S(1)} %get-tuple-element.86), channel_id=1, source_target_pairs={{0,2},{2,0},{1,3},{3,1},{4,6},{6,4},{5,7},{7,5},{8,10},{10,8},{9,1... | collective-permute-start | bytes 49160 | tf_op jit(solution)/shard_map/ppermute | solution.py:618
  31.7 1.3 %collective-permute-start.15 = (bf16[1,4,32,128]{3,2,1,0:T(8,128)(2,1)S(1)}, bf16[1,4,32,128]{3,2,1,0:T(8,128)(2,1)S(1)}, u32[]{:S(2)}, u32[]{:S(2)}) collective-permute-start(bf16[1,4,32,128]{3,2,1,0:T(8,128)(2,1)S(1)} %get-tuple-element.90), channel_id=1, source_target_pairs={{0,1},{1,0},{2,3},{3,2},{4,5},{5,4},{6,7},{7,6},{8,9},{9,8},{10,11... | collective-permute-start | bytes 98312 | tf_op jit(solution)/shard_map/ppermute | solution.py:600
  31.8 7.8 %collective-permute-start.18 = (f32[4,64,256]{2,1,0:T(8,128)S(1)}, f32[4,64,256]{2,1,0:T(8,128)S(1)}, u32[]{:S(2)}, u32[]{:S(2)}) collective-permute-start(f32[4,64,256]{2,1,0:T(8,128)S(1)} %shard_map.219.own.p_ref), channel_id=1, source_target_pairs={{0,1},{1,0},{2,3},{3,2},{4,5},{5,4},{6,7},{7,6},{8,9},{9,8},{10,11... | collective-permute-start | bytes 786440 | tf_op jit(solution)/shard_map/ppermute | solution.py:600
  33.0 5.6 %collective-permute-start.16 = (bf16[4,4,32,128]{3,2,1,0:T(8,128)(2,1)S(1)}, bf16[4,4,32,128]{3,2,1,0:T(8,128)(2,1)S(1)}, u32[]{:S(2)}, u32[]{:S(2)}) collective-permute-start(bf16[4,4,32,128]{3,2,1,0:T(8,128)(2,1)S(1)} %fusion), channel_id=1, source_target_pairs={{0,2},{2,0},{1,3},{3,1},{4,6},{6,4},{5,7},{7,5},{8,10},{10,8},{9,1... | collective-permute-start | bytes 393224 | tf_op jit(solution)/shard_map/ppermute | solution.py:603
  37.5 9.5 %copy-start.2 = (bf16[640,80]{1,0:T(8,128)(2,1)S(1)}, bf16[640,80]{1,0:T(8,128)(2,1)}, u32[]{:S(2)}) copy-start(bf16[640,80]{1,0:T(8,128)(2,1)} %constant.34.clone.repeat_ref) | copy-start | bytes 307204
  38.7 5.0 %collective-permute-start.17 = (bf16[4,4,32,128]{3,2,1,0:T(8,128)(2,1)S(1)}, bf16[4,4,32,128]{3,2,1,0:T(8,128)(2,1)S(1)}, u32[]{:S(2)}, u32[]{:S(2)}) collective-permute-start(bf16[4,4,32,128]{3,2,1,0:T(8,128)(2,1)S(1)} %fusion.2), channel_id=1, source_target_pairs={{0,4},{4,0},{8,12},{12,8},{1,5},{5,1},{9,13},{13,9},{2,6},{6,2},{1... | collective-permute-start | bytes 393224 | tf_op jit(solution)/shard_map/ppermute | solution.py:603
  43.8 7.0 %collective-permute-start.19 = (bf16[4,4,32,128]{3,2,1,0:T(8,128)(2,1)S(1)}, bf16[4,4,32,128]{3,2,1,0:T(8,128)(2,1)S(1)}, u32[]{:S(2)}, u32[]{:S(2)}) collective-permute-start(bf16[4,4,32,128]{3,2,1,0:T(8,128)(2,1)S(1)} %fusion.1), channel_id=1, source_target_pairs={{0,12},{4,8},{8,4},{12,0},{1,13},{5,9},{9,5},{13,1},{2,14},{6,10},... | collective-permute-start | bytes 393224 | tf_op jit(solution)/shard_map/ppermute | solution.py:603
  47.4 3.6 %copy-start = (bf16[128,512]{1,0:T(8,128)(2,1)S(1)}, bf16[128,512]{1,0:T(8,128)(2,1)}, u32[]{:S(2)}) copy-start(bf16[128,512]{1,0:T(8,128)(2,1)} %constant.36.clone.table_z) | copy-start | bytes 393220
  47.4 3.6 %copy-start.1 = (bf16[2,64,64]{2,1,0:T(8,128)(2,1)S(1)}, bf16[2,64,64]{2,1,0:T(8,128)(2,1)}, u32[]{:S(2)}) copy-start(bf16[2,64,64]{2,1,0:T(8,128)(2,1)} %constant.35.clone.table_y) | copy-start | bytes 49156
  50.9 1.4 %collective-permute-start.20 = (bf16[4,4,32,128]{3,2,1,0:T(8,128)(2,1)S(1)}, bf16[4,4,32,128]{3,2,1,0:T(8,128)(2,1)S(1)}, u32[]{:S(2)}, u32[]{:S(2)}) collective-permute-start(bf16[4,4,32,128]{3,2,1,0:T(8,128)(2,1)S(1)} %get-tuple-element.108), channel_id=1, source_target_pairs={{0,1},{1,0},{2,3},{3,2},{4,5},{5,4},{6,7},{7,6},{8,9},{9,8},{10,11... | collective-permute-start | bytes 393224 | tf_op jit(solution)/shard_map/ppermute | solution.py:600
